TPU v7x, 32 devices: a whole 2x2x4 slice. The times are simulated.
32 devices in a mesh: dp: 8 (over z, y), mp: 4 (over x, core).
Axes of the slice: x: 2, y: 2, z: 4, core: 2. Of those that a mesh axis runs over, the one named last changes fastest.
Arguments:
- inputs: bfloat16 [4, 40, 197, 768], P(None, 'dp'), may hold values from -6 to 6
- cotangent: bfloat16 [4, 40, 197, 768], P(None, 'dp'), may hold values from -6 to 6
- counts: int32 [4, 8], P(None, 'dp'), may hold values from 3 to 5, as said below
- norm_gain: float32 [768], replicated, may hold values from 0.5 to 1.5
- norm_shift: float32 [768], replicated, may hold values from -1.75 to 1.75
- qkv_weight: bfloat16 [768, 2304], P('dp', 'mp'), may hold values from -0.21875 to 0.21875
- query_bias: float32 [768], P('mp'), may hold values from -1.75 to 1.75
- value_bias: float32 [768], P('mp'), may hold values from -1.75 to 1.75
- out_weight: bfloat16 [768, 768], P('mp', 'dp'), may hold values from -0.875 to 0.875
- out_bias: float32 [768], replicated, may hold values from -1.75 to 1.75
- mlp_gain: float32 [768], replicated, may hold values from 0.5 to 1.5
- mlp_shift: float32 [768], replicated, may hold values from -1.75 to 1.75
- hidden_weight: bfloat16 [768, 3072], P('dp', 'mp'), may hold values from -0.21875 to 0.21875
- hidden_bias: float32 [3072], P('mp'), may hold values from -1.75 to 1.75
- down_weight: bfloat16 [3072, 768], P('mp', 'dp'), may hold values from -0.109375 to 0.109375
- down_bias: float32 [768], replicated, may hold values from -1.75 to 1.75
Outputs:
- block_out: bfloat16 [4, 40, 197, 768], P(None, 'dp')
- input_grad: bfloat16 [4, 40, 197, 768], P(None, 'dp')
- grad_norm_gain: float32 [768], replicated
- grad_norm_shift: float32 [768], replicated
- grad_qkv_weight: float32 [768, 2304], P('dp', 'mp')
- grad_query_bias: float32 [768], P('mp')
- grad_value_bias: float32 [768], P('mp')
- grad_out_weight: float32 [768, 768], P('mp', 'dp')
- grad_out_bias: float32 [768], replicated
- grad_mlp_gain: float32 [768], replicated
- grad_mlp_shift: float32 [768], replicated
- grad_hidden_weight: float32 [768, 3072], P('dp', 'mp')
- grad_hidden_bias: float32 [3072], P('mp')
- grad_down_weight: float32 [3072, 768], P('mp', 'dp')
- grad_down_bias: float32 [768], replicated
Inputs may be any that keep to these rules, and one draw needn't show every extreme that they name: Live images fill the first counts[m, b] slots of block b; in every micro-batch some block holds 5 live images.
All inputs are finite; a program needn't handle non-finite values.
Results may differ from a plain program's by a relative error of at most 0.019.
Values may be sent and summed in bfloat16 or wider, within the bound.
No kernel may reach another device: no remote copies, remote signals or barrier semaphores. Data moves between devices by JAX's collectives and lax.ppermute only.
A program may use at most 256 MiB of HBM per device.

v0:
```python
import jax
import jax.numpy as jnp
from jax import lax
from jax.sharding import PartitionSpec as P

HEAD_DIM = 64


NORM_EPS = 1e-06
CONTRACT_ROWS = (((0,), (0,)), ((), ()))
CONTRACT_COLS = (((1,), (1,)), ((), ()))


def norm_stats(values):
    center = jnp.mean(values, axis=-1, keepdims=True)
    offset = values - center
    spread = jnp.mean(offset * offset, axis=-1, keepdims=True)
    scale_inv = lax.rsqrt(spread + NORM_EPS)
    return (offset * scale_inv, scale_inv)


def norm_back(upstream, normal, scale_inv, gain_vec):
    scaled = upstream * gain_vec
    return scale_inv * (
        scaled
        - jnp.mean(scaled, axis=-1, keepdims=True)
        - normal * jnp.mean(scaled * normal, axis=-1, keepdims=True)
    )


def gelu_exact(values):
    return 0.5 * values * (1.0 + lax.erf(values * 0.7071067811865476))


def gelu_slope(values):
    return (
        0.5 * (1.0 + lax.erf(values * 0.7071067811865476))
        + values * jnp.exp(-0.5 * values * values) * 0.3989422804014327
    )


def rows_dot(former, latter):
    return lax.dot_general(former, latter, CONTRACT_ROWS, preferred_element_type=jnp.float32)


def cols_dot(former, latter):
    return lax.dot_general(former, latter, CONTRACT_COLS, preferred_element_type=jnp.float32)


def on_device(
    inputs,
    cotangent,
    counts,
    norm_gain,
    norm_shift,
    qkv_weight,
    query_bias,
    value_bias,
    out_weight,
    out_bias,
    mlp_gain,
    mlp_shift,
    hidden_weight,
    hidden_bias,
    down_weight,
    down_bias,
):
    batches, slot_count, length, model_width = inputs.shape
    row_count = slot_count * length
    qkv_cols = qkv_weight.shape[1]
    local_width = qkv_cols // 3
    local_heads = local_width // HEAD_DIM
    hidden_cols = hidden_weight.shape[1]
    qkv_shape = (slot_count, length, 3, local_heads, HEAD_DIM)
    slot_ids = jnp.arange(slot_count, dtype=jnp.int32)
    key_zeros = jnp.zeros((local_width,), jnp.float32)
    bias_row = jnp.concatenate([query_bias, key_zeros, value_bias])
    full_qkv = jnp.zeros((model_width, qkv_cols), jnp.float32)
    full_out = jnp.zeros((local_width, model_width), jnp.float32)
    full_hidden = jnp.zeros((model_width, hidden_cols), jnp.float32)
    full_down = jnp.zeros((hidden_cols, model_width), jnp.float32)
    width_zeros = jnp.zeros((model_width,), jnp.float32)
    sum_norm_gain = width_zeros
    sum_norm_shift = width_zeros
    sum_out_bias = width_zeros
    sum_mlp_gain = width_zeros
    sum_mlp_shift = width_zeros
    sum_down_bias = width_zeros
    sum_query_bias = jnp.zeros((local_width,), jnp.float32)
    sum_value_bias = jnp.zeros((local_width,), jnp.float32)
    sum_hidden_bias = jnp.zeros((hidden_cols,), jnp.float32)
    out_blocks = []
    grad_blocks = []
    for micro_step in range(batches):
        qkv_full, out_full, hidden_full, down_full = (
            lax.all_gather(qkv_weight, "dp", axis=0, tiled=True),
            lax.all_gather(out_weight, "dp", axis=1, tiled=True),
            lax.all_gather(hidden_weight, "dp", axis=0, tiled=True),
            lax.all_gather(down_weight, "dp", axis=1, tiled=True),
        )
        live_mask = (slot_ids < counts[micro_step, 0]).astype(jnp.float32)
        tokens = inputs[micro_step].reshape(row_count, model_width).astype(jnp.float32)
        normal_one, inv_one = norm_stats(tokens)
        normed_one = (normal_one * norm_gain + norm_shift).astype(jnp.bfloat16)
        projected = (
            jnp.dot(normed_one, qkv_full, preferred_element_type=jnp.float32) + bias_row
        ).astype(jnp.bfloat16)
        projected = projected.reshape(qkv_shape)
        queries = projected[:, :, 0]
        key_vecs = projected[:, :, 1]
        value_vecs = projected[:, :, 2]
        scores = (
            jnp.einsum("islh,itlh->ilst", queries, key_vecs, preferred_element_type=jnp.float32)
            * 0.125
        )
        row_max = jnp.max(scores, axis=-1, keepdims=True)
        exp_scores = jnp.exp(scores - row_max)
        exp_total = jnp.sum(exp_scores, axis=-1, keepdims=True)
        attn_probs = exp_scores / exp_total
        log_total = row_max + jnp.log(exp_total)
        mixed_low = jnp.einsum(
            "ilst,itlh->islh",
            attn_probs.astype(jnp.bfloat16),
            value_vecs,
            preferred_element_type=jnp.float32,
        ).astype(jnp.bfloat16)
        mixed_low = mixed_low.reshape(row_count, local_width)
        attended = lax.psum(
            jnp.dot(mixed_low, out_full, preferred_element_type=jnp.float32).astype(jnp.bfloat16),
            "mp",
        ).astype(jnp.float32)
        middle = tokens + (attended + out_bias)
        normal_two, inv_two = norm_stats(middle)
        normed_two = (normal_two * mlp_gain + mlp_shift).astype(jnp.bfloat16)
        pre_act = jnp.dot(normed_two, hidden_full, preferred_element_type=jnp.float32) + hidden_bias
        activated = gelu_exact(pre_act).astype(jnp.bfloat16)
        mlp_out = lax.psum(
            jnp.dot(activated, down_full, preferred_element_type=jnp.float32).astype(jnp.bfloat16),
            "mp",
        ).astype(jnp.float32)
        result = (middle + mlp_out + down_bias).reshape(slot_count, length, model_width)
        out_blocks.append((result * live_mask[:, None, None]).astype(jnp.bfloat16))
        qkv_back, out_back, hidden_back, down_back = (
            lax.all_gather(qkv_weight, "dp", axis=0, tiled=True),
            lax.all_gather(out_weight, "dp", axis=1, tiled=True),
            lax.all_gather(hidden_weight, "dp", axis=0, tiled=True),
            lax.all_gather(down_weight, "dp", axis=1, tiled=True),
        )
        upstream = (cotangent[micro_step].astype(jnp.float32) * live_mask[:, None, None]).reshape(
            row_count, model_width
        )
        upstream_low = upstream.astype(jnp.bfloat16)
        sum_down_bias = sum_down_bias + jnp.sum(upstream, axis=0)
        step_down = rows_dot(activated, upstream_low)
        act_grad = cols_dot(upstream_low, down_back)
        pre_grad = (act_grad * gelu_slope(pre_act)).astype(jnp.bfloat16)
        sum_hidden_bias = sum_hidden_bias + jnp.sum(pre_grad.astype(jnp.float32), axis=0)
        step_hidden = rows_dot(normed_two, pre_grad)
        normed_two_grad = lax.psum(
            cols_dot(pre_grad, hidden_back).astype(jnp.bfloat16), "mp"
        ).astype(jnp.float32)
        sum_mlp_gain = sum_mlp_gain + jnp.sum(normed_two_grad * normal_two, axis=0)
        sum_mlp_shift = sum_mlp_shift + jnp.sum(normed_two_grad, axis=0)
        middle_grad = upstream + norm_back(normed_two_grad, normal_two, inv_two, mlp_gain)
        middle_low = middle_grad.astype(jnp.bfloat16)
        sum_out_bias = sum_out_bias + jnp.sum(middle_grad, axis=0)
        step_out = rows_dot(mixed_low, middle_low)
        mixed_grad = cols_dot(middle_low, out_back).astype(jnp.bfloat16)
        mixed_grad = mixed_grad.reshape(slot_count, length, local_heads, HEAD_DIM)
        scores_again = (
            jnp.einsum("islh,itlh->ilst", queries, key_vecs, preferred_element_type=jnp.float32)
            * 0.125
        )
        probs_again = jnp.exp(scores_again - log_total)
        value_grad = jnp.einsum(
            "ilst,islh->itlh",
            probs_again.astype(jnp.bfloat16),
            mixed_grad,
            preferred_element_type=jnp.float32,
        )
        prob_grad = jnp.einsum(
            "islh,itlh->ilst", mixed_grad, value_vecs, preferred_element_type=jnp.float32
        )
        score_grad = (
            probs_again * (prob_grad - jnp.sum(probs_again * prob_grad, axis=-1, keepdims=True))
        ).astype(jnp.bfloat16)
        query_grad = (
            jnp.einsum("ilst,itlh->islh", score_grad, key_vecs, preferred_element_type=jnp.float32)
            * 0.125
        )
        key_grad = (
            jnp.einsum("ilst,islh->itlh", score_grad, queries, preferred_element_type=jnp.float32)
            * 0.125
        )
        qkv_grad = (
            jnp.stack([query_grad, key_grad, value_grad], axis=2)
            .astype(jnp.bfloat16)
            .reshape(row_count, qkv_cols)
        )
        column_sums = jnp.sum(qkv_grad.astype(jnp.float32), axis=0)
        sum_query_bias = sum_query_bias + column_sums[:local_width]
        sum_value_bias = sum_value_bias + column_sums[2 * local_width :]
        step_qkv = rows_dot(normed_one, qkv_grad)
        normed_one_grad = lax.psum(cols_dot(qkv_grad, qkv_back).astype(jnp.bfloat16), "mp").astype(
            jnp.float32
        )
        sum_norm_gain = sum_norm_gain + jnp.sum(normed_one_grad * normal_one, axis=0)
        sum_norm_shift = sum_norm_shift + jnp.sum(normed_one_grad, axis=0)
        token_grad = middle_grad + norm_back(normed_one_grad, normal_one, inv_one, norm_gain)
        grad_blocks.append(token_grad.reshape(slot_count, length, model_width).astype(jnp.bfloat16))
        full_qkv = full_qkv + step_qkv
        full_out = full_out + step_out
        full_hidden = full_hidden + step_hidden
        full_down = full_down + step_down
    shard_qkv, shard_out, shard_hidden, shard_down = (
        lax.psum_scatter(
            full_qkv.astype(jnp.bfloat16), "dp", scatter_dimension=0, tiled=True
        ).astype(jnp.float32),
        lax.psum_scatter(
            full_out.astype(jnp.bfloat16), "dp", scatter_dimension=1, tiled=True
        ).astype(jnp.float32),
        lax.psum_scatter(
            full_hidden.astype(jnp.bfloat16), "dp", scatter_dimension=0, tiled=True
        ).astype(jnp.float32),
        lax.psum_scatter(
            full_down.astype(jnp.bfloat16), "dp", scatter_dimension=1, tiled=True
        ).astype(jnp.float32),
    )
    (
        sum_norm_gain,
        sum_norm_shift,
        sum_query_bias,
        sum_value_bias,
        sum_out_bias,
        sum_mlp_gain,
        sum_mlp_shift,
        sum_hidden_bias,
        sum_down_bias,
    ) = lax.psum(
        (
            sum_norm_gain,
            sum_norm_shift,
            sum_query_bias,
            sum_value_bias,
            sum_out_bias,
            sum_mlp_gain,
            sum_mlp_shift,
            sum_hidden_bias,
            sum_down_bias,
        ),
        "dp",
    )
    return (
        jnp.stack(out_blocks, axis=0),
        jnp.stack(grad_blocks, axis=0),
        sum_norm_gain,
        sum_norm_shift,
        shard_qkv,
        sum_query_bias,
        sum_value_bias,
        shard_out,
        sum_out_bias,
        sum_mlp_gain,
        sum_mlp_shift,
        shard_hidden,
        sum_hidden_bias,
        shard_down,
        sum_down_bias,
    )


def solution(mesh):
    return jax.shard_map(
        on_device,
        mesh=mesh,
        in_specs=(
            P(None, "dp", None, None),
            P(None, "dp", None, None),
            P(None, "dp"),
            P(),
            P(),
            P("dp", "mp"),
            P("mp"),
            P("mp"),
            P("mp", "dp"),
            P(),
            P(),
            P(),
            P("dp", "mp"),
            P("mp"),
            P("mp", "dp"),
            P(),
        ),
        out_specs=(
            P(None, "dp", None, None),
            P(None, "dp", None, None),
            P(),
            P(),
            P("dp", "mp"),
            P("mp"),
            P("mp"),
            P("mp", "dp"),
            P(),
            P(),
            P(),
            P("dp", "mp"),
            P("mp"),
            P("mp", "dp"),
            P(),
        ),
        check_vma=False,
    )
```

profile of v0, /device:TPU:0, one launch (start us, length us, event | category | flops | bytes accessed | tf_op | source)
XLA Modules:
  0.0 1082.7 jit_solution(157889262844806807)
XLA Ops:
  8.1 58.7 %convert_reduce_fusion.18 = (f32[5,197]{1,0:T(8,128)S(1)}, f32[5,197]{1,0:T(8,128)S(1)}, f32[5,197]{1,0:T(8,128)S(1)}, f32[5,197]{1,0:T(8,128)S(1)}) fusion(bf16[4,5,197,768]{3,0,2,1:T(4,128)(2,1)} %param.16), kind=kLoop, calls=%fused_computation.196 | loop fusion | flops 6047900 | bytes 6067600 | tf_op jit(solution)/shard_map/reduce_sum | solution.py:15
  67.0 67.0 %multiply_reduce_fusion.15 = (f32[5,197]{1,0:T(8,128)S(1)}, f32[5,197]{1,0:T(8,128)S(1)}, f32[5,197]{1,0:T(8,128)}, f32[5,197]{1,0:T(8,128)}, f32[5,197,768]{2,1...) fusion(f32[5,197]{1,0:T(8,128)S(1)} %broadcast_multiply_fusion.3, ...), kind=kLoop, calls=%fused_computation.205 | loop fusion | flops 12099740 | bytes 18187040 | tf_op jit(solution)/shard_map/reduce_sum | solution.py:17
  137.2 34.5 %all_gather.8 = bf16[768,576]{1,0:T(8,128)(2,1)S(1)} all-gather(bf16[96,576]{1,0:T(8,128)(2,1)S(1)} %copy-done.117), channel_id=1, replica_groups=mesh['dp'=8,'mp'=4] {'dp'}, dimensions={0}, use_global_device_ids=true | all-gather | bytes 995328 | tf_op jit(solution)/shard_map/all_gather | solution.py:96
  185.9 31.0 %all_gather.9 = bf16[192,768]{0,1:T(8,128)(2,1)S(1)} all-gather(bf16[192,96]{0,1:T(8,128)(2,1)S(1)} %copy.133), channel_id=1, replica_groups=mesh['dp'=8,'mp'=4] {'dp'}, dimensions={1}, use_global_device_ids=true | all-gather | bytes 331776 | tf_op jit(solution)/shard_map/all_gather | solution.py:97
  223.6 5.2 reshape.699
  244.5 4.9 reshape.702
  263.9 4.8 reshape.705
  276.8 17.8 %fusion.220 = (bf16[1,5,197,768]{3,0,2,1:T(2,128)(2,1)S(1)}, bf16[1,5,197,768]{3,0,2,1:T(2,128)(2,1)S(1)}, bf16[1,5,197,768]{3,0,2,1:T(2,128)(2,1)}, bf16[1,5,197,768]{3,0,2,1:T(2,128)(2,1)}) fusion(bf16[4,5,197,768]{3,0,2,1:T(4,128)(2,1)} %param.17), kind=kLoop, calls=%fused_computation.446 | loop fusion | bytes 12103680 | tf_op jit(solution)/shard_map/slice | solution.py:149
  327.8 65.3 %all-reduce.12.cloned.1.call-done = (bf16[985,768]{1,0:T(8,128)(2,1)}, bf16[985,768]{1,0:T(8,128)(2,1)}, bf16[985,768]{1,0:T(8,128)(2,1)}, bf16[985,768]{1,0:T(8,128)(2,1)}) async-done(((bf16[985,768]{1,0:T(8,128)(2,1)}, bf16[985,768]{1,0:T(8,128)(2,1)}, bf16[985,768]{1,0:T(8,128)(2,1)}, bf16[985,768]{1,0:T(8,128)(2,1)}), (bf16[985,768]{1,0:T(8,128)(2,1)}, bf16[985,768]{1,0:T(8,128)(2,1)}, ...) | async-done | bytes 6051856 | tf_op jit(solution)/shard_map/psum | solution.py:128
  393.1 7.2 fusion.216
  415.7 5.9 multiply_convert_fusion.11
  421.6 6.0 convert_reduce_fusion.11
  454.3 55.3 %convert_reduce_fusion.20 = (bf16[5,197,768]{2,1,0:T(8,128)(2,1)}, bf16[5,197,768]{2,1,0:T(8,128)(2,1)}, bf16[5,197,768]{2,1,0:T(8,128)(2,1)}, bf16[5,197,768]{2,1,0:T(8,128)(2,1)}) fusion(f32[5,197]{1,0:T(8,128)S(1)} %add_rsqrt_fusion, f32[768]{0:T(1024)} %param.20, f32[768]{0:T(1024)S(1)} %copy-done.124, f32[5,197]{1,0:T(8,128)S(1)} %broadcast_multiply_fusion, ...), kind=kLoop, calls=%fused_computation.198 | loop fusion | flops 18155520 | bytes 12141344 | tf_op jit(solution)/shard_map/convert_element_type | solution.py:104
  557.1 13.3 %all-reduce.10.cloned.1.call-done = (bf16[985,768]{1,0:T(8,128)(2,1)}, bf16[985,768]{1,0:T(8,128)(2,1)}, bf16[985,768]{1,0:T(8,128)(2,1)}, bf16[985,768]{1,0:T(8,128)(2,1)}) async-done(((bf16[985,768]{1,0:T(8,128)(2,1)}, bf16[985,768]{1,0:T(8,128)(2,1)}, bf16[985,768]{1,0:T(8,128)(2,1)}, bf16[985,768]{1,0:T(8,128)(2,1)}), (bf16[985,768]{1,0:T(8,128)(2,1)}, bf16[985,768]{1,0:T(8,128)(2,1)}, ...) | async-done | bytes 6051856 | tf_op jit(solution)/shard_map/psum | solution.py:159
  570.5 5.6 fusion.66
  576.1 7.4 fusion.210
  598.8 4.8 fusion.208
  690.4 5.7 add_convert_fusion.14
  718.3 20.0 %reduce-scatter.13.cloned.1.call-done = bf16[96,192]{1,0:T(8,128)(2,1)} async-done(((bf16[768,192]{1,0:T(8,128)(2,1)}), bf16[96,192]{1,0:T(8,128)(2,1)}) %reduce-scatter.13.cloned.1.call-update) | async-done | bytes 36880
  739.9 65.2 %reduce-scatter.7.cloned.1.call-done = bf16[96,576]{1,0:T(8,128)(2,1)} async-done(((bf16[768,576]{1,0:T(8,128)(2,1)}), bf16[96,576]{1,0:T(8,128)(2,1)}) %reduce-scatter.7.cloned.1.call-update) | async-done | bytes 110608 | tf_op jit(solution)/shard_map/reduce_scatter | solution.py:216
  806.7 122.0 %all-reduce.8.cloned.1.call-done = (bf16[985,768]{1,0:T(8,128)(2,1)}, bf16[985,768]{1,0:T(8,128)(2,1)}, bf16[985,768]{1,0:T(8,128)(2,1)}, bf16[985,768]{1,0:T(8,...) async-done(((bf16[985,768]{1,0:T(8,128)(2,1)}, bf16[985,768]{1,0:T(8,128)(2,1)}, ...) | async-done | bytes 12103696 | tf_op jit(solution)/shard_map/psum | solution.py:137
  928.7 10.2 add_add_fusion.6
  953.0 8.2 fusion.67
  961.3 8.1 fusion.75
  972.9 9.4 convert_element_type.753
  982.3 5.0 convert_element_type.754
  987.3 5.0 convert_element_type.752
  992.2 9.7 convert_element_type.755
  1002.0 6.2 multiply_reduce_fusion.2
  1015.9 5.0 copy.181
  1020.9 16.6 %pad_maximum_fusion.1 = bf16[4,5,197,768]{3,0,2,1:T(4,128)(2,1)} fusion(bf16[1,5,197,768]{3,0,2,1:T(2,128)(2,1)} %convert_element_type.755, bf16[1,5,197,768]{3,0,2,1:T(2,128)(2,1)} %convert_element_type.754, bf16[1,5,197,768]{3,0,2,1:T(2,128)(2,1)} %convert_element_type.753, bf16[1,5,197,768]{3,0,2,1:T(2,128)(2,1)} %convert_element_type.752), kind=kLoop, calls=%fused_computation.1 | loop fusion | flops 24207360 | bytes 12103680 | tf_op jit(solution)/shard_map/stack | solution.py:255
  1037.5 37.7 %all-reduce = (f32[768]{0:T(1024)}, f32[768]{0:T(1024)}, f32[192]{0:T(256)}, f32[192]{0:T(256)}, f32[768]{0:T(1024)}, /*index=5*/f32[768]{0:T(1024)}, f32[768]{0:T(1024)}, f32[768]{0:T(1024)}, f32[768]{0:T(1024)}) all-reduce(f32[768]{0:T(1024)S(1)} %get-tuple-element.244, ...), channel_id=1, replica_groups=mesh['dp'=8,'mp'=4] {'dp'}, use_global_device_ids=true, to_apply=%region_64.0 | all-reduce | flops 5760 | bytes 46080 | tf_op jit(solution)/shard_map/psum | solution.py:239
  (714 shorter events, 336.0 us)
Async XLA Ops:
  8.0 385.1 %all-reduce.12.cloned.1.call-start = ((), (), s32[]{:S(2)}) async-start(), calls=%async_computation.12 | async-start | bytes 12189696 | tf_op jit(solution)/shard_map/psum | solution.py:128
  66.8 104.9 %copy-start.143 = (f32[985]{0:T(1024)}, f32[985]{0:T(1024)S(1)}, u32[]{:S(2)}) copy-start(f32[985]{0:T(1024)S(1)} %div.137) | copy-start | bytes 11824
  66.9 152.2 %copy-start.139 = (f32[985]{0:T(1024)}, f32[985]{0:T(1024)S(1)}, u32[]{:S(2)}) copy-start(f32[985]{0:T(1024)S(1)} %div.144) | copy-start | bytes 11824
  67.0 173.6 %copy-start.141 = (f32[985]{0:T(1024)}, f32[985]{0:T(1024)S(1)}, u32[]{:S(2)}) copy-start(f32[985]{0:T(1024)S(1)} %div.151) | copy-start | bytes 11824
  134.7 37.0 %copy-start.215 = (f32[192]{0:T(256)S(1)}, f32[192]{0:T(256)}, u32[]{:S(2)}) copy-start(f32[192]{0:T(256)} %param.23) | copy-start | bytes 2308
  134.7 37.0 %copy-start.216 = (f32[192]{0:T(256)S(1)}, f32[192]{0:T(256)}, u32[]{:S(2)}) copy-start(f32[192]{0:T(256)} %param.22) | copy-start | bytes 2308
  134.7 37.9 %copy-start.123 = (f32[768]{0:T(1024)S(1)}, f32[768]{0:T(1024)}, u32[]{:S(2)}) copy-start(f32[768]{0:T(1024)} %param.19) | copy-start | bytes 9220
  134.7 37.9 %copy-start.199 = (f32[768]{0:T(1024)S(1)}, f32[768]{0:T(1024)}, u32[]{:S(2)}) copy-start(f32[768]{0:T(1024)} %param.20) | copy-start | bytes 9220
  137.0 38.0 %copy-start.31 = (f32[985,768]{1,0:T(8,128)}, f32[985,768]{1,0:T(8,128)S(1)}, u32[]{:S(2)}) copy-start(f32[985,768]{1,0:T(8,128)S(1)} %reshape.712) | copy-start | bytes 9077764
  137.1 44.5 %copy-start.147 = (f32[985]{0:T(1024)}, f32[985]{0:T(1024)S(1)}, u32[]{:S(2)}) copy-start(f32[985]{0:T(1024)S(1)} %rsqrt.81) | copy-start | bytes 11824
  172.6 46.5 %copy-start.206 = (f32[576]{0:T(1024)}, f32[576]{0:T(1024)S(1)}, u32[]{:S(2)}) copy-start(f32[576]{0:T(1024)S(1)} %pad_maximum_fusion.2) | copy-start | bytes 6916
  275.6 130.6 %all-gather.3.cloned.1.call-start = ((), (), s32[]{:S(2)}) async-start(), calls=%async_computation.4 | async-start | bytes 1327104 | tf_op jit(solution)/shard_map/all_gather | solution.py:98
  276.2 145.5 %all-gather.5.cloned.1.call-start = ((), (), s32[]{:S(2)}) async-start(), calls=%async_computation.5 | async-start | bytes 1327104 | tf_op jit(solution)/shard_map/all_gather | solution.py:99
  276.7 293.7 %all-reduce.10.cloned.1.call-start = ((), (), s32[]{:S(2)}) async-start(), calls=%async_computation.11 | async-start | bytes 12189696 | tf_op jit(solution)/shard_map/psum | solution.py:159
  294.6 18.6 %copy-start.43 = (bf16[1,5,197,768]{3,0,2,1:T(2,128)(2,1)}, bf16[1,5,197,768]{3,0,2,1:T(2,128)(2,1)S(1)}, u32[]{:S(2)}) copy-start(bf16[1,5,197,768]{3,0,2,1:T(2,128)(2,1)S(1)} %get-tuple-element.143) | copy-start | bytes 4538884
  322.5 70.6 %copy-start.198 = (f32[768]{0:T(1024)S(1)}, f32[768]{0:T(1024)}, u32[]{:S(2)}) copy-start(f32[768]{0:T(1024)} %param.25) | copy-start | bytes 9220
  327.1 66.1 %copy-start.213 = (f32[5]{0:T(128)}, f32[5]{0:T(128)S(1)}, u32[]{:S(2)}) copy-start(f32[5]{0:T(128)S(1)} %compare_convert_fusion) | copy-start | bytes 64
  400.4 170.0 %copy-start.8 = (f32[985,768]{1,0:T(8,128)}, f32[985,768]{1,0:T(8,128)S(1)}, u32[]{:S(2)}) copy-start(f32[985,768]{1,0:T(8,128)S(1)} %get-tuple-element.199) | copy-start | bytes 9077764
  453.6 260.7 %reduce-scatter.11.cloned.1.call-start = ((), (), s32[]{:S(2)}) async-start(), calls=%async_computation.8 | async-start | bytes 1327104 | tf_op jit(solution)/shard_map/reduce_scatter | solution.py:225
  524.6 191.8 %reduce-scatter.9.cloned.1.call-start = ((), (), s32[]{:S(2)}) async-start(), calls=%async_computation.7 | async-start | bytes 1327104 | tf_op jit(solution)/shard_map/reduce_scatter | solution.py:222
  549.6 188.7 %reduce-scatter.13.cloned.1.call-start = ((), (), s32[]{:S(2)}) async-start(), calls=%async_computation.9 | async-start | bytes 442368
  675.7 129.3 %reduce-scatter.7.cloned.1.call-start = ((), (), s32[]{:S(2)}) async-start(), calls=%async_computation.6 | async-start | bytes 1105920 | tf_op jit(solution)/shard_map/reduce_scatter | solution.py:216
  696.1 232.6 %all-reduce.8.cloned.1.call-start = ((), (), s32[]{:S(2)}) async-start(), calls=%async_computation.10 | async-start | bytes 24379392 | tf_op jit(solution)/shard_map/psum | solution.py:137
  713.8 214.9 %copy-start.10 = (f32[985,768]{1,0:T(8,128)S(1)}, f32[985,768]{1,0:T(8,128)}, u32[]{:S(2)}) copy-start(f32[985,768]{1,0:T(8,128)} %copy-done.8) | copy-start | bytes 9077764
  713.8 214.9 %copy-start.201 = (f32[768]{0:T(1024)S(1)}, f32[768]{0:T(1024)}, u32[]{:S(2)}) copy-start(f32[768]{0:T(1024)} %param.31) | copy-start | bytes 9220
  952.9 8.3 copy-start.32
  952.9 8.3 copy-start.34
  952.9 8.3 copy-start.36
  972.9 9.4 copy-start.62
  992.2 9.7 copy-start.48
  992.2 9.7 copy-start.208
  992.2 9.7 copy-start.212
  (220 other events, 770.2 us)
Sparse Core Ops, SparseCore 0:
  275.7 117.3 all-reduce.11
  453.8 116.6 all-reduce.9
  714.0 214.6 all-reduce.7
Sparse Core Ops, SparseCore 1:
  278.2 42.2 all-gather.2
  322.5 39.6 all-gather.4
  524.7 64.9 reduce-scatter.10
  593.0 63.9 reduce-scatter.8
  675.8 62.4 reduce-scatter.12
  741.7 63.4 reduce-scatter.6
where the time goes:
time: 1090 us; the launch traced here: 1080 us
  other arithmetic  306 us (28%)
  waiting for transfers between devices  287 us (26%)
  local copies, waits for them, and re-layouts  200 us (18%)
  matrix products  166 us (15%)
  blocking collectives  103 us (9%)
  between operations  18.2 us (2%)
    psum x1, waiting for transfers between devices, on_device(): lax.psum(jnp.dot(activated, down_full, preferred_element_type=jnp.float32...  122 us
    reduce_sum x5, other arithmetic, norm_stats(): spread = jnp.mean(offset * offset, axis=-1, keepdims=True)  69.6 us
    reduce_sum x2, other arithmetic, norm_stats(): center = jnp.mean(values, axis=-1, keepdims=True)  65.9 us
    psum x1, waiting for transfers between devices, on_device(): lax.psum(jnp.dot(mixed_low, out_full, preferred_element_type=jnp.float32)...  65.3 us
    reduce_scatter x1, waiting for transfers between devices, on_device(): lax.psum_scatter(full_qkv.astype(jnp.bfloat16), 'dp', scatter_dimension=0...  65.2 us
    convert_element_type x1, other arithmetic, on_device(): normed_one = (normal_one * norm_gain + norm_shift).astype(jnp.bfloat16)  55.3 us
    dot_general x16, matrix products, cols_dot(): lax.dot_general(former, latter, CONTRACT_COLS, preferred_element_type=jnp...  43.8 us
    dot_general x16, matrix products, rows_dot(): lax.dot_general(former, latter, CONTRACT_ROWS, preferred_element_type=jnp...  41.5 us
  transfers between devices with their start and end apart: 9, of which 5 were waited for; matrix products, arithmetic and copies ran while one was open for 29% of the time, Pallas kernels for 0%

commit v1 on v0

v1 whole, which is shorter than its diff:
```python
import functools
import jax
import jax.numpy as jnp
from jax import lax
from jax.experimental import pallas as pl
from jax.experimental.pallas import tpu as pltpu
from jax.sharding import PartitionSpec as P

HEAD_DIM = 64
NORM_EPS = 1e-06
SLOT_ROWS = 200
ROWS = 1024
BF = jnp.bfloat16
F32 = jnp.float32
NT = (((1,), (1,)), ((), ()))
NN = (((1,), (0,)), ((), ()))
TN = (((0,), (0,)), ((), ()))


def dot(a, b, dims=NN):
    return lax.dot_general(a, b, dims, preferred_element_type=F32)


def norm_stats(values):
    center = jnp.mean(values, axis=-1, keepdims=True)
    offset = values - center
    spread = jnp.mean(offset * offset, axis=-1, keepdims=True)
    scale_inv = lax.rsqrt(spread + NORM_EPS)
    return offset * scale_inv, scale_inv


def norm_back(upstream, normal, scale_inv, gain_vec):
    scaled = upstream * gain_vec
    return scale_inv * (
        scaled
        - jnp.mean(scaled, axis=-1, keepdims=True)
        - normal * jnp.mean(scaled * normal, axis=-1, keepdims=True)
    )


def colsum(values):
    return jnp.sum(values, axis=0, keepdims=True)


def call(body, outs, ins, in_specs=None, out_specs=None, grid=None, scratch=(), flops=0, nbytes=0, limit=60, **kw):
    full = lambda a: pl.BlockSpec(a.shape, (lambda *_: (0,) * len(a.shape)))
    if in_specs is None:
        in_specs = [None] * len(ins)
    if out_specs is None:
        out_specs = [None] * len(outs)
    in_specs = [full(a) if s is None else s for a, s in zip(ins, in_specs)]
    out_specs = [full(a) if s is None else s for a, s in zip(outs, out_specs)]
    nbytes = sum(a.size * a.dtype.itemsize for a in ins) + sum(a.size * a.dtype.itemsize for a in outs)
    return pl.pallas_call(
        body,
        out_shape=tuple(outs),
        grid=(1,) if grid is None else grid,
        in_specs=in_specs,
        out_specs=tuple(out_specs),
        scratch_shapes=list(scratch),
        compiler_params=pltpu.CompilerParams(vmem_limit_bytes=limit * 1024 * 1024),
        cost_estimate=pl.CostEstimate(flops=flops, bytes_accessed=nbytes, transcendentals=0),
        **kw,
    )(*ins)


def sds(shape, dtype):
    return jax.ShapeDtypeStruct(shape, dtype)


def loop(n, fn):
    lax.fori_loop(0, n, lambda i, c: (fn(i), c)[1], 0)


def cut(i, size):
    return pl.ds(pl.multiple_of(i * size, size), size)


def qkv_body(x_ref, gain_ref, shift_ref, wa_ref, bias_ref, h_ref, qkv_ref, wq_ref, wo_ref):
    parts, groups, sub, _ = wa_ref.shape
    width = x_ref.shape[1]
    local = width // groups
    for j in range(groups):
        w = wa_ref[:, j].reshape(parts * sub, 4 * local)
        for s in range(3):
            wq_ref[:, s * width + j * local : s * width + (j + 1) * local] = w[:, s * local : (s + 1) * local]
        wo_ref[:, j * local : (j + 1) * local] = w[:, 3 * local :]

    def norm(i):
        rows = cut(i, 128)
        normal, _ = norm_stats(x_ref[rows, :].astype(F32))
        h_ref[rows, :] = (normal * gain_ref[...] + shift_ref[...]).astype(BF)

    loop(ROWS // 128, norm)

    def project(n):
        cols = cut(n, 256)
        qkv_ref[:, cols] = (dot(h_ref[...], wq_ref[:, cols]) + bias_ref[:, cols]).astype(BF)

    loop(3 * width // 256, project)


def attend_body(slots, length, q_ref, k_ref, v_ref, o_ref, p_ref):
    low_half = lax.broadcasted_iota(jnp.int32, (SLOT_ROWS, 2 * HEAD_DIM), 1) < HEAD_DIM
    valid = lax.broadcasted_iota(jnp.int32, (SLOT_ROWS, SLOT_ROWS), 1) < length

    def image(i):
        rows = cut(i, SLOT_ROWS)
        q = q_ref[rows, :] * jnp.bfloat16(0.125)
        k = k_ref[rows, :]
        v = v_ref[rows, :]
        zero = jnp.zeros_like(q)
        mixed = []
        for h in range(2):
            s = dot(jnp.where(low_half if h == 0 else ~low_half, q, zero), k, NT)
            s = jnp.where(valid, s, -1e30)
            e = jnp.exp(s - jnp.max(s, axis=-1, keepdims=True))
            p = (e * (1.0 / jnp.sum(e, axis=-1, keepdims=True))).astype(BF)
            p_ref[h, i] = p
            mixed.append(dot(p, v))
        o_ref[rows, :] = jnp.where(low_half, mixed[0], mixed[1]).astype(BF)

    loop(slots, image)
    tail = slots * SLOT_ROWS
    o_ref[tail:, :] = jnp.zeros((ROWS - tail, 2 * HEAD_DIM), BF)


def mix_body(x_ref, o_ref, wo_ref, bias_ref, gain_ref, shift_ref, mid_ref, h_ref):
    mid_ref[...] = dot(o_ref[...], wo_ref[...], NT)

    def norm(i):
        rows = cut(i, 128)
        mid = x_ref[rows, :].astype(F32) + (mid_ref[rows, :] + bias_ref[...])
        mid_ref[rows, :] = mid
        normal, _ = norm_stats(mid)
        h_ref[rows, :] = (normal * gain_ref[...] + shift_ref[...]).astype(BF)

    loop(mid_ref.shape[0] // 128, norm)


def hidden_body(h_ref, w_ref, bias_ref, act_ref, slope_ref):
    parts, _, sub, cols = w_ref.shape
    w = w_ref[:, 0].reshape(parts * sub, cols)

    def chunk(i):
        rows = cut(i, 256)
        u = dot(h_ref[rows, :], w) + bias_ref[...]
        half = 0.5 * (1.0 + lax.erf(u * 0.7071067811865476))
        act_ref[rows, :] = (u * half).astype(BF)
        slope_ref[rows, :] = (half + u * jnp.exp(-0.5 * u * u) * 0.3989422804014327).astype(BF)

    loop(ROWS // 256, chunk)


def down_body(slots, length, live_ref, act_ref, wc_ref, mid_ref, bias_ref, out_ref, acc_ref):
    parts, groups, sub, cols = wc_ref.shape
    for j in range(groups):
        part = dot(act_ref[:, j * cols : (j + 1) * cols], wc_ref[:, j].reshape(parts * sub, cols), NT)
        if j == 0:
            acc_ref[...] = part
        else:
            acc_ref[...] += part
    for i in range(slots):
        rows = slice(i * SLOT_ROWS, (i + 1) * SLOT_ROWS)
        live = jnp.where(i < live_ref[0], 1.0, 0.0)
        value = (mid_ref[rows, :] + acc_ref[rows, :] + bias_ref[...]) * live
        out_ref[i] = value[:length].astype(BF)


def outer_body(left_ref, right_ref, g_ref, t_ref):
    @pl.when(pl.program_id(0) == 0)
    def _():
        t_ref[...] = left_ref[...].T

    parts, _, sub, cols = g_ref.shape
    g_ref[:, 0] = dot(t_ref[...], right_ref[...]).astype(BF).reshape(parts, sub, cols)


def dact_body(dy_ref, wc_ref, slope_ref, du_ref, sum_ref):
    parts, _, sub, cols = wc_ref.shape
    w = wc_ref[:, 0].reshape(parts * sub, cols)
    total = jnp.zeros((1, cols), F32)
    for i in range(ROWS // 256):
        rows = slice(i * 256, (i + 1) * 256)
        du = (dot(dy_ref[rows, :], w) * slope_ref[rows, :].astype(F32)).astype(BF)
        du_ref[rows, :] = du
        total = total + colsum(du.astype(F32))
    sum_ref[...] = jnp.broadcast_to(total, sum_ref.shape)


def mid_back_body(dy_ref, du_ref, wb_ref, mid_ref, gain_ref, dmid_ref, dlow_ref, sums_ref, acc_ref):
    parts, groups, sub, cols = wb_ref.shape
    for j in range(groups):
        part = dot(du_ref[:, j * cols : (j + 1) * cols], wb_ref[:, j].reshape(parts * sub, cols), NT)
        if j == 0:
            acc_ref[...] = part
        else:
            acc_ref[...] += part
    width = dy_ref.shape[1]

    def chunk(i, sums):
        rows = cut(i, 128)
        dh = acc_ref[rows, :]
        normal, scale_inv = norm_stats(mid_ref[rows, :])
        dy = dy_ref[rows, :].astype(F32)
        dmid = dy + norm_back(dh, normal, scale_inv, gain_ref[...])
        dmid_ref[rows, :] = dmid
        dlow_ref[rows, :] = dmid.astype(BF)
        new = (colsum(dh * normal), colsum(dh), colsum(dmid), colsum(dy))
        return tuple(a + b for a, b in zip(sums, new))

    zero = jnp.zeros((1, width), F32)
    sums = lax.fori_loop(0, ROWS // 128, chunk, (zero,) * 4)
    for n in range(4):
        sums_ref[n : n + 1, :] = sums[n]


def out_back_body(dlow_ref, o_ref, wo_ref, do_ref, g_ref):
    do_ref[...] = dot(dlow_ref[...], wo_ref[...]).astype(BF)
    parts, groups, sub, local = g_ref.shape
    g = dot(dlow_ref[...].T, o_ref[...]).astype(BF)
    for j in range(groups):
        g_ref[:, j] = g[:, j * local : (j + 1) * local].reshape(parts, sub, local)


def attend_back_body(slots, q_ref, k_ref, v_ref, p_ref, do_ref, dq_ref, dk_ref, dv_ref):
    low_half = lax.broadcasted_iota(jnp.int32, (SLOT_ROWS, 2 * HEAD_DIM), 1) < HEAD_DIM

    def image(i):
        rows = cut(i, SLOT_ROWS)
        q = q_ref[rows, :] * jnp.bfloat16(0.125)
        k = k_ref[rows, :] * jnp.bfloat16(0.125)
        v = v_ref[rows, :]
        do = do_ref[rows, :]
        zero = jnp.zeros_like(q)
        grads = []
        for h in range(2):
            mask = low_half if h == 0 else ~low_half
            p = p_ref[h, i]
            pf = p.astype(F32)
            dv = dot(p, do, TN)
            dp = dot(jnp.where(mask, do, zero), v, NT)
            ds = (pf * (dp - jnp.sum(pf * dp, axis=-1, keepdims=True))).astype(BF)
            grads.append((dot(ds, k), dot(ds, q, TN), dv))
        for ref, a, b in zip((dq_ref, dk_ref, dv_ref), *grads):
            ref[rows, :] = jnp.where(low_half, a, b).astype(BF)

    loop(slots, image)
    tail = slots * SLOT_ROWS
    for ref in (dq_ref, dk_ref, dv_ref):
        ref[tail:, :] = jnp.zeros((ROWS - tail, 2 * HEAD_DIM), BF)


def qkv_outer_body(h_ref, dq_ref, dk_ref, dv_ref, g_ref, sums_ref, t_ref):
    t_ref[...] = h_ref[...].T
    parts, groups, sub, cols = g_ref.shape
    local = cols // 3
    for s, ref in enumerate((dq_ref, dk_ref, dv_ref)):
        g = dot(t_ref[...], ref[...]).astype(BF)
        for j in range(groups):
            g_ref[:, j, :, s * local : (s + 1) * local] = g[:, j * local : (j + 1) * local].reshape(parts, sub, local)
        if s != 1:
            n = 0 if s == 0 else 1
            sums_ref[n : n + 1, :] = colsum(ref[...].astype(F32))


def input_back_body(slots, length, x_ref, dq_ref, dk_ref, dv_ref, wq_ref, dmid_ref, gain_ref, out_ref, sums_ref, acc_ref):
    width = x_ref.shape[1]
    for s, ref in enumerate((dq_ref, dk_ref, dv_ref)):
        part = dot(ref[...], wq_ref[:, s * width : (s + 1) * width], NT)
        if s == 0:
            acc_ref[...] = part
        else:
            acc_ref[...] += part

    sums = [jnp.zeros((1, width), F32)] * 2
    for i in range(slots):
        rows = slice(i * SLOT_ROWS, (i + 1) * SLOT_ROWS)
        dh = acc_ref[rows, :]
        normal, scale_inv = norm_stats(x_ref[rows, :].astype(F32))
        grad = dmid_ref[rows, :] + norm_back(dh, normal, scale_inv, gain_ref[...])
        out_ref[i] = grad[:length].astype(BF)
        sums[0] = sums[0] + colsum(dh * normal)
        sums[1] = sums[1] + colsum(dh)
    for n in range(2):
        sums_ref[n : n + 1, :] = sums[n]


def on_device(
    inputs,
    cotangent,
    counts,
    norm_gain,
    norm_shift,
    qkv_weight,
    query_bias,
    value_bias,
    out_weight,
    out_bias,
    mlp_gain,
    mlp_shift,
    hidden_weight,
    hidden_bias,
    down_weight,
    down_bias,
):
    batches, slots, length, width = inputs.shape
    sub = qkv_weight.shape[0]
    local = qkv_weight.shape[1] // 3
    units = hidden_weight.shape[1]
    parts, groups = width // sub, width // local
    ff = units * groups
    axes = ("dp", "mp")
    mine = lax.axis_index("mp")

    def padded(tokens):
        tokens = jnp.pad(tokens, ((0, 0), (0, SLOT_ROWS - length), (0, 0)))
        return jnp.pad(tokens.reshape(slots * SLOT_ROWS, width), ((0, ROWS - slots * SLOT_ROWS), (0, 0)))

    pick = lambda a: lax.dynamic_index_in_dim(a, mine, 0, keepdims=False)
    live = pick(counts)
    x = padded(pick(inputs))
    mask = (jnp.arange(slots, dtype=jnp.int32) < live[0]).astype(BF)
    dy = padded(pick(cotangent) * mask[:, None, None])
    row = lambda v: v.reshape(1, -1)

    shard = jnp.concatenate([qkv_weight, out_weight.T, hidden_weight, down_weight.T], axis=1)
    every = lax.all_gather(shard, axes, axis=0, tiled=False).reshape(parts, groups, sub, -1)
    piece = lambda n: lax.slice_in_dim(every, n * 4 * local, (n + 1) * 4 * local, axis=3)
    wa, wb, wc = piece(0), piece(1), piece(2)
    biases = lax.all_gather(jnp.concatenate([query_bias, value_bias, hidden_bias]), "mp", axis=0, tiled=False)
    qb, vb, hb = (biases[:, a:b].reshape(-1) for a, b in ((0, local), (local, 2 * local), (2 * local, None)))
    bias_row = row(jnp.concatenate([qb, jnp.zeros_like(qb), vb]))

    mm = 2 * ROWS * width * width
    t_bf = lambda n: sds((ROWS, n), BF)
    t_f = lambda n: sds((ROWS, n), F32)
    h1, qkv, wq, wo = call(
        qkv_body,
        [t_bf(width), t_bf(3 * width), sds((width, 3 * width), BF), sds((width, width), BF)],
        [x, row(norm_gain), row(norm_shift), wa, bias_row],
        flops=3 * mm,
    )
    pair = 2 * HEAD_DIM
    pairs = width // pair
    head = lambda s: pl.BlockSpec((ROWS, pair), lambda i: (0, s * pairs + i))
    p_spec = pl.BlockSpec((2, slots, SLOT_ROWS, SLOT_ROWS), lambda i: (i, 0, 0, 0))
    p_shape = sds((2 * pairs, slots, SLOT_ROWS, SLOT_ROWS), BF)
    mixed, probs = call(
        functools.partial(attend_body, slots, length),
        [t_bf(width), p_shape],
        [qkv, qkv, qkv],
        [head(0), head(1), head(2)],
        [head(0), p_spec],
        (pairs,),
        flops=mm,
    )
    rows256 = pl.BlockSpec((256, width), lambda i: (i, 0))
    middle, h2 = call(
        mix_body,
        [t_f(width), t_bf(width)],
        [x, mixed, wo, row(out_bias), row(mlp_gain), row(mlp_shift)],
        [rows256, rows256, None, None, None, None],
        [rows256, rows256],
        (ROWS // 256,),
        flops=mm,
    )
    step = 256
    per = units // step
    wcols = pl.BlockSpec((parts, 1, sub, step), lambda i: (0, i // per, 0, i % per))
    tcols = pl.BlockSpec((ROWS, step), lambda i: (0, i))
    vcols = lambda n: pl.BlockSpec((n, step), lambda i: (0, i))
    act, slope = call(
        hidden_body,
        [t_bf(ff), t_bf(ff)],
        [h2, wb, row(hb)],
        [None, wcols, vcols(1)],
        [tcols, tcols],
        (ff // step,),
        flops=4 * mm,
    )
    smem = pl.BlockSpec(memory_space=pltpu.SMEM)
    (block_out,) = call(
        functools.partial(down_body, slots, length),
        [sds((slots, length, width), BF)],
        [live, act, wc, middle, row(down_bias)],
        [smem, None, None, None, None],
        scratch=[pltpu.VMEM((ROWS, width), F32)],
        flops=4 * mm,
    )
    g_shape = lambda n: sds((parts, groups, sub, n), BF)

    def outer(left, right):
        (g,) = call(
            outer_body,
            [g_shape(units)],
            [left, right],
            [None, tcols],
            [wcols],
            (ff // step,),
            scratch=[pltpu.VMEM((width, ROWS), BF)],
            flops=4 * mm,
        )
        return g

    g_down = outer(dy, act)
    du, sum_hidden = call(
        dact_body,
        [t_bf(ff), sds((8, ff), F32)],
        [dy, wc, slope],
        [None, wcols, tcols],
        [tcols, vcols(8)],
        (ff // step,),
        flops=4 * mm,
    )
    g_hidden = outer(h2, du)
    dmid, dlow, sums_mid = call(
        mid_back_body,
        [t_f(width), t_bf(width), sds((8, width), F32)],
        [dy, du, wb, middle, row(mlp_gain)],
        scratch=[pltpu.VMEM((ROWS, width), F32)],
        flops=4 * mm,
    )
    do, g_out = call(
        out_back_body,
        [t_bf(width), g_shape(local)],
        [dlow, mixed, wo],
        flops=2 * mm,
    )
    dq, dk, dv = call(
        functools.partial(attend_back_body, slots),
        [t_bf(width)] * 3,
        [qkv, qkv, qkv, probs, do],
        [head(0), head(1), head(2), p_spec, head(0)],
        [head(0)] * 3,
        (pairs,),
        flops=2 * mm,
    )
    g_qkv, sums_qkv = call(
        qkv_outer_body,
        [g_shape(3 * local), sds((8, width), F32)],
        [h1, dq, dk, dv],
        scratch=[pltpu.VMEM((width, ROWS), BF)],
        flops=3 * mm,
    )
    input_grad, sums_in = call(
        functools.partial(input_back_body, slots, length),
        [sds((slots, length, width), BF), sds((8, width), F32)],
        [x, dq, dk, dv, wq, dmid, row(norm_gain)],
        scratch=[pltpu.VMEM((ROWS, width), F32)],
        flops=3 * mm,
    )

    gather = lambda a: lax.all_gather(a, "mp", axis=0, tiled=False)
    scatter = lambda g: lax.psum_scatter(
        g.reshape(parts * groups, sub, -1), axes, scatter_dimension=0, tiled=False
    ).astype(F32)
    s_down, s_hidden, s_out, s_qkv = scatter(g_down), scatter(g_hidden), scatter(g_out), scatter(g_qkv)
    sums = jnp.concatenate(
        [sums_in[:2].reshape(-1), sums_mid[:4].reshape(-1), sums_qkv[:2].reshape(-1), sum_hidden[0]]
    )
    sums = lax.psum(sums, axes)
    vec = [sums[n * width : (n + 1) * width] for n in range(8)]
    own = lambda v, n: lax.dynamic_slice_in_dim(v, mine * n, n, 0)
    return (
        gather(block_out),
        gather(input_grad),
        vec[0],
        vec[1],
        s_qkv,
        own(vec[6], local),
        own(vec[7], local),
        s_out.T,
        vec[4],
        vec[2],
        vec[3],
        s_hidden,
        own(sums[8 * width :], units),
        s_down.T,
        vec[5],
    )


def solution(mesh):
    token = P(None, "dp", None, None)
    weight, turned = P("dp", "mp"), P("mp", "dp")
    return jax.shard_map(
        on_device,
        mesh=mesh,
        in_specs=(token, token, P(None, "dp"), P(), P(), weight, P("mp"), P("mp"), turned)
        + (P(), P(), P(), weight, P("mp"), turned, P()),
        out_specs=(token, token, P(), P(), weight, P("mp"), P("mp"), turned)
        + (P(), P(), P(), weight, P("mp"), turned, P()),
        check_vma=False,
    )
```

time: 1090 us -> 784 us (0.72)
  other arithmetic: 306 us -> 7.25 us
  Pallas kernels: 0 us -> 196 us
  matrix products: 166 us -> 0 us
  waiting for transfers between devices: 287 us -> 453 us
  local copies, waits for them, and re-layouts: 200 us -> 60.5 us
  blocking collectives: 103 us -> 45.4 us
    reduce_scatter x3 -> x4, waiting for transfers between devices: 65.2 us -> 292 us  [on_device(): lax.psum_scatter(g.reshape(parts * groups, sub, -1), axes, scatter_dimens...]
    psum x3 -> x0, waiting for transfers between devices: 201 us -> none  [the longest x1 122 us: on_device(): lax.psum(jnp.dot(activated, down_full, preferred_element_type=jnp.float32...]
    pallas_call x0 -> x13, Pallas kernels: none -> 196 us  [call(): pl.pallas_call(body, out_shape=tuple(outs), grid=(1,) if grid is None els...]
    reduce_sum x23 -> x0, other arithmetic: 189 us -> none  [the longest x5 69.6 us: norm_stats(): spread = jnp.mean(offset * offset, axis=-1, keepdims=True)]
    dot_general x72 -> x0, matrix products: 166 us -> none  [the longest x16 43.8 us: cols_dot(): lax.dot_general(former, latter, CONTRACT_COLS, preferred_element_type=jnp...]
    all_gather x2 -> x3, waiting for transfers between devices: 0.01 us -> 161 us  [the longest x2 83.8 us: on_device(): gather = lambda a: lax.all_gather(a, 'mp', axis=0, tiled=False)]
    convert_element_type x28 -> x0, local copies, waits for them, and re-layouts: 87.7 us -> none  [the longest x4 29 us: on_device(): token_grad.reshape(slot_count, length, model_width).astype(jnp.bfloat16)]
    convert_element_type x18 -> x3, other arithmetic: 79.8 us -> 3.9 us  [the longest x2 3.25 us: on_device(): scatter = lambda g: lax.psum_scatter(g.reshape(parts * groups, sub, -1),...]
  transfers between devices with their start and end apart: 9 -> 7, of which waited for: 5 -> 6; matrix products, arithmetic and copies ran while one was open for 29% -> 6% of each run, Pallas kernels for 0% -> 11%
where the time goes in v1:
time: 784 us; the launch traced here: 777 us
  waiting for transfers between devices  453 us (58%)
  Pallas kernels  196 us (25%)
  local copies, waits for them, and re-layouts  60.5 us (8%)
  blocking collectives  45.4 us (6%)
  between operations  14.8 us (2%)
    reduce_scatter x4, waiting for transfers between devices, on_device(): lax.psum_scatter(g.reshape(parts * groups, sub, -1), axes, scatter_dimens...  292 us
    pallas_call x13, Pallas kernels, call(): pl.pallas_call(body, out_shape=tuple(outs), grid=(1,) if grid is None els...  196 us
    all_gather x2, waiting for transfers between devices, on_device(): gather = lambda a: lax.all_gather(a, 'mp', axis=0, tiled=False)  83.8 us
    all_gather x1, waiting for transfers between devices, on_device(): lax.all_gather(shard, axes, axis=0, tiled=False)  76.9 us
    psum x1, blocking collectives, on_device(): sums = lax.psum(sums, axes)  39.1 us
    unnamed x32, local copies, waits for them, and re-layouts  19.3 us
  transfers between devices with their start and end apart: 7, of which 6 were waited for; matrix products, arithmetic and copies ran while one was open for 6% of the time, Pallas kernels for 11%

profile of v1, /device:TPU:0, one launch (start us, length us, event | category | flops | bytes accessed | tf_op | source)
XLA Modules:
  0.0 776.9 jit_solution(15156339779320192633)
XLA Ops:
  8.1 1.9 concatenate.12
  10.1 12.3 %constant_dynamic-slice_fusion = (bf16[1,5,197,768]{3,0,2,1:T(2,128)(2,1)S(1)}, bf16[1,5,197,768]{3,0,2,1:T(2,128)(2,1)}) fusion(bf16[4,5,197,768]{3,0,2,1:T(4,128)(2,1)} %param.17, s32[]{:T(128)S(6)} %select_n.14, bf16[4,5,197,768]{3,0,2,1:T(4,128)(2,1)} %param.16), kind=kLoop, calls=%fused_computation.12 | loop fusion | bytes 6051844 | tf_op jit(solution)/shard_map/jit(dynamic_index_in_dim)/dynamic_slice | solution.py:320
  22.5 2.3 copy.56
  26.3 6.3 all-gather.4
  39.9 76.9 %all-gather.9.cloned.1.call-done = bf16[3072,2304]{1,0:T(8,128)(2,1)} async-done(((bf16[96,2304]{1,0:T(8,128)(2,1)}), bf16[3072,2304]{1,0:T(8,128)(2,1)}) %all-gather.9.cloned.1.call-update) | async-done | bytes 14155792 | tf_op jit(solution)/shard_map/all_gather | solution.py:328
  116.7 11.6 %fusion.1 = (bf16[8,4,96,768]{3,2,1,0:T(8,128)(2,1)}, bf16[8,4,96,768]{3,2,1,0:T(8,128)(2,1)}, bf16[8,4,96,768]{3,2,1,0:T(8,128)(2,1)}) fusion(bf16[8,4,96,2304]{3,2,1,0:T(8,128)(2,1)} %bitcast.44), kind=kLoop, calls=%fused_computation.15 | loop fusion | bytes 28311552 | tf_op jit(solution)/shard_map/slice | solution.py:329
  128.3 14.7 %shard_map.271 = (bf16[1024,768]{1,0:T(8,128)(2,1)}, bf16[1024,2304]{1,0:T(8,128)(2,1)}, bf16[768,2304]{1,0:T(8,128)(2,1)}, bf16[768,768]{1,0:T(8,128)(2,1)}) custom-call(bf16[1024,768]{1,0:T(8,128)(2,1)} %pad.15.x_ref, f32[1,768]{1,0:T(1,128)} %reshape.104.gain_ref, f32[1,768]{1,0:T(1,128)} %reshape.105.shift_ref, ...), custom_call_target="tpu_custom_call" | custom-call | flops 3623878656 | bytes 17316864 | tf_op jit(solution)/shard_map/pallas_call | solution.py:54
  143.0 29.1 %shard_map.272 = (bf16[1024,768]{1,0:T(8,128)(2,1)}, bf16[12,5,200,200]{3,2,1,0:T(8,128)(2,1)}) custom-call(bf16[1024,2304]{1,0:T(8,128)(2,1)} %get-tuple-element.39.q_ref.k_ref.v_ref, bf16[1024,2304]{1,0:T(8,128)(2,1)} %get-tuple-element.39.q_ref.k_ref.v_ref, bf16[1024,2304]{1,0:T(8,128)(2,1)} %get-tuple-element.39.q_ref.k_ref.v_ref), custom_call_target="tpu_custom_call" | custom-call | flops 1207959552 | bytes 20528640 | tf_op jit(solution)/shard_map/pallas_call | solution.py:54
  172.2 7.2 shard_map.273
  179.4 20.3 %shard_map.274 = (bf16[1024,3072]{1,0:T(8,128)(2,1)}, bf16[1024,3072]{1,0:T(8,128)(2,1)}) custom-call(bf16[1024,768]{1,0:T(8,128)(2,1)} %get-tuple-element.42.h_ref.left_ref, bf16[8,4,96,768]{3,2,1,0:T(8,128)(2,1)} %get-tuple-element.109.w_ref.wb_ref, f32[1,3072]{1,0:T(1,128)} %bitcast.59), custom_call_target="tpu_custom_call" | custom-call | flops 4831838208 | bytes 18886656 | tf_op jit(solution)/shard_map/pallas_call | solution.py:54
  199.7 14.1 %shard_map.276 = (bf16[1024,3072]{1,0:T(8,128)(2,1)}, f32[8,3072]{1,0:T(8,128)}) custom-call(bf16[1024,768]{1,0:T(8,128)(2,1)} %pad.17.dy_ref.left_ref, bf16[8,4,96,768]{3,2,1,0:T(8,128)(2,1)} %get-tuple-element.108.wc_ref, bf16[1024,3072]{1,0:T(8,128)(2,1)} %get-tuple-element.46.slope_ref), custom_call_target="tpu_custom_call" | custom-call | flops 4831838208 | bytes 18972672 | tf_op jit(solution)/shard_map/pallas_call | solution.py:54
  213.8 16.1 %shard_map.277 = (f32[1024,768]{1,0:T(8,128)}, bf16[1024,768]{1,0:T(8,128)(2,1)}, f32[8,768]{1,0:T(8,128)}) custom-call(bf16[1024,768]{1,0:T(8,128)(2,1)} %pad.17.dy_ref.left_ref, bf16[1024,3072]{1,0:T(8,128)(2,1)} %get-tuple-element.47.du_ref.right_ref, bf16[8,4,96,768]{3,2,1,0:T(8,128)(2,1)} %get-tuple-element.109.w_ref.wb_ref, ...), custom_call_target="tpu_custom_call" | custom-call | flops 4831838208 | bytes 20474880 | tf_op jit(solution)/shard_map/pallas_call | solution.py:54
  229.9 6.0 shard_map.278
  235.9 2.7 copy.44
  238.9 29.3 %shard_map.279 = (bf16[1024,768]{1,0:T(8,128)(2,1)}, bf16[1024,768]{1,0:T(8,128)(2,1)}, bf16[1024,768]{1,0:T(8,128)(2,1)}) custom-call(bf16[1024,2304]{1,0:T(8,128)(2,1)} %get-tuple-element.39.q_ref.k_ref.v_ref, bf16[1024,2304]{1,0:T(8,128)(2,1)} %get-tuple-element.39.q_ref.k_ref.v_ref, bf16[1024,2304]{1,0:T(8,128)(2,1)} %get-tuple-element.39.q_ref.k_ref.v_ref, ...), custom_call_target="tpu_custom_call" | custom-call | flops 2415919104 | bytes 25247232 | tf_op jit(solution)/shard_map/pallas_call | solution.py:54
  268.2 8.8 %shard_map.281 = (bf16[8,4,96,576]{3,2,1,0:T(8,128)(2,1)}, f32[8,768]{1,0:T(8,128)}) custom-call(bf16[1024,768]{1,0:T(8,128)(2,1)} %get-tuple-element.58.h_ref, bf16[1024,768]{1,0:T(8,128)(2,1)} %get-tuple-element.50.dq_ref, bf16[1024,768]{1,0:T(8,128)(2,1)} %get-tuple-element.51.dk_ref, bf16[1024,768]{1,0:T(8,128)(2,1)} %get-tuple-element.52.dv_ref), custom_call_target="tpu_custom_call" | custom-call | flops 3623878656 | bytes 9854976 | tf_op jit(solution)/shard_map/pallas_call | solution.py:54
  277.1 13.2 %shard_map.282 = bf16[8,4,96,768]{3,2,1,0:T(8,128)(2,1)} custom-call(bf16[1024,768]{1,0:T(8,128)(2,1)} %get-tuple-element.42.h_ref.left_ref, bf16[1024,3072]{1,0:T(8,128)(2,1)} %get-tuple-element.47.du_ref.right_ref), custom_call_target="tpu_custom_call" | custom-call | flops 4831838208 | bytes 12582912 | tf_op jit(solution)/shard_map/pallas_call | solution.py:54
  290.4 13.3 %shard_map.283 = bf16[8,4,96,768]{3,2,1,0:T(8,128)(2,1)} custom-call(bf16[1024,768]{1,0:T(8,128)(2,1)} %pad.17.dy_ref.left_ref, bf16[1024,3072]{1,0:T(8,128)(2,1)} %get-tuple-element.43.act_ref.right_ref), custom_call_target="tpu_custom_call" | custom-call | flops 4831838208 | bytes 12582912 | tf_op jit(solution)/shard_map/pallas_call | solution.py:54
  303.8 11.2 %shard_map.280 = (bf16[5,197,768]{2,1,0:T(8,128)(2,1)}, f32[8,768]{1,0:T(8,128)}) custom-call(bf16[1024,768]{1,0:T(8,128)(2,1)} %pad.15.x_ref, bf16[1024,768]{1,0:T(8,128)(2,1)} %get-tuple-element.50.dq_ref, bf16[1024,768]{1,0:T(8,128)(2,1)} %get-tuple-element.51.dk_ref, bf16[1024,768]{1,0:T(8,128)(2,1)} %get-tuple-element.52.dv_ref, ...), custom_call_target="tpu_custom_call" | custom-call | flops 3623878656 | bytes 14516736 | tf_op jit(solution)/shard_map/pallas_call | solution.py:54
  316.0 12.1 %shard_map.275 = bf16[5,197,768]{2,1,0:T(8,128)(2,1)} custom-call(s32[1]{0:T(128)} %bitcast.live_ref, bf16[1024,3072]{1,0:T(8,128)(2,1)} %get-tuple-element.43.act_ref.right_ref, bf16[8,4,96,768]{3,2,1,0:T(8,128)(2,1)} %get-tuple-element.108.wc_ref, f32[1024,768]{1,0:T(8,128)} %get-tuple-element.44.mid_ref, f32[1,768]{1,0:T(1,128)} %reshape.113.bias_ref), custom_call_target="tpu_custom_call" | custom-call | flops 4831838208 | bytes 15671812 | tf_op jit(solution)/shard_map/pallas_call | solution.py:54
  330.6 39.1 %psum.7 = f32[9216]{0:T(1024)S(1)} all-reduce(f32[9216]{0:T(1024)S(1)} %pad_maximum_fusion), channel_id=1, replica_groups=mesh['dp'=8,'mp'=4] {'dp','mp'}, use_global_device_ids=true, to_apply=%region_0.1 | all-reduce | flops 9216 | bytes 73728 | tf_op jit(solution)/shard_map/psum | solution.py:462
  372.2 1.4 convert_bitcast_fusion.1
  373.7 70.7 %reduce-scatter.5.cloned.1.call-done = bf16[1,96,576]{2,1,0:T(8,128)(2,1)} async-done(((bf16[32,96,576]{2,1,0:T(8,128)(2,1)}), bf16[1,96,576]{2,1,0:T(8,128)(2,1)}) %reduce-scatter.5.cloned.1.call-update) | async-done | bytes 110608 | tf_op jit(solution)/shard_map/reduce_scatter | solution.py:455
  444.4 1.6 bitcast_convert_fusion.1
  446.0 111.0 %reduce-scatter.9.cloned.1.call-done = bf16[1,96,768]{2,1,0:T(8,128)(2,1)} async-done(((bf16[32,96,768]{2,1,0:T(8,128)(2,1)}), bf16[1,96,768]{2,1,0:T(8,128)(2,1)}) %reduce-scatter.9.cloned.1.call-update) | async-done | bytes 147472 | tf_op jit(solution)/shard_map/reduce_scatter | solution.py:455
  557.0 1.6 bitcast_convert_fusion
  558.7 110.1 %reduce-scatter.11.cloned.1.call-done = bf16[1,96,768]{2,1,0:T(8,128)(2,1)} async-done(((bf16[32,96,768]{2,1,0:T(8,128)(2,1)}), bf16[1,96,768]{2,1,0:T(8,128)(2,1)}) %reduce-scatter.11.cloned.1.call-update) | async-done | bytes 147472 | tf_op jit(solution)/shard_map/reduce_scatter | solution.py:455
  668.7 1.6 convert_bitcast_fusion
  670.4 44.4 %all-gather.13.cloned.1.call-done = bf16[20,197,768]{2,1,0:T(8,128)(2,1)} async-done(((bf16[5,197,768]{2,1,0:T(8,128)(2,1)}), bf16[20,197,768]{2,1,0:T(8,128)(2,1)}) %all-gather.13.cloned.1.call-update) | async-done | bytes 6051856 | tf_op jit(solution)/shard_map/all_gather | solution.py:454
  714.8 7.7 copy.46
  722.5 39.4 %all-gather.11.cloned.1.call-done = bf16[20,197,768]{2,1,0:T(8,128)(2,1)} async-done(((bf16[5,197,768]{2,1,0:T(8,128)(2,1)}), bf16[20,197,768]{2,1,0:T(8,128)(2,1)}) %all-gather.11.cloned.1.call-update) | async-done | bytes 6051856 | tf_op jit(solution)/shard_map/all_gather | solution.py:454
  761.9 7.7 copy.45
  (77 shorter events, 16.1 us)
Async XLA Ops:
  7.2 29.8 %copy-start = (s32[4,1]{0,1:T(1,128)S(1)}, s32[4,1]{0,1:T(1,128)}, u32[]{:S(2)}) copy-start(s32[4,1]{0,1:T(1,128)} %param.18) | copy-start | bytes 52
  7.2 109.5 %all-gather.9.cloned.1.call-start = ((), (), s32[]{:S(2)}) async-start(), calls=%async_computation.8 | async-start | bytes 14598144 | tf_op jit(solution)/shard_map/all_gather | solution.py:328
  10.1 362.2 %reduce-scatter.7.cloned.1.call-start = ((), (), s32[]{:S(2)}) async-start(), calls=%async_computation.5 | async-start | bytes 1622016 | tf_op jit(solution)/shard_map/reduce_scatter | solution.py:455
  24.7 1.5 copy-start.3
  24.7 1.5 copy-start.10
  24.7 1.5 copy-start.11
  24.7 8.7 %copy-start.4 = (f32[768]{0:T(1024)S(1)}, f32[768]{0:T(1024)}, u32[]{:S(2)}) copy-start(f32[768]{0:T(1024)} %param.19) | copy-start | bytes 9220
  24.8 9.3 %copy-start.5 = (f32[768]{0:T(1024)S(1)}, f32[768]{0:T(1024)}, u32[]{:S(2)}) copy-start(f32[768]{0:T(1024)} %param.20) | copy-start | bytes 9220
  24.8 9.8 %copy-start.6 = (f32[768]{0:T(1024)S(1)}, f32[768]{0:T(1024)}, u32[]{:S(2)}) copy-start(f32[768]{0:T(1024)} %param.26) | copy-start | bytes 9220
  24.8 10.4 %copy-start.7 = (f32[768]{0:T(1024)S(1)}, f32[768]{0:T(1024)}, u32[]{:S(2)}) copy-start(f32[768]{0:T(1024)} %param.25) | copy-start | bytes 9220
  24.8 11.0 %copy-start.8 = (f32[768]{0:T(1024)S(1)}, f32[768]{0:T(1024)}, u32[]{:S(2)}) copy-start(f32[768]{0:T(1024)} %param.27) | copy-start | bytes 9220
  238.6 205.8 %reduce-scatter.5.cloned.1.call-start = ((), (), s32[]{:S(2)}) async-start(), calls=%async_computation.4 | async-start | bytes 4055040 | tf_op jit(solution)/shard_map/reduce_scatter | solution.py:455
  277.1 280.0 %reduce-scatter.9.cloned.1.call-start = ((), (), s32[]{:S(2)}) async-start(), calls=%async_computation.6 | async-start | bytes 4866048 | tf_op jit(solution)/shard_map/reduce_scatter | solution.py:455
  290.4 378.4 %reduce-scatter.11.cloned.1.call-start = ((), (), s32[]{:S(2)}) async-start(), calls=%async_computation.7 | async-start | bytes 4866048 | tf_op jit(solution)/shard_map/reduce_scatter | solution.py:455
  303.8 411.0 %all-gather.13.cloned.1.call-start = ((), (), s32[]{:S(2)}) async-start(), calls=%async_computation.10 | async-start | bytes 7680000 | tf_op jit(solution)/shard_map/all_gather | solution.py:454
  303.8 11.6 %copy-start.9 = (f32[768]{0:T(1024)S(1)}, f32[768]{0:T(1024)}, u32[]{:S(2)}) copy-start(f32[768]{0:T(1024)} %param.31) | copy-start | bytes 9220
  315.1 446.8 %all-gather.11.cloned.1.call-start = ((), (), s32[]{:S(2)}) async-start(), calls=%async_computation.9 | async-start | bytes 7680000 | tf_op jit(solution)/shard_map/all_gather | solution.py:454
  316.0 13.6 %copy-start.2 = (f32[8,768]{1,0:T(8,128)S(1)}, f32[8,768]{1,0:T(8,128)}, u32[]{:S(2)}) copy-start(f32[8,768]{1,0:T(8,128)} %get-tuple-element.57) | copy-start | bytes 73732
  761.9 7.7 copy-start.1
Sparse Core Ops, SparseCore 0:
  11.5 105.2 all-gather.8
  238.8 96.3 reduce-scatter.6
  340.6 103.7 reduce-scatter.4
  450.3 106.6 reduce-scatter.8
  562.4 106.3 reduce-scatter.10
  670.2 44.5 all-gather.12
  716.3 45.5 all-gather.10

commit v2 on v1

--- a/solution.py
+++ b/solution.py
@@ -42,7 +42,7 @@
     return jnp.sum(values, axis=0, keepdims=True)
 
 
-def call(body, outs, ins, in_specs=None, out_specs=None, grid=None, scratch=(), flops=0, nbytes=0, limit=60, **kw):
+def call(body, outs, ins, in_specs=None, out_specs=None, grid=None, scratch=(), flops=0, nbytes=0, limit=60, name=None, **kw):
     full = lambda a: pl.BlockSpec(a.shape, (lambda *_: (0,) * len(a.shape)))
     if in_specs is None:
         in_specs = [None] * len(ins)
@@ -59,6 +59,7 @@
         out_specs=tuple(out_specs),
         scratch_shapes=list(scratch),
         compiler_params=pltpu.CompilerParams(vmem_limit_bytes=limit * 1024 * 1024),
+        name=name,
         cost_estimate=pl.CostEstimate(flops=flops, bytes_accessed=nbytes, transcendentals=0),
         **kw,
     )(*ins)
@@ -76,12 +77,47 @@
     return pl.ds(pl.multiple_of(i * size, size), size)
 
 
-def qkv_body(x_ref, gain_ref, shift_ref, wa_ref, bias_ref, h_ref, qkv_ref, wq_ref, wo_ref):
-    parts, groups, sub, _ = wa_ref.shape
+def prep_body(slots, length, info_ref, x_ref, cot_ref, xo_ref, dy_ref):
+    xo_ref[...] = jnp.zeros_like(xo_ref)
+    dy_ref[...] = jnp.zeros_like(dy_ref)
+    for i in range(slots):
+        rows = slice(i * SLOT_ROWS, i * SLOT_ROWS + length)
+        xo_ref[rows, :] = x_ref[0, i]
+
+        @pl.when(i < info_ref[1])
+        def _():
+            dy_ref[rows, :] = cot_ref[0, i]
+
+
+def place_chunks(info_ref, own_refs, other_refs, buf_ref):
+    sub = own_refs[0].shape[1]
+    for k, (own, other) in enumerate(zip(own_refs, other_refs)):
+        rows = pl.ds(pl.multiple_of(info_ref[2 + k] * sub, sub), sub)
+        buf_ref[0, rows, :] = own[0]
+        buf_ref[2, rows, :] = own[1]
+        buf_ref[1, rows, :] = other[0]
+        buf_ref[3, rows, :] = other[1]
+
+
+def qkv_ring_body(info_ref, x_ref, gain_ref, shift_ref, bias_ref, *refs):
+    n = (len(refs) - 5) // 2
+    own_refs, other_refs = refs[:n], refs[n : 2 * n]
+    h_ref, qkv_ref, wq_ref, wo_ref, buf_ref = refs[2 * n :]
+    place_chunks(info_ref, own_refs, other_refs, buf_ref)
+    groups = buf_ref.shape[0]
+    qkv_rest(lambda j: buf_ref[lax.bitwise_xor(info_ref[0], j)], groups, x_ref, gain_ref, shift_ref, bias_ref, h_ref, qkv_ref, wq_ref, wo_ref)
+
+
+def qkv_gathered_body(x_ref, gain_ref, shift_ref, bias_ref, wa_ref, h_ref, qkv_ref, wq_ref, wo_ref):
+    parts, groups, sub, cols = wa_ref.shape
+    qkv_rest(lambda j: wa_ref[:, j].reshape(parts * sub, cols), groups, x_ref, gain_ref, shift_ref, bias_ref, h_ref, qkv_ref, wq_ref, wo_ref)
+
+
+def qkv_rest(piece, groups, x_ref, gain_ref, shift_ref, bias_ref, h_ref, qkv_ref, wq_ref, wo_ref):
     width = x_ref.shape[1]
     local = width // groups
     for j in range(groups):
-        w = wa_ref[:, j].reshape(parts * sub, 4 * local)
+        w = piece(j)
         for s in range(3):
             wq_ref[:, s * width + j * local : s * width + (j + 1) * local] = w[:, s * local : (s + 1) * local]
         wo_ref[:, j * local : (j + 1) * local] = w[:, 3 * local :]
@@ -152,7 +188,7 @@
     loop(ROWS // 256, chunk)
 
 
-def down_body(slots, length, live_ref, act_ref, wc_ref, mid_ref, bias_ref, out_ref, acc_ref):
+def down_body(slots, length, info_ref, act_ref, wc_ref, mid_ref, bias_ref, all_ref, out_ref, acc_ref):
     parts, groups, sub, cols = wc_ref.shape
     for j in range(groups):
         part = dot(act_ref[:, j * cols : (j + 1) * cols], wc_ref[:, j].reshape(parts * sub, cols), NT)
@@ -162,18 +198,32 @@
             acc_ref[...] += part
     for i in range(slots):
         rows = slice(i * SLOT_ROWS, (i + 1) * SLOT_ROWS)
-        live = jnp.where(i < live_ref[0], 1.0, 0.0)
-        value = (mid_ref[rows, :] + acc_ref[rows, :] + bias_ref[...]) * live
-        out_ref[i] = value[:length].astype(BF)
-
-
-def outer_body(left_ref, right_ref, g_ref, t_ref):
-    @pl.when(pl.program_id(0) == 0)
+        live = jnp.where(i < info_ref[1], 1.0, 0.0)
+        value = ((mid_ref[rows, :] + acc_ref[rows, :] + bias_ref[...]) * live)[:length].astype(BF)
+        out_ref[i] = value
+        all_ref[0, i] = value
+
+
+def outer_body(h_ref, dy_ref, du_ref, act_ref, g_ref, t_ref):
+    step = pl.program_id(0)
+    half = pl.num_programs(0) // 2
+    parts, _, sub, cols = g_ref.shape
+
+    @pl.when(step == 0)
     def _():
-        t_ref[...] = left_ref[...].T
-
-    parts, _, sub, cols = g_ref.shape
-    g_ref[:, 0] = dot(t_ref[...], right_ref[...]).astype(BF).reshape(parts, sub, cols)
+        t_ref[...] = dy_ref[...].T
+
+    @pl.when(step == half)
+    def _():
+        t_ref[...] = h_ref[...].T
+
+    @pl.when(step < half)
+    def _():
+        g_ref[:, 0] = dot(t_ref[...], act_ref[...]).astype(BF).reshape(parts, sub, cols)
+
+    @pl.when(step >= half)
+    def _():
+        g_ref[:, 0] = dot(t_ref[...], du_ref[...]).astype(BF).reshape(parts, sub, cols)
 
 
 def dact_body(dy_ref, wc_ref, slope_ref, du_ref, sum_ref):
@@ -215,12 +265,8 @@
         sums_ref[n : n + 1, :] = sums[n]
 
 
-def out_back_body(dlow_ref, o_ref, wo_ref, do_ref, g_ref):
+def out_back_body(dlow_ref, wo_ref, do_ref):
     do_ref[...] = dot(dlow_ref[...], wo_ref[...]).astype(BF)
-    parts, groups, sub, local = g_ref.shape
-    g = dot(dlow_ref[...].T, o_ref[...]).astype(BF)
-    for j in range(groups):
-        g_ref[:, j] = g[:, j * local : (j + 1) * local].reshape(parts, sub, local)
 
 
 def attend_back_body(slots, q_ref, k_ref, v_ref, p_ref, do_ref, dq_ref, dk_ref, dv_ref):
@@ -251,20 +297,45 @@
         ref[tail:, :] = jnp.zeros((ROWS - tail, 2 * HEAD_DIM), BF)
 
 
-def qkv_outer_body(h_ref, dq_ref, dk_ref, dv_ref, g_ref, sums_ref, t_ref):
-    t_ref[...] = h_ref[...].T
-    parts, groups, sub, cols = g_ref.shape
-    local = cols // 3
+def small_outer(h_ref, dq_ref, dk_ref, dv_ref, dlow_ref, o_ref, sums_ref, store):
+    ht = h_ref[...].T
     for s, ref in enumerate((dq_ref, dk_ref, dv_ref)):
-        g = dot(t_ref[...], ref[...]).astype(BF)
-        for j in range(groups):
-            g_ref[:, j, :, s * local : (s + 1) * local] = g[:, j * local : (j + 1) * local].reshape(parts, sub, local)
+        store(s, dot(ht, ref[...]).astype(BF))
         if s != 1:
             n = 0 if s == 0 else 1
             sums_ref[n : n + 1, :] = colsum(ref[...].astype(F32))
-
-
-def input_back_body(slots, length, x_ref, dq_ref, dk_ref, dv_ref, wq_ref, dmid_ref, gain_ref, out_ref, sums_ref, acc_ref):
+    store(3, dot(dlow_ref[...].T, o_ref[...]).astype(BF))
+
+
+def outer_ring_body(info_ref, h_ref, dq_ref, dk_ref, dv_ref, dlow_ref, o_ref, keep_ref, send_ref, sums_ref, buf_ref):
+    groups = buf_ref.shape[0]
+    local = h_ref.shape[1] // groups
+    slots, _, sub, _ = keep_ref.shape
+
+    def store(s, g):
+        for j in range(groups):
+            buf_ref[j, :, s * local : (s + 1) * local] = g[:, j * local : (j + 1) * local]
+
+    small_outer(h_ref, dq_ref, dk_ref, dv_ref, dlow_ref, o_ref, sums_ref, store)
+    for k in range(slots):
+        rows = pl.ds(pl.multiple_of(info_ref[2 + k] * sub, sub), sub)
+        for rel in range(4):
+            ref = send_ref if rel % 2 else keep_ref
+            ref[k, rel // 2] = buf_ref[lax.bitwise_xor(info_ref[0], rel), rows, :]
+
+
+def outer_plain_body(h_ref, dq_ref, dk_ref, dv_ref, dlow_ref, o_ref, g_ref, sums_ref):
+    parts, groups, sub, cols = g_ref.shape
+    local = cols // 4
+
+    def store(s, g):
+        for j in range(groups):
+            g_ref[:, j, :, s * local : (s + 1) * local] = g[:, j * local : (j + 1) * local].reshape(parts, sub, local)
+
+    small_outer(h_ref, dq_ref, dk_ref, dv_ref, dlow_ref, o_ref, sums_ref, store)
+
+
+def input_back_body(slots, length, info_ref, x_ref, dq_ref, dk_ref, dv_ref, wq_ref, dmid_ref, gain_ref, all_ref, out_ref, sums_ref, acc_ref):
     width = x_ref.shape[1]
     for s, ref in enumerate((dq_ref, dk_ref, dv_ref)):
         part = dot(ref[...], wq_ref[:, s * width : (s + 1) * width], NT)
@@ -279,7 +350,9 @@
         dh = acc_ref[rows, :]
         normal, scale_inv = norm_stats(x_ref[rows, :].astype(F32))
         grad = dmid_ref[rows, :] + norm_back(dh, normal, scale_inv, gain_ref[...])
-        out_ref[i] = grad[:length].astype(BF)
+        grad = grad[:length].astype(BF)
+        out_ref[i] = grad
+        all_ref[0, i] = grad
         sums[0] = sums[0] + colsum(dh * normal)
         sums[1] = sums[1] + colsum(dh)
     for n in range(2):
@@ -312,35 +385,89 @@
     ff = units * groups
     axes = ("dp", "mp")
     mine = lax.axis_index("mp")
-
-    def padded(tokens):
-        tokens = jnp.pad(tokens, ((0, 0), (0, SLOT_ROWS - length), (0, 0)))
-        return jnp.pad(tokens.reshape(slots * SLOT_ROWS, width), ((0, ROWS - slots * SLOT_ROWS), (0, 0)))
-
-    pick = lambda a: lax.dynamic_index_in_dim(a, mine, 0, keepdims=False)
-    live = pick(counts)
-    x = padded(pick(inputs))
-    mask = (jnp.arange(slots, dtype=jnp.int32) < live[0]).astype(BF)
-    dy = padded(pick(cotangent) * mask[:, None, None])
+    ring = sub % 32 == 0
+
+    cycle = list(range(0, parts, 2)) + list(range(parts - 1, 0, -2))
+    place = [cycle.index(d) for d in range(parts)]
+    here = jnp.array(place, jnp.int32)[lax.axis_index("dp")]
+    owner = jnp.array(cycle, jnp.int32)
+    right = [(cycle[p], cycle[(p + 1) % parts]) for p in range(parts)]
+    left = [(b, a) for a, b in right]
+    far = parts // 2
+    mp_swap = lambda a, bit: lax.ppermute(a, "mp", [(j, j ^ bit) for j in range(groups)])
+    dp_swap = lambda a, bit: lax.ppermute(a, "dp", [(d, d ^ bit) for d in range(parts)])
+    to_right = lambda a: lax.ppermute(a, "dp", right)
+    to_left = lambda a: lax.ppermute(a, "dp", left)
     row = lambda v: v.reshape(1, -1)
-
-    shard = jnp.concatenate([qkv_weight, out_weight.T, hidden_weight, down_weight.T], axis=1)
-    every = lax.all_gather(shard, axes, axis=0, tiled=False).reshape(parts, groups, sub, -1)
-    piece = lambda n: lax.slice_in_dim(every, n * 4 * local, (n + 1) * 4 * local, axis=3)
-    wa, wb, wc = piece(0), piece(1), piece(2)
-    biases = lax.all_gather(jnp.concatenate([query_bias, value_bias, hidden_bias]), "mp", axis=0, tiled=False)
+    live = lax.dynamic_index_in_dim(counts, mine, 0, keepdims=False)[0]
+
+    def info_of(offsets):
+        return jnp.concatenate([jnp.stack([mine, live]), owner[(here + jnp.array(offsets, jnp.int32)) % parts]])
+
+    smem = pl.BlockSpec(memory_space=pltpu.SMEM)
+    info = jnp.stack([mine, live])
+
+    shard_bc = jnp.concatenate([hidden_weight, down_weight.T], axis=1)
+    bc = lax.all_gather(shard_bc, axes, axis=0, tiled=False).reshape(parts, groups, sub, 2 * units)
+    shard_a = jnp.concatenate([qkv_weight, out_weight.T], axis=1)
+    vectors = jnp.concatenate([query_bias, value_bias, hidden_bias])
+    if ring:
+        mate = mp_swap(shard_a, 2)
+        start = jnp.stack([shard_a, mate])
+        chunks = [start]
+        offsets = [0]
+        rights, lefts = start, start
+        for k in range(1, far + 1):
+            rights = to_right(rights)
+            chunks.append(rights)
+            offsets.append(-k)
+            if k < far:
+                lefts = to_left(lefts)
+                chunks.append(lefts)
+                offsets.append(k)
+        others = [mp_swap(c, 1) for c in chunks]
+        ring_info = info_of(offsets)
+    else:
+        wa = lax.all_gather(shard_a, axes, axis=0, tiled=False).reshape(parts, groups, sub, 4 * local)
+    two = jnp.stack([vectors, mp_swap(vectors, 1)])
+    four = jnp.concatenate([two, mp_swap(two, 2)])
+    biases = four[jnp.arange(groups) ^ mine]
     qb, vb, hb = (biases[:, a:b].reshape(-1) for a, b in ((0, local), (local, 2 * local), (2 * local, None)))
     bias_row = row(jnp.concatenate([qb, jnp.zeros_like(qb), vb]))
 
     mm = 2 * ROWS * width * width
     t_bf = lambda n: sds((ROWS, n), BF)
     t_f = lambda n: sds((ROWS, n), F32)
-    h1, qkv, wq, wo = call(
-        qkv_body,
-        [t_bf(width), t_bf(3 * width), sds((width, 3 * width), BF), sds((width, width), BF)],
-        [x, row(norm_gain), row(norm_shift), wa, bias_row],
-        flops=3 * mm,
-    )
+    block = lambda shape: pl.BlockSpec(shape, lambda i, info: (0,) * len(shape))
+    mine_block = pl.BlockSpec((1, slots, length, width), lambda i, info: (info[0], 0, 0, 0))
+    x, dy = pl.pallas_call(
+        functools.partial(prep_body, slots, length),
+        out_shape=(t_bf(width), t_bf(width)),
+        grid_spec=pltpu.PrefetchScalarGridSpec(
+            num_scalar_prefetch=1,
+            grid=(1,),
+            in_specs=[mine_block, mine_block],
+            out_specs=[block((ROWS, width)), block((ROWS, width))],
+        ),
+        compiler_params=pltpu.CompilerParams(vmem_limit_bytes=24 * 1024 * 1024),
+        cost_estimate=pl.CostEstimate(flops=0, bytes_accessed=8 * ROWS * width, transcendentals=0),
+        name="prep",
+    )(info, inputs, cotangent)
+
+    qkv_outs = [t_bf(width), t_bf(3 * width), sds((width, 3 * width), BF), sds((width, width), BF)]
+    qkv_ins = [x, row(norm_gain), row(norm_shift), bias_row]
+    if ring:
+        h1, qkv, wq, wo = call(
+            qkv_ring_body,
+            qkv_outs,
+            [ring_info] + qkv_ins + chunks + others,
+            [smem] + [None] * (len(qkv_ins) + 2 * len(chunks)),
+            scratch=[pltpu.VMEM((groups, width, 4 * local), BF)],
+            flops=3 * mm,
+            name="qkv",
+        )
+    else:
+        h1, qkv, wq, wo = call(qkv_gathered_body, qkv_outs, qkv_ins + [wa], flops=3 * mm, name="qkv")
     pair = 2 * HEAD_DIM
     pairs = width // pair
     head = lambda s: pl.BlockSpec((ROWS, pair), lambda i: (0, s * pairs + i))
@@ -354,6 +481,7 @@
         [head(0), p_spec],
         (pairs,),
         flops=mm,
+        name="attend",
     )
     rows256 = pl.BlockSpec((256, width), lambda i: (i, 0))
     middle, h2 = call(
@@ -364,69 +492,108 @@
         [rows256, rows256],
         (ROWS // 256,),
         flops=mm,
+        name="mix",
     )
     step = 256
     per = units // step
-    wcols = pl.BlockSpec((parts, 1, sub, step), lambda i: (0, i // per, 0, i % per))
+    steps = ff // step
+    wcols = lambda n: pl.BlockSpec((parts, 1, sub, step), lambda i: (0, i // per, 0, n * per + i % per))
+    piece = lambda n: pl.BlockSpec((parts, groups, sub, units), lambda i: (0, 0, 0, n))
     tcols = pl.BlockSpec((ROWS, step), lambda i: (0, i))
     vcols = lambda n: pl.BlockSpec((n, step), lambda i: (0, i))
     act, slope = call(
         hidden_body,
         [t_bf(ff), t_bf(ff)],
-        [h2, wb, row(hb)],
-        [None, wcols, vcols(1)],
+        [h2, bc, row(hb)],
+        [None, wcols(0), vcols(1)],
         [tcols, tcols],
-        (ff // step,),
+        (steps,),
         flops=4 * mm,
-    )
-    smem = pl.BlockSpec(memory_space=pltpu.SMEM)
-    (block_out,) = call(
-        functools.partial(down_body, slots, length),
-        [sds((slots, length, width), BF)],
-        [live, act, wc, middle, row(down_bias)],
-        [smem, None, None, None, None],
-        scratch=[pltpu.VMEM((ROWS, width), F32)],
-        flops=4 * mm,
-    )
-    g_shape = lambda n: sds((parts, groups, sub, n), BF)
-
-    def outer(left, right):
-        (g,) = call(
-            outer_body,
-            [g_shape(units)],
-            [left, right],
-            [None, tcols],
-            [wcols],
-            (ff // step,),
-            scratch=[pltpu.VMEM((width, ROWS), BF)],
-            flops=4 * mm,
-        )
-        return g
-
-    g_down = outer(dy, act)
+        name="hidden",
+    )
     du, sum_hidden = call(
         dact_body,
         [t_bf(ff), sds((8, ff), F32)],
-        [dy, wc, slope],
-        [None, wcols, tcols],
+        [dy, bc, slope],
+        [None, wcols(1), tcols],
         [tcols, vcols(8)],
-        (ff // step,),
+        (steps,),
         flops=4 * mm,
-    )
-    g_hidden = outer(h2, du)
+        name="dact",
+    )
+    (g_bc,) = call(
+        outer_body,
+        [sds((parts, groups, sub, 2 * units), BF)],
+        [h2, dy, du, act],
+        [
+            None,
+            None,
+            pl.BlockSpec((ROWS, step), lambda i: (0, jnp.maximum(i - steps, 0))),
+            pl.BlockSpec((ROWS, step), lambda i: (0, jnp.minimum(i, steps - 1))),
+        ],
+        [
+            pl.BlockSpec(
+                (parts, 1, sub, step),
+                lambda i: (0, (i % steps) // per, 0, jnp.where(i < steps, per, 0) + i % per),
+            )
+        ],
+        (2 * steps,),
+        scratch=[pltpu.VMEM((width, ROWS), BF)],
+        flops=8 * mm,
+        name="outer_bc",
+    )
+    s_bc = lax.psum_scatter(
+        g_bc.reshape(parts * groups, sub, 2 * units), axes, scatter_dimension=0, tiled=False
+    ).astype(F32)
+
+    out_shape = sds((batches, slots, length, width), BF)
+    own_shape = sds((slots, length, width), BF)
+
+    def with_slot(body, outs, ins, flops, name):
+        fixed = lambda a: pl.BlockSpec(a.shape, lambda i, info: (0,) * len(a.shape))
+        return pl.pallas_call(
+            body,
+            out_shape=tuple(outs),
+            grid_spec=pltpu.PrefetchScalarGridSpec(
+                num_scalar_prefetch=1,
+                grid=(1,),
+                in_specs=[fixed(a) if s is None else s for a, s in ins],
+                out_specs=[mine_block] + [fixed(a) for a in outs[1:]],
+                scratch_shapes=[pltpu.VMEM((ROWS, width), F32)],
+            ),
+            compiler_params=pltpu.CompilerParams(vmem_limit_bytes=60 * 1024 * 1024),
+            cost_estimate=pl.CostEstimate(
+                flops=flops, bytes_accessed=sum(a.size * a.dtype.itemsize for a, _ in ins), transcendentals=0
+            ),
+            name=name,
+        )(info, *[a for a, _ in ins])
+
+    def spread(all_out, own):
+        crossed = mp_swap(own, 2)
+        for rel, value in ((1, mp_swap(own, 1)), (2, crossed), (3, mp_swap(crossed, 1))):
+            all_out = lax.dynamic_update_index_in_dim(all_out, value, mine ^ rel, 0)
+        return all_out
+
+    piece_c = pl.BlockSpec((parts, groups, sub, units), lambda i, info: (0, 0, 0, 1))
+    all_out, own_out = with_slot(
+        functools.partial(down_body, slots, length),
+        [out_shape, own_shape],
+        [(act, None), (bc, piece_c), (middle, None), (row(down_bias), None)],
+        4 * mm,
+        "down",
+    )
+    all_out = spread(all_out, own_out)
+
     dmid, dlow, sums_mid = call(
         mid_back_body,
         [t_f(width), t_bf(width), sds((8, width), F32)],
-        [dy, du, wb, middle, row(mlp_gain)],
+        [dy, du, bc, middle, row(mlp_gain)],
+        [None, None, piece(0), None, None],
         scratch=[pltpu.VMEM((ROWS, width), F32)],
         flops=4 * mm,
-    )
-    do, g_out = call(
-        out_back_body,
-        [t_bf(width), g_shape(local)],
-        [dlow, mixed, wo],
-        flops=2 * mm,
-    )
+        name="mid_back",
+    )
+    (do,) = call(out_back_body, [t_bf(width)], [dlow, wo], flops=mm, name="out_back")
     dq, dk, dv = call(
         functools.partial(attend_back_body, slots),
         [t_bf(width)] * 3,
@@ -435,48 +602,90 @@
         [head(0)] * 3,
         (pairs,),
         flops=2 * mm,
-    )
-    g_qkv, sums_qkv = call(
-        qkv_outer_body,
-        [g_shape(3 * local), sds((8, width), F32)],
-        [h1, dq, dk, dv],
-        scratch=[pltpu.VMEM((width, ROWS), BF)],
-        flops=3 * mm,
-    )
-    input_grad, sums_in = call(
+        name="attend_back",
+    )
+    outer_ins = [h1, dq, dk, dv, dlow, mixed]
+    sum_shape = sds((8, width), F32)
+    if ring:
+        send_order = []
+        for k in range(far, 0, -1):
+            send_order.append(k)
+            if k > 1:
+                send_order.append(1 - k)
+        send_order.append(0)
+        half_shape = sds((parts, 2, sub, 4 * local), BF)
+        keep, send, sums_qkv = call(
+            outer_ring_body,
+            [half_shape, half_shape, sum_shape],
+            [info_of(send_order)] + outer_ins,
+            [smem] + [None] * len(outer_ins),
+            scratch=[pltpu.VMEM((groups, width, 4 * local), BF)],
+            flops=4 * mm,
+            name="outer_a",
+        )
+        cuts = [0, 2, 4, parts]
+        got = [mp_swap(send[a:b], 1) for a, b in zip(cuts, cuts[1:])]
+        got = [(a, g) for a, g in zip(cuts, got)]
+
+        def term(offset):
+            n = send_order.index(offset)
+            a, g = [(a, g) for a, g in got if a <= n][-1]
+            return keep[n].astype(F32) + g[n - a].astype(F32)
+
+        rights = to_right(term(far).astype(BF))
+        lefts = to_left(term(1 - far).astype(BF))
+        for k in range(far - 1, 0, -1):
+            rights = to_right((term(k) + rights.astype(F32)).astype(BF))
+            if k > 1:
+                lefts = to_left((term(1 - k) + lefts.astype(F32)).astype(BF))
+        total = term(0) + rights.astype(F32) + lefts.astype(F32)
+        s_a = total[0] + mp_swap(total[1].astype(BF), 2).astype(F32)
+    else:
+        g_a, sums_qkv = call(
+            outer_plain_body,
+            [sds((parts, groups, sub, 4 * local), BF), sum_shape],
+            outer_ins,
+            flops=4 * mm,
+            name="outer_a",
+        )
+        s_a = lax.psum_scatter(
+            g_a.reshape(parts * groups, sub, 4 * local), axes, scatter_dimension=0, tiled=False
+        ).astype(F32)
+    all_grad, own_grad, sums_in = with_slot(
         functools.partial(input_back_body, slots, length),
-        [sds((slots, length, width), BF), sds((8, width), F32)],
-        [x, dq, dk, dv, wq, dmid, row(norm_gain)],
-        scratch=[pltpu.VMEM((ROWS, width), F32)],
-        flops=3 * mm,
-    )
-
-    gather = lambda a: lax.all_gather(a, "mp", axis=0, tiled=False)
-    scatter = lambda g: lax.psum_scatter(
-        g.reshape(parts * groups, sub, -1), axes, scatter_dimension=0, tiled=False
-    ).astype(F32)
-    s_down, s_hidden, s_out, s_qkv = scatter(g_down), scatter(g_hidden), scatter(g_out), scatter(g_qkv)
+        [out_shape, own_shape, sum_shape],
+        [(x, None), (dq, None), (dk, None), (dv, None), (wq, None), (dmid, None), (row(norm_gain), None)],
+        3 * mm,
+        "input_back",
+    )
+    all_grad = spread(all_grad, own_grad)
+
     sums = jnp.concatenate(
         [sums_in[:2].reshape(-1), sums_mid[:4].reshape(-1), sums_qkv[:2].reshape(-1), sum_hidden[0]]
     )
-    sums = lax.psum(sums, axes)
+    for bit in (1, 2):
+        sums = sums + mp_swap(sums, bit)
+    bit = 1
+    while bit < parts:
+        sums = sums + dp_swap(sums, bit)
+        bit *= 2
     vec = [sums[n * width : (n + 1) * width] for n in range(8)]
     own = lambda v, n: lax.dynamic_slice_in_dim(v, mine * n, n, 0)
     return (
-        gather(block_out),
-        gather(input_grad),
+        all_out,
+        all_grad,
         vec[0],
         vec[1],
-        s_qkv,
+        s_a[:, : 3 * local],
         own(vec[6], local),
         own(vec[7], local),
-        s_out.T,
+        s_a[:, 3 * local :].T,
         vec[4],
         vec[2],
         vec[3],
-        s_hidden,
+        s_bc[:, :units],
         own(sums[8 * width :], units),
-        s_down.T,
+        s_bc[:, units:].T,
         vec[5],
     )
 

time: 784 us -> 418 us (0.53)
  waiting for transfers between devices: 453 us -> 84.5 us
  blocking collectives: 45.4 us -> 0 us
  starting transfers between devices: 0.75 us -> 33.1 us
  other arithmetic: 7.25 us -> 17.2 us
    reduce_scatter x4 -> x1, waiting for transfers between devices: 292 us -> 0.01 us  [on_device(): lax.psum_scatter(g_bc.reshape(parts * groups, sub, 2 * units), axes, scat...]
    all_gather x3 -> x1, waiting for transfers between devices: 161 us -> 0.01 us  [on_device(): lax.all_gather(shard_bc, axes, axis=0, tiled=False)]
    ppermute x0 -> x40, waiting for transfers between devices: none -> 84.4 us  [the longest x23 36.6 us: on_device(): lax.ppermute(a, 'mp', [(j, j ^ bit) for j in range(groups)])]
    psum x1 -> x0, blocking collectives: 39.1 us -> none  [on_device(): sums = lax.psum(sums, axes)]
    ppermute x0 -> x40, starting transfers between devices: none -> 33.1 us  [the longest x8 14.8 us: on_device(): to_right = lambda a: lax.ppermute(a, 'dp', right)]
    pallas_call x0 -> x3, Pallas kernels: none -> 26.7 us  [the longest x2 25.8 us: with_slot(): pl.pallas_call(body, out_shape=tuple(outs), grid_spec=pltpu.PrefetchScala...]
    pallas_call x13 -> x10, Pallas kernels: 196 us -> 174 us  [call(): pl.pallas_call(body, out_shape=tuple(outs), grid=(1,) if grid is None els...]
    dynamic_update_slice x0 -> x6, local copies, waits for them, and re-layouts: none -> 15.9 us  [spread(): all_out = lax.dynamic_update_index_in_dim(all_out, value, mine ^ rel, 0)]
  transfers between devices with their start and end apart: 7 -> 42, of which waited for: 6 -> 17; matrix products, arithmetic and copies ran while one was open for 6% -> 17% of each run, Pallas kernels for 11% -> 34%
where the time goes in v2:
time: 418 us; the launch traced here: 411 us
  Pallas kernels  200 us (48%)
  waiting for transfers between devices  84.5 us (20%)
  local copies, waits for them, and re-layouts  60.7 us (15%)
  starting transfers between devices  33.1 us (8%)
  other arithmetic  17.2 us (4%)
  between operations  14.9 us (4%)
    pallas_call x10, Pallas kernels, call(): pl.pallas_call(body, out_shape=tuple(outs), grid=(1,) if grid is None els...  174 us
    ppermute x23, waiting for transfers between devices, on_device(): lax.ppermute(a, 'mp', [(j, j ^ bit) for j in range(groups)])  36.6 us
    pallas_call x2, Pallas kernels, with_slot(): pl.pallas_call(body, out_shape=tuple(outs), grid_spec=pltpu.PrefetchScala...  25.8 us
    unnamed x70, local copies, waits for them, and re-layouts  25.5 us
    ppermute x8, waiting for transfers between devices, on_device(): to_right = lambda a: lax.ppermute(a, 'dp', right)  23.9 us
    ppermute x6, waiting for transfers between devices, on_device(): to_left = lambda a: lax.ppermute(a, 'dp', left)  21.2 us
    dynamic_update_slice x6, local copies, waits for them, and re-layouts, spread(): all_out = lax.dynamic_update_index_in_dim(all_out, value, mine ^ rel, 0)  15.9 us
    ppermute x8, starting transfers between devices, on_device(): to_right = lambda a: lax.ppermute(a, 'dp', right)  14.8 us
  transfers between devices with their start and end apart: 42, of which 17 were waited for; matrix products, arithmetic and copies ran while one was open for 17% of the time, Pallas kernels for 34%

profile of v2, /device:TPU:0, one launch (start us, length us, event | category | flops | bytes accessed | tf_op | source)
XLA Modules:
  0.0 410.9 jit_solution(3310399652436624561)
XLA Ops:
  10.9 3.0 collective-permute-start.2
  21.3 8.3 %collective-permute-done.3.refs_1_ = bf16[2,96,768]{2,1,0:T(8,128)(2,1)S(1)} collective-permute-done((bf16[2,96,768]{2,1,0:T(8,128)(2,1)S(1)}, bf16[2,96,768]{2,1,0:T(8,128)(2,1)S(1)}, u32[]{:S(2)}, u32[]{:S(2)}) %collective-permute-start.3) | collective-permute-done | bytes 294944 | tf_op jit(solution)/shard_map/ppermute | solution.py:399
  34.9 3.9 collective-permute-done.5.refs_3_
  43.4 3.7 copy.41.x_ref
  55.5 3.3 collective-permute-start.9
  60.2 6.5 %collective-permute-done.8.refs_6_ = bf16[2,96,768]{2,1,0:T(8,128)(2,1)S(1)} collective-permute-done((bf16[2,96,768]{2,1,0:T(8,128)(2,1)}, bf16[2,96,768]{2,1,0:T(8,128)(2,1)S(1)}, u32[]{:S(2)}, u32[]{:S(2)}) %collective-permute-start.8) | collective-permute-done | bytes 294944 | tf_op jit(solution)/shard_map/ppermute | solution.py:400
  70.3 15.4 %qkv.1 = (bf16[1024,768]{1,0:T(8,128)(2,1)}, bf16[1024,2304]{1,0:T(8,128)(2,1)}, bf16[768,2304]{1,0:T(8,128)(2,1)}, bf16[768,768]{1,0:T(8,128)(2,1)}) custom-call(s32[10]{0:T(128)} %pad_add_fusion.1.info_ref, bf16[1024,768]{1,0:T(8,128)(2,1)} %copy-done.4, f32[1,768]{1,0:T(1,128)} %reshape.119.gain_ref, f32[1,768]{1,0:T(1,128)} %reshape.120.shift_ref, ...), custom_call_target="tpu_custom_call" | custom-call | flops 3623878656 | bytes 17316904 | tf_op jit(solution)/shard_map/qkv/pallas_call | solution.py:54
  85.7 29.2 %attend.1 = (bf16[1024,768]{1,0:T(8,128)(2,1)}, bf16[12,5,200,200]{3,2,1,0:T(8,128)(2,1)}) custom-call(bf16[1024,2304]{1,0:T(8,128)(2,1)} %get-tuple-element.44.q_ref.k_ref.v_ref, bf16[1024,2304]{1,0:T(8,128)(2,1)} %get-tuple-element.44.q_ref.k_ref.v_ref, bf16[1024,2304]{1,0:T(8,128)(2,1)} %get-tuple-element.44.q_ref.k_ref.v_ref), custom_call_target="tpu_custom_call" | custom-call | flops 1207959552 | bytes 20528640 | tf_op jit(solution)/shard_map/attend/pallas_call | solution.py:54
  114.9 7.3 %mix.1 = (f32[1024,768]{1,0:T(8,128)}, bf16[1024,768]{1,0:T(8,128)(2,1)}) custom-call(bf16[1024,768]{1,0:T(8,128)(2,1)} %copy-done.4, bf16[1024,768]{1,0:T(8,128)(2,1)} %get-tuple-element.45.o_ref, bf16[768,768]{1,0:T(8,128)(2,1)} %get-tuple-element.46.wo_ref, f32[1,768]{1,0:T(1,128)} %reshape.124.bias_ref, f32[1,768]{1,0:T(1,128)} %reshape.125.gain_ref, ...), custom_call_target="tpu_custom_call" | custom-call | flops 1207959552 | bytes 9053184 | tf_op jit(solution)/shard_map/mix/pallas_call | solution.py:54
  122.1 20.3 %hidden.1 = (bf16[1024,3072]{1,0:T(8,128)(2,1)}, bf16[1024,3072]{1,0:T(8,128)(2,1)}) custom-call(bf16[1024,768]{1,0:T(8,128)(2,1)} %get-tuple-element.47.h_ref, bf16[8,4,96,1536]{3,2,1,0:T(8,128)(2,1)} %bitcast.70, f32[1,3072]{1,0:T(1,128)} %bitcast.83), custom_call_target="tpu_custom_call" | custom-call | flops 4831838208 | bytes 23605248 | tf_op jit(solution)/shard_map/hidden/pallas_call | solution.py:54
  142.4 14.2 %dact.1 = (bf16[1024,3072]{1,0:T(8,128)(2,1)}, f32[8,3072]{1,0:T(8,128)}) custom-call(bf16[1024,768]{1,0:T(8,128)(2,1)} %copy-done.2, bf16[8,4,96,1536]{3,2,1,0:T(8,128)(2,1)} %bitcast.71, bf16[1024,3072]{1,0:T(8,128)(2,1)} %get-tuple-element.54.slope_ref), custom_call_target="tpu_custom_call" | custom-call | flops 4831838208 | bytes 23691264 | tf_op jit(solution)/shard_map/dact/pallas_call | solution.py:54
  156.6 25.1 %outer_bc.1 = bf16[8,4,96,1536]{3,2,1,0:T(8,128)(2,1)} custom-call(bf16[1024,768]{1,0:T(8,128)(2,1)} %get-tuple-element.47.h_ref, bf16[1024,768]{1,0:T(8,128)(2,1)} %copy-done.2, bf16[1024,3072]{1,0:T(8,128)(2,1)} %get-tuple-element.55.du_ref, bf16[1024,3072]{1,0:T(8,128)(2,1)} %get-tuple-element.48.act_ref), custom_call_target="tpu_custom_call" | custom-call | flops 9663676416 | bytes 25165824 | tf_op jit(solution)/shard_map/outer_bc/pallas_call | solution.py:54
  183.6 16.1 %mid_back.1 = (f32[1024,768]{1,0:T(8,128)}, bf16[1024,768]{1,0:T(8,128)(2,1)}, f32[8,768]{1,0:T(8,128)}) custom-call(bf16[1024,768]{1,0:T(8,128)(2,1)} %copy-done.2, bf16[1024,3072]{1,0:T(8,128)(2,1)} %get-tuple-element.55.du_ref, bf16[8,4,96,1536]{3,2,1,0:T(8,128)(2,1)} %bitcast.72, f32[1024,768]{1,0:T(8,128)} %get-tuple-element.49.mid_ref, ...), custom_call_target="tpu_custom_call" | custom-call | flops 4831838208 | bytes 25193472 | tf_op jit(solution)/shard_map/mid_back/pallas_call | solution.py:54
  199.7 4.4 %out_back.1.do_ref = bf16[1024,768]{1,0:T(8,128)(2,1)} custom-call(bf16[1024,768]{1,0:T(8,128)(2,1)} %get-tuple-element.56.dlow_ref, bf16[768,768]{1,0:T(8,128)(2,1)} %get-tuple-element.46.wo_ref), custom_call_target="tpu_custom_call" | custom-call | flops 1207959552 | bytes 4325376 | tf_op jit(solution)/shard_map/out_back/pallas_call | solution.py:54
  204.2 29.7 %attend_back.1 = (bf16[1024,768]{1,0:T(8,128)(2,1)}, bf16[1024,768]{1,0:T(8,128)(2,1)}, bf16[1024,768]{1,0:T(8,128)(2,1)}) custom-call(bf16[1024,2304]{1,0:T(8,128)(2,1)} %get-tuple-element.44.q_ref.k_ref.v_ref, bf16[1024,2304]{1,0:T(8,128)(2,1)} %get-tuple-element.44.q_ref.k_ref.v_ref, bf16[1024,2304]{1,0:T(8,128)(2,1)} %get-tuple-element.44.q_ref.k_ref.v_ref, ...), custom_call_target="tpu_custom_call" | custom-call | flops 2415919104 | bytes 25247232 | tf_op jit(solution)/shard_map/attend_back/pallas_call | solution.py:54
  233.8 12.0 %outer_a.1 = (bf16[8,2,96,768]{3,2,1,0:T(8,128)(2,1)}, bf16[8,2,96,768]{3,2,1,0:T(8,128)(2,1)}, f32[8,768]{1,0:T(8,128)}) custom-call(s32[10]{0:T(128)} %pad_add_fusion.3.info_ref, bf16[1024,768]{1,0:T(8,128)(2,1)} %get-tuple-element.66.h_ref, bf16[1024,768]{1,0:T(8,128)(2,1)} %get-tuple-element.57.dq_ref, bf16[1024,768]{1,0:T(8,128)(2,1)} %get-tuple-element.58.dk_ref, ...), custom_call_target="tpu_custom_call" | custom-call | flops 4831838208 | bytes 14180392 | tf_op jit(solution)/shard_map/outer_a/pallas_call | solution.py:54
  249.2 12.7 %input_back.1 = (bf16[4,5,197,768]{3,2,1,0:T(8,128)(2,1)}, bf16[5,197,768]{2,1,0:T(8,128)(2,1)}, f32[8,768]{1,0:T(8,128)}) custom-call(s32[2]{0:T(128)} %copy-done.3, bf16[1024,768]{1,0:T(8,128)(2,1)} %copy-done.4, bf16[1024,768]{1,0:T(8,128)(2,1)} %get-tuple-element.57.dq_ref, bf16[1024,768]{1,0:T(8,128)(2,1)} %get-tuple-element.58.dk_ref, ...), custom_call_target="tpu_custom_call" | custom-call | flops 3623878656 | bytes 12979200 | tf_op jit(solution)/shard_map/input_back/pallas_call | solution.py:554
  265.1 4.8 %collective-permute-done.25 = f32[9216]{0:T(1024)S(1)} collective-permute-done((f32[9216]{0:T(1024)S(1)}, f32[9216]{0:T(1024)S(1)}, u32[]{:S(2)}, u32[]{:S(2)}) %collective-permute-start.25) | collective-permute-done | bytes 36896 | tf_op jit(solution)/shard_map/ppermute | solution.py:397
  279.6 13.1 %down.1 = (bf16[4,5,197,768]{3,2,1,0:T(8,128)(2,1)}, bf16[5,197,768]{2,1,0:T(8,128)(2,1)}) custom-call(s32[2]{0:T(128)} %copy-done.3, bf16[1024,3072]{1,0:T(8,128)(2,1)} %get-tuple-element.48.act_ref, bf16[8,4,96,1536]{3,2,1,0:T(8,128)(2,1)} %bitcast.73, f32[1024,768]{1,0:T(8,128)} %get-tuple-element.49.mid_ref, f32[1,768]{1,0:T(1,128)} %reshape.128.bias_ref), custom_call_target="tpu_custom_call" | custom-call | flops 4831838208 | bytes 18877440 | tf_op jit(solution)/shard_map/down/pallas_call | solution.py:554
  294.8 2.7 collective-permute-done.36
  300.8 2.8 collective-permute-done.28
  303.5 6.9 %collective-permute-done.33 = bf16[2,96,768]{2,1,0:T(8,128)(2,1)S(1)} collective-permute-done((bf16[2,96,768]{2,1,0:T(8,128)(2,1)S(1)}, bf16[2,96,768]{2,1,0:T(8,128)(2,1)S(1)}, u32[]{:S(2)}, u32[]{:S(2)}) %collective-permute-start.33) | collective-permute-done | bytes 294944 | tf_op jit(solution)/shard_map/ppermute | solution.py:399
  313.6 11.3 %collective-permute-done.37 = bf16[2,96,768]{2,1,0:T(8,128)(2,1)S(1)} collective-permute-done((bf16[2,96,768]{2,1,0:T(8,128)(2,1)S(1)}, bf16[2,96,768]{2,1,0:T(8,128)(2,1)S(1)}, u32[]{:S(2)}, u32[]{:S(2)}) %collective-permute-start.37) | collective-permute-done | bytes 294944 | tf_op jit(solution)/shard_map/ppermute | solution.py:400
  329.8 4.1 %collective-permute-done.34 = bf16[2,96,768]{2,1,0:T(8,128)(2,1)S(1)} collective-permute-done((bf16[2,96,768]{2,1,0:T(8,128)(2,1)S(1)}, bf16[2,96,768]{2,1,0:T(8,128)(2,1)S(1)}, u32[]{:S(2)}, u32[]{:S(2)}) %collective-permute-start.34) | collective-permute-done | bytes 294944 | tf_op jit(solution)/shard_map/ppermute | solution.py:399
  337.3 26.7 %collective-permute-done.19 = bf16[5,197,768]{2,1,0:T(8,128)(2,1)} collective-permute-done((bf16[5,197,768]{2,1,0:T(8,128)(2,1)}, bf16[5,197,768]{2,1,0:T(8,128)(2,1)}, u32[]{:S(2)}, u32[]{:S(2)}) %collective-permute-start.19) | collective-permute-done | bytes 1512992 | tf_op jit(solution)/shard_map/ppermute | solution.py:397
  364.1 2.7 bitcast_dynamic-update-slice_fusion.2
  366.7 2.7 bitcast_dynamic-update-slice_fusion.1
  373.8 2.7 bitcast_dynamic-update-slice_fusion.4
  376.4 3.1 collective-permute-done.39
  381.1 2.6 bitcast_dynamic-update-slice_fusion
  383.7 7.7 %copy.45 = bf16[4,5,197,768]{3,0,2,1:T(4,128)(2,1)} copy(bf16[4,5,197,768]{3,2,1,0:T(8,128)(2,1)} %bitcast_dynamic-update-slice_fusion) | data formatting | bytes 12103680
  394.0 7.7 %copy.44 = bf16[4,5,197,768]{3,0,2,1:T(4,128)(2,1)} copy(bf16[4,5,197,768]{3,2,1,0:T(8,128)(2,1)} %bitcast_dynamic-update-slice_fusion.3) | data formatting | bytes 12103680
  (209 shorter events, 79.3 us)
Async XLA Ops:
  7.2 114.9 %all-gather.3.cloned.1.call-start = ((), (), s32[]{:S(2)}) async-start(), calls=%async_computation.2 | async-start | bytes 9732096 | tf_op jit(solution)/shard_map/all_gather | solution.py:411
  9.0 392.8 %reduce-scatter.2.cloned.1.call-start = ((), (), s32[]{:S(2)}) async-start(), calls=%async_computation.1 | async-start | bytes 9732096 | tf_op jit(solution)/shard_map/reduce_scatter | solution.py:545
  10.9 6.9 %collective-permute-start.2 = (bf16[96,768]{1,0:T(8,128)(2,1)S(1)}, bf16[96,768]{1,0:T(8,128)(2,1)S(1)}, u32[]{:S(2)}, u32[]{:S(2)}) collective-permute-start(bf16[96,768]{1,0:T(8,128)(2,1)S(1)} %pad_maximum_fusion.2), channel_id=1, source_target_pairs={{0,2},{1,3},{2,0},{3,1},{4,6},{5,7},{6,4},{7,5},{8,10},{9,11},{10,... | collective-permute-start | bytes 442376 | tf_op jit(solution)/shard_map/ppermute | solution.py:397
  14.8 18.9 %collective-permute-start = (f32[1152]{0:T(1024)S(1)}, f32[1152]{0:T(1024)S(1)}, u32[]{:S(2)}, u32[]{:S(2)}) collective-permute-start(f32[1152]{0:T(1024)S(1)} %concatenate.26), channel_id=1, source_target_pairs={{0,1},{1,0},{2,3},{3,2},{4,5},{5,4},{6,7},{7,6},{8,9},{9,8},{10,11... | collective-permute-start | bytes 13832 | tf_op jit(solution)/shard_map/ppermute | solution.py:397
  17.9 11.8 %collective-permute-start.3 = (bf16[2,96,768]{2,1,0:T(8,128)(2,1)S(1)}, bf16[2,96,768]{2,1,0:T(8,128)(2,1)S(1)}, u32[]{:S(2)}, u32[]{:S(2)}) collective-permute-start(bf16[2,96,768]{2,1,0:T(8,128)(2,1)S(1)} %pad_maximum_fusion.refs_0_), channel_id=1, source_target_pairs={{0,8},{8,16},{16,24},{24,28},{28,20},{20,12},{12,4},{4,0},{1,9},{9... | collective-permute-start | bytes 884744 | tf_op jit(solution)/shard_map/ppermute | solution.py:399
  21.1 13.2 %collective-permute-start.4 = (bf16[2,96,768]{2,1,0:T(8,128)(2,1)S(1)}, bf16[2,96,768]{2,1,0:T(8,128)(2,1)S(1)}, u32[]{:S(2)}, u32[]{:S(2)}) collective-permute-start(bf16[2,96,768]{2,1,0:T(8,128)(2,1)S(1)} %pad_maximum_fusion.refs_0_), channel_id=1, source_target_pairs={{8,0},{16,8},{24,16},{28,24},{20,28},{12,20},{4,12},{0,4},{9,1},{1... | collective-permute-start | bytes 884744 | tf_op jit(solution)/shard_map/ppermute | solution.py:400
  29.6 9.2 %collective-permute-start.5 = (bf16[2,96,768]{2,1,0:T(8,128)(2,1)S(1)}, bf16[2,96,768]{2,1,0:T(8,128)(2,1)}, u32[]{:S(2)}, u32[]{:S(2)}) collective-permute-start(bf16[2,96,768]{2,1,0:T(8,128)(2,1)S(1)} %collective-permute-done.3.refs_1_), channel_id=1, source_target_pairs={{0,8},{8,16},{16,24},{24,28},{28,20},{20,12},{12,4},{4,0},{1,9},{9... | collective-permute-start | bytes 884744 | tf_op jit(solution)/shard_map/ppermute | solution.py:399
  34.3 20.6 %collective-permute-start.6 = (bf16[2,96,768]{2,1,0:T(8,128)(2,1)S(1)}, bf16[2,96,768]{2,1,0:T(8,128)(2,1)}, u32[]{:S(2)}, u32[]{:S(2)}) collective-permute-start(bf16[2,96,768]{2,1,0:T(8,128)(2,1)S(1)} %collective-permute-done.4.refs_2_), channel_id=1, source_target_pairs={{8,0},{16,8},{24,16},{28,24},{20,28},{12,20},{4,12},{0,4},{9,1},{1... | collective-permute-start | bytes 884744 | tf_op jit(solution)/shard_map/ppermute | solution.py:400
  38.9 16.6 %collective-permute-start.7 = (bf16[2,96,768]{2,1,0:T(8,128)(2,1)}, bf16[2,96,768]{2,1,0:T(8,128)(2,1)}, u32[]{:S(2)}, u32[]{:S(2)}) collective-permute-start(bf16[2,96,768]{2,1,0:T(8,128)(2,1)} %collective-permute-done.5.refs_3_), channel_id=1, source_target_pairs={{0,8},{8,16},{16,24},{24,28},{28,20},{20,12},{12,4},{4,0},{1,9},{9... | collective-permute-start | bytes 884744 | tf_op jit(solution)/shard_map/ppermute | solution.py:399
  41.5 13.4 %collective-permute-start.1 = (f32[2,1152]{1,0:T(2,128)S(1)}, f32[2,1152]{1,0:T(2,128)S(1)}, u32[]{:S(2)}, u32[]{:S(2)}) collective-permute-start(f32[2,1152]{1,0:T(2,128)S(1)} %pad_maximum_fusion.6), channel_id=1, source_target_pairs={{0,2},{1,3},{2,0},{3,1},{4,6},{5,7},{6,4},{7,5},{8,10},{9,11},{10,... | collective-permute-start | bytes 27656 | tf_op jit(solution)/shard_map/ppermute | solution.py:397
  54.9 11.8 %collective-permute-start.8 = (bf16[2,96,768]{2,1,0:T(8,128)(2,1)}, bf16[2,96,768]{2,1,0:T(8,128)(2,1)S(1)}, u32[]{:S(2)}, u32[]{:S(2)}) collective-permute-start(bf16[2,96,768]{2,1,0:T(8,128)(2,1)} %collective-permute-done.6.refs_4_), channel_id=1, source_target_pairs={{8,0},{16,8},{24,16},{28,24},{20,28},{12,20},{4,12},{0,4},{9,1},{1... | collective-permute-start | bytes 884744 | tf_op jit(solution)/shard_map/ppermute | solution.py:400
  55.5 11.9 %collective-permute-start.9 = (bf16[2,96,768]{2,1,0:T(8,128)(2,1)}, bf16[2,96,768]{2,1,0:T(8,128)(2,1)S(1)}, u32[]{:S(2)}, u32[]{:S(2)}) collective-permute-start(bf16[2,96,768]{2,1,0:T(8,128)(2,1)} %collective-permute-done.7.refs_5_), channel_id=1, source_target_pairs={{0,8},{8,16},{16,24},{24,28},{28,20},{20,12},{12,4},{4,0},{1,9},{9... | collective-permute-start | bytes 884744 | tf_op jit(solution)/shard_map/ppermute | solution.py:399
  59.6 9.0 %collective-permute-start.13 = (bf16[2,96,768]{2,1,0:T(8,128)(2,1)}, bf16[2,96,768]{2,1,0:T(8,128)(2,1)S(1)}, u32[]{:S(2)}, u32[]{:S(2)}) collective-permute-start(bf16[2,96,768]{2,1,0:T(8,128)(2,1)} %collective-permute-done.5.refs_3_), channel_id=1, source_target_pairs={{0,1},{1,0},{2,3},{3,2},{4,5},{5,4},{6,7},{7,6},{8,9},{9,8},{10,11... | collective-permute-start | bytes 884744 | tf_op jit(solution)/shard_map/ppermute | solution.py:397
  59.6 9.0 %collective-permute-start.14 = (bf16[2,96,768]{2,1,0:T(8,128)(2,1)}, bf16[2,96,768]{2,1,0:T(8,128)(2,1)S(1)}, u32[]{:S(2)}, u32[]{:S(2)}) collective-permute-start(bf16[2,96,768]{2,1,0:T(8,128)(2,1)} %collective-permute-done.6.refs_4_), channel_id=1, source_target_pairs={{0,1},{1,0},{2,3},{3,2},{4,5},{5,4},{6,7},{7,6},{8,9},{9,8},{10,11... | collective-permute-start | bytes 884744 | tf_op jit(solution)/shard_map/ppermute | solution.py:397
  60.1 8.5 %collective-permute-start.15 = (bf16[2,96,768]{2,1,0:T(8,128)(2,1)}, bf16[2,96,768]{2,1,0:T(8,128)(2,1)S(1)}, u32[]{:S(2)}, u32[]{:S(2)}) collective-permute-start(bf16[2,96,768]{2,1,0:T(8,128)(2,1)} %collective-permute-done.7.refs_5_), channel_id=1, source_target_pairs={{0,1},{1,0},{2,3},{3,2},{4,5},{5,4},{6,7},{7,6},{8,9},{9,8},{10,11... | collective-permute-start | bytes 884744 | tf_op jit(solution)/shard_map/ppermute | solution.py:397
  248.2 27.1 %collective-permute-start.31 = (bf16[2,2,96,768]{3,2,1,0:T(8,128)(2,1)}, bf16[2,2,96,768]{3,2,1,0:T(8,128)(2,1)}, u32[]{:S(2)}, u32[]{:S(2)}) collective-permute-start(bf16[2,2,96,768]{3,2,1,0:T(8,128)(2,1)} %get-tuple-element.108), channel_id=1, source_target_pairs={{0,1},{1,0},{2,3},{3,2},{4,5},{5,4},{6,7},{7,6},{8,9},{9,8},{10,11... | collective-permute-start | bytes 1769480 | tf_op jit(solution)/shard_map/ppermute | solution.py:397
  273.8 18.9 %collective-permute-start.30 = (bf16[2,2,96,768]{3,2,1,0:T(8,128)(2,1)}, bf16[2,2,96,768]{3,2,1,0:T(8,128)(2,1)}, u32[]{:S(2)}, u32[]{:S(2)}) collective-permute-start(bf16[2,2,96,768]{3,2,1,0:T(8,128)(2,1)} %get-tuple-element.107), channel_id=1, source_target_pairs={{0,1},{1,0},{2,3},{3,2},{4,5},{5,4},{6,7},{7,6},{8,9},{9,8},{10,11... | collective-permute-start | bytes 1769480 | tf_op jit(solution)/shard_map/ppermute | solution.py:397
  273.9 36.6 %collective-permute-start.29 = (bf16[4,2,96,768]{3,2,1,0:T(8,128)(2,1)S(1)}, bf16[4,2,96,768]{3,2,1,0:T(8,128)(2,1)}, u32[]{:S(2)}, u32[]{:S(2)}) collective-permute-start(bf16[4,2,96,768]{3,2,1,0:T(8,128)(2,1)S(1)} %slice.134), channel_id=1, source_target_pairs={{0,1},{1,0},{2,3},{3,2},{4,5},{5,4},{6,7},{7,6},{8,9},{9,8},{10,11... | collective-permute-start | bytes 3538952 | tf_op jit(solution)/shard_map/ppermute | solution.py:397
  274.4 18.3 %collective-permute-start.27 = (f32[9216]{0:T(1024)S(1)}, f32[9216]{0:T(1024)S(1)}, u32[]{:S(2)}, u32[]{:S(2)}) collective-permute-start(f32[9216]{0:T(1024)S(1)} %add.163), channel_id=1, source_target_pairs={{0,8},{4,12},{8,0},{12,4},{16,24},{20,28},{24,16},{28,20},{1,9},{5... | collective-permute-start | bytes 110600 | tf_op jit(solution)/shard_map/ppermute | solution.py:398
  277.3 16.0 %collective-permute-start.32 = (bf16[2,96,768]{2,1,0:T(8,128)(2,1)}, bf16[2,96,768]{2,1,0:T(8,128)(2,1)S(1)}, u32[]{:S(2)}, u32[]{:S(2)}) collective-permute-start(bf16[2,96,768]{2,1,0:T(8,128)(2,1)} %get-tuple-element.105), channel_id=1, source_target_pairs={{0,8},{8,16},{16,24},{24,28},{28,20},{20,12},{12,4},{4,0},{1,9},{9... | collective-permute-start | bytes 884744 | tf_op jit(solution)/shard_map/ppermute | solution.py:399
  278.5 19.0 %collective-permute-start.36 = (bf16[2,96,768]{2,1,0:T(8,128)(2,1)}, bf16[2,96,768]{2,1,0:T(8,128)(2,1)}, u32[]{:S(2)}, u32[]{:S(2)}) collective-permute-start(bf16[2,96,768]{2,1,0:T(8,128)(2,1)} %get-tuple-element.106), channel_id=1, source_target_pairs={{8,0},{16,8},{24,16},{28,24},{20,28},{12,20},{4,12},{0,4},{9,1},{1... | collective-permute-start | bytes 884744 | tf_op jit(solution)/shard_map/ppermute | solution.py:400
  292.7 44.2 %collective-permute-start.21 = (bf16[5,197,768]{2,1,0:T(8,128)(2,1)}, bf16[5,197,768]{2,1,0:T(8,128)(2,1)}, u32[]{:S(2)}, u32[]{:S(2)}) collective-permute-start(bf16[5,197,768]{2,1,0:T(8,128)(2,1)} %get-tuple-element.63), channel_id=1, source_target_pairs={{0,1},{1,0},{2,3},{3,2},{4,5},{5,4},{6,7},{7,6},{8,9},{9,8},{10,11... | collective-permute-start | bytes 4538888 | tf_op jit(solution)/shard_map/ppermute | solution.py:397
  292.7 44.6 %collective-permute-start.22 = (bf16[5,197,768]{2,1,0:T(8,128)(2,1)}, bf16[5,197,768]{2,1,0:T(8,128)(2,1)}, u32[]{:S(2)}, u32[]{:S(2)}) collective-permute-start(bf16[5,197,768]{2,1,0:T(8,128)(2,1)} %get-tuple-element.63), channel_id=1, source_target_pairs={{0,2},{1,3},{2,0},{3,1},{4,6},{5,7},{6,4},{7,5},{8,10},{9,11},{10,... | collective-permute-start | bytes 4538888 | tf_op jit(solution)/shard_map/ppermute | solution.py:397
  293.4 70.7 %collective-permute-start.19 = (bf16[5,197,768]{2,1,0:T(8,128)(2,1)}, bf16[5,197,768]{2,1,0:T(8,128)(2,1)}, u32[]{:S(2)}, u32[]{:S(2)}) collective-permute-start(bf16[5,197,768]{2,1,0:T(8,128)(2,1)} %get-tuple-element.51), channel_id=1, source_target_pairs={{0,2},{1,3},{2,0},{3,1},{4,6},{5,7},{6,4},{7,5},{8,10},{9,11},{10,... | collective-permute-start | bytes 4538888 | tf_op jit(solution)/shard_map/ppermute | solution.py:397
  303.5 6.9 %collective-permute-start.33 = (bf16[2,96,768]{2,1,0:T(8,128)(2,1)S(1)}, bf16[2,96,768]{2,1,0:T(8,128)(2,1)S(1)}, u32[]{:S(2)}, u32[]{:S(2)}) collective-permute-start(bf16[2,96,768]{2,1,0:T(8,128)(2,1)S(1)} %get-tuple-element.103), channel_id=1, source_target_pairs={{0,8},{8,16},{16,24},{24,28},{28,20},{20,12},{12,4},{4,0},{1,9},{9... | collective-permute-start | bytes 884744 | tf_op jit(solution)/shard_map/ppermute | solution.py:399
  310.5 58.9 %collective-permute-start.18 = (bf16[5,197,768]{2,1,0:T(8,128)(2,1)}, bf16[5,197,768]{2,1,0:T(8,128)(2,1)}, u32[]{:S(2)}, u32[]{:S(2)}) collective-permute-start(bf16[5,197,768]{2,1,0:T(8,128)(2,1)} %get-tuple-element.51), channel_id=1, source_target_pairs={{0,1},{1,0},{2,3},{3,2},{4,5},{5,4},{6,7},{7,6},{8,9},{9,8},{10,11... | collective-permute-start | bytes 4538888 | tf_op jit(solution)/shard_map/ppermute | solution.py:397
  310.5 14.4 %collective-permute-start.37 = (bf16[2,96,768]{2,1,0:T(8,128)(2,1)S(1)}, bf16[2,96,768]{2,1,0:T(8,128)(2,1)S(1)}, u32[]{:S(2)}, u32[]{:S(2)}) collective-permute-start(bf16[2,96,768]{2,1,0:T(8,128)(2,1)S(1)} %get-tuple-element.104), channel_id=1, source_target_pairs={{8,0},{16,8},{24,16},{28,24},{20,28},{12,20},{4,12},{0,4},{9,1},{1... | collective-permute-start | bytes 884744 | tf_op jit(solution)/shard_map/ppermute | solution.py:400
  324.9 9.0 %collective-permute-start.34 = (bf16[2,96,768]{2,1,0:T(8,128)(2,1)S(1)}, bf16[2,96,768]{2,1,0:T(8,128)(2,1)S(1)}, u32[]{:S(2)}, u32[]{:S(2)}) collective-permute-start(bf16[2,96,768]{2,1,0:T(8,128)(2,1)S(1)} %fusion.3), channel_id=1, source_target_pairs={{0,8},{8,16},{16,24},{24,28},{28,20},{20,12},{12,4},{4,0},{1,9},{9... | collective-permute-start | bytes 884744 | tf_op jit(solution)/shard_map/ppermute | solution.py:399
  335.3 36.8 %collective-permute-start.35 = (bf16[2,96,768]{2,1,0:T(8,128)(2,1)S(1)}, bf16[2,96,768]{2,1,0:T(8,128)(2,1)S(1)}, u32[]{:S(2)}, u32[]{:S(2)}) collective-permute-start(bf16[2,96,768]{2,1,0:T(8,128)(2,1)S(1)} %get-tuple-element.101), channel_id=1, source_target_pairs={{0,8},{8,16},{16,24},{24,28},{28,20},{20,12},{12,4},{4,0},{1,9},{9... | collective-permute-start | bytes 884744 | tf_op jit(solution)/shard_map/ppermute | solution.py:399
  336.9 35.1 %collective-permute-start.38 = (bf16[2,96,768]{2,1,0:T(8,128)(2,1)S(1)}, bf16[2,96,768]{2,1,0:T(8,128)(2,1)S(1)}, u32[]{:S(2)}, u32[]{:S(2)}) collective-permute-start(bf16[2,96,768]{2,1,0:T(8,128)(2,1)S(1)} %get-tuple-element.102), channel_id=1, source_target_pairs={{8,0},{16,8},{24,16},{28,24},{20,28},{12,20},{4,12},{0,4},{9,1},{1... | collective-permute-start | bytes 884744 | tf_op jit(solution)/shard_map/ppermute | solution.py:400
  337.3 43.7 %collective-permute-start.23 = (bf16[5,197,768]{2,1,0:T(8,128)(2,1)}, bf16[5,197,768]{2,1,0:T(8,128)(2,1)}, u32[]{:S(2)}, u32[]{:S(2)}) collective-permute-start(bf16[5,197,768]{2,1,0:T(8,128)(2,1)} %collective-permute-done.22), channel_id=1, source_target_pairs={{0,1},{1,0},{2,3},{3,2},{4,5},{5,4},{6,7},{7,6},{8,9},{9,8},{10,11... | collective-permute-start | bytes 4538888 | tf_op jit(solution)/shard_map/ppermute | solution.py:397
  364.1 27.3 %collective-permute-start.20 = (bf16[5,197,768]{2,1,0:T(8,128)(2,1)}, bf16[5,197,768]{2,1,0:T(8,128)(2,1)}, u32[]{:S(2)}, u32[]{:S(2)}) collective-permute-start(bf16[5,197,768]{2,1,0:T(8,128)(2,1)} %collective-permute-done.19), channel_id=1, source_target_pairs={{0,1},{1,0},{2,3},{3,2},{4,5},{5,4},{6,7},{7,6},{8,9},{9,8},{10,11... | collective-permute-start | bytes 4538888 | tf_op jit(solution)/shard_map/ppermute | solution.py:397
  (41 other events, 353.9 us)
Sparse Core Ops, SparseCore 0:
  10.9 88.7 all-gather.2
  181.8 145.2 reduce-scatter.1

commit v3 on v2

--- a/solution.py
+++ b/solution.py
@@ -10,6 +10,7 @@
 NORM_EPS = 1e-06
 SLOT_ROWS = 200
 ROWS = 1024
+UNROLL = 5
 BF = jnp.bfloat16
 F32 = jnp.float32
 NT = (((1,), (1,)), ((), ()))
@@ -69,8 +70,8 @@
     return jax.ShapeDtypeStruct(shape, dtype)
 
 
-def loop(n, fn):
-    lax.fori_loop(0, n, lambda i, c: (fn(i), c)[1], 0)
+def loop(n, fn, unroll=1):
+    lax.fori_loop(0, n, lambda i, c: (fn(i), c)[1], 0, unroll=unroll)
 
 
 def cut(i, size):
@@ -89,23 +90,25 @@
             dy_ref[rows, :] = cot_ref[0, i]
 
 
-def place_chunks(info_ref, own_refs, other_refs, buf_ref):
-    sub = own_refs[0].shape[1]
-    for k, (own, other) in enumerate(zip(own_refs, other_refs)):
-        rows = pl.ds(pl.multiple_of(info_ref[2 + k] * sub, sub), sub)
-        buf_ref[0, rows, :] = own[0]
-        buf_ref[2, rows, :] = own[1]
-        buf_ref[1, rows, :] = other[0]
-        buf_ref[3, rows, :] = other[1]
+def place_chunks(info_ref, refs, buf_ref):
+    sub = refs[0].shape[1]
+
+    def put(n, ref):
+        rows = pl.ds(pl.multiple_of(info_ref[2 + n] * sub, sub), sub)
+        for j in range(ref.shape[0]):
+            buf_ref[j, rows, :] = ref[j]
+
+    for n, ref in enumerate(refs[:-2]):
+        put(n, ref)
+    even = info_ref[0] % 2 == 0
+    pl.when(even)(lambda: put(len(refs) - 2, refs[-2]))
+    pl.when(~even)(lambda: put(len(refs) - 2, refs[-1]))
 
 
 def qkv_ring_body(info_ref, x_ref, gain_ref, shift_ref, bias_ref, *refs):
-    n = (len(refs) - 5) // 2
-    own_refs, other_refs = refs[:n], refs[n : 2 * n]
-    h_ref, qkv_ref, wq_ref, wo_ref, buf_ref = refs[2 * n :]
-    place_chunks(info_ref, own_refs, other_refs, buf_ref)
-    groups = buf_ref.shape[0]
-    qkv_rest(lambda j: buf_ref[lax.bitwise_xor(info_ref[0], j)], groups, x_ref, gain_ref, shift_ref, bias_ref, h_ref, qkv_ref, wq_ref, wo_ref)
+    h_ref, qkv_ref, wq_ref, wo_ref, buf_ref = refs[-5:]
+    place_chunks(info_ref, refs[:-5], buf_ref)
+    qkv_rest(lambda j: buf_ref[j], buf_ref.shape[0], x_ref, gain_ref, shift_ref, bias_ref, h_ref, qkv_ref, wq_ref, wo_ref)
 
 
 def qkv_gathered_body(x_ref, gain_ref, shift_ref, bias_ref, wa_ref, h_ref, qkv_ref, wq_ref, wo_ref):
@@ -138,25 +141,25 @@
 
 def attend_body(slots, length, q_ref, k_ref, v_ref, o_ref, p_ref):
     low_half = lax.broadcasted_iota(jnp.int32, (SLOT_ROWS, 2 * HEAD_DIM), 1) < HEAD_DIM
-    valid = lax.broadcasted_iota(jnp.int32, (SLOT_ROWS, SLOT_ROWS), 1) < length
+    valid = lax.broadcasted_iota(jnp.int32, (SLOT_ROWS, SLOT_ROWS), 0) < length
 
     def image(i):
         rows = cut(i, SLOT_ROWS)
         q = q_ref[rows, :] * jnp.bfloat16(0.125)
         k = k_ref[rows, :]
-        v = v_ref[rows, :]
-        zero = jnp.zeros_like(q)
+        v_t = v_ref[rows, :].T
+        zero = jnp.zeros_like(k)
         mixed = []
         for h in range(2):
-            s = dot(jnp.where(low_half if h == 0 else ~low_half, q, zero), k, NT)
+            s = dot(jnp.where(low_half if h == 0 else ~low_half, k, zero), q, NT)
             s = jnp.where(valid, s, -1e30)
-            e = jnp.exp(s - jnp.max(s, axis=-1, keepdims=True))
-            p = (e * (1.0 / jnp.sum(e, axis=-1, keepdims=True))).astype(BF)
+            e = jnp.exp(s - jnp.max(s, axis=0, keepdims=True))
+            p = (e * (1.0 / jnp.sum(e, axis=0, keepdims=True))).astype(BF)
             p_ref[h, i] = p
-            mixed.append(dot(p, v))
-        o_ref[rows, :] = jnp.where(low_half, mixed[0], mixed[1]).astype(BF)
-
-    loop(slots, image)
+            mixed.append(dot(v_t[h * HEAD_DIM : (h + 1) * HEAD_DIM], p))
+        o_ref[rows, :] = jnp.concatenate(mixed, axis=0).T.astype(BF)
+
+    loop(slots, image, UNROLL)
     tail = slots * SLOT_ROWS
     o_ref[tail:, :] = jnp.zeros((ROWS - tail, 2 * HEAD_DIM), BF)
 
@@ -188,7 +191,7 @@
     loop(ROWS // 256, chunk)
 
 
-def down_body(slots, length, info_ref, act_ref, wc_ref, mid_ref, bias_ref, all_ref, out_ref, acc_ref):
+def down_body(slots, info_ref, act_ref, wc_ref, mid_ref, bias_ref, out_ref, acc_ref):
     parts, groups, sub, cols = wc_ref.shape
     for j in range(groups):
         part = dot(act_ref[:, j * cols : (j + 1) * cols], wc_ref[:, j].reshape(parts * sub, cols), NT)
@@ -199,9 +202,22 @@
     for i in range(slots):
         rows = slice(i * SLOT_ROWS, (i + 1) * SLOT_ROWS)
         live = jnp.where(i < info_ref[1], 1.0, 0.0)
-        value = ((mid_ref[rows, :] + acc_ref[rows, :] + bias_ref[...]) * live)[:length].astype(BF)
-        out_ref[i] = value
-        all_ref[0, i] = value
+        out_ref[rows, :] = ((mid_ref[rows, :] + acc_ref[rows, :] + bias_ref[...]) * live).astype(BF)
+
+
+def weave_body(length, info_ref, a_ref, b_ref, c_ref, d_ref, o_ref):
+    def part(start, n, keep):
+        x = jnp.concatenate([r[start : start + n, :] for r in (a_ref, b_ref, c_ref, d_ref)], axis=0)
+        row = lax.broadcasted_iota(jnp.int32, (4 * n, 4 * n), 0)
+        col = lax.broadcasted_iota(jnp.int32, (4 * n, 4 * n), 1)
+        take = jnp.where(lax.bitwise_xor(row % 4, info_ref[0]) * n + row // 4 == col, 1.0, 0.0).astype(BF)
+        y = dot(take, x).astype(BF).reshape(n, 4, x.shape[1])
+        o_ref[0, start : start + keep] = y[:keep]
+
+    full = length // 64 * 64
+    for start in range(0, full, 64):
+        part(start, 64, 64)
+    part(full, 8, length - full)
 
 
 def outer_body(h_ref, dy_ref, du_ref, act_ref, g_ref, t_ref):
@@ -275,23 +291,23 @@
     def image(i):
         rows = cut(i, SLOT_ROWS)
         q = q_ref[rows, :] * jnp.bfloat16(0.125)
-        k = k_ref[rows, :] * jnp.bfloat16(0.125)
+        k_t = (k_ref[rows, :] * jnp.bfloat16(0.125)).T
         v = v_ref[rows, :]
         do = do_ref[rows, :]
-        zero = jnp.zeros_like(q)
+        zero = jnp.zeros_like(v)
         grads = []
         for h in range(2):
-            mask = low_half if h == 0 else ~low_half
             p = p_ref[h, i]
             pf = p.astype(F32)
-            dv = dot(p, do, TN)
-            dp = dot(jnp.where(mask, do, zero), v, NT)
-            ds = (pf * (dp - jnp.sum(pf * dp, axis=-1, keepdims=True))).astype(BF)
-            grads.append((dot(ds, k), dot(ds, q, TN), dv))
-        for ref, a, b in zip((dq_ref, dk_ref, dv_ref), *grads):
-            ref[rows, :] = jnp.where(low_half, a, b).astype(BF)
-
-    loop(slots, image)
+            dp = dot(jnp.where(low_half if h == 0 else ~low_half, v, zero), do, NT)
+            ds = (pf * (dp - jnp.sum(pf * dp, axis=0, keepdims=True))).astype(BF)
+            grads.append((dot(k_t[h * HEAD_DIM : (h + 1) * HEAD_DIM], ds), dot(ds, q), dot(p, do)))
+        (dq0, dk0, dv0), (dq1, dk1, dv1) = grads
+        dq_ref[rows, :] = jnp.concatenate([dq0, dq1], axis=0).T.astype(BF)
+        dk_ref[rows, :] = jnp.where(low_half, dk0, dk1).astype(BF)
+        dv_ref[rows, :] = jnp.where(low_half, dv0, dv1).astype(BF)
+
+    loop(slots, image, UNROLL)
     tail = slots * SLOT_ROWS
     for ref in (dq_ref, dk_ref, dv_ref):
         ref[tail:, :] = jnp.zeros((ROWS - tail, 2 * HEAD_DIM), BF)
@@ -317,11 +333,11 @@
             buf_ref[j, :, s * local : (s + 1) * local] = g[:, j * local : (j + 1) * local]
 
     small_outer(h_ref, dq_ref, dk_ref, dv_ref, dlow_ref, o_ref, sums_ref, store)
-    for k in range(slots):
-        rows = pl.ds(pl.multiple_of(info_ref[2 + k] * sub, sub), sub)
-        for rel in range(4):
-            ref = send_ref if rel % 2 else keep_ref
-            ref[k, rel // 2] = buf_ref[lax.bitwise_xor(info_ref[0], rel), rows, :]
+    for n in range(2 * slots):
+        rows = pl.ds(pl.multiple_of(info_ref[2 + n] * sub, sub), sub)
+        ref = keep_ref if n < slots else send_ref
+        for j in range(groups):
+            ref[n % slots, j] = buf_ref[j, rows, :]
 
 
 def outer_plain_body(h_ref, dq_ref, dk_ref, dv_ref, dlow_ref, o_ref, g_ref, sums_ref):
@@ -335,7 +351,7 @@
     small_outer(h_ref, dq_ref, dk_ref, dv_ref, dlow_ref, o_ref, sums_ref, store)
 
 
-def input_back_body(slots, length, info_ref, x_ref, dq_ref, dk_ref, dv_ref, wq_ref, dmid_ref, gain_ref, all_ref, out_ref, sums_ref, acc_ref):
+def input_back_body(slots, x_ref, dq_ref, dk_ref, dv_ref, wq_ref, dmid_ref, gain_ref, out_ref, sums_ref, acc_ref):
     width = x_ref.shape[1]
     for s, ref in enumerate((dq_ref, dk_ref, dv_ref)):
         part = dot(ref[...], wq_ref[:, s * width : (s + 1) * width], NT)
@@ -350,9 +366,7 @@
         dh = acc_ref[rows, :]
         normal, scale_inv = norm_stats(x_ref[rows, :].astype(F32))
         grad = dmid_ref[rows, :] + norm_back(dh, normal, scale_inv, gain_ref[...])
-        grad = grad[:length].astype(BF)
-        out_ref[i] = grad
-        all_ref[0, i] = grad
+        out_ref[rows, :] = grad.astype(BF)
         sums[0] = sums[0] + colsum(dh * normal)
         sums[1] = sums[1] + colsum(dh)
     for n in range(2):
@@ -391,49 +405,30 @@
     place = [cycle.index(d) for d in range(parts)]
     here = jnp.array(place, jnp.int32)[lax.axis_index("dp")]
     owner = jnp.array(cycle, jnp.int32)
-    right = [(cycle[p], cycle[(p + 1) % parts]) for p in range(parts)]
-    left = [(b, a) for a, b in right]
     far = parts // 2
     mp_swap = lambda a, bit: lax.ppermute(a, "mp", [(j, j ^ bit) for j in range(groups)])
     dp_swap = lambda a, bit: lax.ppermute(a, "dp", [(d, d ^ bit) for d in range(parts)])
-    to_right = lambda a: lax.ppermute(a, "dp", right)
-    to_left = lambda a: lax.ppermute(a, "dp", left)
+
+    def hop(a, odd=True):
+        pairs = []
+        for p in range(parts):
+            for j in range(groups):
+                if j % 2 == 0:
+                    pairs.append((cycle[p] * groups + j, cycle[(p + 1) % parts] * groups + j))
+                elif odd:
+                    pairs.append((cycle[p] * groups + j, cycle[(p - 1) % parts] * groups + j))
+        return lax.ppermute(a, axes, pairs)
+
+    even = mine % 2 == 0
+    side = jnp.where(even, 1, -1)
     row = lambda v: v.reshape(1, -1)
     live = lax.dynamic_index_in_dim(counts, mine, 0, keepdims=False)[0]
 
     def info_of(offsets):
-        return jnp.concatenate([jnp.stack([mine, live]), owner[(here + jnp.array(offsets, jnp.int32)) % parts]])
+        return jnp.concatenate([jnp.stack([mine, live]), owner[(here + jnp.stack(offsets)) % parts]])
 
     smem = pl.BlockSpec(memory_space=pltpu.SMEM)
     info = jnp.stack([mine, live])
-
-    shard_bc = jnp.concatenate([hidden_weight, down_weight.T], axis=1)
-    bc = lax.all_gather(shard_bc, axes, axis=0, tiled=False).reshape(parts, groups, sub, 2 * units)
-    shard_a = jnp.concatenate([qkv_weight, out_weight.T], axis=1)
-    vectors = jnp.concatenate([query_bias, value_bias, hidden_bias])
-    if ring:
-        mate = mp_swap(shard_a, 2)
-        start = jnp.stack([shard_a, mate])
-        chunks = [start]
-        offsets = [0]
-        rights, lefts = start, start
-        for k in range(1, far + 1):
-            rights = to_right(rights)
-            chunks.append(rights)
-            offsets.append(-k)
-            if k < far:
-                lefts = to_left(lefts)
-                chunks.append(lefts)
-                offsets.append(k)
-        others = [mp_swap(c, 1) for c in chunks]
-        ring_info = info_of(offsets)
-    else:
-        wa = lax.all_gather(shard_a, axes, axis=0, tiled=False).reshape(parts, groups, sub, 4 * local)
-    two = jnp.stack([vectors, mp_swap(vectors, 1)])
-    four = jnp.concatenate([two, mp_swap(two, 2)])
-    biases = four[jnp.arange(groups) ^ mine]
-    qb, vb, hb = (biases[:, a:b].reshape(-1) for a, b in ((0, local), (local, 2 * local), (2 * local, None)))
-    bias_row = row(jnp.concatenate([qb, jnp.zeros_like(qb), vb]))
 
     mm = 2 * ROWS * width * width
     t_bf = lambda n: sds((ROWS, n), BF)
@@ -454,14 +449,44 @@
         name="prep",
     )(info, inputs, cotangent)
 
+    shard_bc = jnp.concatenate([hidden_weight, down_weight.T], axis=1)
+    bc = lax.all_gather(shard_bc, axes, axis=0, tiled=False).reshape(parts, groups, sub, 2 * units)
+    shard_a = jnp.concatenate([qkv_weight, out_weight.T], axis=1)
+    vectors = jnp.concatenate([query_bias, value_bias, hidden_bias])
+    if ring:
+        two = jnp.stack([shard_a, mp_swap(shard_a, 2)])
+        near = mp_swap(two, 1)
+        rel = [two[0], near[0], two[1], near[1]]
+        rel = [jnp.where(even, rel[j], rel[j ^ 1]) for j in range(groups)]
+        start = jnp.stack([jnp.where(mine < 2, rel[j], rel[j ^ 2]) for j in range(groups)])
+        chunks, offsets = [start], [jnp.int32(0)]
+        held = start
+        for k in range(1, far):
+            held = hop(held)
+            if k == 1:
+                held, x, dy = lax.optimization_barrier((held, x, dy))
+            chunks += [held, mp_swap(held, 1)]
+            offsets += [-k * side, k * side]
+        held = hop(held, False)
+        chunks += [held, mp_swap(held, 1)]
+        offsets += [jnp.int32(far)]
+        ring_info = info_of(offsets)
+    else:
+        wa = lax.all_gather(shard_a, axes, axis=0, tiled=False).reshape(parts, groups, sub, 4 * local)
+    two = jnp.stack([vectors, mp_swap(vectors, 1)])
+    four = jnp.concatenate([two, mp_swap(two, 2)])
+    biases = four[jnp.arange(groups) ^ mine]
+    qb, vb, hb = (biases[:, a:b].reshape(-1) for a, b in ((0, local), (local, 2 * local), (2 * local, None)))
+    bias_row = row(jnp.concatenate([qb, jnp.zeros_like(qb), vb]))
+
     qkv_outs = [t_bf(width), t_bf(3 * width), sds((width, 3 * width), BF), sds((width, width), BF)]
     qkv_ins = [x, row(norm_gain), row(norm_shift), bias_row]
     if ring:
         h1, qkv, wq, wo = call(
             qkv_ring_body,
             qkv_outs,
-            [ring_info] + qkv_ins + chunks + others,
-            [smem] + [None] * (len(qkv_ins) + 2 * len(chunks)),
+            [ring_info] + qkv_ins + chunks,
+            [smem] + [None] * (len(qkv_ins) + len(chunks)),
             scratch=[pltpu.VMEM((groups, width, 4 * local), BF)],
             flops=3 * mm,
             name="qkv",
@@ -494,20 +519,17 @@
         flops=mm,
         name="mix",
     )
-    step = 256
-    per = units // step
-    steps = ff // step
-    wcols = lambda n: pl.BlockSpec((parts, 1, sub, step), lambda i: (0, i // per, 0, n * per + i % per))
+    wcols = lambda n: pl.BlockSpec((parts, 1, sub, units), lambda i: (0, i, 0, n))
     piece = lambda n: pl.BlockSpec((parts, groups, sub, units), lambda i: (0, 0, 0, n))
-    tcols = pl.BlockSpec((ROWS, step), lambda i: (0, i))
-    vcols = lambda n: pl.BlockSpec((n, step), lambda i: (0, i))
+    tcols = pl.BlockSpec((ROWS, units), lambda i: (0, i))
+    vcols = lambda n: pl.BlockSpec((n, units), lambda i: (0, i))
     act, slope = call(
         hidden_body,
         [t_bf(ff), t_bf(ff)],
         [h2, bc, row(hb)],
         [None, wcols(0), vcols(1)],
         [tcols, tcols],
-        (steps,),
+        (groups,),
         flops=4 * mm,
         name="hidden",
     )
@@ -517,7 +539,7 @@
         [dy, bc, slope],
         [None, wcols(1), tcols],
         [tcols, vcols(8)],
-        (steps,),
+        (groups,),
         flops=4 * mm,
         name="dact",
     )
@@ -528,16 +550,15 @@
         [
             None,
             None,
-            pl.BlockSpec((ROWS, step), lambda i: (0, jnp.maximum(i - steps, 0))),
-            pl.BlockSpec((ROWS, step), lambda i: (0, jnp.minimum(i, steps - 1))),
+            pl.BlockSpec((ROWS, units), lambda i: (0, jnp.maximum(i - groups, 0))),
+            pl.BlockSpec((ROWS, units), lambda i: (0, jnp.minimum(i, groups - 1))),
         ],
         [
             pl.BlockSpec(
-                (parts, 1, sub, step),
-                lambda i: (0, (i % steps) // per, 0, jnp.where(i < steps, per, 0) + i % per),
+                (parts, 1, sub, units), lambda i: (0, i % groups, 0, jnp.where(i < groups, 1, 0))
             )
         ],
-        (2 * steps,),
+        (2 * groups,),
         scratch=[pltpu.VMEM((width, ROWS), BF)],
         flops=8 * mm,
         name="outer_bc",
@@ -546,43 +567,36 @@
         g_bc.reshape(parts * groups, sub, 2 * units), axes, scatter_dimension=0, tiled=False
     ).astype(F32)
 
-    out_shape = sds((batches, slots, length, width), BF)
-    own_shape = sds((slots, length, width), BF)
-
-    def with_slot(body, outs, ins, flops, name):
-        fixed = lambda a: pl.BlockSpec(a.shape, lambda i, info: (0,) * len(a.shape))
-        return pl.pallas_call(
-            body,
-            out_shape=tuple(outs),
-            grid_spec=pltpu.PrefetchScalarGridSpec(
-                num_scalar_prefetch=1,
-                grid=(1,),
-                in_specs=[fixed(a) if s is None else s for a, s in ins],
-                out_specs=[mine_block] + [fixed(a) for a in outs[1:]],
-                scratch_shapes=[pltpu.VMEM((ROWS, width), F32)],
-            ),
-            compiler_params=pltpu.CompilerParams(vmem_limit_bytes=60 * 1024 * 1024),
-            cost_estimate=pl.CostEstimate(
-                flops=flops, bytes_accessed=sum(a.size * a.dtype.itemsize for a, _ in ins), transcendentals=0
-            ),
-            name=name,
-        )(info, *[a for a, _ in ins])
-
-    def spread(all_out, own):
+    own_shape = sds((slots * SLOT_ROWS, width), BF)
+
+    def spread(own):
         crossed = mp_swap(own, 2)
-        for rel, value in ((1, mp_swap(own, 1)), (2, crossed), (3, mp_swap(crossed, 1))):
-            all_out = lax.dynamic_update_index_in_dim(all_out, value, mine ^ rel, 0)
-        return all_out
-
-    piece_c = pl.BlockSpec((parts, groups, sub, units), lambda i, info: (0, 0, 0, 1))
-    all_out, own_out = with_slot(
-        functools.partial(down_body, slots, length),
-        [out_shape, own_shape],
-        [(act, None), (bc, piece_c), (middle, None), (row(down_bias), None)],
-        4 * mm,
-        "down",
-    )
-    all_out = spread(all_out, own_out)
+        image = pl.BlockSpec((SLOT_ROWS, width), lambda i: (i, 0))
+        (woven,) = call(
+            functools.partial(weave_body, length),
+            [sds((slots, length, groups, width), BF)],
+            [info, own, mp_swap(own, 1), crossed, mp_swap(crossed, 1)],
+            [smem] + [image] * 4,
+            [pl.BlockSpec((1, length, groups, width), lambda i: (i, 0, 0, 0))],
+            (slots,),
+            flops=mm,
+            limit=16,
+            name="weave",
+        )
+        return woven.transpose(2, 0, 1, 3)
+
+    act_late, g_bc_tie = lax.optimization_barrier((act, g_bc))
+    (own_out,) = call(
+        functools.partial(down_body, slots),
+        [own_shape],
+        [info, act_late, bc, middle, row(down_bias)],
+        [smem, None, piece(1), None, None],
+        scratch=[pltpu.VMEM((ROWS, width), F32)],
+        flops=4 * mm,
+        name="down",
+    )
+    all_out = spread(own_out)
+    du, _ = lax.optimization_barrier((du, own_out))
 
     dmid, dlow, sums_mid = call(
         mid_back_body,
@@ -604,42 +618,36 @@
         flops=2 * mm,
         name="attend_back",
     )
+    def scatter_ring(keep, send):
+        first, rest = mp_swap(send[:1], 1), mp_swap(send[1:], 1)
+        total = keep[0].astype(F32) + first[0].astype(F32)
+        for k in range(1, far):
+            moved = hop(total.astype(BF))
+            total = keep[k].astype(F32) + rest[k - 1].astype(F32) + moved.astype(F32)
+        total = total.astype(BF)
+        total = jnp.where(even, hop(total, False), total).reshape(2, 2, sub, -1)
+        split = lambda a, b, first: (jnp.where(first, a, b), jnp.where(first, b, a))
+        mine_half, other_half = split(total[:, 0], total[:, 1], even)
+        total = mine_half.astype(F32) + mp_swap(other_half, 1).astype(F32)
+        mine_half, other_half = split(total[0], total[1], mine < 2)
+        return mine_half + mp_swap(other_half.astype(BF), 2).astype(F32)
+
     outer_ins = [h1, dq, dk, dv, dlow, mixed]
     sum_shape = sds((8, width), F32)
     if ring:
-        send_order = []
-        for k in range(far, 0, -1):
-            send_order.append(k)
-            if k > 1:
-                send_order.append(1 - k)
-        send_order.append(0)
-        half_shape = sds((parts, 2, sub, 4 * local), BF)
+        leave = [jnp.where(even, far - k, k + 1 - far) for k in range(far)]
+        stay = [jnp.where(even, k + 1 - far, far - k) for k in range(far)]
+        half_shape = sds((far, groups, sub, 4 * local), BF)
         keep, send, sums_qkv = call(
             outer_ring_body,
             [half_shape, half_shape, sum_shape],
-            [info_of(send_order)] + outer_ins,
+            [info_of(leave + stay)] + outer_ins,
             [smem] + [None] * len(outer_ins),
             scratch=[pltpu.VMEM((groups, width, 4 * local), BF)],
             flops=4 * mm,
             name="outer_a",
         )
-        cuts = [0, 2, 4, parts]
-        got = [mp_swap(send[a:b], 1) for a, b in zip(cuts, cuts[1:])]
-        got = [(a, g) for a, g in zip(cuts, got)]
-
-        def term(offset):
-            n = send_order.index(offset)
-            a, g = [(a, g) for a, g in got if a <= n][-1]
-            return keep[n].astype(F32) + g[n - a].astype(F32)
-
-        rights = to_right(term(far).astype(BF))
-        lefts = to_left(term(1 - far).astype(BF))
-        for k in range(far - 1, 0, -1):
-            rights = to_right((term(k) + rights.astype(F32)).astype(BF))
-            if k > 1:
-                lefts = to_left((term(1 - k) + lefts.astype(F32)).astype(BF))
-        total = term(0) + rights.astype(F32) + lefts.astype(F32)
-        s_a = total[0] + mp_swap(total[1].astype(BF), 2).astype(F32)
+        s_a = scatter_ring(keep, send)
     else:
         g_a, sums_qkv = call(
             outer_plain_body,
@@ -651,14 +659,15 @@
         s_a = lax.psum_scatter(
             g_a.reshape(parts * groups, sub, 4 * local), axes, scatter_dimension=0, tiled=False
         ).astype(F32)
-    all_grad, own_grad, sums_in = with_slot(
-        functools.partial(input_back_body, slots, length),
-        [out_shape, own_shape, sum_shape],
-        [(x, None), (dq, None), (dk, None), (dv, None), (wq, None), (dmid, None), (row(norm_gain), None)],
-        3 * mm,
-        "input_back",
-    )
-    all_grad = spread(all_grad, own_grad)
+    own_grad, sums_in = call(
+        functools.partial(input_back_body, slots),
+        [own_shape, sum_shape],
+        [x, dq, dk, dv, wq, dmid, row(norm_gain)],
+        scratch=[pltpu.VMEM((ROWS, width), F32)],
+        flops=3 * mm,
+        name="input_back",
+    )
+    all_grad = spread(own_grad)
 
     sums = jnp.concatenate(
         [sums_in[:2].reshape(-1), sums_mid[:4].reshape(-1), sums_qkv[:2].reshape(-1), sum_hidden[0]]

time: 418 us -> 407 us (0.974)
  waiting for transfers between devices: 84.5 us -> 118 us
  local copies, waits for them, and re-layouts: 60.7 us -> 32.4 us
  Pallas kernels: 200 us -> 176 us
  starting transfers between devices: 33.1 us -> 43 us
    pallas_call x2 -> x0, Pallas kernels: 25.8 us -> none  [with_slot(): pl.pallas_call(body, out_shape=tuple(outs), grid_spec=pltpu.PrefetchScala...]
    ppermute x14 -> x8, waiting for transfers between devices: 45 us -> 64.6 us  [hop(): return lax.ppermute(a, axes, pairs)]
    dynamic_update_slice x6 -> x0, local copies, waits for them, and re-layouts: 15.9 us -> none  [spread(): all_out = lax.dynamic_update_index_in_dim(all_out, value, mine ^ rel, 0)]
    unnamed x70 -> x68, local copies, waits for them, and re-layouts: 25.5 us -> 14.5 us
    ppermute x23 -> x20, waiting for transfers between devices: 36.6 us -> 45.5 us  [on_device(): lax.ppermute(a, 'mp', [(j, j ^ bit) for j in range(groups)])]
    ppermute x23 -> x20, starting transfers between devices: 8.79 us -> 16.5 us  [on_device(): lax.ppermute(a, 'mp', [(j, j ^ bit) for j in range(groups)])]
    ppermute x14 -> x8, starting transfers between devices: 19.7 us -> 25.8 us  [hop(): return lax.ppermute(a, axes, pairs)]
    ppermute x3, waiting for transfers between devices: 2.77 us -> 7.55 us  [on_device(): lax.ppermute(a, 'dp', [(d, d ^ bit) for d in range(parts)])]
  transfers between devices with their start and end apart: 42 -> 33, of which waited for: 17 -> 12; matrix products, arithmetic and copies ran while one was open for 17% -> 10% of each run, Pallas kernels for 34% -> 33%
where the time goes in v3:
time: 407 us; the launch traced here: 402 us
  Pallas kernels  176 us (43%)
  waiting for transfers between devices  118 us (29%)
  starting transfers between devices  43 us (11%)
  local copies, waits for them, and re-layouts  32.4 us (8%)
  other arithmetic  17.5 us (4%)
  between operations  15.2 us (4%)
    pallas_call x14, Pallas kernels, call(): pl.pallas_call(body, out_shape=tuple(outs), grid=(1,) if grid is None els...  175 us
    ppermute x8, waiting for transfers between devices, hop(): return lax.ppermute(a, axes, pairs)  64.6 us
    ppermute x20, waiting for transfers between devices, on_device(): lax.ppermute(a, 'mp', [(j, j ^ bit) for j in range(groups)])  45.5 us
    ppermute x8, starting transfers between devices, hop(): return lax.ppermute(a, axes, pairs)  25.8 us
    ppermute x20, starting transfers between devices, on_device(): lax.ppermute(a, 'mp', [(j, j ^ bit) for j in range(groups)])  16.5 us
    unnamed x68, local copies, waits for them, and re-layouts  14.5 us
  transfers between devices with their start and end apart: 33, of which 12 were waited for; matrix products, arithmetic and copies ran while one was open for 10% of the time, Pallas kernels for 33%

profile of v3, /device:TPU:0, one launch (start us, length us, event | category | flops | bytes accessed | tf_op | source)
XLA Modules:
  0.0 401.8 jit_solution(6294602201530694264)
XLA Ops:
  11.0 3.0 collective-permute-start
  15.0 2.9 collective-permute-done
  21.7 3.9 copy.40.x_ref
  31.3 4.1 %collective-permute-done.2.refs_1_ = bf16[4,96,768]{2,1,0:T(8,128)(2,1)} collective-permute-done((bf16[4,96,768]{2,1,0:T(8,128)(2,1)S(1)}, bf16[4,96,768]{2,1,0:T(8,128)(2,1)}, u32[]{:S(2)}, u32[]{:S(2)}) %collective-permute-start.2) | collective-permute-done | bytes 589856 | tf_op jit(solution)/shard_map/ppermute | solution.py:420
  38.0 14.7 %collective-permute-done.6.refs_3_ = bf16[4,96,768]{2,1,0:T(8,128)(2,1)S(1)} collective-permute-done((bf16[4,96,768]{2,1,0:T(8,128)(2,1)}, bf16[4,96,768]{2,1,0:T(8,128)(2,1)S(1)}, u32[]{:S(2)}, u32[]{:S(2)}) %collective-permute-start.6) | collective-permute-done | bytes 589856 | tf_op jit(solution)/shard_map/ppermute | solution.py:420
  52.7 4.6 %collective-permute-start.8 = (bf16[4,96,768]{2,1,0:T(8,128)(2,1)S(1)}, bf16[4,96,768]{2,1,0:T(8,128)(2,1)S(1)}, u32[]{:S(2)}, u32[]{:S(2)}) collective-permute-start(bf16[4,96,768]{2,1,0:T(8,128)(2,1)S(1)} %collective-permute-done.6.refs_3_), channel_id=1, source_target_pairs={{0,8},{1,5},{2,10},{3,7},{8,16},{9,1},{10,18},{11,3},{16,24},{17,9... | collective-permute-start | bytes 1769480 | tf_op jit(solution)/shard_map/ppermute | solution.py:420
  58.9 5.8 %collective-permute-done.8.refs_5_ = bf16[4,96,768]{2,1,0:T(8,128)(2,1)S(1)} collective-permute-done((bf16[4,96,768]{2,1,0:T(8,128)(2,1)S(1)}, bf16[4,96,768]{2,1,0:T(8,128)(2,1)S(1)}, u32[]{:S(2)}, u32[]{:S(2)}) %collective-permute-start.8) | collective-permute-done | bytes 589856 | tf_op jit(solution)/shard_map/ppermute | solution.py:420
  64.7 5.1 %collective-permute-start.10 = (bf16[4,96,768]{2,1,0:T(8,128)(2,1)S(1)}, bf16[4,96,768]{2,1,0:T(8,128)(2,1)S(1)}, u32[]{:S(2)}, u32[]{:S(2)}) collective-permute-start(bf16[4,96,768]{2,1,0:T(8,128)(2,1)S(1)} %collective-permute-done.8.refs_5_), channel_id=1, source_target_pairs={{0,8},{2,10},{8,16},{10,18},{16,24},{18,26},{24,28},{26,30},{28,20... | collective-permute-start | bytes 1769480 | tf_op jit(solution)/shard_map/ppermute | solution.py:420
  70.6 6.4 %collective-permute-start.4 = (f32[2,1152]{1,0:T(2,128)S(1)}, f32[2,1152]{1,0:T(2,128)S(1)}, u32[]{:S(2)}, u32[]{:S(2)}) collective-permute-start(f32[2,1152]{1,0:T(2,128)S(1)} %pad_maximum_fusion.7), channel_id=1, source_target_pairs={{0,2},{1,3},{2,0},{3,1},{4,6},{5,7},{6,4},{7,5},{8,10},{9,11},{10,... | collective-permute-start | bytes 27656 | tf_op jit(solution)/shard_map/ppermute | solution.py:409
  81.6 8.6 %collective-permute-done.10.refs_7_ = bf16[4,96,768]{2,1,0:T(8,128)(2,1)S(1)} collective-permute-done((bf16[4,96,768]{2,1,0:T(8,128)(2,1)S(1)}, bf16[4,96,768]{2,1,0:T(8,128)(2,1)S(1)}, u32[]{:S(2)}, u32[]{:S(2)}) %collective-permute-start.10) | collective-permute-done | bytes 589856 | tf_op jit(solution)/shard_map/ppermute | solution.py:420
  93.3 15.9 %qkv.1 = (bf16[1024,768]{1,0:T(8,128)(2,1)}, bf16[1024,2304]{1,0:T(8,128)(2,1)}, bf16[768,2304]{1,0:T(8,128)(2,1)}, bf16[768,768]{1,0:T(8,128)(2,1)}) custom-call(s32[10]{0:T(128)} %pad_add_fusion.1.info_ref, bf16[1024,768]{1,0:T(8,128)(2,1)} %copy-done.6, f32[1,768]{1,0:T(1,128)} %reshape.425.gain_ref, f32[1,768]{1,0:T(1,128)} %reshape.426.shift_ref, ...), custom_call_target="tpu_custom_call" | custom-call | flops 3623878656 | bytes 17906728 | tf_op jit(solution)/shard_map/qkv/pallas_call | solution.py:55
  109.3 16.5 %attend.1 = (bf16[1024,768]{1,0:T(8,128)(2,1)}, bf16[12,5,200,200]{3,2,1,0:T(8,128)(2,1)}) custom-call(bf16[1024,2304]{1,0:T(8,128)(2,1)} %get-tuple-element.49.q_ref.k_ref.v_ref, bf16[1024,2304]{1,0:T(8,128)(2,1)} %get-tuple-element.49.q_ref.k_ref.v_ref, bf16[1024,2304]{1,0:T(8,128)(2,1)} %get-tuple-element.49.q_ref.k_ref.v_ref), custom_call_target="tpu_custom_call" | custom-call | flops 1207959552 | bytes 20528640 | tf_op jit(solution)/shard_map/attend/pallas_call | solution.py:55
  125.8 7.2 %mix.1 = (f32[1024,768]{1,0:T(8,128)}, bf16[1024,768]{1,0:T(8,128)(2,1)}) custom-call(bf16[1024,768]{1,0:T(8,128)(2,1)} %copy-done.6, bf16[1024,768]{1,0:T(8,128)(2,1)} %get-tuple-element.50.o_ref, bf16[768,768]{1,0:T(8,128)(2,1)} %get-tuple-element.51.wo_ref, f32[1,768]{1,0:T(1,128)} %reshape.430.bias_ref, f32[1,768]{1,0:T(1,128)} %reshape.431.gain_ref, ...), custom_call_target="tpu_custom_call" | custom-call | flops 1207959552 | bytes 9053184 | tf_op jit(solution)/shard_map/mix/pallas_call | solution.py:55
  133.0 15.7 %hidden.1 = (bf16[1024,3072]{1,0:T(8,128)(2,1)}, bf16[1024,3072]{1,0:T(8,128)(2,1)}) custom-call(bf16[1024,768]{1,0:T(8,128)(2,1)} %get-tuple-element.52.h_ref, bf16[8,4,96,1536]{3,2,1,0:T(8,128)(2,1)} %bitcast.104, f32[1,3072]{1,0:T(1,128)} %bitcast.121), custom_call_target="tpu_custom_call" | custom-call | flops 4831838208 | bytes 23605248 | tf_op jit(solution)/shard_map/hidden/pallas_call | solution.py:55
  148.7 10.6 %dact.1 = (bf16[1024,3072]{1,0:T(8,128)(2,1)}, f32[8,3072]{1,0:T(8,128)}) custom-call(bf16[1024,768]{1,0:T(8,128)(2,1)} %copy-done.3, bf16[8,4,96,1536]{3,2,1,0:T(8,128)(2,1)} %bitcast.105, bf16[1024,3072]{1,0:T(8,128)(2,1)} %get-tuple-element.55.slope_ref), custom_call_target="tpu_custom_call" | custom-call | flops 4831838208 | bytes 23691264 | tf_op jit(solution)/shard_map/dact/pallas_call | solution.py:55
  159.3 17.6 %outer_bc.1 = bf16[8,4,96,1536]{3,2,1,0:T(8,128)(2,1)} custom-call(bf16[1024,768]{1,0:T(8,128)(2,1)} %get-tuple-element.52.h_ref, bf16[1024,768]{1,0:T(8,128)(2,1)} %copy-done.3, bf16[1024,3072]{1,0:T(8,128)(2,1)} %get-tuple-element.60.du_ref, bf16[1024,3072]{1,0:T(8,128)(2,1)} %get-tuple-element.57.act_ref), custom_call_target="tpu_custom_call" | custom-call | flops 9663676416 | bytes 25165824 | tf_op jit(solution)/shard_map/outer_bc/pallas_call | solution.py:55
  180.0 11.7 %down.1.a_ref = bf16[1000,768]{1,0:T(8,128)(2,1)} custom-call(s32[2]{0:T(128)} %copy-done.4, bf16[1024,3072]{1,0:T(8,128)(2,1)} %get-tuple-element.57.act_ref, bf16[8,4,96,1536]{3,2,1,0:T(8,128)(2,1)} %bitcast.106, f32[1024,768]{1,0:T(8,128)} %get-tuple-element.58.mid_ref, f32[1,768]{1,0:T(1,128)} %reshape.434.bias_ref), custom_call_target="tpu_custom_call" | custom-call | flops 4831838208 | bytes 20413448 | tf_op jit(solution)/shard_map/down/pallas_call | solution.py:55
  191.7 16.8 %mid_back.1 = (f32[1024,768]{1,0:T(8,128)}, bf16[1024,768]{1,0:T(8,128)(2,1)}, f32[8,768]{1,0:T(8,128)}) custom-call(bf16[1024,768]{1,0:T(8,128)(2,1)} %copy-done.3, bf16[1024,3072]{1,0:T(8,128)(2,1)} %get-tuple-element.60.du_ref, bf16[8,4,96,1536]{3,2,1,0:T(8,128)(2,1)} %bitcast.107, f32[1024,768]{1,0:T(8,128)} %get-tuple-element.58.mid_ref, ...), custom_call_target="tpu_custom_call" | custom-call | flops 4831838208 | bytes 25193472 | tf_op jit(solution)/shard_map/mid_back/pallas_call | solution.py:55
  208.5 4.4 %out_back.1.do_ref = bf16[1024,768]{1,0:T(8,128)(2,1)} custom-call(bf16[1024,768]{1,0:T(8,128)(2,1)} %get-tuple-element.61.dlow_ref, bf16[768,768]{1,0:T(8,128)(2,1)} %get-tuple-element.51.wo_ref), custom_call_target="tpu_custom_call" | custom-call | flops 1207959552 | bytes 4325376 | tf_op jit(solution)/shard_map/out_back/pallas_call | solution.py:55
  212.9 21.6 %attend_back.1 = (bf16[1024,768]{1,0:T(8,128)(2,1)}, bf16[1024,768]{1,0:T(8,128)(2,1)}, bf16[1024,768]{1,0:T(8,128)(2,1)}) custom-call(bf16[1024,2304]{1,0:T(8,128)(2,1)} %get-tuple-element.49.q_ref.k_ref.v_ref, bf16[1024,2304]{1,0:T(8,128)(2,1)} %get-tuple-element.49.q_ref.k_ref.v_ref, bf16[1024,2304]{1,0:T(8,128)(2,1)} %get-tuple-element.49.q_ref.k_ref.v_ref, ...), custom_call_target="tpu_custom_call" | custom-call | flops 2415919104 | bytes 25247232 | tf_op jit(solution)/shard_map/attend_back/pallas_call | solution.py:55
  234.5 11.2 %outer_a.1 = (bf16[4,4,96,768]{3,2,1,0:T(8,128)(2,1)}, bf16[4,4,96,768]{3,2,1,0:T(8,128)(2,1)}, f32[8,768]{1,0:T(8,128)}) custom-call(s32[10]{0:T(128)} %pad_add_fusion.3.info_ref, bf16[1024,768]{1,0:T(8,128)(2,1)} %get-tuple-element.70.h_ref, bf16[1024,768]{1,0:T(8,128)(2,1)} %get-tuple-element.62.dq_ref, bf16[1024,768]{1,0:T(8,128)(2,1)} %get-tuple-element.63.dk_ref, ...), custom_call_target="tpu_custom_call" | custom-call | flops 4831838208 | bytes 14180392 | tf_op jit(solution)/shard_map/outer_a/pallas_call | solution.py:55
  249.4 3.0 collective-permute-done.24
  252.5 6.9 %collective-permute-start.25 = (bf16[4,96,768]{2,1,0:T(8,128)(2,1)S(1)}, bf16[4,96,768]{2,1,0:T(8,128)(2,1)S(1)}, u32[]{:S(2)}, u32[]{:S(2)}) collective-permute-start(bf16[4,96,768]{2,1,0:T(8,128)(2,1)S(1)} %fusion.3), channel_id=1, source_target_pairs={{0,8},{1,5},{2,10},{3,7},{8,16},{9,1},{10,18},{11,3},{16,24},{17,9... | collective-permute-start | bytes 1769480 | tf_op jit(solution)/shard_map/ppermute | solution.py:420
  259.4 19.9 %collective-permute-done.25 = bf16[4,96,768]{2,1,0:T(8,128)(2,1)S(1)} collective-permute-done((bf16[4,96,768]{2,1,0:T(8,128)(2,1)S(1)}, bf16[4,96,768]{2,1,0:T(8,128)(2,1)S(1)}, u32[]{:S(2)}, u32[]{:S(2)}) %collective-permute-start.25) | collective-permute-done | bytes 589856 | tf_op jit(solution)/shard_map/ppermute | solution.py:420
  282.2 11.2 %input_back.1 = (bf16[1000,768]{1,0:T(8,128)(2,1)}, f32[8,768]{1,0:T(8,128)}) custom-call(bf16[1024,768]{1,0:T(8,128)(2,1)} %copy-done.6, bf16[1024,768]{1,0:T(8,128)(2,1)} %get-tuple-element.62.dq_ref, bf16[1024,768]{1,0:T(8,128)(2,1)} %get-tuple-element.63.dk_ref, bf16[1024,768]{1,0:T(8,128)(2,1)} %get-tuple-element.64.dv_ref, ...), custom_call_target="tpu_custom_call" | custom-call | flops 3623878656 | bytes 14539776 | tf_op jit(solution)/shard_map/input_back/pallas_call | solution.py:55
  298.9 11.5 %collective-permute-done.27 = bf16[4,96,768]{2,1,0:T(8,128)(2,1)} collective-permute-done((bf16[4,96,768]{2,1,0:T(8,128)(2,1)}, bf16[4,96,768]{2,1,0:T(8,128)(2,1)}, u32[]{:S(2)}, u32[]{:S(2)}) %collective-permute-start.27) | collective-permute-done | bytes 589856 | tf_op jit(solution)/shard_map/ppermute | solution.py:420
  312.1 4.7 %collective-permute-start.28 = (bf16[4,96,768]{2,1,0:T(8,128)(2,1)S(1)}, bf16[4,96,768]{2,1,0:T(8,128)(2,1)S(1)}, u32[]{:S(2)}, u32[]{:S(2)}) collective-permute-start(bf16[4,96,768]{2,1,0:T(8,128)(2,1)S(1)} %fusion.2), channel_id=1, source_target_pairs={{0,8},{2,10},{8,16},{10,18},{16,24},{18,26},{24,28},{26,30},{28,20... | collective-permute-start | bytes 1769480 | tf_op jit(solution)/shard_map/ppermute | solution.py:420
  318.3 38.0 %collective-permute-done.19 = f32[9216]{0:T(1024)S(1)} collective-permute-done((f32[9216]{0:T(1024)S(1)}, f32[9216]{0:T(1024)S(1)}, u32[]{:S(2)}, u32[]{:S(2)}) %collective-permute-start.19) | collective-permute-done | bytes 36896 | tf_op jit(solution)/shard_map/ppermute | solution.py:409
  356.6 3.7 collective-permute-done.20
  360.4 3.9 collective-permute-done.21
  376.2 8.1 %weave.3 = bf16[5,197,4,768]{3,2,1,0:T(4,128)(2,1)} custom-call(s32[2]{0:T(128)S(1)} %copy-done.5, bf16[1000,768]{1,0:T(8,128)(2,1)} %get-tuple-element.67.a_ref, bf16[1000,768]{1,0:T(8,128)(2,1)} %collective-permute-done.15.b_ref, bf16[1000,768]{1,0:T(8,128)(2,1)} %collective-permute-done.16.c_ref, bf16[1000,768]{1,0:T(8,128)(2,1)} %collective-permute-done.17.d_ref), custom_call_target="tpu_custom_call" | custom-call | flops 1207959552 | bytes 12195848 | tf_op jit(solution)/shard_map/weave/pallas_call | solution.py:55
  384.3 6.7 %weave.2 = bf16[5,197,4,768]{3,2,1,0:T(4,128)(2,1)} custom-call(s32[2]{0:T(128)S(1)} %copy-done.5, bf16[1000,768]{1,0:T(8,128)(2,1)S(1)} %copy-done.2, bf16[1000,768]{1,0:T(8,128)(2,1)} %collective-permute-done.12.b_ref, bf16[1000,768]{1,0:T(8,128)(2,1)S(1)} %collective-permute-done.13.c_ref, bf16[1000,768]{1,0:T(8,128)(2,1)} %collective-permute-done.14.d_ref), custom_call_target="tpu_custom_call" | custom-call | flops 1207959552 | bytes 12195848 | tf_op jit(solution)/shard_map/weave/pallas_call | solution.py:55
  (192 shorter events, 60.9 us)
Async XLA Ops:
  7.2 125.8 %all-gather.3.cloned.1.call-start = ((), (), s32[]{:S(2)}) async-start(), calls=%async_computation.2 | async-start | bytes 9732096 | tf_op jit(solution)/shard_map/all_gather | solution.py:453
  9.0 383.5 %reduce-scatter.2.cloned.1.call-start = ((), (), s32[]{:S(2)}) async-start(), calls=%async_computation.1 | async-start | bytes 9732096 | tf_op jit(solution)/shard_map/reduce_scatter | solution.py:566
  11.0 6.9 %collective-permute-start = (bf16[96,768]{1,0:T(8,128)(2,1)S(1)}, bf16[96,768]{1,0:T(8,128)(2,1)S(1)}, u32[]{:S(2)}, u32[]{:S(2)}) collective-permute-start(bf16[96,768]{1,0:T(8,128)(2,1)S(1)} %pad_maximum_fusion.3), channel_id=1, source_target_pairs={{0,2},{1,3},{2,0},{3,1},{4,6},{5,7},{6,4},{7,5},{8,10},{9,11},{10,... | collective-permute-start | bytes 442376 | tf_op jit(solution)/shard_map/ppermute | solution.py:409
  19.8 15.6 %collective-permute-start.2 = (bf16[4,96,768]{2,1,0:T(8,128)(2,1)S(1)}, bf16[4,96,768]{2,1,0:T(8,128)(2,1)}, u32[]{:S(2)}, u32[]{:S(2)}) collective-permute-start(bf16[4,96,768]{2,1,0:T(8,128)(2,1)S(1)} %pad_maximum_fusion.refs_0_), channel_id=1, source_target_pairs={{0,8},{1,5},{2,10},{3,7},{8,16},{9,1},{10,18},{11,3},{16,24},{17,9... | collective-permute-start | bytes 1769480 | tf_op jit(solution)/shard_map/ppermute | solution.py:420
  35.4 17.3 %collective-permute-start.6 = (bf16[4,96,768]{2,1,0:T(8,128)(2,1)}, bf16[4,96,768]{2,1,0:T(8,128)(2,1)S(1)}, u32[]{:S(2)}, u32[]{:S(2)}) collective-permute-start(bf16[4,96,768]{2,1,0:T(8,128)(2,1)} %collective-permute-done.2.refs_1_), channel_id=1, source_target_pairs={{0,8},{1,5},{2,10},{3,7},{8,16},{9,1},{10,18},{11,3},{16,24},{17,9... | collective-permute-start | bytes 1769480 | tf_op jit(solution)/shard_map/ppermute | solution.py:420
  52.7 12.0 %collective-permute-start.8 = (bf16[4,96,768]{2,1,0:T(8,128)(2,1)S(1)}, bf16[4,96,768]{2,1,0:T(8,128)(2,1)S(1)}, u32[]{:S(2)}, u32[]{:S(2)}) collective-permute-start(bf16[4,96,768]{2,1,0:T(8,128)(2,1)S(1)} %collective-permute-done.6.refs_3_), channel_id=1, source_target_pairs={{0,8},{1,5},{2,10},{3,7},{8,16},{9,1},{10,18},{11,3},{16,24},{17,9... | collective-permute-start | bytes 1769480 | tf_op jit(solution)/shard_map/ppermute | solution.py:420
  57.4 13.2 %collective-permute-start.3 = (f32[1152]{0:T(1024)S(1)}, f32[1152]{0:T(1024)S(1)}, u32[]{:S(2)}, u32[]{:S(2)}) collective-permute-start(f32[1152]{0:T(1024)S(1)} %concatenate.41), channel_id=1, source_target_pairs={{0,1},{1,0},{2,3},{3,2},{4,5},{5,4},{6,7},{7,6},{8,9},{9,8},{10,11... | collective-permute-start | bytes 13832 | tf_op jit(solution)/shard_map/ppermute | solution.py:409
  64.7 25.5 %collective-permute-start.10 = (bf16[4,96,768]{2,1,0:T(8,128)(2,1)S(1)}, bf16[4,96,768]{2,1,0:T(8,128)(2,1)S(1)}, u32[]{:S(2)}, u32[]{:S(2)}) collective-permute-start(bf16[4,96,768]{2,1,0:T(8,128)(2,1)S(1)} %collective-permute-done.8.refs_5_), channel_id=1, source_target_pairs={{0,8},{2,10},{8,16},{10,18},{16,24},{18,26},{24,28},{26,30},{28,20... | collective-permute-start | bytes 1769480 | tf_op jit(solution)/shard_map/ppermute | solution.py:420
  70.6 19.7 %collective-permute-start.4 = (f32[2,1152]{1,0:T(2,128)S(1)}, f32[2,1152]{1,0:T(2,128)S(1)}, u32[]{:S(2)}, u32[]{:S(2)}) collective-permute-start(f32[2,1152]{1,0:T(2,128)S(1)} %pad_maximum_fusion.7), channel_id=1, source_target_pairs={{0,2},{1,3},{2,0},{3,1},{4,6},{5,7},{6,4},{7,5},{8,10},{9,11},{10,... | collective-permute-start | bytes 27656 | tf_op jit(solution)/shard_map/ppermute | solution.py:409
  81.1 11.2 %collective-permute-start.5 = (bf16[4,96,768]{2,1,0:T(8,128)(2,1)}, bf16[4,96,768]{2,1,0:T(8,128)(2,1)S(1)}, u32[]{:S(2)}, u32[]{:S(2)}) collective-permute-start(bf16[4,96,768]{2,1,0:T(8,128)(2,1)} %collective-permute-done.2.refs_1_), channel_id=1, source_target_pairs={{0,1},{1,0},{2,3},{3,2},{4,5},{5,4},{6,7},{7,6},{8,9},{9,8},{10,11... | collective-permute-start | bytes 1769480 | tf_op jit(solution)/shard_map/ppermute | solution.py:409
  81.1 11.2 %collective-permute-start.7 = (bf16[4,96,768]{2,1,0:T(8,128)(2,1)S(1)}, bf16[4,96,768]{2,1,0:T(8,128)(2,1)S(1)}, u32[]{:S(2)}, u32[]{:S(2)}) collective-permute-start(bf16[4,96,768]{2,1,0:T(8,128)(2,1)S(1)} %collective-permute-done.6.refs_3_), channel_id=1, source_target_pairs={{0,1},{1,0},{2,3},{3,2},{4,5},{5,4},{6,7},{7,6},{8,9},{9,8},{10,11... | collective-permute-start | bytes 1769480 | tf_op jit(solution)/shard_map/ppermute | solution.py:409
  81.6 10.7 %collective-permute-start.9 = (bf16[4,96,768]{2,1,0:T(8,128)(2,1)S(1)}, bf16[4,96,768]{2,1,0:T(8,128)(2,1)}, u32[]{:S(2)}, u32[]{:S(2)}) collective-permute-start(bf16[4,96,768]{2,1,0:T(8,128)(2,1)S(1)} %collective-permute-done.8.refs_5_), channel_id=1, source_target_pairs={{0,1},{1,0},{2,3},{3,2},{4,5},{5,4},{6,7},{7,6},{8,9},{9,8},{10,11... | collective-permute-start | bytes 1769480 | tf_op jit(solution)/shard_map/ppermute | solution.py:409
  90.2 2.1 collective-permute-start.11
  247.5 31.9 %collective-permute-start.23 = (bf16[3,4,96,768]{3,2,1,0:T(8,128)(2,1)S(1)}, bf16[3,4,96,768]{3,2,1,0:T(8,128)(2,1)S(1)}, u32[]{:S(2)}, u32[]{:S(2)}) collective-permute-start(bf16[3,4,96,768]{3,2,1,0:T(8,128)(2,1)S(1)} %slice.117), channel_id=1, source_target_pairs={{0,1},{1,0},{2,3},{3,2},{4,5},{5,4},{6,7},{7,6},{8,9},{9,8},{10,11... | collective-permute-start | bytes 5308424 | tf_op jit(solution)/shard_map/ppermute | solution.py:409
  249.3 3.0 collective-permute-start.24
  252.5 26.8 %collective-permute-start.25 = (bf16[4,96,768]{2,1,0:T(8,128)(2,1)S(1)}, bf16[4,96,768]{2,1,0:T(8,128)(2,1)S(1)}, u32[]{:S(2)}, u32[]{:S(2)}) collective-permute-start(bf16[4,96,768]{2,1,0:T(8,128)(2,1)S(1)} %fusion.3), channel_id=1, source_target_pairs={{0,8},{1,5},{2,10},{3,7},{8,16},{9,1},{10,18},{11,3},{16,24},{17,9... | collective-permute-start | bytes 1769480 | tf_op jit(solution)/shard_map/ppermute | solution.py:420
  280.7 13.2 %collective-permute-start.26 = (bf16[4,96,768]{2,1,0:T(8,128)(2,1)}, bf16[4,96,768]{2,1,0:T(8,128)(2,1)}, u32[]{:S(2)}, u32[]{:S(2)}) collective-permute-start(bf16[4,96,768]{2,1,0:T(8,128)(2,1)} %fusion), channel_id=1, source_target_pairs={{0,8},{1,5},{2,10},{3,7},{8,16},{9,1},{10,18},{11,3},{16,24},{17,9... | collective-permute-start | bytes 1769480 | tf_op jit(solution)/shard_map/ppermute | solution.py:420
  280.7 83.9 %collective-permute-start.13 = (bf16[1000,768]{1,0:T(8,128)(2,1)S(1)}, bf16[1000,768]{1,0:T(8,128)(2,1)S(1)}, u32[]{:S(2)}, u32[]{:S(2)}) collective-permute-start(bf16[1000,768]{1,0:T(8,128)(2,1)S(1)} %copy-done.2), channel_id=1, source_target_pairs={{0,2},{1,3},{2,0},{3,1},{4,6},{5,7},{6,4},{7,5},{8,10},{9,11},{10,... | collective-permute-start | bytes 4608008 | tf_op jit(solution)/shard_map/ppermute | solution.py:409
  293.4 70.9 %collective-permute-start.16 = (bf16[1000,768]{1,0:T(8,128)(2,1)}, bf16[1000,768]{1,0:T(8,128)(2,1)}, u32[]{:S(2)}, u32[]{:S(2)}) collective-permute-start(bf16[1000,768]{1,0:T(8,128)(2,1)} %get-tuple-element.67.a_ref), channel_id=1, source_target_pairs={{0,2},{1,3},{2,0},{3,1},{4,6},{5,7},{6,4},{7,5},{8,10},{9,11},{10,... | collective-permute-start | bytes 4608008 | tf_op jit(solution)/shard_map/ppermute | solution.py:409
  296.4 14.0 %collective-permute-start.27 = (bf16[4,96,768]{2,1,0:T(8,128)(2,1)}, bf16[4,96,768]{2,1,0:T(8,128)(2,1)}, u32[]{:S(2)}, u32[]{:S(2)}) collective-permute-start(bf16[4,96,768]{2,1,0:T(8,128)(2,1)} %fusion.1), channel_id=1, source_target_pairs={{0,8},{1,5},{2,10},{3,7},{8,16},{9,1},{10,18},{11,3},{16,24},{17,9... | collective-permute-start | bytes 1769480 | tf_op jit(solution)/shard_map/ppermute | solution.py:420
  298.9 17.9 %collective-permute-start.18 = (f32[9216]{0:T(1024)S(1)}, f32[9216]{0:T(1024)S(1)}, u32[]{:S(2)}, u32[]{:S(2)}) collective-permute-start(f32[9216]{0:T(1024)S(1)} %pad_maximum_fusion.4), channel_id=1, source_target_pairs={{0,1},{1,0},{2,3},{3,2},{4,5},{5,4},{6,7},{7,6},{8,9},{9,8},{10,11... | collective-permute-start | bytes 110600 | tf_op jit(solution)/shard_map/ppermute | solution.py:409
  312.1 52.9 %collective-permute-start.28 = (bf16[4,96,768]{2,1,0:T(8,128)(2,1)S(1)}, bf16[4,96,768]{2,1,0:T(8,128)(2,1)S(1)}, u32[]{:S(2)}, u32[]{:S(2)}) collective-permute-start(bf16[4,96,768]{2,1,0:T(8,128)(2,1)S(1)} %fusion.2), channel_id=1, source_target_pairs={{0,8},{2,10},{8,16},{10,18},{16,24},{18,26},{24,28},{26,30},{28,20... | collective-permute-start | bytes 1769480 | tf_op jit(solution)/shard_map/ppermute | solution.py:420
  316.8 39.6 %collective-permute-start.19 = (f32[9216]{0:T(1024)S(1)}, f32[9216]{0:T(1024)S(1)}, u32[]{:S(2)}, u32[]{:S(2)}) collective-permute-start(f32[9216]{0:T(1024)S(1)} %fusion.13), channel_id=1, source_target_pairs={{0,2},{1,3},{2,0},{3,1},{4,6},{5,7},{6,4},{7,5},{8,10},{9,11},{10,... | collective-permute-start | bytes 110600 | tf_op jit(solution)/shard_map/ppermute | solution.py:409
  356.4 4.0 collective-permute-start.20
  360.3 4.0 collective-permute-start.21
  360.3 15.9 %collective-permute-start.15 = (bf16[1000,768]{1,0:T(8,128)(2,1)}, bf16[1000,768]{1,0:T(8,128)(2,1)}, u32[]{:S(2)}, u32[]{:S(2)}) collective-permute-start(bf16[1000,768]{1,0:T(8,128)(2,1)} %get-tuple-element.67.a_ref), channel_id=1, source_target_pairs={{0,1},{1,0},{2,3},{3,2},{4,5},{5,4},{6,7},{7,6},{8,9},{9,8},{10,11... | collective-permute-start | bytes 4608008 | tf_op jit(solution)/shard_map/ppermute | solution.py:409
  364.3 20.0 %collective-permute-start.12 = (bf16[1000,768]{1,0:T(8,128)(2,1)S(1)}, bf16[1000,768]{1,0:T(8,128)(2,1)}, u32[]{:S(2)}, u32[]{:S(2)}) collective-permute-start(bf16[1000,768]{1,0:T(8,128)(2,1)S(1)} %copy-done.2), channel_id=1, source_target_pairs={{0,1},{1,0},{2,3},{3,2},{4,5},{5,4},{6,7},{7,6},{8,9},{9,8},{10,11... | collective-permute-start | bytes 4608008 | tf_op jit(solution)/shard_map/ppermute | solution.py:409
  364.3 6.6 %collective-permute-start.22 = (f32[9216]{0:T(1024)S(1)}, f32[9216]{0:T(1024)S(1)}, u32[]{:S(2)}, u32[]{:S(2)}) collective-permute-start(f32[9216]{0:T(1024)S(1)} %add.164), channel_id=1, source_target_pairs={{0,16},{4,20},{8,24},{12,28},{16,0},{20,4},{24,8},{28,12},{1,17},{... | collective-permute-start | bytes 110600 | tf_op jit(solution)/shard_map/ppermute | solution.py:410
  364.6 11.6 %collective-permute-start.17 = (bf16[1000,768]{1,0:T(8,128)(2,1)}, bf16[1000,768]{1,0:T(8,128)(2,1)}, u32[]{:S(2)}, u32[]{:S(2)}) collective-permute-start(bf16[1000,768]{1,0:T(8,128)(2,1)} %collective-permute-done.16.c_ref), channel_id=1, source_target_pairs={{0,1},{1,0},{2,3},{3,2},{4,5},{5,4},{6,7},{7,6},{8,9},{9,8},{10,11... | collective-permute-start | bytes 4608008 | tf_op jit(solution)/shard_map/ppermute | solution.py:409
  365.0 19.3 %collective-permute-start.14 = (bf16[1000,768]{1,0:T(8,128)(2,1)S(1)}, bf16[1000,768]{1,0:T(8,128)(2,1)}, u32[]{:S(2)}, u32[]{:S(2)}) collective-permute-start(bf16[1000,768]{1,0:T(8,128)(2,1)S(1)} %collective-permute-done.13.c_ref), channel_id=1, source_target_pairs={{0,1},{1,0},{2,3},{3,2},{4,5},{5,4},{6,7},{7,6},{8,9},{9,8},{10,11... | collective-permute-start | bytes 4608008 | tf_op jit(solution)/shard_map/ppermute | solution.py:409
  370.9 2.6 collective-permute-start.29
  374.7 16.3 %collective-permute-start.30 = (bf16[96,768]{0,1:T(8,128)(2,1)S(1)}, bf16[96,768]{0,1:T(8,128)(2,1)S(1)}, u32[]{:S(2)}, u32[]{:S(2)}) collective-permute-start(bf16[96,768]{0,1:T(8,128)(2,1)S(1)} %fusion.4), channel_id=1, source_target_pairs={{0,2},{1,3},{2,0},{3,1},{4,6},{5,7},{6,4},{7,5},{8,10},{9,11},{10,... | collective-permute-start | bytes 442376 | tf_op jit(solution)/shard_map/ppermute | solution.py:409
  (31 other events, 589.6 us)
Sparse Core Ops, SparseCore 0:
  11.5 90.1 all-gather.2
  177.0 153.5 reduce-scatter.1

commit v4 on v3

--- a/solution.py
+++ b/solution.py
@@ -5,6 +5,7 @@
 from jax.experimental import pallas as pl
 from jax.experimental.pallas import tpu as pltpu
 from jax.sharding import PartitionSpec as P
+
 
 HEAD_DIM = 64
 NORM_EPS = 1e-06
@@ -15,7 +16,6 @@
 F32 = jnp.float32
 NT = (((1,), (1,)), ((), ()))
 NN = (((1,), (0,)), ((), ()))
-TN = (((0,), (0,)), ((), ()))
 
 
 def dot(a, b, dims=NN):
@@ -43,7 +43,7 @@
     return jnp.sum(values, axis=0, keepdims=True)
 
 
-def call(body, outs, ins, in_specs=None, out_specs=None, grid=None, scratch=(), flops=0, nbytes=0, limit=60, name=None, **kw):
+def call(body, outs, ins, in_specs=None, out_specs=None, grid=None, scratch=(), flops=0, nbytes=0, limit=60, **kw):
     full = lambda a: pl.BlockSpec(a.shape, (lambda *_: (0,) * len(a.shape)))
     if in_specs is None:
         in_specs = [None] * len(ins)
@@ -60,7 +60,6 @@
         out_specs=tuple(out_specs),
         scratch_shapes=list(scratch),
         compiler_params=pltpu.CompilerParams(vmem_limit_bytes=limit * 1024 * 1024),
-        name=name,
         cost_estimate=pl.CostEstimate(flops=flops, bytes_accessed=nbytes, transcendentals=0),
         **kw,
     )(*ins)
@@ -90,25 +89,29 @@
             dy_ref[rows, :] = cot_ref[0, i]
 
 
-def place_chunks(info_ref, refs, buf_ref):
-    sub = refs[0].shape[1]
-
-    def put(n, ref):
+def place(info_ref, refs, buf_ref, group=0):
+    for n, ref in enumerate(refs):
+        sub = ref.shape[1]
         rows = pl.ds(pl.multiple_of(info_ref[2 + n] * sub, sub), sub)
-        for j in range(ref.shape[0]):
-            buf_ref[j, rows, :] = ref[j]
-
-    for n, ref in enumerate(refs[:-2]):
-        put(n, ref)
-    even = info_ref[0] % 2 == 0
-    pl.when(even)(lambda: put(len(refs) - 2, refs[-2]))
-    pl.when(~even)(lambda: put(len(refs) - 2, refs[-1]))
+        buf_ref[rows, :] = ref[group]
+
+
+def weights(info_ref, refs, buf_ref):
+    if len(refs) == 1:
+        parts, groups, sub, cols = refs[0].shape
+        return [refs[0][:, j].reshape(parts * sub, cols) for j in range(groups)]
+    groups = refs[0].shape[0]
+    for j in range(groups):
+        place(info_ref, refs, buf_ref.at[j], j)
+    return [buf_ref[j] for j in range(groups)]
 
 
 def qkv_ring_body(info_ref, x_ref, gain_ref, shift_ref, bias_ref, *refs):
     h_ref, qkv_ref, wq_ref, wo_ref, buf_ref = refs[-5:]
-    place_chunks(info_ref, refs[:-5], buf_ref)
-    qkv_rest(lambda j: buf_ref[j], buf_ref.shape[0], x_ref, gain_ref, shift_ref, bias_ref, h_ref, qkv_ref, wq_ref, wo_ref)
+    groups = buf_ref.shape[0]
+    for j in range(groups):
+        place(info_ref, refs[:-5], buf_ref.at[j], j)
+    qkv_rest(lambda j: buf_ref[j], groups, x_ref, gain_ref, shift_ref, bias_ref, h_ref, qkv_ref, wq_ref, wo_ref)
 
 
 def qkv_gathered_body(x_ref, gain_ref, shift_ref, bias_ref, wa_ref, h_ref, qkv_ref, wq_ref, wo_ref):
@@ -177,9 +180,9 @@
     loop(mid_ref.shape[0] // 128, norm)
 
 
-def hidden_body(h_ref, w_ref, bias_ref, act_ref, slope_ref):
-    parts, _, sub, cols = w_ref.shape
-    w = w_ref[:, 0].reshape(parts * sub, cols)
+def hidden_body(info_ref, h_ref, bias_ref, *refs):
+    act_ref, slope_ref, buf_ref = refs[-3:]
+    (w,) = weights(info_ref, refs[:-3], buf_ref)
 
     def chunk(i):
         rows = cut(i, 256)
@@ -191,14 +194,19 @@
     loop(ROWS // 256, chunk)
 
 
-def down_body(slots, info_ref, act_ref, wc_ref, mid_ref, bias_ref, out_ref, acc_ref):
-    parts, groups, sub, cols = wc_ref.shape
-    for j in range(groups):
-        part = dot(act_ref[:, j * cols : (j + 1) * cols], wc_ref[:, j].reshape(parts * sub, cols), NT)
+def wide_dot(left_ref, ws, acc_ref):
+    for j, w in enumerate(ws):
+        cols = w.shape[1]
+        part = dot(left_ref[:, j * cols : (j + 1) * cols], w, NT)
         if j == 0:
             acc_ref[...] = part
         else:
             acc_ref[...] += part
+
+
+def down_body(slots, info_ref, act_ref, mid_ref, bias_ref, *refs):
+    out_ref, acc_ref, buf_ref = refs[-3:]
+    wide_dot(act_ref, weights(info_ref, refs[:-3], buf_ref), acc_ref)
     for i in range(slots):
         rows = slice(i * SLOT_ROWS, (i + 1) * SLOT_ROWS)
         live = jnp.where(i < info_ref[1], 1.0, 0.0)
@@ -220,10 +228,9 @@
     part(full, 8, length - full)
 
 
-def outer_body(h_ref, dy_ref, du_ref, act_ref, g_ref, t_ref):
+def outer_steps(h_ref, dy_ref, du_ref, act_ref, t_ref, store):
     step = pl.program_id(0)
     half = pl.num_programs(0) // 2
-    parts, _, sub, cols = g_ref.shape
 
     @pl.when(step == 0)
     def _():
@@ -233,18 +240,35 @@
     def _():
         t_ref[...] = h_ref[...].T
 
-    @pl.when(step < half)
-    def _():
-        g_ref[:, 0] = dot(t_ref[...], act_ref[...]).astype(BF).reshape(parts, sub, cols)
-
-    @pl.when(step >= half)
-    def _():
-        g_ref[:, 0] = dot(t_ref[...], du_ref[...]).astype(BF).reshape(parts, sub, cols)
-
-
-def dact_body(dy_ref, wc_ref, slope_ref, du_ref, sum_ref):
-    parts, _, sub, cols = wc_ref.shape
-    w = wc_ref[:, 0].reshape(parts * sub, cols)
+    pl.when(step < half)(lambda: store(dot(t_ref[...], act_ref[...]).astype(BF)))
+    pl.when(step >= half)(lambda: store(dot(t_ref[...], du_ref[...]).astype(BF)))
+
+
+def outer_body(h_ref, dy_ref, du_ref, act_ref, g_ref, t_ref):
+    parts, _, sub, cols = g_ref.shape
+
+    def store(g):
+        g_ref[:, 0] = g.reshape(parts, sub, cols)
+
+    outer_steps(h_ref, dy_ref, du_ref, act_ref, t_ref, store)
+
+
+def outer_halves_body(info_ref, h_ref, dy_ref, du_ref, act_ref, *refs):
+    halves, t_ref, buf_ref = refs[:-2], refs[-2], refs[-1]
+
+    def store(g):
+        buf_ref[...] = g
+        for n, ref in enumerate(halves):
+            sub = ref.shape[1]
+            ref[0] = buf_ref[pl.ds(pl.multiple_of(info_ref[2 + n] * sub, sub), sub), :]
+
+    outer_steps(h_ref, dy_ref, du_ref, act_ref, t_ref, store)
+
+
+def dact_body(info_ref, dy_ref, slope_ref, *refs):
+    du_ref, sum_ref, buf_ref = refs[-3:]
+    (w,) = weights(info_ref, refs[:-3], buf_ref)
+    cols = w.shape[1]
     total = jnp.zeros((1, cols), F32)
     for i in range(ROWS // 256):
         rows = slice(i * 256, (i + 1) * 256)
@@ -254,14 +278,9 @@
     sum_ref[...] = jnp.broadcast_to(total, sum_ref.shape)
 
 
-def mid_back_body(dy_ref, du_ref, wb_ref, mid_ref, gain_ref, dmid_ref, dlow_ref, sums_ref, acc_ref):
-    parts, groups, sub, cols = wb_ref.shape
-    for j in range(groups):
-        part = dot(du_ref[:, j * cols : (j + 1) * cols], wb_ref[:, j].reshape(parts * sub, cols), NT)
-        if j == 0:
-            acc_ref[...] = part
-        else:
-            acc_ref[...] += part
+def mid_back_body(info_ref, dy_ref, du_ref, mid_ref, gain_ref, *refs):
+    dmid_ref, dlow_ref, sums_ref, acc_ref, buf_ref = refs[-5:]
+    wide_dot(du_ref, weights(info_ref, refs[:-5], buf_ref), acc_ref)
     width = dy_ref.shape[1]
 
     def chunk(i, sums):
@@ -285,7 +304,8 @@
     do_ref[...] = dot(dlow_ref[...], wo_ref[...]).astype(BF)
 
 
-def attend_back_body(slots, q_ref, k_ref, v_ref, p_ref, do_ref, dq_ref, dk_ref, dv_ref):
+def attend_back_body(slots, q_ref, k_ref, v_ref, p_ref, do_ref, *refs):
+    dq_ref, dk_ref, dv_ref = refs[-3:]
     low_half = lax.broadcasted_iota(jnp.int32, (SLOT_ROWS, 2 * HEAD_DIM), 1) < HEAD_DIM
 
     def image(i):
@@ -323,21 +343,21 @@
     store(3, dot(dlow_ref[...].T, o_ref[...]).astype(BF))
 
 
-def outer_ring_body(info_ref, h_ref, dq_ref, dk_ref, dv_ref, dlow_ref, o_ref, keep_ref, send_ref, sums_ref, buf_ref):
+def outer_ring_body(info_ref, h_ref, dq_ref, dk_ref, dv_ref, dlow_ref, o_ref, *refs):
+    halves, sums_ref, buf_ref = refs[:-2], refs[-2], refs[-1]
     groups = buf_ref.shape[0]
     local = h_ref.shape[1] // groups
-    slots, _, sub, _ = keep_ref.shape
 
     def store(s, g):
         for j in range(groups):
             buf_ref[j, :, s * local : (s + 1) * local] = g[:, j * local : (j + 1) * local]
 
     small_outer(h_ref, dq_ref, dk_ref, dv_ref, dlow_ref, o_ref, sums_ref, store)
-    for n in range(2 * slots):
+    for n, ref in enumerate(halves):
+        sub = ref.shape[1]
         rows = pl.ds(pl.multiple_of(info_ref[2 + n] * sub, sub), sub)
-        ref = keep_ref if n < slots else send_ref
         for j in range(groups):
-            ref[n % slots, j] = buf_ref[j, rows, :]
+            ref[j] = buf_ref[j, rows, :]
 
 
 def outer_plain_body(h_ref, dq_ref, dk_ref, dv_ref, dlow_ref, o_ref, g_ref, sums_ref):
@@ -373,25 +393,11 @@
         sums_ref[n : n + 1, :] = sums[n]
 
 
-def on_device(
-    inputs,
-    cotangent,
-    counts,
-    norm_gain,
-    norm_shift,
-    qkv_weight,
-    query_bias,
-    value_bias,
-    out_weight,
-    out_bias,
-    mlp_gain,
-    mlp_shift,
-    hidden_weight,
-    hidden_bias,
-    down_weight,
-    down_bias,
+def block_step(
+    inputs, cotangent, counts, norm_gain, norm_shift, qkv_weight, query_bias, value_bias,
+    out_weight, out_bias, mlp_gain, mlp_shift, hidden_weight, hidden_bias, down_weight, down_bias,
 ):
-    batches, slots, length, width = inputs.shape
+    _, slots, length, width = inputs.shape
     sub = qkv_weight.shape[0]
     local = qkv_weight.shape[1] // 3
     units = hidden_weight.shape[1]
@@ -420,7 +426,6 @@
         return lax.ppermute(a, axes, pairs)
 
     even = mine % 2 == 0
-    side = jnp.where(even, 1, -1)
     row = lambda v: v.reshape(1, -1)
     live = lax.dynamic_index_in_dim(counts, mine, 0, keepdims=False)[0]
 
@@ -449,30 +454,78 @@
         name="prep",
     )(info, inputs, cotangent)
 
+    def scatter_ring(halves):
+        got = [mp_swap(send, 1) for send in halves[far:]]
+
+        def term(n):
+            return halves[n].astype(F32) + got[n].astype(F32)
+
+        total = term(0)
+        for k in range(1, far):
+            moved = hop(total.astype(BF))
+            total = term(k) + moved.astype(F32)
+        total = total.astype(BF)
+        last = hop(total, False)
+        total = jnp.where(even, last, total).reshape(2, 2, sub, -1)
+        split = lambda a, b, first: (jnp.where(first, a, b), jnp.where(first, b, a))
+        mine_half, other_half = split(total[:, 0], total[:, 1], even)
+        total = mine_half.astype(F32) + mp_swap(other_half, 1).astype(F32)
+        mine_half, other_half = split(total[0], total[1], mine < 2)
+        return mine_half + mp_swap(other_half.astype(BF), 2).astype(F32)
+
+    leave = [jnp.where(even, far - k, k + 1 - far) for k in range(far)]
+    stay = [jnp.where(even, k + 1 - far, far - k) for k in range(far)]
+    halves = lambda n: [sds((groups, sub, n), BF)] * (2 * far)
+
     shard_bc = jnp.concatenate([hidden_weight, down_weight.T], axis=1)
-    bc = lax.all_gather(shard_bc, axes, axis=0, tiled=False).reshape(parts, groups, sub, 2 * units)
     shard_a = jnp.concatenate([qkv_weight, out_weight.T], axis=1)
     vectors = jnp.concatenate([query_bias, value_bias, hidden_bias])
-    if ring:
-        two = jnp.stack([shard_a, mp_swap(shard_a, 2)])
+
+    def chip_chunk(shard):
+        two = jnp.stack([shard, mp_swap(shard, 2)])
         near = mp_swap(two, 1)
         rel = [two[0], near[0], two[1], near[1]]
         rel = [jnp.where(even, rel[j], rel[j ^ 1]) for j in range(groups)]
-        start = jnp.stack([jnp.where(mine < 2, rel[j], rel[j ^ 2]) for j in range(groups)])
-        chunks, offsets = [start], [jnp.int32(0)]
-        held = start
+        return jnp.stack([jnp.where(mine < 2, rel[j], rel[j ^ 2]) for j in range(groups)])
+
+    def gather_ring(start, between):
+        chunks, held = [start], start
         for k in range(1, far):
             held = hop(held)
+            held = between(k, held)
+            chunks += [held, mp_swap(held, 1)]
+        half = hop(jnp.where(even, held[: groups // 2], held[groups // 2 :]))
+        other = mp_swap(half, 1)
+        first, second = jnp.where(even, half, other), jnp.where(even, other, half)
+        return chunks + [jnp.concatenate([first, second])], half
+
+    if ring:
+        side = jnp.where(even, 1, -1)
+        offsets = [jnp.int32(0)]
+        for k in range(1, far):
+            offsets += [-k * side, k * side]
+        ring_info = info_of(offsets + [jnp.int32(far)])
+        start_bc = chip_chunk(shard_bc)
+        prepared = (x, dy)
+
+        def between(k, held):
+            nonlocal prepared
             if k == 1:
-                held, x, dy = lax.optimization_barrier((held, x, dy))
-            chunks += [held, mp_swap(held, 1)]
-            offsets += [-k * side, k * side]
-        held = hop(held, False)
-        chunks += [held, mp_swap(held, 1)]
-        offsets += [jnp.int32(far)]
-        ring_info = info_of(offsets)
+                held, prepared = lax.optimization_barrier((held, prepared))
+            return held
+
+        chunks, last = gather_ring(chip_chunk(shard_a), between)
+        x, dy = prepared
+        start_bc, last = lax.optimization_barrier((start_bc, last))
+        bc, _ = gather_ring(start_bc, lambda k, held: held)
+        piece = lambda n: [pl.BlockSpec((groups, sub, units), lambda i: (0, 0, n))] * len(bc)
+        wcols = lambda n: [pl.BlockSpec((1, sub, units), lambda i: (i, 0, n))] * len(bc)
     else:
+        ring_info = info
         wa = lax.all_gather(shard_a, axes, axis=0, tiled=False).reshape(parts, groups, sub, 4 * local)
+        bc = [lax.all_gather(shard_bc, axes, axis=0, tiled=False).reshape(parts, groups, sub, 2 * units)]
+        piece = lambda n: [pl.BlockSpec((parts, groups, sub, units), lambda i: (0, 0, 0, n))]
+        wcols = lambda n: [pl.BlockSpec((parts, 1, sub, units), lambda i: (0, i, 0, n))]
     two = jnp.stack([vectors, mp_swap(vectors, 1)])
     four = jnp.concatenate([two, mp_swap(two, 2)])
     biases = four[jnp.arange(groups) ^ mine]
@@ -489,10 +542,9 @@
             [smem] + [None] * (len(qkv_ins) + len(chunks)),
             scratch=[pltpu.VMEM((groups, width, 4 * local), BF)],
             flops=3 * mm,
-            name="qkv",
         )
     else:
-        h1, qkv, wq, wo = call(qkv_gathered_body, qkv_outs, qkv_ins + [wa], flops=3 * mm, name="qkv")
+        h1, qkv, wq, wo = call(qkv_gathered_body, qkv_outs, qkv_ins + [wa], flops=3 * mm)
     pair = 2 * HEAD_DIM
     pairs = width // pair
     head = lambda s: pl.BlockSpec((ROWS, pair), lambda i: (0, s * pairs + i))
@@ -506,7 +558,6 @@
         [head(0), p_spec],
         (pairs,),
         flops=mm,
-        name="attend",
     )
     rows256 = pl.BlockSpec((256, width), lambda i: (i, 0))
     middle, h2 = call(
@@ -517,55 +568,65 @@
         [rows256, rows256],
         (ROWS // 256,),
         flops=mm,
-        name="mix",
-    )
-    wcols = lambda n: pl.BlockSpec((parts, 1, sub, units), lambda i: (0, i, 0, n))
-    piece = lambda n: pl.BlockSpec((parts, groups, sub, units), lambda i: (0, 0, 0, n))
+    )
     tcols = pl.BlockSpec((ROWS, units), lambda i: (0, i))
     vcols = lambda n: pl.BlockSpec((n, units), lambda i: (0, i))
+    group_buf = lambda n: pltpu.VMEM((n, width, units), BF)
     act, slope = call(
         hidden_body,
         [t_bf(ff), t_bf(ff)],
-        [h2, bc, row(hb)],
-        [None, wcols(0), vcols(1)],
+        [ring_info, h2, row(hb)] + bc,
+        [smem, None, vcols(1)] + wcols(0),
         [tcols, tcols],
         (groups,),
+        scratch=[group_buf(1)],
         flops=4 * mm,
-        name="hidden",
     )
     du, sum_hidden = call(
         dact_body,
         [t_bf(ff), sds((8, ff), F32)],
-        [dy, bc, slope],
-        [None, wcols(1), tcols],
+        [ring_info, dy, slope] + bc,
+        [smem, None, tcols] + wcols(1),
         [tcols, vcols(8)],
         (groups,),
+        scratch=[group_buf(1)],
         flops=4 * mm,
-        name="dact",
-    )
-    (g_bc,) = call(
-        outer_body,
-        [sds((parts, groups, sub, 2 * units), BF)],
-        [h2, dy, du, act],
-        [
-            None,
-            None,
-            pl.BlockSpec((ROWS, units), lambda i: (0, jnp.maximum(i - groups, 0))),
-            pl.BlockSpec((ROWS, units), lambda i: (0, jnp.minimum(i, groups - 1))),
-        ],
-        [
-            pl.BlockSpec(
-                (parts, 1, sub, units), lambda i: (0, i % groups, 0, jnp.where(i < groups, 1, 0))
-            )
-        ],
-        (2 * groups,),
-        scratch=[pltpu.VMEM((width, ROWS), BF)],
-        flops=8 * mm,
-        name="outer_bc",
-    )
-    s_bc = lax.psum_scatter(
-        g_bc.reshape(parts * groups, sub, 2 * units), axes, scatter_dimension=0, tiled=False
-    ).astype(F32)
+    )
+    outer_in_specs = [
+        None,
+        None,
+        pl.BlockSpec((ROWS, units), lambda i: (0, jnp.maximum(i - groups, 0))),
+        pl.BlockSpec((ROWS, units), lambda i: (0, jnp.minimum(i, groups - 1))),
+    ]
+    outer_map = lambda i: (0, i % groups, 0, jnp.where(i < groups, 1, 0))
+    transposed = pltpu.VMEM((width, ROWS), BF)
+    if ring:
+        halves_bc = call(
+            outer_halves_body,
+            halves(2 * units),
+            [info_of(leave + stay), h2, dy, du, act],
+            [smem] + outer_in_specs,
+            [pl.BlockSpec((1, sub, units), lambda i: outer_map(i)[1:])] * (2 * far),
+            (2 * groups,),
+            scratch=[transposed, pltpu.VMEM((width, units), BF)],
+            flops=8 * mm,
+        )
+        s_bc = scatter_ring(halves_bc)
+        g_bc = halves_bc[0]
+    else:
+        (g_bc,) = call(
+            outer_body,
+            [sds((parts, groups, sub, 2 * units), BF)],
+            [h2, dy, du, act],
+            outer_in_specs,
+            [pl.BlockSpec((parts, 1, sub, units), outer_map)],
+            (2 * groups,),
+            scratch=[transposed],
+            flops=8 * mm,
+        )
+        s_bc = lax.psum_scatter(
+            g_bc.reshape(parts * groups, sub, 2 * units), axes, scatter_dimension=0, tiled=False
+        ).astype(F32)
 
     own_shape = sds((slots * SLOT_ROWS, width), BF)
 
@@ -581,19 +642,18 @@
             (slots,),
             flops=mm,
             limit=16,
-            name="weave",
         )
         return woven.transpose(2, 0, 1, 3)
 
-    act_late, g_bc_tie = lax.optimization_barrier((act, g_bc))
+    down_info = jnp.concatenate([info, ring_info[2:]])
+    act_late, _ = lax.optimization_barrier((act, g_bc))
     (own_out,) = call(
         functools.partial(down_body, slots),
         [own_shape],
-        [info, act_late, bc, middle, row(down_bias)],
-        [smem, None, piece(1), None, None],
-        scratch=[pltpu.VMEM((ROWS, width), F32)],
+        [down_info, act_late, middle, row(down_bias)] + bc,
+        [smem, None, None, None] + piece(1),
+        scratch=[pltpu.VMEM((ROWS, width), F32), group_buf(groups)],
         flops=4 * mm,
-        name="down",
     )
     all_out = spread(own_out)
     du, _ = lax.optimization_barrier((du, own_out))
@@ -601,60 +661,46 @@
     dmid, dlow, sums_mid = call(
         mid_back_body,
         [t_f(width), t_bf(width), sds((8, width), F32)],
-        [dy, du, bc, middle, row(mlp_gain)],
-        [None, None, piece(0), None, None],
-        scratch=[pltpu.VMEM((ROWS, width), F32)],
+        [ring_info, dy, du, middle, row(mlp_gain)] + bc,
+        [smem, None, None, None, None] + piece(0),
+        scratch=[pltpu.VMEM((ROWS, width), F32), group_buf(groups)],
         flops=4 * mm,
-        name="mid_back",
-    )
-    (do,) = call(out_back_body, [t_bf(width)], [dlow, wo], flops=mm, name="out_back")
-    dq, dk, dv = call(
-        functools.partial(attend_back_body, slots),
-        [t_bf(width)] * 3,
-        [qkv, qkv, qkv, probs, do],
-        [head(0), head(1), head(2), p_spec, head(0)],
-        [head(0)] * 3,
-        (pairs,),
-        flops=2 * mm,
-        name="attend_back",
-    )
-    def scatter_ring(keep, send):
-        first, rest = mp_swap(send[:1], 1), mp_swap(send[1:], 1)
-        total = keep[0].astype(F32) + first[0].astype(F32)
-        for k in range(1, far):
-            moved = hop(total.astype(BF))
-            total = keep[k].astype(F32) + rest[k - 1].astype(F32) + moved.astype(F32)
-        total = total.astype(BF)
-        total = jnp.where(even, hop(total, False), total).reshape(2, 2, sub, -1)
-        split = lambda a, b, first: (jnp.where(first, a, b), jnp.where(first, b, a))
-        mine_half, other_half = split(total[:, 0], total[:, 1], even)
-        total = mine_half.astype(F32) + mp_swap(other_half, 1).astype(F32)
-        mine_half, other_half = split(total[0], total[1], mine < 2)
-        return mine_half + mp_swap(other_half.astype(BF), 2).astype(F32)
-
+    )
+    (do,) = call(out_back_body, [t_bf(width)], [dlow, wo], flops=mm)
+    grads = []
+    hbm = pl.BlockSpec(memory_space=pl.ANY)
+    calls = 3 if pairs % 3 == 0 else 1
+    for n in range(calls):
+        first = n * pairs // calls
+        at = lambda s, first=first: pl.BlockSpec((ROWS, pair), lambda i: (0, s * pairs + first + i))
+        grads = call(
+            functools.partial(attend_back_body, slots),
+            [t_bf(width)] * 3,
+            [qkv, qkv, qkv, probs, do] + list(grads),
+            [at(0), at(1), at(2), pl.BlockSpec((2, slots, SLOT_ROWS, SLOT_ROWS), lambda i, first=first: (first + i, 0, 0, 0)), at(0)]
+            + [hbm] * len(grads),
+            [at(0)] * 3,
+            (pairs // calls,),
+            flops=2 * mm // calls,
+            limit=24,
+            input_output_aliases={5 + m: m for m in range(len(grads))},
+        )
+    dq, dk, dv = grads
     outer_ins = [h1, dq, dk, dv, dlow, mixed]
     sum_shape = sds((8, width), F32)
     if ring:
-        leave = [jnp.where(even, far - k, k + 1 - far) for k in range(far)]
-        stay = [jnp.where(even, k + 1 - far, far - k) for k in range(far)]
-        half_shape = sds((far, groups, sub, 4 * local), BF)
-        keep, send, sums_qkv = call(
+        *halves_a, sums_qkv = call(
             outer_ring_body,
-            [half_shape, half_shape, sum_shape],
+            halves(4 * local) + [sum_shape],
             [info_of(leave + stay)] + outer_ins,
             [smem] + [None] * len(outer_ins),
             scratch=[pltpu.VMEM((groups, width, 4 * local), BF)],
             flops=4 * mm,
-            name="outer_a",
         )
-        s_a = scatter_ring(keep, send)
+        s_a = scatter_ring(halves_a)
     else:
         g_a, sums_qkv = call(
-            outer_plain_body,
-            [sds((parts, groups, sub, 4 * local), BF), sum_shape],
-            outer_ins,
-            flops=4 * mm,
-            name="outer_a",
+            outer_plain_body, [sds((parts, groups, sub, 4 * local), BF), sum_shape], outer_ins, flops=4 * mm
         )
         s_a = lax.psum_scatter(
             g_a.reshape(parts * groups, sub, 4 * local), axes, scatter_dimension=0, tiled=False
@@ -665,19 +711,17 @@
         [x, dq, dk, dv, wq, dmid, row(norm_gain)],
         scratch=[pltpu.VMEM((ROWS, width), F32)],
         flops=3 * mm,
-        name="input_back",
-    )
-    all_grad = spread(own_grad)
-
+    )
     sums = jnp.concatenate(
         [sums_in[:2].reshape(-1), sums_mid[:4].reshape(-1), sums_qkv[:2].reshape(-1), sum_hidden[0]]
     )
-    for bit in (1, 2):
-        sums = sums + mp_swap(sums, bit)
+    all_grad = spread(own_grad)
+    sums = sums + mp_swap(sums, 1)
     bit = 1
     while bit < parts:
         sums = sums + dp_swap(sums, bit)
         bit *= 2
+    sums = sums + mp_swap(sums, 2)
     vec = [sums[n * width : (n + 1) * width] for n in range(8)]
     own = lambda v, n: lax.dynamic_slice_in_dim(v, mine * n, n, 0)
     return (
@@ -703,7 +747,7 @@
     token = P(None, "dp", None, None)
     weight, turned = P("dp", "mp"), P("mp", "dp")
     return jax.shard_map(
-        on_device,
+        block_step,
         mesh=mesh,
         in_specs=(token, token, P(None, "dp"), P(), P(), weight, P("mp"), P("mp"), turned)
         + (P(), P(), P(), weight, P("mp"), turned, P()),

time: 407 us -> 439 us (1.079)
  waiting for transfers between devices: 118 us -> 136 us
  local copies, waits for them, and re-layouts: 32.4 us -> 49.1 us
  between operations: 15.2 us -> 1.46 us
  other arithmetic: 17.5 us -> 25.2 us
    ppermute x23 -> x37, waiting for transfers between devices: 53 us -> 70.5 us  [the longest x34 38.8 us: block_step(): lax.ppermute(a, 'mp', [(j, j ^ bit) for j in range(groups)])]
    unnamed x68 -> x88, local copies, waits for them, and re-layouts: 14.5 us -> 23.1 us
    select_n x2 -> x7, other arithmetic: 0.07 us -> 5.94 us  [the longest x2 2.53 us: scatter_ring(): total = jnp.where(even, last, total).reshape(2, 2, sub, -1)]
    ppermute x8 -> x16, starting transfers between devices: 25.8 us -> 27 us  [hop(): return lax.ppermute(a, axes, pairs)]
    ppermute x8 -> x16, waiting for transfers between devices: 64.6 us -> 65.4 us  [hop(): return lax.ppermute(a, axes, pairs)]
    ppermute x23 -> x37, starting transfers between devices: 17.1 us -> 17.6 us  [the longest x34 15.8 us: block_step(): lax.ppermute(a, 'mp', [(j, j ^ bit) for j in range(groups)])]
    pallas_call x14 -> x16, Pallas kernels: 175 us -> 175 us  [call(): pl.pallas_call(body, out_shape=tuple(outs), grid=(1,) if grid is None els...]
  transfers between devices with their start and end apart: 33 -> 53, of which waited for: 12 -> 18; matrix products, arithmetic and copies ran while one was open for 10% -> 14% of each run, Pallas kernels for 33% -> 30%
where the time goes in v4:
time: 439 us; the launch traced here: 432 us
  Pallas kernels  176 us (40%)
  waiting for transfers between devices  136 us (31%)
  local copies, waits for them, and re-layouts  49.1 us (11%)
  starting transfers between devices  44.6 us (10%)
  other arithmetic  25.2 us (6%)
    pallas_call x16, Pallas kernels, call(): pl.pallas_call(body, out_shape=tuple(outs), grid=(1,) if grid is None els...  175 us
    ppermute x16, waiting for transfers between devices, hop(): return lax.ppermute(a, axes, pairs)  65.4 us
    ppermute x34, waiting for transfers between devices, block_step(): lax.ppermute(a, 'mp', [(j, j ^ bit) for j in range(groups)])  38.8 us
    ppermute x3, waiting for transfers between devices, block_step(): lax.ppermute(a, 'dp', [(d, d ^ bit) for d in range(parts)])  31.6 us
    ppermute x16, starting transfers between devices, hop(): return lax.ppermute(a, axes, pairs)  27 us
    unnamed x88, local copies, waits for them, and re-layouts  23.1 us
    ppermute x34, starting transfers between devices, block_step(): lax.ppermute(a, 'mp', [(j, j ^ bit) for j in range(groups)])  15.8 us
  transfers between devices with their start and end apart: 53, of which 18 were waited for; matrix products, arithmetic and copies ran while one was open for 14% of the time, Pallas kernels for 30%

profile of v4, /device:TPU:0, one launch (start us, length us, event | category | flops | bytes accessed | tf_op | source)
XLA Modules:
  0.0 432.3 jit_solution(15991405210009885705)
XLA Ops:
  2.6 3.0 collective-permute-start
  13.3 3.7 copy.48.x_ref
  24.9 6.7 %collective-permute-done.6.refs_3_ = bf16[4,96,768]{2,1,0:T(8,128)(2,1)S(1)} collective-permute-done((bf16[4,96,768]{2,1,0:T(8,128)(2,1)}, bf16[4,96,768]{2,1,0:T(8,128)(2,1)S(1)}, u32[]{:S(2)}, u32[]{:S(2)}) %collective-permute-start.6) | collective-permute-done | bytes 589856 | tf_op jit(solution)/shard_map/ppermute | solution.py:426
  33.6 7.9 %collective-permute-done.8.refs_5_ = bf16[4,96,768]{2,1,0:T(8,128)(2,1)S(1)} collective-permute-done((bf16[4,96,768]{2,1,0:T(8,128)(2,1)S(1)}, bf16[4,96,768]{2,1,0:T(8,128)(2,1)S(1)}, u32[]{:S(2)}, u32[]{:S(2)}) %collective-permute-start.8) | collective-permute-done | bytes 589856 | tf_op jit(solution)/shard_map/ppermute | solution.py:426
  43.9 4.4 %collective-permute-done.10 = bf16[2,96,768]{2,1,0:T(8,128)(2,1)S(1)} collective-permute-done((bf16[2,96,768]{2,1,0:T(8,128)(2,1)S(1)}, bf16[2,96,768]{2,1,0:T(8,128)(2,1)S(1)}, u32[]{:S(2)}, u32[]{:S(2)}) %collective-permute-start.10) | collective-permute-done | bytes 294944 | tf_op jit(solution)/shard_map/ppermute | solution.py:426
  50.1 14.4 %collective-permute-done.14.refs_1_ = bf16[4,96,1536]{2,1,0:T(8,128)(2,1)S(1)} collective-permute-done((bf16[4,96,1536]{2,1,0:T(8,128)(2,1)S(1)}, bf16[4,96,1536]{2,1,0:T(8,128)(2,1)S(1)}, u32[]{:S(2)}, u32[]{:S(2)}) %collective-permute-start.14) | collective-permute-done | bytes 1179680 | tf_op jit(solution)/shard_map/ppermute | solution.py:426
  70.4 10.4 %collective-permute-done.16.refs_3_ = bf16[4,96,1536]{2,1,0:T(8,128)(2,1)} collective-permute-done((bf16[4,96,1536]{2,1,0:T(8,128)(2,1)S(1)}, bf16[4,96,1536]{2,1,0:T(8,128)(2,1)}, u32[]{:S(2)}, u32[]{:S(2)}) %collective-permute-start.16) | collective-permute-done | bytes 1179680 | tf_op jit(solution)/shard_map/ppermute | solution.py:426
  109.0 5.3 %collective-permute-done.20 = bf16[2,96,1536]{2,1,0:T(8,128)(2,1)} collective-permute-done((bf16[2,96,1536]{2,1,0:T(8,128)(2,1)}, bf16[2,96,1536]{2,1,0:T(8,128)(2,1)}, u32[]{:S(2)}, u32[]{:S(2)}) %collective-permute-start.20) | collective-permute-done | bytes 589856 | tf_op jit(solution)/shard_map/ppermute | solution.py:426
  116.2 15.2 %shard_map.289 = (bf16[1024,768]{1,0:T(8,128)(2,1)}, bf16[1024,2304]{1,0:T(8,128)(2,1)}, bf16[768,2304]{1,0:T(8,128)(2,1)}, bf16[768,768]{1,0:T(8,128)(2,1)}) custom-call(s32[10]{0:T(128)} %get-tuple-element.175.info_ref, bf16[1024,768]{1,0:T(8,128)(2,1)} %copy-done.11, f32[1,768]{1,0:T(1,128)} %reshape.418.gain_ref, f32[1,768]{1,0:T(1,128)} %reshape.419.shift_ref, ...), custom_call_target="tpu_custom_call" | custom-call | flops 3623878656 | bytes 17316904 | tf_op jit(solution)/shard_map/pallas_call | solution.py:55
  131.5 16.5 %shard_map.290 = (bf16[1024,768]{1,0:T(8,128)(2,1)}, bf16[12,5,200,200]{3,2,1,0:T(8,128)(2,1)}) custom-call(bf16[1024,2304]{1,0:T(8,128)(2,1)} %get-tuple-element.70.q_ref.k_ref.v_ref, bf16[1024,2304]{1,0:T(8,128)(2,1)} %get-tuple-element.70.q_ref.k_ref.v_ref, bf16[1024,2304]{1,0:T(8,128)(2,1)} %get-tuple-element.70.q_ref.k_ref.v_ref), custom_call_target="tpu_custom_call" | custom-call | flops 1207959552 | bytes 20528640 | tf_op jit(solution)/shard_map/pallas_call | solution.py:55
  148.0 7.2 %shard_map.291 = (f32[1024,768]{1,0:T(8,128)}, bf16[1024,768]{1,0:T(8,128)(2,1)}) custom-call(bf16[1024,768]{1,0:T(8,128)(2,1)} %copy-done.11, bf16[1024,768]{1,0:T(8,128)(2,1)} %get-tuple-element.71.o_ref, bf16[768,768]{1,0:T(8,128)(2,1)} %get-tuple-element.72.wo_ref, f32[1,768]{1,0:T(1,128)} %reshape.423.bias_ref, f32[1,768]{1,0:T(1,128)} %reshape.424.gain_ref, ...), custom_call_target="tpu_custom_call" | custom-call | flops 1207959552 | bytes 9053184 | tf_op jit(solution)/shard_map/pallas_call | solution.py:55
  158.8 16.0 %shard_map.292 = (bf16[1024,3072]{1,0:T(8,128)(2,1)}, bf16[1024,3072]{1,0:T(8,128)(2,1)}) custom-call(s32[10]{0:T(128)} %get-tuple-element.175.info_ref, bf16[1024,768]{1,0:T(8,128)(2,1)} %get-tuple-element.73.h_ref, f32[1,3072]{1,0:T(1,128)} %bitcast.162, bf16[4,96,1536]{2,1,0:T(8,128)(2,1)} %copy-done.13, bf16[4,96,1536]{2,1,0:T(8,128)(2,1)} %copy-done.15, ...), custom_call_target="tpu_custom_call" | custom-call | flops 4831838208 | bytes 23605288 | tf_op jit(solution)/shard_map/pallas_call | solution.py:55
  174.7 11.5 %shard_map.293 = (bf16[1024,3072]{1,0:T(8,128)(2,1)}, f32[8,3072]{1,0:T(8,128)}) custom-call(s32[10]{0:T(128)} %get-tuple-element.175.info_ref, bf16[1024,768]{1,0:T(8,128)(2,1)} %copy-done.9, bf16[1024,3072]{1,0:T(8,128)(2,1)} %get-tuple-element.77.slope_ref, bf16[4,96,1536]{2,1,0:T(8,128)(2,1)} %copy-done.13, bf16[4,96,1536]{2,1,0:T(8,128)(2,1)} %copy-done.15, ...), custom_call_target="tpu_custom_call" | custom-call | flops 4831838208 | bytes 23691304 | tf_op jit(solution)/shard_map/pallas_call | solution.py:55
  186.3 18.1 %shard_map.294 = (bf16[4,96,1536]{2,1,0:T(8,128)(2,1)}, bf16[4,96,1536]{2,1,0:T(8,128)(2,1)}, bf16[4,96,1536]{2,1,0:T(8,128)(2,1)}, bf16[4,96,1536]{2,1,0:T(8,12...) custom-call(s32[10]{0:T(128)} %get-tuple-element.176.info_ref, ...), custom_call_target="tpu_custom_call" | custom-call | flops 9663676416 | bytes 25165864 | tf_op jit(solution)/shard_map/pallas_call | solution.py:55
  205.1 11.7 %shard_map.295.a_ref = bf16[1000,768]{1,0:T(8,128)(2,1)} custom-call(s32[10]{0:T(128)} %get-tuple-element.175.info_ref, bf16[1024,3072]{1,0:T(8,128)(2,1)} %get-tuple-element.80.act_ref, f32[1024,768]{1,0:T(8,128)} %get-tuple-element.81.mid_ref, f32[1,768]{1,0:T(1,128)} %reshape.426.bias_ref, bf16[4,96,1536]{2,1,0:T(8,128)(2,1)} %copy-done.13, ...), custom_call_target="tpu_custom_call" | custom-call | flops 4831838208 | bytes 20413480 | tf_op jit(solution)/shard_map/pallas_call | solution.py:55
  219.2 16.6 %shard_map.297 = (f32[1024,768]{1,0:T(8,128)}, bf16[1024,768]{1,0:T(8,128)(2,1)}, f32[8,768]{1,0:T(8,128)}) custom-call(s32[10]{0:T(128)} %get-tuple-element.175.info_ref, bf16[1024,768]{1,0:T(8,128)(2,1)} %copy-done.9, bf16[1024,3072]{1,0:T(8,128)(2,1)} %get-tuple-element.83.du_ref, f32[1024,768]{1,0:T(8,128)} %get-tuple-element.81.mid_ref, ...), custom_call_target="tpu_custom_call" | custom-call | flops 4831838208 | bytes 25193512 | tf_op jit(solution)/shard_map/pallas_call | solution.py:55
  237.5 4.3 shard_map.298.do_ref
  248.3 6.9 %shard_map.299 = (bf16[1024,768]{1,0:T(8,128)(2,1)S(1)}, bf16[1024,768]{1,0:T(8,128)(2,1)S(1)}, bf16[1024,768]{1,0:T(8,128)(2,1)S(1)}) custom-call(bf16[1024,2304]{1,0:T(8,128)(2,1)S(1)} %copy-done.2, bf16[1024,2304]{1,0:T(8,128)(2,1)S(1)} %copy-done.2, bf16[1024,2304]{1,0:T(8,128)(2,1)S(1)} %copy-done.2, bf16[12,5,200,200]{3,2,1,0:T(8,128)(2,1)S(1)} %copy-done.3, ...), custom_call_target="tpu_custom_call" | custom-call | flops 805306368 | bytes 25247232 | tf_op jit(solution)/shard_map/pallas_call | solution.py:55
  255.2 6.9 %shard_map.300 = (bf16[1024,768]{1,0:T(8,128)(2,1)S(1)}, bf16[1024,768]{1,0:T(8,128)(2,1)S(1)}, bf16[1024,768]{1,0:T(8,128)(2,1)S(1)}) custom-call(bf16[1024,2304]{1,0:T(8,128)(2,1)S(1)} %copy-done.2, bf16[1024,2304]{1,0:T(8,128)(2,1)S(1)} %copy-done.2, bf16[1024,2304]{1,0:T(8,128)(2,1)S(1)} %copy-done.2, ...), custom_call_target="tpu_custom_call", output_to_operand_aliasing={{0}: (5, {}), {1}: (6, {}), {2}: (7, {})} | custom-call | flops 805306368 | bytes 29965824 | tf_op jit(solution)/shard_map/pallas_call | solution.py:55
  262.1 7.1 %shard_map.301 = (bf16[1024,768]{1,0:T(8,128)(2,1)S(1)}, bf16[1024,768]{1,0:T(8,128)(2,1)S(1)}, bf16[1024,768]{1,0:T(8,128)(2,1)S(1)}) custom-call(bf16[1024,2304]{1,0:T(8,128)(2,1)S(1)} %copy-done.2, bf16[1024,2304]{1,0:T(8,128)(2,1)S(1)} %copy-done.2, bf16[1024,2304]{1,0:T(8,128)(2,1)S(1)} %copy-done.2, ...), custom_call_target="tpu_custom_call", output_to_operand_aliasing={{0}: (5, {}), {1}: (6, {}), {2}: (7, {})} | custom-call | flops 805306368 | bytes 29965824 | tf_op jit(solution)/shard_map/pallas_call | solution.py:55
  272.7 11.2 %shard_map.302 = (bf16[1000,768]{1,0:T(8,128)(2,1)}, f32[8,768]{1,0:T(8,128)}) custom-call(bf16[1024,768]{1,0:T(8,128)(2,1)} %copy-done.11, bf16[1024,768]{1,0:T(8,128)(2,1)} %copy-done.5, bf16[1024,768]{1,0:T(8,128)(2,1)} %copy-done.6, bf16[1024,768]{1,0:T(8,128)(2,1)} %copy-done.7, bf16[768,2304]{1,0:T(8,128)(2,1)} %get-tuple-element.94.wq_ref, ...), custom_call_target="tpu_custom_call" | custom-call | flops 3623878656 | bytes 14539776 | tf_op jit(solution)/shard_map/pallas_call | solution.py:55
  284.6 11.1 %shard_map.304 = (bf16[4,96,768]{2,1,0:T(8,128)(2,1)}, bf16[4,96,768]{2,1,0:T(8,128)(2,1)}, bf16[4,96,768]{2,1,0:T(8,128)(2,1)}, bf16[4,96,768]{2,1,0:T(8,128)(2...) custom-call(s32[10]{0:T(128)} %get-tuple-element.176.info_ref, ...), custom_call_target="tpu_custom_call" | custom-call | flops 4831838208 | bytes 14180392 | tf_op jit(solution)/shard_map/pallas_call | solution.py:55
  304.9 18.2 %collective-permute-done.29 = f32[9216]{0:T(1024)S(1)} collective-permute-done((f32[9216]{0:T(1024)S(1)}, f32[9216]{0:T(1024)S(1)}, u32[]{:S(2)}, u32[]{:S(2)}) %collective-permute-start.29) | collective-permute-done | bytes 36896 | tf_op jit(solution)/shard_map/ppermute | solution.py:416
  324.1 3.6 collective-permute-done.30
  330.9 7.7 %collective-permute-done.38 = bf16[4,96,768]{2,1,0:T(8,128)(2,1)S(1)} collective-permute-done((bf16[4,96,768]{2,1,0:T(8,128)(2,1)S(1)}, bf16[4,96,768]{2,1,0:T(8,128)(2,1)S(1)}, u32[]{:S(2)}, u32[]{:S(2)}) %collective-permute-start.38) | collective-permute-done | bytes 589856 | tf_op jit(solution)/shard_map/ppermute | solution.py:426
  339.9 9.8 %collective-permute-done.31 = f32[9216]{0:T(1024)S(1)} collective-permute-done((f32[9216]{0:T(1024)S(1)}, f32[9216]{0:T(1024)S(1)}, u32[]{:S(2)}, u32[]{:S(2)}) %collective-permute-start.31) | collective-permute-done | bytes 36896 | tf_op jit(solution)/shard_map/ppermute | solution.py:416
  352.1 8.6 %collective-permute-done.39 = bf16[4,96,768]{2,1,0:T(8,128)(2,1)S(1)} collective-permute-done((bf16[4,96,768]{2,1,0:T(8,128)(2,1)S(1)}, bf16[4,96,768]{2,1,0:T(8,128)(2,1)S(1)}, u32[]{:S(2)}, u32[]{:S(2)}) %collective-permute-start.39) | collective-permute-done | bytes 589856 | tf_op jit(solution)/shard_map/ppermute | solution.py:426
  367.2 22.7 %collective-permute-done.32 = f32[9216]{0:T(1024)S(1)} collective-permute-done((f32[9216]{0:T(1024)S(1)}, f32[9216]{0:T(1024)S(1)}, u32[]{:S(2)}, u32[]{:S(2)}) %collective-permute-start.32) | collective-permute-done | bytes 36896 | tf_op jit(solution)/shard_map/ppermute | solution.py:415
  401.1 7.4 %shard_map.296 = bf16[5,197,4,768]{3,2,1,0:T(4,128)(2,1)} custom-call(s32[2]{0:T(128)S(1)} %pad_add_fusion.info_ref, bf16[1000,768]{1,0:T(8,128)(2,1)S(1)} %copy-done.8, bf16[1000,768]{1,0:T(8,128)(2,1)} %collective-permute-done.22.b_ref, bf16[1000,768]{1,0:T(8,128)(2,1)} %collective-permute-done.23.c_ref, bf16[1000,768]{1,0:T(8,128)(2,1)} %collective-permute-done.24.d_ref), custom_call_target="tpu_custom_call" | custom-call | flops 1207959552 | bytes 12195848 | tf_op jit(solution)/shard_map/pallas_call | solution.py:55
  410.5 7.4 %shard_map.303 = bf16[5,197,4,768]{3,2,1,0:T(4,128)(2,1)} custom-call(s32[2]{0:T(128)S(1)} %pad_add_fusion.info_ref, bf16[1000,768]{1,0:T(8,128)(2,1)S(1)} %copy-done.10, bf16[1000,768]{1,0:T(8,128)(2,1)} %collective-permute-done.25.b_ref, bf16[1000,768]{1,0:T(8,128)(2,1)} %collective-permute-done.26.c_ref, bf16[1000,768]{1,0:T(8,128)(2,1)} %collective-permute-done.27.d_ref), custom_call_target="tpu_custom_call" | custom-call | flops 1207959552 | bytes 12195848 | tf_op jit(solution)/shard_map/pallas_call | solution.py:55
  420.5 5.4 %collective-permute-done.42 = bf16[96,768]{0,1:T(8,128)(2,1)S(1)} collective-permute-done((bf16[96,768]{0,1:T(8,128)(2,1)S(1)}, bf16[96,768]{0,1:T(8,128)(2,1)S(1)}, u32[]{:S(2)}, u32[]{:S(2)}) %collective-permute-start.42) | collective-permute-done | bytes 147488 | tf_op jit(solution)/shard_map/ppermute | solution.py:415
  427.4 3.8 collective-permute-done.52
  (267 shorter events, 120.2 us)
Async XLA Ops:
  48.3 16.2 %collective-permute-start.14 = (bf16[4,96,1536]{2,1,0:T(8,128)(2,1)S(1)}, bf16[4,96,1536]{2,1,0:T(8,128)(2,1)S(1)}, u32[]{:S(2)}, u32[]{:S(2)}) collective-permute-start(bf16[4,96,1536]{2,1,0:T(8,128)(2,1)S(1)} %pad_maximum_fusion.refs_0_), channel_id=1, source_target_pairs={{0,8},{1,5},{2,10},{3,7},{8,16},{9,1},{10,18},{11,3},{16,24},{17,9... | collective-permute-start | bytes 3538952 | tf_op jit(solution)/shard_map/ppermute | solution.py:426
  64.5 16.3 %collective-permute-start.16 = (bf16[4,96,1536]{2,1,0:T(8,128)(2,1)S(1)}, bf16[4,96,1536]{2,1,0:T(8,128)(2,1)}, u32[]{:S(2)}, u32[]{:S(2)}) collective-permute-start(bf16[4,96,1536]{2,1,0:T(8,128)(2,1)S(1)} %collective-permute-done.14.refs_1_), channel_id=1, source_target_pairs={{0,8},{1,5},{2,10},{3,7},{8,16},{9,1},{10,18},{11,3},{16,24},{17,9... | collective-permute-start | bytes 3538952 | tf_op jit(solution)/shard_map/ppermute | solution.py:426
  67.7 20.1 %collective-permute-start.3 = (f32[1152]{0:T(1024)}, f32[1152]{0:T(1024)}, u32[]{:S(2)}, u32[]{:S(2)}) collective-permute-start(f32[1152]{0:T(1024)} %concatenate.50), channel_id=1, source_target_pairs={{0,1},{1,0},{2,3},{3,2},{4,5},{5,4},{6,7},{7,6},{8,9},{9,8},{10,11... | collective-permute-start | bytes 13832 | tf_op jit(solution)/shard_map/ppermute | solution.py:415
  80.8 21.8 %collective-permute-start.18 = (bf16[4,96,1536]{2,1,0:T(8,128)(2,1)}, bf16[4,96,1536]{2,1,0:T(8,128)(2,1)S(1)}, u32[]{:S(2)}, u32[]{:S(2)}) collective-permute-start(bf16[4,96,1536]{2,1,0:T(8,128)(2,1)} %collective-permute-done.16.refs_3_), channel_id=1, source_target_pairs={{0,8},{1,5},{2,10},{3,7},{8,16},{9,1},{10,18},{11,3},{16,24},{17,9... | collective-permute-start | bytes 3538952 | tf_op jit(solution)/shard_map/ppermute | solution.py:426
  101.6 14.1 %collective-permute-start.5 = (bf16[4,96,768]{2,1,0:T(8,128)(2,1)}, bf16[4,96,768]{2,1,0:T(8,128)(2,1)}, u32[]{:S(2)}, u32[]{:S(2)}) collective-permute-start(bf16[4,96,768]{2,1,0:T(8,128)(2,1)} %collective-permute-done.2.refs_1_), channel_id=1, source_target_pairs={{0,1},{1,0},{2,3},{3,2},{4,5},{5,4},{6,7},{7,6},{8,9},{9,8},{10,11... | collective-permute-start | bytes 1769480 | tf_op jit(solution)/shard_map/ppermute | solution.py:415
  101.6 14.1 %collective-permute-start.7 = (bf16[4,96,768]{2,1,0:T(8,128)(2,1)}, bf16[4,96,768]{2,1,0:T(8,128)(2,1)}, u32[]{:S(2)}, u32[]{:S(2)}) collective-permute-start(bf16[4,96,768]{2,1,0:T(8,128)(2,1)} %copy-done.35), channel_id=1, source_target_pairs={{0,1},{1,0},{2,3},{3,2},{4,5},{5,4},{6,7},{7,6},{8,9},{9,8},{10,11... | collective-permute-start | bytes 1769480 | tf_op jit(solution)/shard_map/ppermute | solution.py:415
  102.1 14.1 %collective-permute-start.9 = (bf16[4,96,768]{2,1,0:T(8,128)(2,1)}, bf16[4,96,768]{2,1,0:T(8,128)(2,1)}, u32[]{:S(2)}, u32[]{:S(2)}) collective-permute-start(bf16[4,96,768]{2,1,0:T(8,128)(2,1)} %copy-done.26), channel_id=1, source_target_pairs={{0,1},{1,0},{2,3},{3,2},{4,5},{5,4},{6,7},{7,6},{8,9},{9,8},{10,11... | collective-permute-start | bytes 1769480 | tf_op jit(solution)/shard_map/ppermute | solution.py:415
  114.3 40.9 %collective-permute-start.21 = (bf16[2,96,1536]{2,1,0:T(8,128)(2,1)}, bf16[2,96,1536]{2,1,0:T(8,128)(2,1)}, u32[]{:S(2)}, u32[]{:S(2)}) collective-permute-start(bf16[2,96,1536]{2,1,0:T(8,128)(2,1)} %collective-permute-done.20), channel_id=1, source_target_pairs={{0,1},{1,0},{2,3},{3,2},{4,5},{5,4},{6,7},{7,6},{8,9},{9,8},{10,11... | collective-permute-start | bytes 1769480 | tf_op jit(solution)/shard_map/ppermute | solution.py:415
  115.2 42.5 %collective-permute-start.15 = (bf16[4,96,1536]{2,1,0:T(8,128)(2,1)S(1)}, bf16[4,96,1536]{2,1,0:T(8,128)(2,1)S(1)}, u32[]{:S(2)}, u32[]{:S(2)}) collective-permute-start(bf16[4,96,1536]{2,1,0:T(8,128)(2,1)S(1)} %collective-permute-done.14.refs_1_), channel_id=1, source_target_pairs={{0,1},{1,0},{2,3},{3,2},{4,5},{5,4},{6,7},{7,6},{8,9},{9,8},{10,11... | collective-permute-start | bytes 3538952 | tf_op jit(solution)/shard_map/ppermute | solution.py:415
  115.7 42.0 %collective-permute-start.17 = (bf16[4,96,1536]{2,1,0:T(8,128)(2,1)}, bf16[4,96,1536]{2,1,0:T(8,128)(2,1)}, u32[]{:S(2)}, u32[]{:S(2)}) collective-permute-start(bf16[4,96,1536]{2,1,0:T(8,128)(2,1)} %collective-permute-done.16.refs_3_), channel_id=1, source_target_pairs={{0,1},{1,0},{2,3},{3,2},{4,5},{5,4},{6,7},{7,6},{8,9},{9,8},{10,11... | collective-permute-start | bytes 3538952 | tf_op jit(solution)/shard_map/ppermute | solution.py:415
  115.8 41.9 %collective-permute-start.19 = (bf16[4,96,1536]{2,1,0:T(8,128)(2,1)S(1)}, bf16[4,96,1536]{2,1,0:T(8,128)(2,1)}, u32[]{:S(2)}, u32[]{:S(2)}) collective-permute-start(bf16[4,96,1536]{2,1,0:T(8,128)(2,1)S(1)} %collective-permute-done.18.refs_5_), channel_id=1, source_target_pairs={{0,1},{1,0},{2,3},{3,2},{4,5},{5,4},{6,7},{7,6},{8,9},{9,8},{10,11... | collective-permute-start | bytes 3538952 | tf_op jit(solution)/shard_map/ppermute | solution.py:415
  204.4 12.9 %collective-permute-start.46 = (bf16[4,96,1536]{2,1,0:T(8,128)(2,1)}, bf16[4,96,1536]{2,1,0:T(8,128)(2,1)S(1)}, u32[]{:S(2)}, u32[]{:S(2)}) collective-permute-start(bf16[4,96,1536]{2,1,0:T(8,128)(2,1)} %get-tuple-element.116), channel_id=1, source_target_pairs={{0,1},{1,0},{2,3},{3,2},{4,5},{5,4},{6,7},{7,6},{8,9},{9,8},{10,11... | collective-permute-start | bytes 3538952 | tf_op jit(solution)/shard_map/ppermute | solution.py:415
  216.8 80.3 %collective-permute-start.45 = (bf16[4,96,1536]{2,1,0:T(8,128)(2,1)}, bf16[4,96,1536]{2,1,0:T(8,128)(2,1)}, u32[]{:S(2)}, u32[]{:S(2)}) collective-permute-start(bf16[4,96,1536]{2,1,0:T(8,128)(2,1)} %get-tuple-element.115), channel_id=1, source_target_pairs={{0,1},{1,0},{2,3},{3,2},{4,5},{5,4},{6,7},{7,6},{8,9},{9,8},{10,11... | collective-permute-start | bytes 3538952 | tf_op jit(solution)/shard_map/ppermute | solution.py:415
  217.6 79.5 %collective-permute-start.47 = (bf16[4,96,1536]{2,1,0:T(8,128)(2,1)S(1)}, bf16[4,96,1536]{2,1,0:T(8,128)(2,1)}, u32[]{:S(2)}, u32[]{:S(2)}) collective-permute-start(bf16[4,96,1536]{2,1,0:T(8,128)(2,1)S(1)} %add_convert_fusion.3), channel_id=1, source_target_pairs={{0,8},{1,5},{2,10},{3,7},{8,16},{9,1},{10,18},{11,3},{16,24},{17,9... | collective-permute-start | bytes 3538952 | tf_op jit(solution)/shard_map/ppermute | solution.py:426
  237.4 90.3 %collective-permute-start.44 = (bf16[4,96,1536]{2,1,0:T(8,128)(2,1)}, bf16[4,96,1536]{2,1,0:T(8,128)(2,1)S(1)}, u32[]{:S(2)}, u32[]{:S(2)}) collective-permute-start(bf16[4,96,1536]{2,1,0:T(8,128)(2,1)} %get-tuple-element.113), channel_id=1, source_target_pairs={{0,1},{1,0},{2,3},{3,2},{4,5},{5,4},{6,7},{7,6},{8,9},{9,8},{10,11... | collective-permute-start | bytes 3538952 | tf_op jit(solution)/shard_map/ppermute | solution.py:415
  296.5 27.2 %collective-permute-start.35 = (bf16[4,96,768]{2,1,0:T(8,128)(2,1)}, bf16[4,96,768]{2,1,0:T(8,128)(2,1)S(1)}, u32[]{:S(2)}, u32[]{:S(2)}) collective-permute-start(bf16[4,96,768]{2,1,0:T(8,128)(2,1)} %get-tuple-element.107), channel_id=1, source_target_pairs={{0,1},{1,0},{2,3},{3,2},{4,5},{5,4},{6,7},{7,6},{8,9},{9,8},{10,11... | collective-permute-start | bytes 1769480 | tf_op jit(solution)/shard_map/ppermute | solution.py:415
  299.7 28.6 %collective-permute-start.48 = (bf16[4,96,1536]{2,1,0:T(8,128)(2,1)S(1)}, bf16[4,96,1536]{2,1,0:T(8,128)(2,1)S(1)}, u32[]{:S(2)}, u32[]{:S(2)}) collective-permute-start(bf16[4,96,1536]{2,1,0:T(8,128)(2,1)S(1)} %add_convert_fusion.2), channel_id=1, source_target_pairs={{0,8},{1,5},{2,10},{3,7},{8,16},{9,1},{10,18},{11,3},{16,24},{17,9... | collective-permute-start | bytes 3538952 | tf_op jit(solution)/shard_map/ppermute | solution.py:426
  301.5 22.2 %collective-permute-start.37 = (bf16[4,96,768]{2,1,0:T(8,128)(2,1)S(1)}, bf16[4,96,768]{2,1,0:T(8,128)(2,1)S(1)}, u32[]{:S(2)}, u32[]{:S(2)}) collective-permute-start(bf16[4,96,768]{2,1,0:T(8,128)(2,1)S(1)} %add_convert_fusion.7), channel_id=1, source_target_pairs={{0,8},{1,5},{2,10},{3,7},{8,16},{9,1},{10,18},{11,3},{16,24},{17,9... | collective-permute-start | bytes 1769480 | tf_op jit(solution)/shard_map/ppermute | solution.py:426
  304.3 18.8 %collective-permute-start.29 = (f32[9216]{0:T(1024)S(1)}, f32[9216]{0:T(1024)S(1)}, u32[]{:S(2)}, u32[]{:S(2)}) collective-permute-start(f32[9216]{0:T(1024)S(1)} %fusion.11), channel_id=1, source_target_pairs={{0,4},{4,0},{8,12},{12,8},{16,20},{20,16},{24,28},{28,24},{1,5},{5... | collective-permute-start | bytes 110600 | tf_op jit(solution)/shard_map/ppermute | solution.py:416
  323.1 40.2 %collective-permute-start.23 = (bf16[1000,768]{1,0:T(8,128)(2,1)S(1)}, bf16[1000,768]{1,0:T(8,128)(2,1)}, u32[]{:S(2)}, u32[]{:S(2)}) collective-permute-start(bf16[1000,768]{1,0:T(8,128)(2,1)S(1)} %copy-done.8), channel_id=1, source_target_pairs={{0,2},{1,3},{2,0},{3,1},{4,6},{5,7},{6,4},{7,5},{8,10},{9,11},{10,... | collective-permute-start | bytes 4608008 | tf_op jit(solution)/shard_map/ppermute | solution.py:415
  323.6 38.1 %collective-permute-start.43 = (bf16[4,96,1536]{2,1,0:T(8,128)(2,1)S(1)}, bf16[4,96,1536]{2,1,0:T(8,128)(2,1)S(1)}, u32[]{:S(2)}, u32[]{:S(2)}) collective-permute-start(bf16[4,96,1536]{2,1,0:T(8,128)(2,1)S(1)} %copy-done.34), channel_id=1, source_target_pairs={{0,1},{1,0},{2,3},{3,2},{4,5},{5,4},{6,7},{7,6},{8,9},{9,8},{10,11... | collective-permute-start | bytes 3538952 | tf_op jit(solution)/shard_map/ppermute | solution.py:415
  327.7 24.2 %collective-permute-start.33 = (bf16[4,96,768]{2,1,0:T(8,128)(2,1)S(1)}, bf16[4,96,768]{2,1,0:T(8,128)(2,1)S(1)}, u32[]{:S(2)}, u32[]{:S(2)}) collective-permute-start(bf16[4,96,768]{2,1,0:T(8,128)(2,1)S(1)} %copy-done.36), channel_id=1, source_target_pairs={{0,1},{1,0},{2,3},{3,2},{4,5},{5,4},{6,7},{7,6},{8,9},{9,8},{10,11... | collective-permute-start | bytes 1769480 | tf_op jit(solution)/shard_map/ppermute | solution.py:415
  330.6 32.9 %collective-permute-start.49 = (bf16[4,96,1536]{2,1,0:T(8,128)(2,1)S(1)}, bf16[4,96,1536]{2,1,0:T(8,128)(2,1)S(1)}, u32[]{:S(2)}, u32[]{:S(2)}) collective-permute-start(bf16[4,96,1536]{2,1,0:T(8,128)(2,1)S(1)} %add_convert_fusion.1), channel_id=1, source_target_pairs={{0,8},{1,5},{2,10},{3,7},{8,16},{9,1},{10,18},{11,3},{16,24},{17,9... | collective-permute-start | bytes 3538952 | tf_op jit(solution)/shard_map/ppermute | solution.py:426
  352.0 42.4 %collective-permute-start.26 = (bf16[1000,768]{1,0:T(8,128)(2,1)S(1)}, bf16[1000,768]{1,0:T(8,128)(2,1)}, u32[]{:S(2)}, u32[]{:S(2)}) collective-permute-start(bf16[1000,768]{1,0:T(8,128)(2,1)S(1)} %copy-done.10), channel_id=1, source_target_pairs={{0,2},{1,3},{2,0},{3,1},{4,6},{5,7},{6,4},{7,5},{8,10},{9,11},{10,... | collective-permute-start | bytes 4608008 | tf_op jit(solution)/shard_map/ppermute | solution.py:415
  360.7 40.3 %collective-permute-start.22 = (bf16[1000,768]{1,0:T(8,128)(2,1)S(1)}, bf16[1000,768]{1,0:T(8,128)(2,1)}, u32[]{:S(2)}, u32[]{:S(2)}) collective-permute-start(bf16[1000,768]{1,0:T(8,128)(2,1)S(1)} %copy-done.8), channel_id=1, source_target_pairs={{0,1},{1,0},{2,3},{3,2},{4,5},{5,4},{6,7},{7,6},{8,9},{9,8},{10,11... | collective-permute-start | bytes 4608008 | tf_op jit(solution)/shard_map/ppermute | solution.py:415
  361.7 28.1 %collective-permute-start.32 = (f32[9216]{0:T(1024)S(1)}, f32[9216]{0:T(1024)S(1)}, u32[]{:S(2)}, u32[]{:S(2)}) collective-permute-start(f32[9216]{0:T(1024)S(1)} %add.184), channel_id=1, source_target_pairs={{0,2},{1,3},{2,0},{3,1},{4,6},{5,7},{6,4},{7,5},{8,10},{9,11},{10,... | collective-permute-start | bytes 110600 | tf_op jit(solution)/shard_map/ppermute | solution.py:415
  363.2 37.8 %collective-permute-start.24 = (bf16[1000,768]{1,0:T(8,128)(2,1)}, bf16[1000,768]{1,0:T(8,128)(2,1)}, u32[]{:S(2)}, u32[]{:S(2)}) collective-permute-start(bf16[1000,768]{1,0:T(8,128)(2,1)} %collective-permute-done.23.c_ref), channel_id=1, source_target_pairs={{0,1},{1,0},{2,3},{3,2},{4,5},{5,4},{6,7},{7,6},{8,9},{9,8},{10,11... | collective-permute-start | bytes 4608008 | tf_op jit(solution)/shard_map/ppermute | solution.py:415
  363.5 30.9 %collective-permute-start.40 = (bf16[4,96,768]{2,1,0:T(8,128)(2,1)}, bf16[4,96,768]{2,1,0:T(8,128)(2,1)}, u32[]{:S(2)}, u32[]{:S(2)}) collective-permute-start(bf16[4,96,768]{2,1,0:T(8,128)(2,1)} %add_convert_fusion.4), channel_id=1, source_target_pairs={{0,8},{2,10},{8,16},{10,18},{16,24},{18,26},{24,28},{26,30},{28,20... | collective-permute-start | bytes 1769480 | tf_op jit(solution)/shard_map/ppermute | solution.py:426
  389.8 18.6 %collective-permute-start.50 = (bf16[4,96,1536]{2,1,0:T(8,128)(2,1)}, bf16[4,96,1536]{2,1,0:T(8,128)(2,1)}, u32[]{:S(2)}, u32[]{:S(2)}) collective-permute-start(bf16[4,96,1536]{2,1,0:T(8,128)(2,1)} %add_convert_fusion), channel_id=1, source_target_pairs={{0,8},{2,10},{8,16},{10,18},{16,24},{18,26},{24,28},{26,30},{28,20... | collective-permute-start | bytes 3538952 | tf_op jit(solution)/shard_map/ppermute | solution.py:426
  394.3 16.1 %collective-permute-start.25 = (bf16[1000,768]{1,0:T(8,128)(2,1)S(1)}, bf16[1000,768]{1,0:T(8,128)(2,1)}, u32[]{:S(2)}, u32[]{:S(2)}) collective-permute-start(bf16[1000,768]{1,0:T(8,128)(2,1)S(1)} %copy-done.10), channel_id=1, source_target_pairs={{0,1},{1,0},{2,3},{3,2},{4,5},{5,4},{6,7},{7,6},{8,9},{9,8},{10,11... | collective-permute-start | bytes 4608008 | tf_op jit(solution)/shard_map/ppermute | solution.py:415
  394.3 16.1 %collective-permute-start.27 = (bf16[1000,768]{1,0:T(8,128)(2,1)}, bf16[1000,768]{1,0:T(8,128)(2,1)}, u32[]{:S(2)}, u32[]{:S(2)}) collective-permute-start(bf16[1000,768]{1,0:T(8,128)(2,1)} %collective-permute-done.26.c_ref), channel_id=1, source_target_pairs={{0,1},{1,0},{2,3},{3,2},{4,5},{5,4},{6,7},{7,6},{8,9},{9,8},{10,11... | collective-permute-start | bytes 4608008 | tf_op jit(solution)/shard_map/ppermute | solution.py:415
  401.0 16.9 %collective-permute-start.41 = (bf16[2,96,768]{1,2,0:T(8,128)(2,1)S(1)}, bf16[2,96,768]{1,2,0:T(8,128)(2,1)S(1)}, u32[]{:S(2)}, u32[]{:S(2)}) collective-permute-start(bf16[2,96,768]{1,2,0:T(8,128)(2,1)S(1)} %select_bitcast_fusion.1), channel_id=1, source_target_pairs={{0,1},{1,0},{2,3},{3,2},{4,5},{5,4},{6,7},{7,6},{8,9},{9,8},{10,11... | collective-permute-start | bytes 884744 | tf_op jit(solution)/shard_map/ppermute | solution.py:415
  (61 other events, 675.3 us)

commit v5 on v4

--- a/solution.py
+++ b/solution.py
@@ -11,7 +11,6 @@
 NORM_EPS = 1e-06
 SLOT_ROWS = 200
 ROWS = 1024
-UNROLL = 5
 BF = jnp.bfloat16
 F32 = jnp.float32
 NT = (((1,), (1,)), ((), ()))
@@ -77,92 +76,90 @@
     return pl.ds(pl.multiple_of(i * size, size), size)
 
 
-def prep_body(slots, length, info_ref, x_ref, cot_ref, xo_ref, dy_ref):
-    xo_ref[...] = jnp.zeros_like(xo_ref)
-    dy_ref[...] = jnp.zeros_like(dy_ref)
+def prep_body(info_ref, in_ref, out_ref):
+    out_ref[...] = jnp.zeros_like(out_ref)
+    _, slots, length, _ = in_ref.shape
     for i in range(slots):
-        rows = slice(i * SLOT_ROWS, i * SLOT_ROWS + length)
-        xo_ref[rows, :] = x_ref[0, i]
 
         @pl.when(i < info_ref[1])
         def _():
-            dy_ref[rows, :] = cot_ref[0, i]
-
-
-def place(info_ref, refs, buf_ref, group=0):
+            out_ref[i * SLOT_ROWS : i * SLOT_ROWS + length, :] = in_ref[0, i]
+
+
+def place(info_ref, refs, dst_ref, group=0, cols=slice(None), into=slice(None)):
+    if len(refs) == 1:
+        parts, _, sub, _ = refs[0].shape
+        dst_ref[:, into] = refs[0][:, group, :, cols].reshape(parts * sub, -1)
+        return
     for n, ref in enumerate(refs):
         sub = ref.shape[1]
         rows = pl.ds(pl.multiple_of(info_ref[2 + n] * sub, sub), sub)
-        buf_ref[rows, :] = ref[group]
-
-
-def weights(info_ref, refs, buf_ref):
-    if len(refs) == 1:
-        parts, groups, sub, cols = refs[0].shape
-        return [refs[0][:, j].reshape(parts * sub, cols) for j in range(groups)]
-    groups = refs[0].shape[0]
-    for j in range(groups):
-        place(info_ref, refs, buf_ref.at[j], j)
-    return [buf_ref[j] for j in range(groups)]
-
-
-def qkv_ring_body(info_ref, x_ref, gain_ref, shift_ref, bias_ref, *refs):
-    h_ref, qkv_ref, wq_ref, wo_ref, buf_ref = refs[-5:]
-    groups = buf_ref.shape[0]
-    for j in range(groups):
-        place(info_ref, refs[:-5], buf_ref.at[j], j)
-    qkv_rest(lambda j: buf_ref[j], groups, x_ref, gain_ref, shift_ref, bias_ref, h_ref, qkv_ref, wq_ref, wo_ref)
-
-
-def qkv_gathered_body(x_ref, gain_ref, shift_ref, bias_ref, wa_ref, h_ref, qkv_ref, wq_ref, wo_ref):
-    parts, groups, sub, cols = wa_ref.shape
-    qkv_rest(lambda j: wa_ref[:, j].reshape(parts * sub, cols), groups, x_ref, gain_ref, shift_ref, bias_ref, h_ref, qkv_ref, wq_ref, wo_ref)
-
-
-def qkv_rest(piece, groups, x_ref, gain_ref, shift_ref, bias_ref, h_ref, qkv_ref, wq_ref, wo_ref):
+        dst_ref[rows, into] = ref[group, :, cols]
+
+
+def qkv_body(info_ref, x_ref, gain_ref, shift_ref, bias_ref, *refs):
+    h_ref, qkv_ref, wq_ref, wo_ref = refs[-4:]
+    chunks = refs[:-4]
     width = x_ref.shape[1]
+    groups = chunks[0].shape[0 if len(chunks) > 1 else 1]
     local = width // groups
-    for j in range(groups):
-        w = piece(j)
-        for s in range(3):
-            wq_ref[:, s * width + j * local : s * width + (j + 1) * local] = w[:, s * local : (s + 1) * local]
-        wo_ref[:, j * local : (j + 1) * local] = w[:, 3 * local :]
-
-    def norm(i):
-        rows = cut(i, 128)
-        normal, _ = norm_stats(x_ref[rows, :].astype(F32))
-        h_ref[rows, :] = (normal * gain_ref[...] + shift_ref[...]).astype(BF)
-
-    loop(ROWS // 128, norm)
-
-    def project(n):
-        cols = cut(n, 256)
-        qkv_ref[:, cols] = (dot(h_ref[...], wq_ref[:, cols]) + bias_ref[:, cols]).astype(BF)
-
-    loop(3 * width // 256, project)
-
-
-def attend_body(slots, length, q_ref, k_ref, v_ref, o_ref, p_ref):
+
+    def columns(s, dst_ref):
+        for j in range(groups):
+            place(info_ref, chunks, dst_ref, j, slice(s * local, (s + 1) * local), slice(j * local, (j + 1) * local))
+
+    step = pl.program_id(0)
+
+    @pl.when(step == 0)
+    def _():
+        def norm(i):
+            rows = cut(i, 128)
+            normal, _ = norm_stats(x_ref[rows, :].astype(F32))
+            h_ref[rows, :] = (normal * gain_ref[...] + shift_ref[...]).astype(BF)
+
+        loop(ROWS // 128, norm, 2)
+        columns(3, wo_ref)
+
+    for s in range(3):
+        pl.when(step == s)(functools.partial(columns, s, wq_ref))
+    qkv_ref[...] = (dot(h_ref[...], wq_ref[...]) + bias_ref[...]).astype(BF)
+
+
+def half_masks():
     low_half = lax.broadcasted_iota(jnp.int32, (SLOT_ROWS, 2 * HEAD_DIM), 1) < HEAD_DIM
-    valid = lax.broadcasted_iota(jnp.int32, (SLOT_ROWS, SLOT_ROWS), 0) < length
-
-    def image(i):
-        rows = cut(i, SLOT_ROWS)
-        q = q_ref[rows, :] * jnp.bfloat16(0.125)
-        k = k_ref[rows, :]
-        v_t = v_ref[rows, :].T
-        zero = jnp.zeros_like(k)
-        mixed = []
+    return low_half, ~low_half
+
+
+def attend_body(slots, length, q_ref, k_ref, v_ref, o_ref, p_ref, s_ref):
+    masks = half_masks()
+    tile = length // 8 * 8
+    valid = lax.broadcasted_iota(jnp.int32, (SLOT_ROWS - tile, SLOT_ROWS), 0) < length - tile
+    rows = [slice(i * SLOT_ROWS, (i + 1) * SLOT_ROWS) for i in range(slots)]
+
+    def scores(i):
+        q = q_ref[rows[i], :] * jnp.bfloat16(0.125)
+        k = k_ref[rows[i], :]
         for h in range(2):
-            s = dot(jnp.where(low_half if h == 0 else ~low_half, k, zero), q, NT)
-            s = jnp.where(valid, s, -1e30)
+            s_ref[h, i] = dot(jnp.where(masks[h], k, jnp.zeros_like(k)), q, NT)
+
+    def softmax(i):
+        for h in range(2):
+            s_ref[h, i, tile:] = jnp.where(valid, s_ref[h, i, tile:], -1e30)
+            s = s_ref[h, i]
             e = jnp.exp(s - jnp.max(s, axis=0, keepdims=True))
-            p = (e * (1.0 / jnp.sum(e, axis=0, keepdims=True))).astype(BF)
-            p_ref[h, i] = p
-            mixed.append(dot(v_t[h * HEAD_DIM : (h + 1) * HEAD_DIM], p))
-        o_ref[rows, :] = jnp.concatenate(mixed, axis=0).T.astype(BF)
-
-    loop(slots, image, UNROLL)
+            p_ref[h, i] = (e * (1.0 / jnp.sum(e, axis=0, keepdims=True))).astype(BF)
+
+    def mix(i):
+        v_t = v_ref[rows[i], :].T
+        mixed = [dot(v_t[h * HEAD_DIM : (h + 1) * HEAD_DIM], p_ref[h, i]) for h in range(2)]
+        o_ref[rows[i], :] = jnp.concatenate(mixed, axis=0).T.astype(BF)
+
+    for i in range(slots):
+        scores(i)
+    for i in range(slots):
+        softmax(i)
+    for i in range(slots):
+        mix(i)
     tail = slots * SLOT_ROWS
     o_ref[tail:, :] = jnp.zeros((ROWS - tail, 2 * HEAD_DIM), BF)
 
@@ -182,7 +179,8 @@
 
 def hidden_body(info_ref, h_ref, bias_ref, *refs):
     act_ref, slope_ref, buf_ref = refs[-3:]
-    (w,) = weights(info_ref, refs[:-3], buf_ref)
+    place(info_ref, refs[:-3], buf_ref)
+    w = buf_ref[...]
 
     def chunk(i):
         rows = cut(i, 256)
@@ -191,26 +189,26 @@
         act_ref[rows, :] = (u * half).astype(BF)
         slope_ref[rows, :] = (half + u * jnp.exp(-0.5 * u * u) * 0.3989422804014327).astype(BF)
 
-    loop(ROWS // 256, chunk)
-
-
-def wide_dot(left_ref, ws, acc_ref):
-    for j, w in enumerate(ws):
-        cols = w.shape[1]
-        part = dot(left_ref[:, j * cols : (j + 1) * cols], w, NT)
-        if j == 0:
-            acc_ref[...] = part
-        else:
-            acc_ref[...] += part
-
-
-def down_body(slots, info_ref, act_ref, mid_ref, bias_ref, *refs):
-    out_ref, acc_ref, buf_ref = refs[-3:]
-    wide_dot(act_ref, weights(info_ref, refs[:-3], buf_ref), acc_ref)
-    for i in range(slots):
-        rows = slice(i * SLOT_ROWS, (i + 1) * SLOT_ROWS)
-        live = jnp.where(i < info_ref[1], 1.0, 0.0)
-        out_ref[rows, :] = ((mid_ref[rows, :] + acc_ref[rows, :] + bias_ref[...]) * live).astype(BF)
+    loop(ROWS // 256, chunk, 4)
+
+
+def wide_dot(info_ref, left_ref, refs, buf_ref):
+    groups, _, cols = buf_ref.shape
+
+    @pl.when(pl.program_id(0) == 0)
+    def _():
+        for j in range(groups):
+            place(info_ref, refs, buf_ref.at[j], j)
+
+    return sum(dot(left_ref[:, j * cols : (j + 1) * cols], buf_ref[j], NT) for j in range(groups))
+
+
+def down_body(info_ref, act_ref, mid_ref, bias_ref, *refs):
+    out_ref, buf_ref = refs[-2:]
+    value = mid_ref[...] + wide_dot(info_ref, act_ref, refs[:-2], buf_ref) + bias_ref[...]
+    rows = out_ref.shape[0]
+    row = pl.program_id(0) * rows + lax.broadcasted_iota(jnp.int32, (rows, 1), 0)
+    out_ref[...] = jnp.where(row < info_ref[1] * SLOT_ROWS, value, 0.0).astype(BF)
 
 
 def weave_body(length, info_ref, a_ref, b_ref, c_ref, d_ref, o_ref):
@@ -267,7 +265,8 @@
 
 def dact_body(info_ref, dy_ref, slope_ref, *refs):
     du_ref, sum_ref, buf_ref = refs[-3:]
-    (w,) = weights(info_ref, refs[:-3], buf_ref)
+    place(info_ref, refs[:-3], buf_ref)
+    w = buf_ref[...]
     cols = w.shape[1]
     total = jnp.zeros((1, cols), F32)
     for i in range(ROWS // 256):
@@ -278,26 +277,24 @@
     sum_ref[...] = jnp.broadcast_to(total, sum_ref.shape)
 
 
+def add_rows(sums_ref, rows):
+    @pl.when(pl.program_id(0) == 0)
+    def _():
+        sums_ref[...] = jnp.zeros_like(sums_ref)
+
+    for n, value in enumerate(rows):
+        sums_ref[n : n + 1, :] += colsum(value)
+
+
 def mid_back_body(info_ref, dy_ref, du_ref, mid_ref, gain_ref, *refs):
-    dmid_ref, dlow_ref, sums_ref, acc_ref, buf_ref = refs[-5:]
-    wide_dot(du_ref, weights(info_ref, refs[:-5], buf_ref), acc_ref)
-    width = dy_ref.shape[1]
-
-    def chunk(i, sums):
-        rows = cut(i, 128)
-        dh = acc_ref[rows, :]
-        normal, scale_inv = norm_stats(mid_ref[rows, :])
-        dy = dy_ref[rows, :].astype(F32)
-        dmid = dy + norm_back(dh, normal, scale_inv, gain_ref[...])
-        dmid_ref[rows, :] = dmid
-        dlow_ref[rows, :] = dmid.astype(BF)
-        new = (colsum(dh * normal), colsum(dh), colsum(dmid), colsum(dy))
-        return tuple(a + b for a, b in zip(sums, new))
-
-    zero = jnp.zeros((1, width), F32)
-    sums = lax.fori_loop(0, ROWS // 128, chunk, (zero,) * 4)
-    for n in range(4):
-        sums_ref[n : n + 1, :] = sums[n]
+    dmid_ref, dlow_ref, sums_ref, buf_ref = refs[-4:]
+    dh = wide_dot(info_ref, du_ref, refs[:-4], buf_ref)
+    normal, scale_inv = norm_stats(mid_ref[...])
+    dy = dy_ref[...].astype(F32)
+    dmid = dy + norm_back(dh, normal, scale_inv, gain_ref[...])
+    dmid_ref[...] = dmid
+    dlow_ref[...] = dmid.astype(BF)
+    add_rows(sums_ref, (dh * normal, dh, dmid, dy))
 
 
 def out_back_body(dlow_ref, wo_ref, do_ref):
@@ -305,29 +302,38 @@
 
 
 def attend_back_body(slots, q_ref, k_ref, v_ref, p_ref, do_ref, *refs):
-    dq_ref, dk_ref, dv_ref = refs[-3:]
-    low_half = lax.broadcasted_iota(jnp.int32, (SLOT_ROWS, 2 * HEAD_DIM), 1) < HEAD_DIM
-
-    def image(i):
-        rows = cut(i, SLOT_ROWS)
-        q = q_ref[rows, :] * jnp.bfloat16(0.125)
-        k_t = (k_ref[rows, :] * jnp.bfloat16(0.125)).T
-        v = v_ref[rows, :]
-        do = do_ref[rows, :]
-        zero = jnp.zeros_like(v)
-        grads = []
+    dq_ref, dk_ref, dv_ref, dp_ref, ds_ref = refs[-5:]
+    masks = half_masks()
+    rows = [slice(i * SLOT_ROWS, (i + 1) * SLOT_ROWS) for i in range(slots)]
+
+    def upstream(i):
+        v = v_ref[rows[i], :]
+        do = do_ref[rows[i], :]
         for h in range(2):
-            p = p_ref[h, i]
-            pf = p.astype(F32)
-            dp = dot(jnp.where(low_half if h == 0 else ~low_half, v, zero), do, NT)
-            ds = (pf * (dp - jnp.sum(pf * dp, axis=0, keepdims=True))).astype(BF)
-            grads.append((dot(k_t[h * HEAD_DIM : (h + 1) * HEAD_DIM], ds), dot(ds, q), dot(p, do)))
-        (dq0, dk0, dv0), (dq1, dk1, dv1) = grads
-        dq_ref[rows, :] = jnp.concatenate([dq0, dq1], axis=0).T.astype(BF)
-        dk_ref[rows, :] = jnp.where(low_half, dk0, dk1).astype(BF)
-        dv_ref[rows, :] = jnp.where(low_half, dv0, dv1).astype(BF)
-
-    loop(slots, image, UNROLL)
+            dp_ref[h, i] = dot(jnp.where(masks[h], v, jnp.zeros_like(v)), do, NT)
+        dv = [dot(p_ref[h, i], do) for h in range(2)]
+        dv_ref[rows[i], :] = jnp.where(masks[0], *dv).astype(BF)
+
+    def softmax_back(i):
+        for h in range(2):
+            p = p_ref[h, i].astype(F32)
+            dp = dp_ref[h, i]
+            ds_ref[h, i] = (p * (dp - jnp.sum(p * dp, axis=0, keepdims=True))).astype(BF)
+
+    def downstream(i):
+        q = q_ref[rows[i], :] * jnp.bfloat16(0.125)
+        k_t = (k_ref[rows[i], :] * jnp.bfloat16(0.125)).T
+        dk = [dot(ds_ref[h, i], q) for h in range(2)]
+        dk_ref[rows[i], :] = jnp.where(masks[0], *dk).astype(BF)
+        dq = [dot(k_t[h * HEAD_DIM : (h + 1) * HEAD_DIM], ds_ref[h, i]) for h in range(2)]
+        dq_ref[rows[i], :] = jnp.concatenate(dq, axis=0).T.astype(BF)
+
+    for i in range(slots):
+        upstream(i)
+    for i in range(slots):
+        softmax_back(i)
+    for i in range(slots):
+        downstream(i)
     tail = slots * SLOT_ROWS
     for ref in (dq_ref, dk_ref, dv_ref):
         ref[tail:, :] = jnp.zeros((ROWS - tail, 2 * HEAD_DIM), BF)
@@ -371,26 +377,14 @@
     small_outer(h_ref, dq_ref, dk_ref, dv_ref, dlow_ref, o_ref, sums_ref, store)
 
 
-def input_back_body(slots, x_ref, dq_ref, dk_ref, dv_ref, wq_ref, dmid_ref, gain_ref, out_ref, sums_ref, acc_ref):
+def input_back_body(x_ref, dq_ref, dk_ref, dv_ref, wq_ref, dmid_ref, gain_ref, out_ref, sums_ref):
     width = x_ref.shape[1]
-    for s, ref in enumerate((dq_ref, dk_ref, dv_ref)):
-        part = dot(ref[...], wq_ref[:, s * width : (s + 1) * width], NT)
-        if s == 0:
-            acc_ref[...] = part
-        else:
-            acc_ref[...] += part
-
-    sums = [jnp.zeros((1, width), F32)] * 2
-    for i in range(slots):
-        rows = slice(i * SLOT_ROWS, (i + 1) * SLOT_ROWS)
-        dh = acc_ref[rows, :]
-        normal, scale_inv = norm_stats(x_ref[rows, :].astype(F32))
-        grad = dmid_ref[rows, :] + norm_back(dh, normal, scale_inv, gain_ref[...])
-        out_ref[rows, :] = grad.astype(BF)
-        sums[0] = sums[0] + colsum(dh * normal)
-        sums[1] = sums[1] + colsum(dh)
-    for n in range(2):
-        sums_ref[n : n + 1, :] = sums[n]
+    dh = sum(
+        dot(ref[...], wq_ref[:, s * width : (s + 1) * width], NT) for s, ref in enumerate((dq_ref, dk_ref, dv_ref))
+    )
+    normal, scale_inv = norm_stats(x_ref[...].astype(F32))
+    out_ref[...] = (dmid_ref[...] + norm_back(dh, normal, scale_inv, gain_ref[...])).astype(BF)
+    add_rows(sums_ref, (dh * normal, dh))
 
 
 def block_step(
@@ -440,22 +434,24 @@
     t_f = lambda n: sds((ROWS, n), F32)
     block = lambda shape: pl.BlockSpec(shape, lambda i, info: (0,) * len(shape))
     mine_block = pl.BlockSpec((1, slots, length, width), lambda i, info: (info[0], 0, 0, 0))
-    x, dy = pl.pallas_call(
-        functools.partial(prep_body, slots, length),
-        out_shape=(t_bf(width), t_bf(width)),
-        grid_spec=pltpu.PrefetchScalarGridSpec(
-            num_scalar_prefetch=1,
-            grid=(1,),
-            in_specs=[mine_block, mine_block],
-            out_specs=[block((ROWS, width)), block((ROWS, width))],
-        ),
-        compiler_params=pltpu.CompilerParams(vmem_limit_bytes=24 * 1024 * 1024),
-        cost_estimate=pl.CostEstimate(flops=0, bytes_accessed=8 * ROWS * width, transcendentals=0),
-        name="prep",
-    )(info, inputs, cotangent)
+
+    def prep(array, count):
+        return pl.pallas_call(
+            prep_body,
+            out_shape=t_bf(width),
+            grid_spec=pltpu.PrefetchScalarGridSpec(
+                num_scalar_prefetch=1, grid=(1,), in_specs=[mine_block], out_specs=block((ROWS, width))
+            ),
+            compiler_params=pltpu.CompilerParams(vmem_limit_bytes=24 * 1024 * 1024),
+            cost_estimate=pl.CostEstimate(flops=0, bytes_accessed=4 * ROWS * width, transcendentals=0),
+        )(jnp.stack([mine, count]), array)
+
+    x = prep(inputs, jnp.int32(slots))
+    dy = prep(cotangent, live)
 
     def scatter_ring(halves):
-        got = [mp_swap(send, 1) for send in halves[far:]]
+        got = [mp_swap(halves[far], 1)]
+        got += [mp_swap(send, 1) for send in halves[far + 1 :]]
 
         def term(n):
             return halves[n].astype(F32) + got[n].astype(F32)
@@ -469,9 +465,11 @@
         total = jnp.where(even, last, total).reshape(2, 2, sub, -1)
         split = lambda a, b, first: (jnp.where(first, a, b), jnp.where(first, b, a))
         mine_half, other_half = split(total[:, 0], total[:, 1], even)
-        total = mine_half.astype(F32) + mp_swap(other_half, 1).astype(F32)
+        other_half = mp_swap(other_half, 1)
+        total = mine_half.astype(F32) + other_half.astype(F32)
         mine_half, other_half = split(total[0], total[1], mine < 2)
-        return mine_half + mp_swap(other_half.astype(BF), 2).astype(F32)
+        other_half = mp_swap(other_half.astype(BF), 2)
+        return lax.optimization_barrier(mine_half + other_half.astype(F32))
 
     leave = [jnp.where(even, far - k, k + 1 - far) for k in range(far)]
     stay = [jnp.where(even, k + 1 - far, far - k) for k in range(far)]
@@ -506,16 +504,15 @@
             offsets += [-k * side, k * side]
         ring_info = info_of(offsets + [jnp.int32(far)])
         start_bc = chip_chunk(shard_bc)
-        prepared = (x, dy)
+        prepared = [x]
 
         def between(k, held):
-            nonlocal prepared
             if k == 1:
-                held, prepared = lax.optimization_barrier((held, prepared))
+                held, prepared[0] = lax.optimization_barrier((held, prepared[0]))
             return held
 
         chunks, last = gather_ring(chip_chunk(shard_a), between)
-        x, dy = prepared
+        (x,) = prepared
         start_bc, last = lax.optimization_barrier((start_bc, last))
         bc, _ = gather_ring(start_bc, lambda k, held: held)
         piece = lambda n: [pl.BlockSpec((groups, sub, units), lambda i: (0, 0, n))] * len(bc)
@@ -532,19 +529,17 @@
     qb, vb, hb = (biases[:, a:b].reshape(-1) for a, b in ((0, local), (local, 2 * local), (2 * local, None)))
     bias_row = row(jnp.concatenate([qb, jnp.zeros_like(qb), vb]))
 
-    qkv_outs = [t_bf(width), t_bf(3 * width), sds((width, 3 * width), BF), sds((width, width), BF)]
-    qkv_ins = [x, row(norm_gain), row(norm_shift), bias_row]
-    if ring:
-        h1, qkv, wq, wo = call(
-            qkv_ring_body,
-            qkv_outs,
-            [ring_info] + qkv_ins + chunks,
-            [smem] + [None] * (len(qkv_ins) + len(chunks)),
-            scratch=[pltpu.VMEM((groups, width, 4 * local), BF)],
-            flops=3 * mm,
-        )
-    else:
-        h1, qkv, wq, wo = call(qkv_gathered_body, qkv_outs, qkv_ins + [wa], flops=3 * mm)
+    third = lambda n: pl.BlockSpec((n, width), lambda i: (0, i))
+    chunks = chunks if ring else [wa]
+    h1, qkv, wq, wo = call(
+        qkv_body,
+        [t_bf(width), t_bf(3 * width), sds((width, 3 * width), BF), sds((width, width), BF)],
+        [ring_info, x, row(norm_gain), row(norm_shift), bias_row] + chunks,
+        [smem, None, None, None, third(1)] + [None] * len(chunks),
+        [None, third(ROWS), third(width), None],
+        (3,),
+        flops=3 * mm,
+    )
     pair = 2 * HEAD_DIM
     pairs = width // pair
     head = lambda s: pl.BlockSpec((ROWS, pair), lambda i: (0, s * pairs + i))
@@ -557,6 +552,7 @@
         [head(0), head(1), head(2)],
         [head(0), p_spec],
         (pairs,),
+        scratch=[pltpu.VMEM((2, slots, SLOT_ROWS, SLOT_ROWS), F32)],
         flops=mm,
     )
     rows256 = pl.BlockSpec((256, width), lambda i: (i, 0))
@@ -579,7 +575,7 @@
         [smem, None, vcols(1)] + wcols(0),
         [tcols, tcols],
         (groups,),
-        scratch=[group_buf(1)],
+        scratch=[pltpu.VMEM((width, units), BF)],
         flops=4 * mm,
     )
     du, sum_hidden = call(
@@ -589,7 +585,7 @@
         [smem, None, tcols] + wcols(1),
         [tcols, vcols(8)],
         (groups,),
-        scratch=[group_buf(1)],
+        scratch=[pltpu.VMEM((width, units), BF)],
         flops=4 * mm,
     )
     outer_in_specs = [
@@ -632,27 +628,32 @@
 
     def spread(own):
         crossed = mp_swap(own, 2)
+        near = mp_swap(own, 1)
+        far_core = mp_swap(crossed, 1)
         image = pl.BlockSpec((SLOT_ROWS, width), lambda i: (i, 0))
         (woven,) = call(
             functools.partial(weave_body, length),
             [sds((slots, length, groups, width), BF)],
-            [info, own, mp_swap(own, 1), crossed, mp_swap(crossed, 1)],
+            [info, own, near, crossed, far_core],
             [smem] + [image] * 4,
             [pl.BlockSpec((1, length, groups, width), lambda i: (i, 0, 0, 0))],
             (slots,),
             flops=mm,
-            limit=16,
+            limit=24,
         )
         return woven.transpose(2, 0, 1, 3)
 
     down_info = jnp.concatenate([info, ring_info[2:]])
     act_late, _ = lax.optimization_barrier((act, g_bc))
+    wide256 = pl.BlockSpec((256, ff), lambda i: (i, 0))
     (own_out,) = call(
-        functools.partial(down_body, slots),
+        down_body,
         [own_shape],
         [down_info, act_late, middle, row(down_bias)] + bc,
-        [smem, None, None, None] + piece(1),
-        scratch=[pltpu.VMEM((ROWS, width), F32), group_buf(groups)],
+        [smem, wide256, rows256, None] + piece(1),
+        [rows256],
+        (ROWS // 256,),
+        scratch=[group_buf(groups)],
         flops=4 * mm,
     )
     all_out = spread(own_out)
@@ -662,30 +663,23 @@
         mid_back_body,
         [t_f(width), t_bf(width), sds((8, width), F32)],
         [ring_info, dy, du, middle, row(mlp_gain)] + bc,
-        [smem, None, None, None, None] + piece(0),
-        scratch=[pltpu.VMEM((ROWS, width), F32), group_buf(groups)],
+        [smem, rows256, wide256, rows256, None] + piece(0),
+        [rows256, rows256, None],
+        (ROWS // 256,),
+        scratch=[group_buf(groups)],
         flops=4 * mm,
     )
     (do,) = call(out_back_body, [t_bf(width)], [dlow, wo], flops=mm)
-    grads = []
-    hbm = pl.BlockSpec(memory_space=pl.ANY)
-    calls = 3 if pairs % 3 == 0 else 1
-    for n in range(calls):
-        first = n * pairs // calls
-        at = lambda s, first=first: pl.BlockSpec((ROWS, pair), lambda i: (0, s * pairs + first + i))
-        grads = call(
-            functools.partial(attend_back_body, slots),
-            [t_bf(width)] * 3,
-            [qkv, qkv, qkv, probs, do] + list(grads),
-            [at(0), at(1), at(2), pl.BlockSpec((2, slots, SLOT_ROWS, SLOT_ROWS), lambda i, first=first: (first + i, 0, 0, 0)), at(0)]
-            + [hbm] * len(grads),
-            [at(0)] * 3,
-            (pairs // calls,),
-            flops=2 * mm // calls,
-            limit=24,
-            input_output_aliases={5 + m: m for m in range(len(grads))},
-        )
-    dq, dk, dv = grads
+    dq, dk, dv = call(
+        functools.partial(attend_back_body, slots),
+        [t_bf(width)] * 3,
+        [qkv, qkv, qkv, probs, do],
+        [head(0), head(1), head(2), p_spec, head(0)],
+        [head(0)] * 3,
+        (pairs,),
+        scratch=[pltpu.VMEM((2, slots, SLOT_ROWS, SLOT_ROWS), dtype) for dtype in (F32, BF)],
+        flops=2 * mm,
+    )
     outer_ins = [h1, dq, dk, dv, dlow, mixed]
     sum_shape = sds((8, width), F32)
     if ring:
@@ -706,22 +700,23 @@
             g_a.reshape(parts * groups, sub, 4 * local), axes, scatter_dimension=0, tiled=False
         ).astype(F32)
     own_grad, sums_in = call(
-        functools.partial(input_back_body, slots),
+        input_back_body,
         [own_shape, sum_shape],
         [x, dq, dk, dv, wq, dmid, row(norm_gain)],
-        scratch=[pltpu.VMEM((ROWS, width), F32)],
+        [rows256] * 4 + [None, rows256, None],
+        [rows256, None],
+        (ROWS // 256,),
         flops=3 * mm,
     )
+
     sums = jnp.concatenate(
         [sums_in[:2].reshape(-1), sums_mid[:4].reshape(-1), sums_qkv[:2].reshape(-1), sum_hidden[0]]
     )
     all_grad = spread(own_grad)
-    sums = sums + mp_swap(sums, 1)
-    bit = 1
-    while bit < parts:
-        sums = sums + dp_swap(sums, bit)
-        bit *= 2
-    sums = sums + mp_swap(sums, 2)
+    steps = [(mp_swap, 1)] + [(dp_swap, 1 << n) for n in range(parts.bit_length() - 1)] + [(mp_swap, 2)]
+    for swap, bit in steps:
+        other = swap(sums, bit)
+        sums = sums + other
     vec = [sums[n * width : (n + 1) * width] for n in range(8)]
     own = lambda v, n: lax.dynamic_slice_in_dim(v, mine * n, n, 0)
     return (

time: 439 us -> 411 us (0.936)
  Pallas kernels: 176 us -> 146 us
  waiting for transfers between devices: 136 us -> 145 us
  local copies, waits for them, and re-layouts: 49.1 us -> 41.6 us
    pallas_call x16 -> x14, Pallas kernels: 175 us -> 145 us  [call(): pl.pallas_call(body, out_shape=tuple(outs), grid=(1,) if grid is None els...]
    unnamed x88 -> x78, local copies, waits for them, and re-layouts: 23.1 us -> 14.8 us
    ppermute x34, waiting for transfers between devices: 38.8 us -> 46 us  [block_step(): lax.ppermute(a, 'mp', [(j, j ^ bit) for j in range(groups)])]
  transfers between devices with their start and end apart: 53 -> 53, of which waited for: 18 -> 19; matrix products, arithmetic and copies ran while one was open for 14% -> 15% of each run, Pallas kernels for 30% -> 26%
where the time goes in v5:
time: 411 us; the launch traced here: 404 us
  Pallas kernels  146 us (36%)
  waiting for transfers between devices  145 us (35%)
  starting transfers between devices  47.1 us (11%)
  local copies, waits for them, and re-layouts  41.6 us (10%)
  other arithmetic  22.6 us (5%)
    pallas_call x14, Pallas kernels, call(): pl.pallas_call(body, out_shape=tuple(outs), grid=(1,) if grid is None els...  145 us
    ppermute x16, waiting for transfers between devices, hop(): return lax.ppermute(a, axes, pairs)  67.7 us
    ppermute x34, waiting for transfers between devices, block_step(): lax.ppermute(a, 'mp', [(j, j ^ bit) for j in range(groups)])  46 us
    ppermute x3, waiting for transfers between devices, block_step(): lax.ppermute(a, 'dp', [(d, d ^ bit) for d in range(parts)])  31.3 us
    ppermute x16, starting transfers between devices, hop(): return lax.ppermute(a, axes, pairs)  28.3 us
    ppermute x34, starting transfers between devices, block_step(): lax.ppermute(a, 'mp', [(j, j ^ bit) for j in range(groups)])  17 us
    unnamed x78, local copies, waits for them, and re-layouts  14.8 us
  transfers between devices with their start and end apart: 53, of which 19 were waited for; matrix products, arithmetic and copies ran while one was open for 15% of the time, Pallas kernels for 26%

profile of v5, /device:TPU:0, one launch (start us, length us, event | category | flops | bytes accessed | tf_op | source)
XLA Modules:
  0.0 404.2 jit_solution(18140593178261953455)
XLA Ops:
  2.6 3.0 collective-permute-start
  13.3 3.5 copy.42.in_ref
  17.7 3.7 collective-permute-done.2.refs_1_
  24.8 6.5 %collective-permute-done.6.refs_3_ = bf16[4,96,768]{2,1,0:T(8,128)(2,1)S(1)} collective-permute-done((bf16[4,96,768]{2,1,0:T(8,128)(2,1)S(1)}, bf16[4,96,768]{2,1,0:T(8,128)(2,1)S(1)}, u32[]{:S(2)}, u32[]{:S(2)}) %collective-permute-start.6) | collective-permute-done | bytes 589856 | tf_op jit(solution)/shard_map/ppermute | solution.py:420
  33.2 7.9 %collective-permute-done.8.refs_5_ = bf16[4,96,768]{2,1,0:T(8,128)(2,1)S(1)} collective-permute-done((bf16[4,96,768]{2,1,0:T(8,128)(2,1)S(1)}, bf16[4,96,768]{2,1,0:T(8,128)(2,1)S(1)}, u32[]{:S(2)}, u32[]{:S(2)}) %collective-permute-start.8) | collective-permute-done | bytes 589856 | tf_op jit(solution)/shard_map/ppermute | solution.py:420
  43.6 4.4 %collective-permute-done.10 = bf16[2,96,768]{2,1,0:T(8,128)(2,1)S(1)} collective-permute-done((bf16[2,96,768]{2,1,0:T(8,128)(2,1)S(1)}, bf16[2,96,768]{2,1,0:T(8,128)(2,1)S(1)}, u32[]{:S(2)}, u32[]{:S(2)}) %collective-permute-start.10) | collective-permute-done | bytes 294944 | tf_op jit(solution)/shard_map/ppermute | solution.py:420
  49.8 14.4 %collective-permute-done.14.refs_1_ = bf16[4,96,1536]{2,1,0:T(8,128)(2,1)S(1)} collective-permute-done((bf16[4,96,1536]{2,1,0:T(8,128)(2,1)S(1)}, bf16[4,96,1536]{2,1,0:T(8,128)(2,1)S(1)}, u32[]{:S(2)}, u32[]{:S(2)}) %collective-permute-start.14) | collective-permute-done | bytes 1179680 | tf_op jit(solution)/shard_map/ppermute | solution.py:420
  70.2 10.3 %collective-permute-done.16.refs_3_ = bf16[4,96,1536]{2,1,0:T(8,128)(2,1)} collective-permute-done((bf16[4,96,1536]{2,1,0:T(8,128)(2,1)S(1)}, bf16[4,96,1536]{2,1,0:T(8,128)(2,1)}, u32[]{:S(2)}, u32[]{:S(2)}) %collective-permute-start.16) | collective-permute-done | bytes 1179680 | tf_op jit(solution)/shard_map/ppermute | solution.py:420
  97.4 3.5 copy.43.in_ref
  109.2 5.8 %collective-permute-done.20 = bf16[2,96,1536]{2,1,0:T(8,128)(2,1)} collective-permute-done((bf16[2,96,1536]{2,1,0:T(8,128)(2,1)S(1)}, bf16[2,96,1536]{2,1,0:T(8,128)(2,1)}, u32[]{:S(2)}, u32[]{:S(2)}) %collective-permute-start.20) | collective-permute-done | bytes 589856 | tf_op jit(solution)/shard_map/ppermute | solution.py:420
  117.0 10.7 %shard_map.290 = (bf16[1024,768]{1,0:T(8,128)(2,1)}, bf16[1024,2304]{1,0:T(8,128)(2,1)}, bf16[768,2304]{1,0:T(8,128)(2,1)}, bf16[768,768]{1,0:T(8,128)(2,1)}) custom-call(s32[10]{0:T(128)} %get-tuple-element.157.info_ref, bf16[1024,768]{1,0:T(8,128)(2,1)} %copy-done.4, f32[1,768]{1,0:T(1,128)} %reshape.418.gain_ref, f32[1,768]{1,0:T(1,128)} %reshape.419.shift_ref, ...), custom_call_target="tpu_custom_call" | custom-call | flops 3623878656 | bytes 17316904 | tf_op jit(solution)/shard_map/pallas_call | solution.py:54
  127.7 9.7 %shard_map.291 = (bf16[1024,768]{1,0:T(8,128)(2,1)}, bf16[12,5,200,200]{3,2,1,0:T(8,128)(2,1)}) custom-call(bf16[1024,2304]{1,0:T(8,128)(2,1)} %get-tuple-element.59.q_ref.k_ref.v_ref, bf16[1024,2304]{1,0:T(8,128)(2,1)} %get-tuple-element.59.q_ref.k_ref.v_ref, bf16[1024,2304]{1,0:T(8,128)(2,1)} %get-tuple-element.59.q_ref.k_ref.v_ref), custom_call_target="tpu_custom_call" | custom-call | flops 1207959552 | bytes 20528640 | tf_op jit(solution)/shard_map/pallas_call | solution.py:54
  137.4 7.2 %shard_map.292 = (f32[1024,768]{1,0:T(8,128)}, bf16[1024,768]{1,0:T(8,128)(2,1)}) custom-call(bf16[1024,768]{1,0:T(8,128)(2,1)} %copy-done.4, bf16[1024,768]{1,0:T(8,128)(2,1)} %get-tuple-element.60.o_ref, bf16[768,768]{1,0:T(8,128)(2,1)} %get-tuple-element.61.wo_ref, f32[1,768]{1,0:T(1,128)} %reshape.423.bias_ref, f32[1,768]{1,0:T(1,128)} %reshape.424.gain_ref, ...), custom_call_target="tpu_custom_call" | custom-call | flops 1207959552 | bytes 9053184 | tf_op jit(solution)/shard_map/pallas_call | solution.py:54
  148.1 12.5 %shard_map.293 = (bf16[1024,3072]{1,0:T(8,128)(2,1)}, bf16[1024,3072]{1,0:T(8,128)(2,1)}) custom-call(s32[10]{0:T(128)} %get-tuple-element.157.info_ref, bf16[1024,768]{1,0:T(8,128)(2,1)} %get-tuple-element.62.h_ref, f32[1,3072]{1,0:T(1,128)} %bitcast.160, bf16[4,96,1536]{2,1,0:T(8,128)(2,1)} %copy-done.7, bf16[4,96,1536]{2,1,0:T(8,128)(2,1)} %copy-done.9, ...), custom_call_target="tpu_custom_call" | custom-call | flops 4831838208 | bytes 23605288 | tf_op jit(solution)/shard_map/pallas_call | solution.py:54
  160.7 11.5 %shard_map.295 = (bf16[1024,3072]{1,0:T(8,128)(2,1)}, f32[8,3072]{1,0:T(8,128)}) custom-call(s32[10]{0:T(128)} %get-tuple-element.157.info_ref, bf16[1024,768]{1,0:T(8,128)(2,1)} %copy-done.2, bf16[1024,3072]{1,0:T(8,128)(2,1)} %get-tuple-element.65.slope_ref, bf16[4,96,1536]{2,1,0:T(8,128)(2,1)} %copy-done.7, bf16[4,96,1536]{2,1,0:T(8,128)(2,1)} %copy-done.9, ...), custom_call_target="tpu_custom_call" | custom-call | flops 4831838208 | bytes 23691304 | tf_op jit(solution)/shard_map/pallas_call | solution.py:54
  172.2 17.9 %shard_map.296 = (bf16[4,96,1536]{2,1,0:T(8,128)(2,1)}, bf16[4,96,1536]{2,1,0:T(8,128)(2,1)}, bf16[4,96,1536]{2,1,0:T(8,128)(2,1)}, bf16[4,96,1536]{2,1,0:T(8,12...) custom-call(s32[10]{0:T(128)} %get-tuple-element.158.info_ref, ...), custom_call_target="tpu_custom_call" | custom-call | flops 9663676416 | bytes 25165864 | tf_op jit(solution)/shard_map/pallas_call | solution.py:54
  190.8 10.5 %shard_map.297.a_ref = bf16[1000,768]{1,0:T(8,128)(2,1)} custom-call(s32[10]{0:T(128)} %get-tuple-element.157.info_ref, bf16[1024,3072]{1,0:T(8,128)(2,1)} %get-tuple-element.68.act_ref, f32[1024,768]{1,0:T(8,128)} %get-tuple-element.69.mid_ref, f32[1,768]{1,0:T(1,128)} %reshape.426.bias_ref, bf16[4,96,1536]{2,1,0:T(8,128)(2,1)} %copy-done.7, ...), custom_call_target="tpu_custom_call" | custom-call | flops 4831838208 | bytes 20413480 | tf_op jit(solution)/shard_map/pallas_call | solution.py:54
  203.7 12.7 %shard_map.299 = (f32[1024,768]{1,0:T(8,128)}, bf16[1024,768]{1,0:T(8,128)(2,1)}, f32[8,768]{1,0:T(8,128)}) custom-call(s32[10]{0:T(128)} %get-tuple-element.157.info_ref, bf16[1024,768]{1,0:T(8,128)(2,1)} %copy-done.2, bf16[1024,3072]{1,0:T(8,128)(2,1)} %get-tuple-element.71.du_ref, f32[1024,768]{1,0:T(8,128)} %get-tuple-element.69.mid_ref, ...), custom_call_target="tpu_custom_call" | custom-call | flops 4831838208 | bytes 25193512 | tf_op jit(solution)/shard_map/pallas_call | solution.py:54
  218.6 4.3 %shard_map.300.do_ref = bf16[1024,768]{1,0:T(8,128)(2,1)} custom-call(bf16[1024,768]{1,0:T(8,128)(2,1)} %get-tuple-element.72.dlow_ref, bf16[768,768]{1,0:T(8,128)(2,1)} %get-tuple-element.61.wo_ref), custom_call_target="tpu_custom_call" | custom-call | flops 1207959552 | bytes 4325376 | tf_op jit(solution)/shard_map/pallas_call | solution.py:54
  222.9 11.8 %shard_map.301 = (bf16[1024,768]{1,0:T(8,128)(2,1)}, bf16[1024,768]{1,0:T(8,128)(2,1)}, bf16[1024,768]{1,0:T(8,128)(2,1)}) custom-call(bf16[1024,2304]{1,0:T(8,128)(2,1)} %get-tuple-element.59.q_ref.k_ref.v_ref, bf16[1024,2304]{1,0:T(8,128)(2,1)} %get-tuple-element.59.q_ref.k_ref.v_ref, bf16[1024,2304]{1,0:T(8,128)(2,1)} %get-tuple-element.59.q_ref.k_ref.v_ref, ...), custom_call_target="tpu_custom_call" | custom-call | flops 2415919104 | bytes 25247232 | tf_op jit(solution)/shard_map/pallas_call | solution.py:54
  234.7 10.0 %shard_map.302 = (bf16[1000,768]{1,0:T(8,128)(2,1)}, f32[8,768]{1,0:T(8,128)}) custom-call(bf16[1024,768]{1,0:T(8,128)(2,1)} %copy-done.4, bf16[1024,768]{1,0:T(8,128)(2,1)} %get-tuple-element.73.dq_ref, bf16[1024,768]{1,0:T(8,128)(2,1)} %get-tuple-element.74.dk_ref, bf16[1024,768]{1,0:T(8,128)(2,1)} %get-tuple-element.75.dv_ref, ...), custom_call_target="tpu_custom_call" | custom-call | flops 3623878656 | bytes 14539776 | tf_op jit(solution)/shard_map/pallas_call | solution.py:54
  246.1 11.2 %shard_map.304 = (bf16[4,96,768]{2,1,0:T(8,128)(2,1)}, bf16[4,96,768]{2,1,0:T(8,128)(2,1)}, bf16[4,96,768]{2,1,0:T(8,128)(2,1)}, bf16[4,96,768]{2,1,0:T(8,128)(2...) custom-call(s32[10]{0:T(128)} %get-tuple-element.158.info_ref, ...), custom_call_target="tpu_custom_call" | custom-call | flops 4831838208 | bytes 14180392 | tf_op jit(solution)/shard_map/pallas_call | solution.py:54
  269.3 17.9 %collective-permute-done.29 = f32[9216]{0:T(1024)S(1)} collective-permute-done((f32[9216]{0:T(1024)S(1)}, f32[9216]{0:T(1024)S(1)}, u32[]{:S(2)}, u32[]{:S(2)}) %collective-permute-start.29) | collective-permute-done | bytes 36896 | tf_op jit(solution)/shard_map/ppermute | solution.py:410
  288.2 3.6 collective-permute-done.30
  294.6 7.6 %collective-permute-done.38 = bf16[4,96,768]{2,1,0:T(8,128)(2,1)S(1)} collective-permute-done((bf16[4,96,768]{2,1,0:T(8,128)(2,1)S(1)}, bf16[4,96,768]{2,1,0:T(8,128)(2,1)S(1)}, u32[]{:S(2)}, u32[]{:S(2)}) %collective-permute-start.38) | collective-permute-done | bytes 589856 | tf_op jit(solution)/shard_map/ppermute | solution.py:420
  303.6 9.8 %collective-permute-done.31 = f32[9216]{0:T(1024)S(1)} collective-permute-done((f32[9216]{0:T(1024)S(1)}, f32[9216]{0:T(1024)S(1)}, u32[]{:S(2)}, u32[]{:S(2)}) %collective-permute-start.31) | collective-permute-done | bytes 36896 | tf_op jit(solution)/shard_map/ppermute | solution.py:410
  317.2 7.0 %collective-permute-done.39 = bf16[4,96,768]{2,1,0:T(8,128)(2,1)S(1)} collective-permute-done((bf16[4,96,768]{2,1,0:T(8,128)(2,1)S(1)}, bf16[4,96,768]{2,1,0:T(8,128)(2,1)S(1)}, u32[]{:S(2)}, u32[]{:S(2)}) %collective-permute-start.39) | collective-permute-done | bytes 589856 | tf_op jit(solution)/shard_map/ppermute | solution.py:420
  332.0 29.5 %collective-permute-done.32 = f32[9216]{0:T(1024)S(1)} collective-permute-done((f32[9216]{0:T(1024)S(1)}, f32[9216]{0:T(1024)S(1)}, u32[]{:S(2)}, u32[]{:S(2)}) %collective-permute-start.32) | collective-permute-done | bytes 36896 | tf_op jit(solution)/shard_map/ppermute | solution.py:409
  372.9 7.4 %shard_map.303 = bf16[5,197,4,768]{3,2,1,0:T(4,128)(2,1)} custom-call(s32[2]{0:T(128)S(1)} %pad_add_fusion.info_ref, bf16[1000,768]{1,0:T(8,128)(2,1)S(1)} %copy-done.5, bf16[1000,768]{1,0:T(8,128)(2,1)} %collective-permute-done.25.b_ref, bf16[1000,768]{1,0:T(8,128)(2,1)} %collective-permute-done.26.c_ref, bf16[1000,768]{1,0:T(8,128)(2,1)} %collective-permute-done.27.d_ref), custom_call_target="tpu_custom_call" | custom-call | flops 1207959552 | bytes 12195848 | tf_op jit(solution)/shard_map/pallas_call | solution.py:54
  382.3 7.4 %shard_map.298 = bf16[5,197,4,768]{3,2,1,0:T(4,128)(2,1)} custom-call(s32[2]{0:T(128)S(1)} %pad_add_fusion.info_ref, bf16[1000,768]{1,0:T(8,128)(2,1)S(1)} %copy-done.3, bf16[1000,768]{1,0:T(8,128)(2,1)} %collective-permute-done.22.b_ref, bf16[1000,768]{1,0:T(8,128)(2,1)} %collective-permute-done.23.c_ref, bf16[1000,768]{1,0:T(8,128)(2,1)} %collective-permute-done.24.d_ref), custom_call_target="tpu_custom_call" | custom-call | flops 1207959552 | bytes 12195848 | tf_op jit(solution)/shard_map/pallas_call | solution.py:54
  392.3 5.4 %collective-permute-done.42 = bf16[96,768]{0,1:T(8,128)(2,1)S(1)} collective-permute-done((bf16[96,768]{0,1:T(8,128)(2,1)S(1)}, bf16[96,768]{0,1:T(8,128)(2,1)S(1)}, u32[]{:S(2)}, u32[]{:S(2)}) %collective-permute-start.42) | collective-permute-done | bytes 147488 | tf_op jit(solution)/shard_map/ppermute | solution.py:409
  399.2 3.8 collective-permute-done.52
  (256 shorter events, 110.1 us)
Async XLA Ops:
  48.0 16.2 %collective-permute-start.14 = (bf16[4,96,1536]{2,1,0:T(8,128)(2,1)S(1)}, bf16[4,96,1536]{2,1,0:T(8,128)(2,1)S(1)}, u32[]{:S(2)}, u32[]{:S(2)}) collective-permute-start(bf16[4,96,1536]{2,1,0:T(8,128)(2,1)S(1)} %pad_maximum_fusion.refs_0_), channel_id=1, source_target_pairs={{0,8},{1,5},{2,10},{3,7},{8,16},{9,1},{10,18},{11,3},{16,24},{17,9... | collective-permute-start | bytes 3538952 | tf_op jit(solution)/shard_map/ppermute | solution.py:420
  64.2 16.4 %collective-permute-start.16 = (bf16[4,96,1536]{2,1,0:T(8,128)(2,1)S(1)}, bf16[4,96,1536]{2,1,0:T(8,128)(2,1)}, u32[]{:S(2)}, u32[]{:S(2)}) collective-permute-start(bf16[4,96,1536]{2,1,0:T(8,128)(2,1)S(1)} %collective-permute-done.14.refs_1_), channel_id=1, source_target_pairs={{0,8},{1,5},{2,10},{3,7},{8,16},{9,1},{10,18},{11,3},{16,24},{17,9... | collective-permute-start | bytes 3538952 | tf_op jit(solution)/shard_map/ppermute | solution.py:420
  66.9 21.2 %collective-permute-start.3 = (f32[1152]{0:T(1024)S(1)}, f32[1152]{0:T(1024)}, u32[]{:S(2)}, u32[]{:S(2)}) collective-permute-start(f32[1152]{0:T(1024)S(1)} %concatenate.50), channel_id=1, source_target_pairs={{0,1},{1,0},{2,3},{3,2},{4,5},{5,4},{6,7},{7,6},{8,9},{9,8},{10,11... | collective-permute-start | bytes 13832 | tf_op jit(solution)/shard_map/ppermute | solution.py:409
  80.5 24.0 %collective-permute-start.18 = (bf16[4,96,1536]{2,1,0:T(8,128)(2,1)}, bf16[4,96,1536]{2,1,0:T(8,128)(2,1)S(1)}, u32[]{:S(2)}, u32[]{:S(2)}) collective-permute-start(bf16[4,96,1536]{2,1,0:T(8,128)(2,1)} %collective-permute-done.16.refs_3_), channel_id=1, source_target_pairs={{0,8},{1,5},{2,10},{3,7},{8,16},{9,1},{10,18},{11,3},{16,24},{17,9... | collective-permute-start | bytes 3538952 | tf_op jit(solution)/shard_map/ppermute | solution.py:420
  88.8 14.1 %collective-permute-start.4 = (f32[2,1152]{1,0:T(2,128)S(1)}, f32[2,1152]{1,0:T(2,128)S(1)}, u32[]{:S(2)}, u32[]{:S(2)}) collective-permute-start(f32[2,1152]{1,0:T(2,128)S(1)} %pad_maximum_fusion.11), channel_id=1, source_target_pairs={{0,2},{1,3},{2,0},{3,1},{4,6},{5,7},{6,4},{7,5},{8,10},{9,11},{10,... | collective-permute-start | bytes 27656 | tf_op jit(solution)/shard_map/ppermute | solution.py:409
  103.4 13.1 %collective-permute-start.5 = (bf16[4,96,768]{2,1,0:T(8,128)(2,1)}, bf16[4,96,768]{2,1,0:T(8,128)(2,1)}, u32[]{:S(2)}, u32[]{:S(2)}) collective-permute-start(bf16[4,96,768]{2,1,0:T(8,128)(2,1)} %copy-done.31), channel_id=1, source_target_pairs={{0,1},{1,0},{2,3},{3,2},{4,5},{5,4},{6,7},{7,6},{8,9},{9,8},{10,11... | collective-permute-start | bytes 1769480 | tf_op jit(solution)/shard_map/ppermute | solution.py:409
  103.5 13.1 %collective-permute-start.7 = (bf16[4,96,768]{2,1,0:T(8,128)(2,1)}, bf16[4,96,768]{2,1,0:T(8,128)(2,1)}, u32[]{:S(2)}, u32[]{:S(2)}) collective-permute-start(bf16[4,96,768]{2,1,0:T(8,128)(2,1)} %copy-done.32), channel_id=1, source_target_pairs={{0,1},{1,0},{2,3},{3,2},{4,5},{5,4},{6,7},{7,6},{8,9},{9,8},{10,11... | collective-permute-start | bytes 1769480 | tf_op jit(solution)/shard_map/ppermute | solution.py:409
  104.0 13.0 %collective-permute-start.9 = (bf16[4,96,768]{2,1,0:T(8,128)(2,1)}, bf16[4,96,768]{2,1,0:T(8,128)(2,1)}, u32[]{:S(2)}, u32[]{:S(2)}) collective-permute-start(bf16[4,96,768]{2,1,0:T(8,128)(2,1)} %copy-done.21), channel_id=1, source_target_pairs={{0,1},{1,0},{2,3},{3,2},{4,5},{5,4},{6,7},{7,6},{8,9},{9,8},{10,11... | collective-permute-start | bytes 1769480 | tf_op jit(solution)/shard_map/ppermute | solution.py:409
  115.1 29.5 %collective-permute-start.21 = (bf16[2,96,1536]{2,1,0:T(8,128)(2,1)}, bf16[2,96,1536]{2,1,0:T(8,128)(2,1)}, u32[]{:S(2)}, u32[]{:S(2)}) collective-permute-start(bf16[2,96,1536]{2,1,0:T(8,128)(2,1)} %collective-permute-done.20), channel_id=1, source_target_pairs={{0,1},{1,0},{2,3},{3,2},{4,5},{5,4},{6,7},{7,6},{8,9},{9,8},{10,11... | collective-permute-start | bytes 1769480 | tf_op jit(solution)/shard_map/ppermute | solution.py:409
  116.0 31.2 %collective-permute-start.15 = (bf16[4,96,1536]{2,1,0:T(8,128)(2,1)S(1)}, bf16[4,96,1536]{2,1,0:T(8,128)(2,1)S(1)}, u32[]{:S(2)}, u32[]{:S(2)}) collective-permute-start(bf16[4,96,1536]{2,1,0:T(8,128)(2,1)S(1)} %collective-permute-done.14.refs_1_), channel_id=1, source_target_pairs={{0,1},{1,0},{2,3},{3,2},{4,5},{5,4},{6,7},{7,6},{8,9},{9,8},{10,11... | collective-permute-start | bytes 3538952 | tf_op jit(solution)/shard_map/ppermute | solution.py:409
  116.5 30.6 %collective-permute-start.17 = (bf16[4,96,1536]{2,1,0:T(8,128)(2,1)}, bf16[4,96,1536]{2,1,0:T(8,128)(2,1)}, u32[]{:S(2)}, u32[]{:S(2)}) collective-permute-start(bf16[4,96,1536]{2,1,0:T(8,128)(2,1)} %collective-permute-done.16.refs_3_), channel_id=1, source_target_pairs={{0,1},{1,0},{2,3},{3,2},{4,5},{5,4},{6,7},{7,6},{8,9},{9,8},{10,11... | collective-permute-start | bytes 3538952 | tf_op jit(solution)/shard_map/ppermute | solution.py:409
  116.5 30.6 %collective-permute-start.19 = (bf16[4,96,1536]{2,1,0:T(8,128)(2,1)S(1)}, bf16[4,96,1536]{2,1,0:T(8,128)(2,1)}, u32[]{:S(2)}, u32[]{:S(2)}) collective-permute-start(bf16[4,96,1536]{2,1,0:T(8,128)(2,1)S(1)} %collective-permute-done.18.refs_5_), channel_id=1, source_target_pairs={{0,1},{1,0},{2,3},{3,2},{4,5},{5,4},{6,7},{7,6},{8,9},{9,8},{10,11... | collective-permute-start | bytes 3538952 | tf_op jit(solution)/shard_map/ppermute | solution.py:409
  201.4 60.4 %collective-permute-start.45 = (bf16[4,96,1536]{2,1,0:T(8,128)(2,1)}, bf16[4,96,1536]{2,1,0:T(8,128)(2,1)}, u32[]{:S(2)}, u32[]{:S(2)}) collective-permute-start(bf16[4,96,1536]{2,1,0:T(8,128)(2,1)} %get-tuple-element.97), channel_id=1, source_target_pairs={{0,1},{1,0},{2,3},{3,2},{4,5},{5,4},{6,7},{7,6},{8,9},{9,8},{10,11... | collective-permute-start | bytes 3538952 | tf_op jit(solution)/shard_map/ppermute | solution.py:409
  202.1 59.7 %collective-permute-start.47 = (bf16[4,96,1536]{2,1,0:T(8,128)(2,1)S(1)}, bf16[4,96,1536]{2,1,0:T(8,128)(2,1)S(1)}, u32[]{:S(2)}, u32[]{:S(2)}) collective-permute-start(bf16[4,96,1536]{2,1,0:T(8,128)(2,1)S(1)} %add_convert_fusion.3), channel_id=1, source_target_pairs={{0,8},{1,5},{2,10},{3,7},{8,16},{9,1},{10,18},{11,3},{16,24},{17,9... | collective-permute-start | bytes 3538952 | tf_op jit(solution)/shard_map/ppermute | solution.py:420
  261.2 26.0 %collective-permute-start.35 = (bf16[4,96,768]{2,1,0:T(8,128)(2,1)}, bf16[4,96,768]{2,1,0:T(8,128)(2,1)S(1)}, u32[]{:S(2)}, u32[]{:S(2)}) collective-permute-start(bf16[4,96,768]{2,1,0:T(8,128)(2,1)} %get-tuple-element.89), channel_id=1, source_target_pairs={{0,1},{1,0},{2,3},{3,2},{4,5},{5,4},{6,7},{7,6},{8,9},{9,8},{10,11... | collective-permute-start | bytes 1769480 | tf_op jit(solution)/shard_map/ppermute | solution.py:409
  261.7 30.0 %collective-permute-start.44 = (bf16[4,96,1536]{2,1,0:T(8,128)(2,1)}, bf16[4,96,1536]{2,1,0:T(8,128)(2,1)S(1)}, u32[]{:S(2)}, u32[]{:S(2)}) collective-permute-start(bf16[4,96,1536]{2,1,0:T(8,128)(2,1)} %get-tuple-element.95), channel_id=1, source_target_pairs={{0,1},{1,0},{2,3},{3,2},{4,5},{5,4},{6,7},{7,6},{8,9},{9,8},{10,11... | collective-permute-start | bytes 3538952 | tf_op jit(solution)/shard_map/ppermute | solution.py:409
  263.8 28.5 %collective-permute-start.48 = (bf16[4,96,1536]{2,1,0:T(8,128)(2,1)S(1)}, bf16[4,96,1536]{2,1,0:T(8,128)(2,1)S(1)}, u32[]{:S(2)}, u32[]{:S(2)}) collective-permute-start(bf16[4,96,1536]{2,1,0:T(8,128)(2,1)S(1)} %add_convert_fusion.2), channel_id=1, source_target_pairs={{0,8},{1,5},{2,10},{3,7},{8,16},{9,1},{10,18},{11,3},{16,24},{17,9... | collective-permute-start | bytes 3538952 | tf_op jit(solution)/shard_map/ppermute | solution.py:420
  265.6 22.2 %collective-permute-start.37 = (bf16[4,96,768]{2,1,0:T(8,128)(2,1)S(1)}, bf16[4,96,768]{2,1,0:T(8,128)(2,1)S(1)}, u32[]{:S(2)}, u32[]{:S(2)}) collective-permute-start(bf16[4,96,768]{2,1,0:T(8,128)(2,1)S(1)} %add_convert_fusion.7), channel_id=1, source_target_pairs={{0,8},{1,5},{2,10},{3,7},{8,16},{9,1},{10,18},{11,3},{16,24},{17,9... | collective-permute-start | bytes 1769480 | tf_op jit(solution)/shard_map/ppermute | solution.py:420
  268.7 18.5 %collective-permute-start.29 = (f32[9216]{0:T(1024)S(1)}, f32[9216]{0:T(1024)S(1)}, u32[]{:S(2)}, u32[]{:S(2)}) collective-permute-start(f32[9216]{0:T(1024)S(1)} %fusion.11), channel_id=1, source_target_pairs={{0,4},{4,0},{8,12},{12,8},{16,20},{20,16},{24,28},{28,24},{1,5},{5... | collective-permute-start | bytes 110600 | tf_op jit(solution)/shard_map/ppermute | solution.py:410
  287.2 28.5 %collective-permute-start.33 = (bf16[4,96,768]{2,1,0:T(8,128)(2,1)S(1)}, bf16[4,96,768]{2,1,0:T(8,128)(2,1)S(1)}, u32[]{:S(2)}, u32[]{:S(2)}) collective-permute-start(bf16[4,96,768]{2,1,0:T(8,128)(2,1)S(1)} %copy-done.33), channel_id=1, source_target_pairs={{0,1},{1,0},{2,3},{3,2},{4,5},{5,4},{6,7},{7,6},{8,9},{9,8},{10,11... | collective-permute-start | bytes 1769480 | tf_op jit(solution)/shard_map/ppermute | solution.py:409
  291.8 33.6 %collective-permute-start.43 = (bf16[4,96,1536]{2,1,0:T(8,128)(2,1)S(1)}, bf16[4,96,1536]{2,1,0:T(8,128)(2,1)S(1)}, u32[]{:S(2)}, u32[]{:S(2)}) collective-permute-start(bf16[4,96,1536]{2,1,0:T(8,128)(2,1)S(1)} %copy-done.30), channel_id=1, source_target_pairs={{0,1},{1,0},{2,3},{3,2},{4,5},{5,4},{6,7},{7,6},{8,9},{9,8},{10,11... | collective-permute-start | bytes 3538952 | tf_op jit(solution)/shard_map/ppermute | solution.py:409
  291.8 36.6 %collective-permute-start.26 = (bf16[1000,768]{1,0:T(8,128)(2,1)S(1)}, bf16[1000,768]{1,0:T(8,128)(2,1)}, u32[]{:S(2)}, u32[]{:S(2)}) collective-permute-start(bf16[1000,768]{1,0:T(8,128)(2,1)S(1)} %copy-done.5), channel_id=1, source_target_pairs={{0,2},{1,3},{2,0},{3,1},{4,6},{5,7},{6,4},{7,5},{8,10},{9,11},{10,... | collective-permute-start | bytes 4608008 | tf_op jit(solution)/shard_map/ppermute | solution.py:409
  293.0 35.4 %collective-permute-start.49 = (bf16[4,96,1536]{2,1,0:T(8,128)(2,1)S(1)}, bf16[4,96,1536]{2,1,0:T(8,128)(2,1)S(1)}, u32[]{:S(2)}, u32[]{:S(2)}) collective-permute-start(bf16[4,96,1536]{2,1,0:T(8,128)(2,1)S(1)} %add_convert_fusion.1), channel_id=1, source_target_pairs={{0,8},{1,5},{2,10},{3,7},{8,16},{9,1},{10,18},{11,3},{16,24},{17,9... | collective-permute-start | bytes 3538952 | tf_op jit(solution)/shard_map/ppermute | solution.py:420
  315.7 50.4 %collective-permute-start.23 = (bf16[1000,768]{1,0:T(8,128)(2,1)S(1)}, bf16[1000,768]{1,0:T(8,128)(2,1)}, u32[]{:S(2)}, u32[]{:S(2)}) collective-permute-start(bf16[1000,768]{1,0:T(8,128)(2,1)S(1)} %copy-done.3), channel_id=1, source_target_pairs={{0,2},{1,3},{2,0},{3,1},{4,6},{5,7},{6,4},{7,5},{8,10},{9,11},{10,... | collective-permute-start | bytes 4608008 | tf_op jit(solution)/shard_map/ppermute | solution.py:409
  324.3 48.5 %collective-permute-start.25 = (bf16[1000,768]{1,0:T(8,128)(2,1)S(1)}, bf16[1000,768]{1,0:T(8,128)(2,1)}, u32[]{:S(2)}, u32[]{:S(2)}) collective-permute-start(bf16[1000,768]{1,0:T(8,128)(2,1)S(1)} %copy-done.5), channel_id=1, source_target_pairs={{0,1},{1,0},{2,3},{3,2},{4,5},{5,4},{6,7},{7,6},{8,9},{9,8},{10,11... | collective-permute-start | bytes 4608008 | tf_op jit(solution)/shard_map/ppermute | solution.py:409
  325.3 36.2 %collective-permute-start.32 = (f32[9216]{0:T(1024)S(1)}, f32[9216]{0:T(1024)S(1)}, u32[]{:S(2)}, u32[]{:S(2)}) collective-permute-start(f32[9216]{0:T(1024)S(1)} %add.184), channel_id=1, source_target_pairs={{0,2},{1,3},{2,0},{3,1},{4,6},{5,7},{6,4},{7,5},{8,10},{9,11},{10,... | collective-permute-start | bytes 110600 | tf_op jit(solution)/shard_map/ppermute | solution.py:409
  328.4 44.4 %collective-permute-start.27 = (bf16[1000,768]{1,0:T(8,128)(2,1)}, bf16[1000,768]{1,0:T(8,128)(2,1)}, u32[]{:S(2)}, u32[]{:S(2)}) collective-permute-start(bf16[1000,768]{1,0:T(8,128)(2,1)} %collective-permute-done.26.c_ref), channel_id=1, source_target_pairs={{0,1},{1,0},{2,3},{3,2},{4,5},{5,4},{6,7},{7,6},{8,9},{9,8},{10,11... | collective-permute-start | bytes 4608008 | tf_op jit(solution)/shard_map/ppermute | solution.py:409
  328.4 37.7 %collective-permute-start.40 = (bf16[4,96,768]{2,1,0:T(8,128)(2,1)}, bf16[4,96,768]{2,1,0:T(8,128)(2,1)}, u32[]{:S(2)}, u32[]{:S(2)}) collective-permute-start(bf16[4,96,768]{2,1,0:T(8,128)(2,1)} %add_convert_fusion.4), channel_id=1, source_target_pairs={{0,8},{2,10},{8,16},{10,18},{16,24},{18,26},{24,28},{26,30},{28,20... | collective-permute-start | bytes 1769480 | tf_op jit(solution)/shard_map/ppermute | solution.py:420
  361.5 18.7 %collective-permute-start.50 = (bf16[4,96,1536]{2,1,0:T(8,128)(2,1)}, bf16[4,96,1536]{2,1,0:T(8,128)(2,1)}, u32[]{:S(2)}, u32[]{:S(2)}) collective-permute-start(bf16[4,96,1536]{2,1,0:T(8,128)(2,1)} %add_convert_fusion), channel_id=1, source_target_pairs={{0,8},{2,10},{8,16},{10,18},{16,24},{18,26},{24,28},{26,30},{28,20... | collective-permute-start | bytes 3538952 | tf_op jit(solution)/shard_map/ppermute | solution.py:420
  366.1 16.1 %collective-permute-start.22 = (bf16[1000,768]{1,0:T(8,128)(2,1)S(1)}, bf16[1000,768]{1,0:T(8,128)(2,1)}, u32[]{:S(2)}, u32[]{:S(2)}) collective-permute-start(bf16[1000,768]{1,0:T(8,128)(2,1)S(1)} %copy-done.3), channel_id=1, source_target_pairs={{0,1},{1,0},{2,3},{3,2},{4,5},{5,4},{6,7},{7,6},{8,9},{9,8},{10,11... | collective-permute-start | bytes 4608008 | tf_op jit(solution)/shard_map/ppermute | solution.py:409
  366.2 16.1 %collective-permute-start.24 = (bf16[1000,768]{1,0:T(8,128)(2,1)}, bf16[1000,768]{1,0:T(8,128)(2,1)}, u32[]{:S(2)}, u32[]{:S(2)}) collective-permute-start(bf16[1000,768]{1,0:T(8,128)(2,1)} %collective-permute-done.23.c_ref), channel_id=1, source_target_pairs={{0,1},{1,0},{2,3},{3,2},{4,5},{5,4},{6,7},{7,6},{8,9},{9,8},{10,11... | collective-permute-start | bytes 4608008 | tf_op jit(solution)/shard_map/ppermute | solution.py:409
  372.8 16.8 %collective-permute-start.41 = (bf16[2,96,768]{1,2,0:T(8,128)(2,1)S(1)}, bf16[2,96,768]{1,2,0:T(8,128)(2,1)S(1)}, u32[]{:S(2)}, u32[]{:S(2)}) collective-permute-start(bf16[2,96,768]{1,2,0:T(8,128)(2,1)S(1)} %select_bitcast_fusion.1), channel_id=1, source_target_pairs={{0,1},{1,0},{2,3},{3,2},{4,5},{5,4},{6,7},{7,6},{8,9},{9,8},{10,11... | collective-permute-start | bytes 884744 | tf_op jit(solution)/shard_map/ppermute | solution.py:409
  (56 other events, 794.3 us)

commit v6 on v5

--- a/solution.py
+++ b/solution.py
@@ -177,19 +177,41 @@
     loop(mid_ref.shape[0] // 128, norm)
 
 
-def hidden_body(info_ref, h_ref, bias_ref, *refs):
-    act_ref, slope_ref, buf_ref = refs[-3:]
-    place(info_ref, refs[:-3], buf_ref)
-    w = buf_ref[...]
-
-    def chunk(i):
-        rows = cut(i, 256)
-        u = dot(h_ref[rows, :], w) + bias_ref[...]
+def hidden_body(n_chunks, info_ref, halves_ref, h_ref, bias_ref, dy_ref, *refs):
+    chunks, outs = refs[:n_chunks], refs[n_chunks:-6]
+    act_ref, du_ref, sum_ref, *grads = outs
+    wb_ref, wc_ref, ht_ref, dyt_ref, gb_ref, gc_ref = refs[-6:]
+    cols = wb_ref.shape[1]
+
+    @pl.when(pl.program_id(0) == 0)
+    def _():
+        ht_ref[...] = h_ref[...].T
+        dyt_ref[...] = dy_ref[...].T
+
+    place(info_ref, chunks, wb_ref, 0, slice(0, cols))
+    place(info_ref, chunks, wc_ref, 0, slice(cols, 2 * cols))
+    total = jnp.zeros((1, cols), F32)
+    for i in range(ROWS // 256):
+        rows = slice(i * 256, (i + 1) * 256)
+        u = dot(h_ref[rows, :], wb_ref[...]) + bias_ref[...]
         half = 0.5 * (1.0 + lax.erf(u * 0.7071067811865476))
         act_ref[rows, :] = (u * half).astype(BF)
-        slope_ref[rows, :] = (half + u * jnp.exp(-0.5 * u * u) * 0.3989422804014327).astype(BF)
-
-    loop(ROWS // 256, chunk, 4)
+        slope = half + u * jnp.exp(-0.5 * u * u) * 0.3989422804014327
+        du = dot(dy_ref[rows, :], wc_ref[...]) * slope
+        du_ref[rows, :] = du.astype(BF)
+        total = total + colsum(du)
+    sum_ref[...] = jnp.broadcast_to(total, sum_ref.shape)
+    gc_ref[...] = dot(dyt_ref[...], act_ref[...]).astype(BF)
+    gb_ref[...] = dot(ht_ref[...], du_ref[...]).astype(BF)
+    for piece, g_ref in enumerate((gb_ref, gc_ref)):
+        lanes = slice(piece * cols, (piece + 1) * cols)
+        if len(grads) == 1:
+            parts, _, sub, _ = grads[0].shape
+            grads[0][:, 0, :, lanes] = g_ref[...].reshape(parts, sub, cols)
+            continue
+        for n, ref in enumerate(grads):
+            sub = ref.shape[1]
+            ref[0, :, lanes] = g_ref[pl.ds(pl.multiple_of(halves_ref[2 + n] * sub, sub), sub), :]
 
 
 def wide_dot(info_ref, left_ref, refs, buf_ref):
@@ -211,7 +233,9 @@
     out_ref[...] = jnp.where(row < info_ref[1] * SLOT_ROWS, value, 0.0).astype(BF)
 
 
-def weave_body(length, info_ref, a_ref, b_ref, c_ref, d_ref, o_ref):
+def weave_body(length, info_ref, a_ref, b_ref, c_ref, d_ref, *refs):
+    o_ref = refs[-1]
+
     def part(start, n, keep):
         x = jnp.concatenate([r[start : start + n, :] for r in (a_ref, b_ref, c_ref, d_ref)], axis=0)
         row = lax.broadcasted_iota(jnp.int32, (4 * n, 4 * n), 0)
@@ -224,57 +248,6 @@
     for start in range(0, full, 64):
         part(start, 64, 64)
     part(full, 8, length - full)
-
-
-def outer_steps(h_ref, dy_ref, du_ref, act_ref, t_ref, store):
-    step = pl.program_id(0)
-    half = pl.num_programs(0) // 2
-
-    @pl.when(step == 0)
-    def _():
-        t_ref[...] = dy_ref[...].T
-
-    @pl.when(step == half)
-    def _():
-        t_ref[...] = h_ref[...].T
-
-    pl.when(step < half)(lambda: store(dot(t_ref[...], act_ref[...]).astype(BF)))
-    pl.when(step >= half)(lambda: store(dot(t_ref[...], du_ref[...]).astype(BF)))
-
-
-def outer_body(h_ref, dy_ref, du_ref, act_ref, g_ref, t_ref):
-    parts, _, sub, cols = g_ref.shape
-
-    def store(g):
-        g_ref[:, 0] = g.reshape(parts, sub, cols)
-
-    outer_steps(h_ref, dy_ref, du_ref, act_ref, t_ref, store)
-
-
-def outer_halves_body(info_ref, h_ref, dy_ref, du_ref, act_ref, *refs):
-    halves, t_ref, buf_ref = refs[:-2], refs[-2], refs[-1]
-
-    def store(g):
-        buf_ref[...] = g
-        for n, ref in enumerate(halves):
-            sub = ref.shape[1]
-            ref[0] = buf_ref[pl.ds(pl.multiple_of(info_ref[2 + n] * sub, sub), sub), :]
-
-    outer_steps(h_ref, dy_ref, du_ref, act_ref, t_ref, store)
-
-
-def dact_body(info_ref, dy_ref, slope_ref, *refs):
-    du_ref, sum_ref, buf_ref = refs[-3:]
-    place(info_ref, refs[:-3], buf_ref)
-    w = buf_ref[...]
-    cols = w.shape[1]
-    total = jnp.zeros((1, cols), F32)
-    for i in range(ROWS // 256):
-        rows = slice(i * 256, (i + 1) * 256)
-        du = (dot(dy_ref[rows, :], w) * slope_ref[rows, :].astype(F32)).astype(BF)
-        du_ref[rows, :] = du
-        total = total + colsum(du.astype(F32))
-    sum_ref[...] = jnp.broadcast_to(total, sum_ref.shape)
 
 
 def add_rows(sums_ref, rows):
@@ -302,7 +275,7 @@
 
 
 def attend_back_body(slots, q_ref, k_ref, v_ref, p_ref, do_ref, *refs):
-    dq_ref, dk_ref, dv_ref, dp_ref, ds_ref = refs[-5:]
+    dq_ref, dk_ref, dv_ref, dp_ref, ds_ref = refs
     masks = half_masks()
     rows = [slice(i * SLOT_ROWS, (i + 1) * SLOT_ROWS) for i in range(slots)]
 
@@ -402,9 +375,8 @@
     ring = sub % 32 == 0
 
     cycle = list(range(0, parts, 2)) + list(range(parts - 1, 0, -2))
-    place = [cycle.index(d) for d in range(parts)]
-    here = jnp.array(place, jnp.int32)[lax.axis_index("dp")]
-    owner = jnp.array(cycle, jnp.int32)
+    at = lax.axis_index("dp")
+    here = jnp.where(at % 2 == 0, at // 2, parts - 1 - at // 2)
     far = parts // 2
     mp_swap = lambda a, bit: lax.ppermute(a, "mp", [(j, j ^ bit) for j in range(groups)])
     dp_swap = lambda a, bit: lax.ppermute(a, "dp", [(d, d ^ bit) for d in range(parts)])
@@ -424,7 +396,9 @@
     live = lax.dynamic_index_in_dim(counts, mine, 0, keepdims=False)[0]
 
     def info_of(offsets):
-        return jnp.concatenate([jnp.stack([mine, live]), owner[(here + jnp.stack(offsets)) % parts]])
+        spots = here + offsets + 2 * parts
+        spots = spots - parts * (spots // parts)
+        return jnp.concatenate([info, jnp.where(spots < far, 2 * spots, 2 * (parts - spots) - 1)])
 
     smem = pl.BlockSpec(memory_space=pltpu.SMEM)
     info = jnp.stack([mine, live])
@@ -471,8 +445,11 @@
         other_half = mp_swap(other_half.astype(BF), 2)
         return lax.optimization_barrier(mine_half + other_half.astype(F32))
 
-    leave = [jnp.where(even, far - k, k + 1 - far) for k in range(far)]
-    stay = [jnp.where(even, k + 1 - far, far - k) for k in range(far)]
+    to_right = jnp.arange(far, 0, -1, dtype=jnp.int32)
+    to_left = jnp.arange(1 - far, 1, dtype=jnp.int32)
+    halves_info = info_of(
+        jnp.concatenate([jnp.where(even, to_right, to_left), jnp.where(even, to_left, to_right)])
+    )
     halves = lambda n: [sds((groups, sub, n), BF)] * (2 * far)
 
     shard_bc = jnp.concatenate([hidden_weight, down_weight.T], axis=1)
@@ -497,38 +474,32 @@
         first, second = jnp.where(even, half, other), jnp.where(even, other, half)
         return chunks + [jnp.concatenate([first, second])], half
 
+    biases = chip_chunk(row(vectors))[:, 0]
+    qb, vb, hb = (biases[:, a:b].reshape(-1) for a, b in ((0, local), (local, 2 * local), (2 * local, None)))
+    bias_row = row(jnp.concatenate([qb, jnp.zeros_like(qb), vb]))
+
     if ring:
-        side = jnp.where(even, 1, -1)
-        offsets = [jnp.int32(0)]
+        offsets = [0]
         for k in range(1, far):
-            offsets += [-k * side, k * side]
-        ring_info = info_of(offsets + [jnp.int32(far)])
+            offsets += [-k, k]
+        ring_info = info_of(jnp.array(offsets + [far], jnp.int32) * jnp.where(even, 1, -1))
         start_bc = chip_chunk(shard_bc)
-        prepared = [x]
+        prepared = [x, (start_bc, bias_row)]
 
         def between(k, held):
-            if k == 1:
-                held, prepared[0] = lax.optimization_barrier((held, prepared[0]))
+            if k <= 2:
+                held, prepared[k - 1] = lax.optimization_barrier((held, prepared[k - 1]))
             return held
 
-        chunks, last = gather_ring(chip_chunk(shard_a), between)
-        (x,) = prepared
-        start_bc, last = lax.optimization_barrier((start_bc, last))
+        chunks, _ = gather_ring(chip_chunk(shard_a), between)
+        x, (start_bc, bias_row) = prepared
         bc, _ = gather_ring(start_bc, lambda k, held: held)
         piece = lambda n: [pl.BlockSpec((groups, sub, units), lambda i: (0, 0, n))] * len(bc)
-        wcols = lambda n: [pl.BlockSpec((1, sub, units), lambda i: (i, 0, n))] * len(bc)
     else:
         ring_info = info
         wa = lax.all_gather(shard_a, axes, axis=0, tiled=False).reshape(parts, groups, sub, 4 * local)
         bc = [lax.all_gather(shard_bc, axes, axis=0, tiled=False).reshape(parts, groups, sub, 2 * units)]
         piece = lambda n: [pl.BlockSpec((parts, groups, sub, units), lambda i: (0, 0, 0, n))]
-        wcols = lambda n: [pl.BlockSpec((parts, 1, sub, units), lambda i: (0, i, 0, n))]
-    two = jnp.stack([vectors, mp_swap(vectors, 1)])
-    four = jnp.concatenate([two, mp_swap(two, 2)])
-    biases = four[jnp.arange(groups) ^ mine]
-    qb, vb, hb = (biases[:, a:b].reshape(-1) for a, b in ((0, local), (local, 2 * local), (2 * local, None)))
-    bias_row = row(jnp.concatenate([qb, jnp.zeros_like(qb), vb]))
-
     third = lambda n: pl.BlockSpec((n, width), lambda i: (0, i))
     chunks = chunks if ring else [wa]
     h1, qkv, wq, wo = call(
@@ -568,80 +539,53 @@
     tcols = pl.BlockSpec((ROWS, units), lambda i: (0, i))
     vcols = lambda n: pl.BlockSpec((n, units), lambda i: (0, i))
     group_buf = lambda n: pltpu.VMEM((n, width, units), BF)
-    act, slope = call(
-        hidden_body,
-        [t_bf(ff), t_bf(ff)],
-        [ring_info, h2, row(hb)] + bc,
-        [smem, None, vcols(1)] + wcols(0),
-        [tcols, tcols],
+    both = [
+        pl.BlockSpec((1, sub, 2 * units), lambda i: (i, 0, 0))
+        if ring
+        else pl.BlockSpec((parts, 1, sub, 2 * units), lambda i: (0, i, 0, 0))
+    ]
+    grad_shapes = halves(2 * units) if ring else [sds((parts, groups, sub, 2 * units), BF)]
+    act, du, sum_hidden, *halves_bc = call(
+        functools.partial(hidden_body, len(bc)),
+        [t_bf(ff), t_bf(ff), sds((8, ff), F32)] + grad_shapes,
+        [ring_info, halves_info if ring else info, h2, row(hb), dy] + bc,
+        [smem, smem, None, vcols(1), None] + both * len(bc),
+        [tcols, tcols, vcols(8)] + both * len(grad_shapes),
         (groups,),
-        scratch=[pltpu.VMEM((width, units), BF)],
-        flops=4 * mm,
-    )
-    du, sum_hidden = call(
-        dact_body,
-        [t_bf(ff), sds((8, ff), F32)],
-        [ring_info, dy, slope] + bc,
-        [smem, None, tcols] + wcols(1),
-        [tcols, vcols(8)],
-        (groups,),
-        scratch=[pltpu.VMEM((width, units), BF)],
-        flops=4 * mm,
-    )
-    outer_in_specs = [
-        None,
-        None,
-        pl.BlockSpec((ROWS, units), lambda i: (0, jnp.maximum(i - groups, 0))),
-        pl.BlockSpec((ROWS, units), lambda i: (0, jnp.minimum(i, groups - 1))),
-    ]
-    outer_map = lambda i: (0, i % groups, 0, jnp.where(i < groups, 1, 0))
-    transposed = pltpu.VMEM((width, ROWS), BF)
+        scratch=[pltpu.VMEM((width, units), BF)] * 2
+        + [pltpu.VMEM((width, ROWS), BF)] * 2
+        + [pltpu.VMEM((width, units), BF)] * 2,
+        flops=16 * mm,
+    )
+    g_bc = halves_bc[0]
     if ring:
-        halves_bc = call(
-            outer_halves_body,
-            halves(2 * units),
-            [info_of(leave + stay), h2, dy, du, act],
-            [smem] + outer_in_specs,
-            [pl.BlockSpec((1, sub, units), lambda i: outer_map(i)[1:])] * (2 * far),
-            (2 * groups,),
-            scratch=[transposed, pltpu.VMEM((width, units), BF)],
-            flops=8 * mm,
-        )
         s_bc = scatter_ring(halves_bc)
-        g_bc = halves_bc[0]
     else:
-        (g_bc,) = call(
-            outer_body,
-            [sds((parts, groups, sub, 2 * units), BF)],
-            [h2, dy, du, act],
-            outer_in_specs,
-            [pl.BlockSpec((parts, 1, sub, units), outer_map)],
-            (2 * groups,),
-            scratch=[transposed],
-            flops=8 * mm,
-        )
         s_bc = lax.psum_scatter(
             g_bc.reshape(parts * groups, sub, 2 * units), axes, scatter_dimension=0, tiled=False
         ).astype(F32)
 
     own_shape = sds((slots * SLOT_ROWS, width), BF)
 
-    def spread(own):
+    def cross(own):
         crossed = mp_swap(own, 2)
         near = mp_swap(own, 1)
-        far_core = mp_swap(crossed, 1)
+        return [own, near, crossed, mp_swap(crossed, 1)]
+
+    def weave(parts_of, first, woven=()):
         image = pl.BlockSpec((SLOT_ROWS, width), lambda i: (i, 0))
         (woven,) = call(
             functools.partial(weave_body, length),
             [sds((slots, length, groups, width), BF)],
-            [info, own, near, crossed, far_core],
-            [smem] + [image] * 4,
-            [pl.BlockSpec((1, length, groups, width), lambda i: (i, 0, 0, 0))],
-            (slots,),
+            [info, *parts_of, *woven],
+            [smem] + [image] * 4 + [pl.BlockSpec(memory_space=pl.ANY)] * len(woven),
+            [pl.BlockSpec((1, length, groups, width), lambda i: (first + i, 0, 0, 0))],
+            (parts_of[0].shape[0] // SLOT_ROWS,),
             flops=mm,
             limit=24,
+            input_output_aliases={5: 0} if woven else {},
         )
-        return woven.transpose(2, 0, 1, 3)
+        return woven
 
     down_info = jnp.concatenate([info, ring_info[2:]])
     act_late, _ = lax.optimization_barrier((act, g_bc))
@@ -656,7 +600,7 @@
         scratch=[group_buf(groups)],
         flops=4 * mm,
     )
-    all_out = spread(own_out)
+    all_out = weave(cross(own_out), 0).transpose(2, 0, 1, 3)
     du, _ = lax.optimization_barrier((du, own_out))
 
     dmid, dlow, sums_mid = call(
@@ -686,7 +630,7 @@
         *halves_a, sums_qkv = call(
             outer_ring_body,
             halves(4 * local) + [sum_shape],
-            [info_of(leave + stay)] + outer_ins,
+            [halves_info] + outer_ins,
             [smem] + [None] * len(outer_ins),
             scratch=[pltpu.VMEM((groups, width, 4 * local), BF)],
             flops=4 * mm,
@@ -699,20 +643,31 @@
         s_a = lax.psum_scatter(
             g_a.reshape(parts * groups, sub, 4 * local), axes, scatter_dimension=0, tiled=False
         ).astype(F32)
-    own_grad, sums_in = call(
-        input_back_body,
-        [own_shape, sum_shape],
-        [x, dq, dk, dv, wq, dmid, row(norm_gain)],
-        [rows256] * 4 + [None, rows256, None],
-        [rows256, None],
-        (ROWS // 256,),
-        flops=3 * mm,
-    )
+    grad_parts, sums_in = [], 0.0
+    for first, count in ((0, slots - slots // 2), (slots - slots // 2, slots // 2)):
+        rows = count * SLOT_ROWS
+        image = pl.BlockSpec(
+            (pl.Element(rows), pl.Element(width)), lambda i, first=first: (first * SLOT_ROWS, 0)
+        )
+        own_grad, sums_part = call(
+            input_back_body,
+            [sds((rows, width), BF), sum_shape],
+            [x, dq, dk, dv, wq, dmid, row(norm_gain)],
+            [image] * 4 + [None, image, None],
+            [None, None],
+            (1,),
+            flops=3 * mm * count // slots,
+        )
+        grad_parts.append((cross(own_grad), first))
+        sums_in = sums_in + sums_part[:2]
 
     sums = jnp.concatenate(
-        [sums_in[:2].reshape(-1), sums_mid[:4].reshape(-1), sums_qkv[:2].reshape(-1), sum_hidden[0]]
-    )
-    all_grad = spread(own_grad)
+        [sums_in.reshape(-1), sums_mid[:4].reshape(-1), sums_qkv[:2].reshape(-1), sum_hidden[0]]
+    )
+    woven = ()
+    for parts_of, first in grad_parts:
+        woven = (weave(parts_of, first, woven),)
+    all_grad = woven[0].transpose(2, 0, 1, 3)
     steps = [(mp_swap, 1)] + [(dp_swap, 1 << n) for n in range(parts.bit_length() - 1)] + [(mp_swap, 2)]
     for swap, bit in steps:
         other = swap(sums, bit)

time: 411 us -> 393 us (0.956)
  Pallas kernels: 146 us -> 137 us
  waiting for transfers between devices: 145 us -> 140 us
    pallas_call x14, Pallas kernels: 145 us -> 135 us  [call(): pl.pallas_call(body, out_shape=tuple(outs), grid=(1,) if grid is None els...]
    unnamed x78 -> x96, local copies, waits for them, and re-layouts: 14.8 us -> 22.2 us
    ppermute x34 -> x37, waiting for transfers between devices: 46 us -> 40.2 us  [block_step(): lax.ppermute(a, 'mp', [(j, j ^ bit) for j in range(groups)])]
    ppermute x16, waiting for transfers between devices: 67.7 us -> 72.7 us  [hop(): return lax.ppermute(a, axes, pairs)]
    convert_element_type x6, other arithmetic: 3.3 us -> 7.95 us  [scatter_ring(): moved = hop(total.astype(BF))]
    ppermute x3, waiting for transfers between devices: 31.3 us -> 26.9 us  [block_step(): lax.ppermute(a, 'dp', [(d, d ^ bit) for d in range(parts)])]
    ppermute x34 -> x37, starting transfers between devices: 17 us -> 18.6 us  [block_step(): lax.ppermute(a, 'mp', [(j, j ^ bit) for j in range(groups)])]
  transfers between devices with their start and end apart: 53 -> 56, of which waited for: 19 -> 19; matrix products, arithmetic and copies ran while one was open for 15% -> 14% of each run, Pallas kernels for 26% -> 28%
where the time goes in v6:
time: 393 us; the launch traced here: 387 us
  waiting for transfers between devices  140 us (36%)
  Pallas kernels  137 us (35%)
  starting transfers between devices  43.5 us (11%)
  local copies, waits for them, and re-layouts  38.5 us (10%)
  other arithmetic  26.5 us (7%)
    pallas_call x14, Pallas kernels, call(): pl.pallas_call(body, out_shape=tuple(outs), grid=(1,) if grid is None els...  135 us
    ppermute x16, waiting for transfers between devices, hop(): return lax.ppermute(a, axes, pairs)  72.7 us
    ppermute x37, waiting for transfers between devices, block_step(): lax.ppermute(a, 'mp', [(j, j ^ bit) for j in range(groups)])  40.2 us
    ppermute x3, waiting for transfers between devices, block_step(): lax.ppermute(a, 'dp', [(d, d ^ bit) for d in range(parts)])  26.9 us
    ppermute x16, starting transfers between devices, hop(): return lax.ppermute(a, axes, pairs)  24.3 us
    unnamed x96, local copies, waits for them, and re-layouts  22.2 us
    ppermute x37, starting transfers between devices, block_step(): lax.ppermute(a, 'mp', [(j, j ^ bit) for j in range(groups)])  18.6 us
    convert_element_type x6, other arithmetic, scatter_ring(): moved = hop(total.astype(BF))  7.95 us
  transfers between devices with their start and end apart: 56, of which 19 were waited for; matrix products, arithmetic and copies ran while one was open for 14% of the time, Pallas kernels for 28%

profile of v6, /device:TPU:0, one launch (start us, length us, event | category | flops | bytes accessed | tf_op | source)
XLA Modules:
  0.0 386.8 jit_solution(3383400400893022247)
XLA Ops:
  8.9 3.5 copy.34.in_ref
  19.7 7.2 %collective-permute-done.2.refs_1_ = bf16[4,96,768]{2,1,0:T(8,128)(2,1)} collective-permute-done((bf16[4,96,768]{2,1,0:T(8,128)(2,1)S(1)}, bf16[4,96,768]{2,1,0:T(8,128)(2,1)}, u32[]{:S(2)}, u32[]{:S(2)}) %collective-permute-start.2) | collective-permute-done | bytes 589856 | tf_op jit(solution)/shard_map/ppermute | solution.py:392
  29.3 7.9 %collective-permute-done.3.refs_3_ = bf16[4,96,768]{2,1,0:T(8,128)(2,1)} collective-permute-done((bf16[4,96,768]{2,1,0:T(8,128)(2,1)}, bf16[4,96,768]{2,1,0:T(8,128)(2,1)}, u32[]{:S(2)}, u32[]{:S(2)}) %collective-permute-start.3) | collective-permute-done | bytes 589856 | tf_op jit(solution)/shard_map/ppermute | solution.py:392
  39.0 14.4 %collective-permute-done.14.refs_1_ = bf16[4,96,1536]{2,1,0:T(8,128)(2,1)S(1)} collective-permute-done((bf16[4,96,1536]{2,1,0:T(8,128)(2,1)S(1)}, bf16[4,96,1536]{2,1,0:T(8,128)(2,1)S(1)}, u32[]{:S(2)}, u32[]{:S(2)}) %collective-permute-start.14) | collective-permute-done | bytes 1179680 | tf_op jit(solution)/shard_map/ppermute | solution.py:392
  55.2 14.5 %collective-permute-done.16.refs_3_ = bf16[4,96,1536]{2,1,0:T(8,128)(2,1)} collective-permute-done((bf16[4,96,1536]{2,1,0:T(8,128)(2,1)S(1)}, bf16[4,96,1536]{2,1,0:T(8,128)(2,1)}, u32[]{:S(2)}, u32[]{:S(2)}) %collective-permute-start.16) | collective-permute-done | bytes 1179680 | tf_op jit(solution)/shard_map/ppermute | solution.py:392
  77.4 6.1 %copy.35.in_ref = bf16[4,5,197,768]{3,2,1,0:T(8,128)(2,1)} copy(bf16[4,5,197,768]{3,0,2,1:T(4,128)(2,1)} %param.18) | data formatting | bytes 12103680 | tf_op args[1]
  88.3 4.2 %collective-permute-done.10.refs_5_ = bf16[4,96,768]{2,1,0:T(8,128)(2,1)} collective-permute-done((bf16[4,96,768]{2,1,0:T(8,128)(2,1)}, bf16[4,96,768]{2,1,0:T(8,128)(2,1)}, u32[]{:S(2)}, u32[]{:S(2)}) %collective-permute-start.10) | collective-permute-done | bytes 589856 | tf_op jit(solution)/shard_map/ppermute | solution.py:392
  95.6 4.8 %collective-permute-done.12 = bf16[2,96,768]{2,1,0:T(8,128)(2,1)S(1)} collective-permute-done((bf16[2,96,768]{2,1,0:T(8,128)(2,1)S(1)}, bf16[2,96,768]{2,1,0:T(8,128)(2,1)S(1)}, u32[]{:S(2)}, u32[]{:S(2)}) %collective-permute-start.12) | collective-permute-done | bytes 294944 | tf_op jit(solution)/shard_map/ppermute | solution.py:392
  105.0 5.6 %collective-permute-done.20 = bf16[2,96,1536]{2,1,0:T(8,128)(2,1)} collective-permute-done((bf16[2,96,1536]{2,1,0:T(8,128)(2,1)S(1)}, bf16[2,96,1536]{2,1,0:T(8,128)(2,1)}, u32[]{:S(2)}, u32[]{:S(2)}) %collective-permute-start.20) | collective-permute-done | bytes 589856 | tf_op jit(solution)/shard_map/ppermute | solution.py:392
  113.8 11.2 %shard_map.281 = (bf16[1024,768]{1,0:T(8,128)(2,1)}, bf16[1024,2304]{1,0:T(8,128)(2,1)}, bf16[768,2304]{1,0:T(8,128)(2,1)}, bf16[768,768]{1,0:T(8,128)(2,1)}) custom-call(s32[10]{0:T(128)} %get-tuple-element.152.info_ref, bf16[1024,768]{1,0:T(8,128)(2,1)} %copy-done.3, f32[1,768]{1,0:T(1,128)} %reshape.200.gain_ref, f32[1,768]{1,0:T(1,128)} %reshape.201.shift_ref, ...), custom_call_target="tpu_custom_call" | custom-call | flops 3623878656 | bytes 17316904 | tf_op jit(solution)/shard_map/pallas_call | solution.py:54
  125.0 9.6 %shard_map.282 = (bf16[1024,768]{1,0:T(8,128)(2,1)}, bf16[12,5,200,200]{3,2,1,0:T(8,128)(2,1)}) custom-call(bf16[1024,2304]{1,0:T(8,128)(2,1)} %get-tuple-element.64.q_ref.k_ref.v_ref, bf16[1024,2304]{1,0:T(8,128)(2,1)} %get-tuple-element.64.q_ref.k_ref.v_ref, bf16[1024,2304]{1,0:T(8,128)(2,1)} %get-tuple-element.64.q_ref.k_ref.v_ref), custom_call_target="tpu_custom_call" | custom-call | flops 1207959552 | bytes 20528640 | tf_op jit(solution)/shard_map/pallas_call | solution.py:54
  134.6 7.2 %shard_map.283 = (f32[1024,768]{1,0:T(8,128)}, bf16[1024,768]{1,0:T(8,128)(2,1)}) custom-call(bf16[1024,768]{1,0:T(8,128)(2,1)} %copy-done.3, bf16[1024,768]{1,0:T(8,128)(2,1)} %get-tuple-element.65.o_ref, bf16[768,768]{1,0:T(8,128)(2,1)} %get-tuple-element.66.wo_ref, f32[1,768]{1,0:T(1,128)} %reshape.205.bias_ref, f32[1,768]{1,0:T(1,128)} %reshape.206.gain_ref, ...), custom_call_target="tpu_custom_call" | custom-call | flops 1207959552 | bytes 9053184 | tf_op jit(solution)/shard_map/pallas_call | solution.py:54
  145.3 28.2 %shard_map.285 = (bf16[1024,3072]{1,0:T(8,128)(2,1)}, bf16[1024,3072]{1,0:T(8,128)(2,1)}, f32[8,3072]{1,0:T(8,128)}, bf16[4,96,1536]{2,1,0:T(8,128)(2,1)}, bf16[...) custom-call(s32[10]{0:T(128)} %get-tuple-element.152.info_ref, ...), custom_call_target="tpu_custom_call" | custom-call | flops 19327352832 | bytes 34713680 | tf_op jit(solution)/shard_map/pallas_call | solution.py:54
  175.0 10.5 %shard_map.286.a_ref = bf16[1000,768]{1,0:T(8,128)(2,1)} custom-call(s32[10]{0:T(128)} %get-tuple-element.152.info_ref, bf16[1024,3072]{1,0:T(8,128)(2,1)} %get-tuple-element.71.act_ref, f32[1024,768]{1,0:T(8,128)} %get-tuple-element.72.mid_ref, f32[1,768]{1,0:T(1,128)} %reshape.208.bias_ref, bf16[4,96,1536]{2,1,0:T(8,128)(2,1)} %copy-done.10, ...), custom_call_target="tpu_custom_call" | custom-call | flops 4831838208 | bytes 20413480 | tf_op jit(solution)/shard_map/pallas_call | solution.py:54
  185.5 12.5 %shard_map.288 = (f32[1024,768]{1,0:T(8,128)}, bf16[1024,768]{1,0:T(8,128)(2,1)}, f32[8,768]{1,0:T(8,128)}) custom-call(s32[10]{0:T(128)} %get-tuple-element.152.info_ref, bf16[1024,768]{1,0:T(8,128)(2,1)} %copy-done.4, bf16[1024,3072]{1,0:T(8,128)(2,1)} %get-tuple-element.75.du_ref, f32[1024,768]{1,0:T(8,128)} %get-tuple-element.72.mid_ref, ...), custom_call_target="tpu_custom_call" | custom-call | flops 4831838208 | bytes 25193512 | tf_op jit(solution)/shard_map/pallas_call | solution.py:54
  198.0 4.4 %shard_map.289.do_ref = bf16[1024,768]{1,0:T(8,128)(2,1)} custom-call(bf16[1024,768]{1,0:T(8,128)(2,1)} %get-tuple-element.76.dlow_ref, bf16[768,768]{1,0:T(8,128)(2,1)} %get-tuple-element.66.wo_ref), custom_call_target="tpu_custom_call" | custom-call | flops 1207959552 | bytes 4325376 | tf_op jit(solution)/shard_map/pallas_call | solution.py:54
  204.6 12.0 %shard_map.290 = (bf16[1024,768]{1,0:T(8,128)(2,1)}, bf16[1024,768]{1,0:T(8,128)(2,1)}, bf16[1024,768]{1,0:T(8,128)(2,1)}) custom-call(bf16[1024,2304]{1,0:T(8,128)(2,1)} %get-tuple-element.64.q_ref.k_ref.v_ref, bf16[1024,2304]{1,0:T(8,128)(2,1)} %get-tuple-element.64.q_ref.k_ref.v_ref, bf16[1024,2304]{1,0:T(8,128)(2,1)} %get-tuple-element.64.q_ref.k_ref.v_ref, ...), custom_call_target="tpu_custom_call" | custom-call | flops 2415919104 | bytes 25247232 | tf_op jit(solution)/shard_map/pallas_call | solution.py:54
  216.6 11.1 %shard_map.295 = (bf16[4,96,768]{2,1,0:T(8,128)(2,1)}, bf16[4,96,768]{2,1,0:T(8,128)(2,1)}, bf16[4,96,768]{2,1,0:T(8,128)(2,1)}, bf16[4,96,768]{2,1,0:T(8,128)(2...) custom-call(s32[10]{0:T(128)} %get-tuple-element.153.halves_ref.info, ...), custom_call_target="tpu_custom_call" | custom-call | flops 4831838208 | bytes 14180392 | tf_op jit(solution)/shard_map/pallas_call | solution.py:54
  228.2 6.0 %shard_map.291 = (bf16[400,768]{1,0:T(8,128)(2,1)}, f32[8,768]{1,0:T(8,128)}) custom-call(bf16[1024,768]{1,0:T(8,128)(2,1)} %copy-done.3, bf16[1024,768]{1,0:T(8,128)(2,1)} %get-tuple-element.77.dq_ref, bf16[1024,768]{1,0:T(8,128)(2,1)} %get-tuple-element.78.dk_ref, bf16[1024,768]{1,0:T(8,128)(2,1)} %get-tuple-element.79.dv_ref, ...), custom_call_target="tpu_custom_call" | custom-call | flops 1449551488 | bytes 13618176 | tf_op jit(solution)/shard_map/pallas_call | solution.py:54
  234.3 7.8 %shard_map.292 = (bf16[600,768]{1,0:T(8,128)(2,1)}, f32[8,768]{1,0:T(8,128)}) custom-call(bf16[1024,768]{1,0:T(8,128)(2,1)} %copy-done.3, bf16[1024,768]{1,0:T(8,128)(2,1)} %get-tuple-element.77.dq_ref, bf16[1024,768]{1,0:T(8,128)(2,1)} %get-tuple-element.78.dk_ref, bf16[1024,768]{1,0:T(8,128)(2,1)} %get-tuple-element.79.dv_ref, ...), custom_call_target="tpu_custom_call" | custom-call | flops 2174327296 | bytes 13925376 | tf_op jit(solution)/shard_map/pallas_call | solution.py:54
  255.1 18.2 %collective-permute-done.32 = f32[9216]{0:T(1024)S(1)} collective-permute-done((f32[9216]{0:T(1024)S(1)}, f32[9216]{0:T(1024)S(1)}, u32[]{:S(2)}, u32[]{:S(2)}) %collective-permute-start.32) | collective-permute-done | bytes 36896 | tf_op jit(solution)/shard_map/ppermute | solution.py:382
  273.3 3.9 %collective-permute-done.33 = f32[9216]{0:T(1024)S(1)} collective-permute-done((f32[9216]{0:T(1024)S(1)}, f32[9216]{0:T(1024)S(1)}, u32[]{:S(2)}, u32[]{:S(2)}) %collective-permute-start.33) | collective-permute-done | bytes 36896 | tf_op jit(solution)/shard_map/ppermute | solution.py:382
  277.3 4.8 %collective-permute-done.34 = f32[9216]{0:T(1024)S(1)} collective-permute-done((f32[9216]{0:T(1024)S(1)}, f32[9216]{0:T(1024)S(1)}, u32[]{:S(2)}, u32[]{:S(2)}) %collective-permute-start.34) | collective-permute-done | bytes 36896 | tf_op jit(solution)/shard_map/ppermute | solution.py:382
  292.1 6.4 %collective-permute-done.41 = bf16[4,96,768]{2,1,0:T(8,128)(2,1)S(1)} collective-permute-done((bf16[4,96,768]{2,1,0:T(8,128)(2,1)S(1)}, bf16[4,96,768]{2,1,0:T(8,128)(2,1)S(1)}, u32[]{:S(2)}, u32[]{:S(2)}) %collective-permute-start.41) | collective-permute-done | bytes 589856 | tf_op jit(solution)/shard_map/ppermute | solution.py:392
  298.8 22.5 %collective-permute-done.26.c_ref = bf16[400,768]{1,0:T(8,128)(2,1)S(1)} collective-permute-done((bf16[400,768]{1,0:T(8,128)(2,1)S(1)}, bf16[400,768]{1,0:T(8,128)(2,1)S(1)}, u32[]{:S(2)}, u32[]{:S(2)}) %collective-permute-start.26) | collective-permute-done | bytes 614432 | tf_op jit(solution)/shard_map/ppermute | solution.py:381
  323.7 7.7 %collective-permute-done.42 = bf16[4,96,768]{2,1,0:T(8,128)(2,1)} collective-permute-done((bf16[4,96,768]{2,1,0:T(8,128)(2,1)S(1)}, bf16[4,96,768]{2,1,0:T(8,128)(2,1)}, u32[]{:S(2)}, u32[]{:S(2)}) %collective-permute-start.42) | collective-permute-done | bytes 589856 | tf_op jit(solution)/shard_map/ppermute | solution.py:392
  335.8 3.2 add_convert_fusion
  344.1 5.4 %shard_map.293.refs_0_ = bf16[5,197,4,768]{3,2,1,0:T(4,128)(2,1)} custom-call(s32[2]{0:T(128)S(1)} %pad_add_fusion.info_ref, bf16[600,768]{1,0:T(8,128)(2,1)} %get-tuple-element.83.a_ref, bf16[600,768]{1,0:T(8,128)(2,1)} %collective-permute-done.28.b_ref, bf16[600,768]{1,0:T(8,128)(2,1)} %collective-permute-done.29.c_ref, ...), custom_call_target="tpu_custom_call" | custom-call | flops 1207959552 | bytes 9738248 | tf_op jit(solution)/shard_map/pallas_call | solution.py:54
  349.5 6.3 %collective-permute-done.23.c_ref = bf16[1000,768]{1,0:T(8,128)(2,1)S(1)} collective-permute-done((bf16[1000,768]{1,0:T(8,128)(2,1)S(1)}, bf16[1000,768]{1,0:T(8,128)(2,1)S(1)}, u32[]{:S(2)}, u32[]{:S(2)}) %collective-permute-start.23) | collective-permute-done | bytes 1536032 | tf_op jit(solution)/shard_map/ppermute | solution.py:381
  365.6 6.7 %shard_map.287 = bf16[5,197,4,768]{3,2,1,0:T(4,128)(2,1)} custom-call(s32[2]{0:T(128)S(1)} %pad_add_fusion.info_ref, bf16[1000,768]{1,0:T(8,128)(2,1)S(1)} %copy-done.5, bf16[1000,768]{1,0:T(8,128)(2,1)} %collective-permute-done.22.b_ref, bf16[1000,768]{1,0:T(8,128)(2,1)S(1)} %collective-permute-done.23.c_ref, bf16[1000,768]{1,0:T(8,128)(2,1)} %collective-permute-done.24.d_ref), custom_call_target="tpu_custom_call" | custom-call | flops 1207959552 | bytes 12195848 | tf_op jit(solution)/shard_map/pallas_call | solution.py:54
  374.9 5.4 %collective-permute-done.45 = bf16[96,768]{0,1:T(8,128)(2,1)S(1)} collective-permute-done((bf16[96,768]{0,1:T(8,128)(2,1)S(1)}, bf16[96,768]{0,1:T(8,128)(2,1)S(1)}, u32[]{:S(2)}, u32[]{:S(2)}) %collective-permute-start.45) | collective-permute-done | bytes 147488 | tf_op jit(solution)/shard_map/ppermute | solution.py:381
  381.8 3.8 collective-permute-done.55
  (275 shorter events, 102.2 us)
Async XLA Ops:
  1.7 13.9 %collective-permute-start.4 = (bf16[96,1536]{1,0:T(8,128)(2,1)S(1)}, bf16[96,1536]{1,0:T(8,128)(2,1)S(1)}, u32[]{:S(2)}, u32[]{:S(2)}) collective-permute-start(bf16[96,1536]{1,0:T(8,128)(2,1)S(1)} %get-tuple-element.137), channel_id=1, source_target_pairs={{0,2},{1,3},{2,0},{3,1},{4,6},{5,7},{6,4},{7,5},{8,10},{9,11},{10,... | collective-permute-start | bytes 884744 | tf_op jit(solution)/shard_map/ppermute | solution.py:381
  15.8 13.1 %collective-permute-start.5 = (bf16[2,96,1536]{2,1,0:T(8,128)(2,1)S(1)}, bf16[2,96,1536]{2,1,0:T(8,128)(2,1)S(1)}, u32[]{:S(2)}, u32[]{:S(2)}) collective-permute-start(bf16[2,96,1536]{2,1,0:T(8,128)(2,1)S(1)} %pad_maximum_fusion.3), channel_id=1, source_target_pairs={{0,1},{1,0},{2,3},{3,2},{4,5},{5,4},{6,7},{7,6},{8,9},{9,8},{10,11... | collective-permute-start | bytes 1769480 | tf_op jit(solution)/shard_map/ppermute | solution.py:381
  27.0 10.2 %collective-permute-start.3 = (bf16[4,96,768]{2,1,0:T(8,128)(2,1)}, bf16[4,96,768]{2,1,0:T(8,128)(2,1)}, u32[]{:S(2)}, u32[]{:S(2)}) collective-permute-start(bf16[4,96,768]{2,1,0:T(8,128)(2,1)} %collective-permute-done.2.refs_1_), channel_id=1, source_target_pairs={{0,8},{1,5},{2,10},{3,7},{8,16},{9,1},{10,18},{11,3},{16,24},{17,9... | collective-permute-start | bytes 1769480 | tf_op jit(solution)/shard_map/ppermute | solution.py:392
  37.2 16.2 %collective-permute-start.14 = (bf16[4,96,1536]{2,1,0:T(8,128)(2,1)S(1)}, bf16[4,96,1536]{2,1,0:T(8,128)(2,1)S(1)}, u32[]{:S(2)}, u32[]{:S(2)}) collective-permute-start(bf16[4,96,1536]{2,1,0:T(8,128)(2,1)S(1)} %pad_maximum_fusion.refs_0_), channel_id=1, source_target_pairs={{0,8},{1,5},{2,10},{3,7},{8,16},{9,1},{10,18},{11,3},{16,24},{17,9... | collective-permute-start | bytes 3538952 | tf_op jit(solution)/shard_map/ppermute | solution.py:392
  53.4 16.3 %collective-permute-start.16 = (bf16[4,96,1536]{2,1,0:T(8,128)(2,1)S(1)}, bf16[4,96,1536]{2,1,0:T(8,128)(2,1)}, u32[]{:S(2)}, u32[]{:S(2)}) collective-permute-start(bf16[4,96,1536]{2,1,0:T(8,128)(2,1)S(1)} %collective-permute-done.14.refs_1_), channel_id=1, source_target_pairs={{0,8},{1,5},{2,10},{3,7},{8,16},{9,1},{10,18},{11,3},{16,24},{17,9... | collective-permute-start | bytes 3538952 | tf_op jit(solution)/shard_map/ppermute | solution.py:392
  69.7 30.7 %collective-permute-start.18 = (bf16[4,96,1536]{2,1,0:T(8,128)(2,1)}, bf16[4,96,1536]{2,1,0:T(8,128)(2,1)S(1)}, u32[]{:S(2)}, u32[]{:S(2)}) collective-permute-start(bf16[4,96,1536]{2,1,0:T(8,128)(2,1)} %collective-permute-done.16.refs_3_), channel_id=1, source_target_pairs={{0,8},{1,5},{2,10},{3,7},{8,16},{9,1},{10,18},{11,3},{16,24},{17,9... | collective-permute-start | bytes 3538952 | tf_op jit(solution)/shard_map/ppermute | solution.py:392
  71.5 21.0 %collective-permute-start.10 = (bf16[4,96,768]{2,1,0:T(8,128)(2,1)}, bf16[4,96,768]{2,1,0:T(8,128)(2,1)}, u32[]{:S(2)}, u32[]{:S(2)}) collective-permute-start(bf16[4,96,768]{2,1,0:T(8,128)(2,1)} %collective-permute-done.3.refs_3_), channel_id=1, source_target_pairs={{0,8},{1,5},{2,10},{3,7},{8,16},{9,1},{10,18},{11,3},{16,24},{17,9... | collective-permute-start | bytes 1769480 | tf_op jit(solution)/shard_map/ppermute | solution.py:392
  110.5 31.3 %collective-permute-start.21 = (bf16[2,96,1536]{2,1,0:T(8,128)(2,1)}, bf16[2,96,1536]{2,1,0:T(8,128)(2,1)}, u32[]{:S(2)}, u32[]{:S(2)}) collective-permute-start(bf16[2,96,1536]{2,1,0:T(8,128)(2,1)} %collective-permute-done.20), channel_id=1, source_target_pairs={{0,1},{1,0},{2,3},{3,2},{4,5},{5,4},{6,7},{7,6},{8,9},{9,8},{10,11... | collective-permute-start | bytes 1769480 | tf_op jit(solution)/shard_map/ppermute | solution.py:381
  111.4 32.9 %collective-permute-start.15 = (bf16[4,96,1536]{2,1,0:T(8,128)(2,1)S(1)}, bf16[4,96,1536]{2,1,0:T(8,128)(2,1)S(1)}, u32[]{:S(2)}, u32[]{:S(2)}) collective-permute-start(bf16[4,96,1536]{2,1,0:T(8,128)(2,1)S(1)} %collective-permute-done.14.refs_1_), channel_id=1, source_target_pairs={{0,1},{1,0},{2,3},{3,2},{4,5},{5,4},{6,7},{7,6},{8,9},{9,8},{10,11... | collective-permute-start | bytes 3538952 | tf_op jit(solution)/shard_map/ppermute | solution.py:381
  111.9 32.4 %collective-permute-start.17 = (bf16[4,96,1536]{2,1,0:T(8,128)(2,1)}, bf16[4,96,1536]{2,1,0:T(8,128)(2,1)}, u32[]{:S(2)}, u32[]{:S(2)}) collective-permute-start(bf16[4,96,1536]{2,1,0:T(8,128)(2,1)} %collective-permute-done.16.refs_3_), channel_id=1, source_target_pairs={{0,1},{1,0},{2,3},{3,2},{4,5},{5,4},{6,7},{7,6},{8,9},{9,8},{10,11... | collective-permute-start | bytes 3538952 | tf_op jit(solution)/shard_map/ppermute | solution.py:381
  112.0 32.3 %collective-permute-start.19 = (bf16[4,96,1536]{2,1,0:T(8,128)(2,1)S(1)}, bf16[4,96,1536]{2,1,0:T(8,128)(2,1)}, u32[]{:S(2)}, u32[]{:S(2)}) collective-permute-start(bf16[4,96,1536]{2,1,0:T(8,128)(2,1)S(1)} %collective-permute-done.18.refs_5_), channel_id=1, source_target_pairs={{0,1},{1,0},{2,3},{3,2},{4,5},{5,4},{6,7},{7,6},{8,9},{9,8},{10,11... | collective-permute-start | bytes 3538952 | tf_op jit(solution)/shard_map/ppermute | solution.py:381
  173.5 28.9 %collective-permute-start.49 = (bf16[4,96,1536]{2,1,0:T(8,128)(2,1)}, bf16[4,96,1536]{2,1,0:T(8,128)(2,1)S(1)}, u32[]{:S(2)}, u32[]{:S(2)}) collective-permute-start(bf16[4,96,1536]{2,1,0:T(8,128)(2,1)} %get-tuple-element.104), channel_id=1, source_target_pairs={{0,1},{1,0},{2,3},{3,2},{4,5},{5,4},{6,7},{7,6},{8,9},{9,8},{10,11... | collective-permute-start | bytes 3538952 | tf_op jit(solution)/shard_map/ppermute | solution.py:381
  174.5 73.2 %collective-permute-start.48 = (bf16[4,96,1536]{2,1,0:T(8,128)(2,1)}, bf16[4,96,1536]{2,1,0:T(8,128)(2,1)}, u32[]{:S(2)}, u32[]{:S(2)}) collective-permute-start(bf16[4,96,1536]{2,1,0:T(8,128)(2,1)} %get-tuple-element.103), channel_id=1, source_target_pairs={{0,1},{1,0},{2,3},{3,2},{4,5},{5,4},{6,7},{7,6},{8,9},{9,8},{10,11... | collective-permute-start | bytes 3538952 | tf_op jit(solution)/shard_map/ppermute | solution.py:381
  174.7 113.5 %collective-permute-start.47 = (bf16[4,96,1536]{2,1,0:T(8,128)(2,1)}, bf16[4,96,1536]{2,1,0:T(8,128)(2,1)}, u32[]{:S(2)}, u32[]{:S(2)}) collective-permute-start(bf16[4,96,1536]{2,1,0:T(8,128)(2,1)} %get-tuple-element.101), channel_id=1, source_target_pairs={{0,1},{1,0},{2,3},{3,2},{4,5},{5,4},{6,7},{7,6},{8,9},{9,8},{10,11... | collective-permute-start | bytes 3538952 | tf_op jit(solution)/shard_map/ppermute | solution.py:381
  202.7 45.0 %collective-permute-start.50 = (bf16[4,96,1536]{2,1,0:T(8,128)(2,1)S(1)}, bf16[4,96,1536]{2,1,0:T(8,128)(2,1)S(1)}, u32[]{:S(2)}, u32[]{:S(2)}) collective-permute-start(bf16[4,96,1536]{2,1,0:T(8,128)(2,1)S(1)} %add_convert_fusion.3), channel_id=1, source_target_pairs={{0,8},{1,5},{2,10},{3,7},{8,16},{9,1},{10,18},{11,3},{16,24},{17,9... | collective-permute-start | bytes 3538952 | tf_op jit(solution)/shard_map/ppermute | solution.py:392
  227.7 23.9 %collective-permute-start.39 = (bf16[4,96,768]{2,1,0:T(8,128)(2,1)}, bf16[4,96,768]{2,1,0:T(8,128)(2,1)}, u32[]{:S(2)}, u32[]{:S(2)}) collective-permute-start(bf16[4,96,768]{2,1,0:T(8,128)(2,1)} %get-tuple-element.97), channel_id=1, source_target_pairs={{0,1},{1,0},{2,3},{3,2},{4,5},{5,4},{6,7},{7,6},{8,9},{9,8},{10,11... | collective-permute-start | bytes 1769480 | tf_op jit(solution)/shard_map/ppermute | solution.py:381
  227.7 54.4 %collective-permute-start.38 = (bf16[4,96,768]{2,1,0:T(8,128)(2,1)}, bf16[4,96,768]{2,1,0:T(8,128)(2,1)}, u32[]{:S(2)}, u32[]{:S(2)}) collective-permute-start(bf16[4,96,768]{2,1,0:T(8,128)(2,1)} %get-tuple-element.95), channel_id=1, source_target_pairs={{0,1},{1,0},{2,3},{3,2},{4,5},{5,4},{6,7},{7,6},{8,9},{9,8},{10,11... | collective-permute-start | bytes 1769480 | tf_op jit(solution)/shard_map/ppermute | solution.py:381
  249.7 39.0 %collective-permute-start.51 = (bf16[4,96,1536]{2,1,0:T(8,128)(2,1)S(1)}, bf16[4,96,1536]{2,1,0:T(8,128)(2,1)S(1)}, u32[]{:S(2)}, u32[]{:S(2)}) collective-permute-start(bf16[4,96,1536]{2,1,0:T(8,128)(2,1)S(1)} %add_convert_fusion.2), channel_id=1, source_target_pairs={{0,8},{1,5},{2,10},{3,7},{8,16},{9,1},{10,18},{11,3},{16,24},{17,9... | collective-permute-start | bytes 3538952 | tf_op jit(solution)/shard_map/ppermute | solution.py:392
  252.9 29.8 %collective-permute-start.40 = (bf16[4,96,768]{2,1,0:T(8,128)(2,1)S(1)}, bf16[4,96,768]{2,1,0:T(8,128)(2,1)S(1)}, u32[]{:S(2)}, u32[]{:S(2)}) collective-permute-start(bf16[4,96,768]{2,1,0:T(8,128)(2,1)S(1)} %add_convert_fusion.7), channel_id=1, source_target_pairs={{0,8},{1,5},{2,10},{3,7},{8,16},{9,1},{10,18},{11,3},{16,24},{17,9... | collective-permute-start | bytes 1769480 | tf_op jit(solution)/shard_map/ppermute | solution.py:392
  254.6 18.7 %collective-permute-start.32 = (f32[9216]{0:T(1024)S(1)}, f32[9216]{0:T(1024)S(1)}, u32[]{:S(2)}, u32[]{:S(2)}) collective-permute-start(f32[9216]{0:T(1024)S(1)} %fusion.11), channel_id=1, source_target_pairs={{0,4},{4,0},{8,12},{12,8},{16,20},{20,16},{24,28},{28,24},{1,5},{5... | collective-permute-start | bytes 110600 | tf_op jit(solution)/shard_map/ppermute | solution.py:382
  286.7 35.5 %collective-permute-start.29 = (bf16[600,768]{1,0:T(8,128)(2,1)}, bf16[600,768]{1,0:T(8,128)(2,1)}, u32[]{:S(2)}, u32[]{:S(2)}) collective-permute-start(bf16[600,768]{1,0:T(8,128)(2,1)} %get-tuple-element.83.a_ref), channel_id=1, source_target_pairs={{0,2},{1,3},{2,0},{3,1},{4,6},{5,7},{6,4},{7,5},{8,10},{9,11},{10,... | collective-permute-start | bytes 2764808 | tf_op jit(solution)/shard_map/ppermute | solution.py:381
  288.2 33.2 %collective-permute-start.26 = (bf16[400,768]{1,0:T(8,128)(2,1)S(1)}, bf16[400,768]{1,0:T(8,128)(2,1)S(1)}, u32[]{:S(2)}, u32[]{:S(2)}) collective-permute-start(bf16[400,768]{1,0:T(8,128)(2,1)S(1)} %copy-done.6), channel_id=1, source_target_pairs={{0,2},{1,3},{2,0},{3,1},{4,6},{5,7},{6,4},{7,5},{8,10},{9,11},{10,... | collective-permute-start | bytes 1843208 | tf_op jit(solution)/shard_map/ppermute | solution.py:381
  291.6 41.5 %collective-permute-start.28 = (bf16[600,768]{1,0:T(8,128)(2,1)}, bf16[600,768]{1,0:T(8,128)(2,1)}, u32[]{:S(2)}, u32[]{:S(2)}) collective-permute-start(bf16[600,768]{1,0:T(8,128)(2,1)} %get-tuple-element.83.a_ref), channel_id=1, source_target_pairs={{0,1},{1,0},{2,3},{3,2},{4,5},{5,4},{6,7},{7,6},{8,9},{9,8},{10,11... | collective-permute-start | bytes 2764808 | tf_op jit(solution)/shard_map/ppermute | solution.py:381
  291.7 42.1 %collective-permute-start.46 = (bf16[4,96,1536]{2,1,0:T(8,128)(2,1)}, bf16[4,96,1536]{2,1,0:T(8,128)(2,1)}, u32[]{:S(2)}, u32[]{:S(2)}) collective-permute-start(bf16[4,96,1536]{2,1,0:T(8,128)(2,1)} %get-tuple-element.99), channel_id=1, source_target_pairs={{0,1},{1,0},{2,3},{3,2},{4,5},{5,4},{6,7},{7,6},{8,9},{9,8},{10,11... | collective-permute-start | bytes 3538952 | tf_op jit(solution)/shard_map/ppermute | solution.py:381
  298.6 35.3 %collective-permute-start.52 = (bf16[4,96,1536]{2,1,0:T(8,128)(2,1)}, bf16[4,96,1536]{2,1,0:T(8,128)(2,1)}, u32[]{:S(2)}, u32[]{:S(2)}) collective-permute-start(bf16[4,96,1536]{2,1,0:T(8,128)(2,1)} %add_convert_fusion.1), channel_id=1, source_target_pairs={{0,8},{1,5},{2,10},{3,7},{8,16},{9,1},{10,18},{11,3},{16,24},{17,9... | collective-permute-start | bytes 3538952 | tf_op jit(solution)/shard_map/ppermute | solution.py:392
  322.2 33.6 %collective-permute-start.23 = (bf16[1000,768]{1,0:T(8,128)(2,1)S(1)}, bf16[1000,768]{1,0:T(8,128)(2,1)S(1)}, u32[]{:S(2)}, u32[]{:S(2)}) collective-permute-start(bf16[1000,768]{1,0:T(8,128)(2,1)S(1)} %copy-done.5), channel_id=1, source_target_pairs={{0,2},{1,3},{2,0},{3,1},{4,6},{5,7},{6,4},{7,5},{8,10},{9,11},{10,... | collective-permute-start | bytes 4608008 | tf_op jit(solution)/shard_map/ppermute | solution.py:381
  333.2 16.3 %collective-permute-start.25 = (bf16[400,768]{1,0:T(8,128)(2,1)S(1)}, bf16[400,768]{1,0:T(8,128)(2,1)S(1)}, u32[]{:S(2)}, u32[]{:S(2)}) collective-permute-start(bf16[400,768]{1,0:T(8,128)(2,1)S(1)} %copy-done.7), channel_id=1, source_target_pairs={{0,1},{1,0},{2,3},{3,2},{4,5},{5,4},{6,7},{7,6},{8,9},{9,8},{10,11... | collective-permute-start | bytes 1843208 | tf_op jit(solution)/shard_map/ppermute | solution.py:381
  333.8 22.0 %collective-permute-start.27 = (bf16[400,768]{1,0:T(8,128)(2,1)S(1)}, bf16[400,768]{1,0:T(8,128)(2,1)S(1)}, u32[]{:S(2)}, u32[]{:S(2)}) collective-permute-start(bf16[400,768]{1,0:T(8,128)(2,1)S(1)} %copy-done.9), channel_id=1, source_target_pairs={{0,1},{1,0},{2,3},{3,2},{4,5},{5,4},{6,7},{7,6},{8,9},{9,8},{10,11... | collective-permute-start | bytes 1843208 | tf_op jit(solution)/shard_map/ppermute | solution.py:381
  333.9 24.5 %collective-permute-start.43 = (bf16[4,96,768]{2,1,0:T(8,128)(2,1)S(1)}, bf16[4,96,768]{2,1,0:T(8,128)(2,1)S(1)}, u32[]{:S(2)}, u32[]{:S(2)}) collective-permute-start(bf16[4,96,768]{2,1,0:T(8,128)(2,1)S(1)} %add_convert_fusion.4), channel_id=1, source_target_pairs={{0,8},{2,10},{8,16},{10,18},{16,24},{18,26},{24,28},{26,30},{28,20... | collective-permute-start | bytes 1769480 | tf_op jit(solution)/shard_map/ppermute | solution.py:392
  339.0 24.5 %collective-permute-start.53 = (bf16[4,96,1536]{2,1,0:T(8,128)(2,1)}, bf16[4,96,1536]{2,1,0:T(8,128)(2,1)}, u32[]{:S(2)}, u32[]{:S(2)}) collective-permute-start(bf16[4,96,1536]{2,1,0:T(8,128)(2,1)} %add_convert_fusion), channel_id=1, source_target_pairs={{0,8},{2,10},{8,16},{10,18},{16,24},{18,26},{24,28},{26,30},{28,20... | collective-permute-start | bytes 3538952 | tf_op jit(solution)/shard_map/ppermute | solution.py:392
  349.5 16.1 %collective-permute-start.22 = (bf16[1000,768]{1,0:T(8,128)(2,1)S(1)}, bf16[1000,768]{1,0:T(8,128)(2,1)}, u32[]{:S(2)}, u32[]{:S(2)}) collective-permute-start(bf16[1000,768]{1,0:T(8,128)(2,1)S(1)} %copy-done.5), channel_id=1, source_target_pairs={{0,1},{1,0},{2,3},{3,2},{4,5},{5,4},{6,7},{7,6},{8,9},{9,8},{10,11... | collective-permute-start | bytes 4608008 | tf_op jit(solution)/shard_map/ppermute | solution.py:381
  374.3 11.4 %collective-permute-start.55 = (bf16[96,1536]{1,0:T(8,128)(2,1)S(1)}, bf16[96,1536]{1,0:T(8,128)(2,1)S(1)}, u32[]{:S(2)}, u32[]{:S(2)}) collective-permute-start(bf16[96,1536]{1,0:T(8,128)(2,1)S(1)} %fusion), channel_id=1, source_target_pairs={{0,2},{1,3},{2,0},{3,1},{4,6},{5,7},{6,4},{7,5},{8,10},{9,11},{10,... | collective-permute-start | bytes 884744 | tf_op jit(solution)/shard_map/ppermute | solution.py:381
  (68 other events, 857.5 us)

commit v7 on v6

--- a/solution.py
+++ b/solution.py
@@ -190,16 +190,18 @@
 
     place(info_ref, chunks, wb_ref, 0, slice(0, cols))
     place(info_ref, chunks, wc_ref, 0, slice(cols, 2 * cols))
-    total = jnp.zeros((1, cols), F32)
-    for i in range(ROWS // 256):
-        rows = slice(i * 256, (i + 1) * 256)
+
+    def chunk(i, total):
+        rows = cut(i, 256)
         u = dot(h_ref[rows, :], wb_ref[...]) + bias_ref[...]
         half = 0.5 * (1.0 + lax.erf(u * 0.7071067811865476))
         act_ref[rows, :] = (u * half).astype(BF)
         slope = half + u * jnp.exp(-0.5 * u * u) * 0.3989422804014327
         du = dot(dy_ref[rows, :], wc_ref[...]) * slope
         du_ref[rows, :] = du.astype(BF)
-        total = total + colsum(du)
+        return total + colsum(du)
+
+    total = lax.fori_loop(0, ROWS // 256, chunk, jnp.zeros((1, cols), F32), unroll=2)
     sum_ref[...] = jnp.broadcast_to(total, sum_ref.shape)
     gc_ref[...] = dot(dyt_ref[...], act_ref[...]).astype(BF)
     gb_ref[...] = dot(ht_ref[...], du_ref[...]).astype(BF)
@@ -274,8 +276,8 @@
     do_ref[...] = dot(dlow_ref[...], wo_ref[...]).astype(BF)
 
 
-def attend_back_body(slots, q_ref, k_ref, v_ref, p_ref, do_ref, *refs):
-    dq_ref, dk_ref, dv_ref, dp_ref, ds_ref = refs
+def attend_back_body(slots, q_ref, k_ref, v_ref, p_ref, do_ref, o_ref, dqkvo_ref, dp_ref, ds_ref):
+    dqkvo_ref[3] = o_ref[...]
     masks = half_masks()
     rows = [slice(i * SLOT_ROWS, (i + 1) * SLOT_ROWS) for i in range(slots)]
 
@@ -285,7 +287,7 @@
         for h in range(2):
             dp_ref[h, i] = dot(jnp.where(masks[h], v, jnp.zeros_like(v)), do, NT)
         dv = [dot(p_ref[h, i], do) for h in range(2)]
-        dv_ref[rows[i], :] = jnp.where(masks[0], *dv).astype(BF)
+        dqkvo_ref[2, rows[i], :] = jnp.where(masks[0], *dv).astype(BF)
 
     def softmax_back(i):
         for h in range(2):
@@ -297,9 +299,9 @@
         q = q_ref[rows[i], :] * jnp.bfloat16(0.125)
         k_t = (k_ref[rows[i], :] * jnp.bfloat16(0.125)).T
         dk = [dot(ds_ref[h, i], q) for h in range(2)]
-        dk_ref[rows[i], :] = jnp.where(masks[0], *dk).astype(BF)
+        dqkvo_ref[1, rows[i], :] = jnp.where(masks[0], *dk).astype(BF)
         dq = [dot(k_t[h * HEAD_DIM : (h + 1) * HEAD_DIM], ds_ref[h, i]) for h in range(2)]
-        dq_ref[rows[i], :] = jnp.concatenate(dq, axis=0).T.astype(BF)
+        dqkvo_ref[0, rows[i], :] = jnp.concatenate(dq, axis=0).T.astype(BF)
 
     for i in range(slots):
         upstream(i)
@@ -308,56 +310,62 @@
     for i in range(slots):
         downstream(i)
     tail = slots * SLOT_ROWS
-    for ref in (dq_ref, dk_ref, dv_ref):
-        ref[tail:, :] = jnp.zeros((ROWS - tail, 2 * HEAD_DIM), BF)
-
-
-def small_outer(h_ref, dq_ref, dk_ref, dv_ref, dlow_ref, o_ref, sums_ref, store):
-    ht = h_ref[...].T
-    for s, ref in enumerate((dq_ref, dk_ref, dv_ref)):
-        store(s, dot(ht, ref[...]).astype(BF))
-        if s != 1:
-            n = 0 if s == 0 else 1
-            sums_ref[n : n + 1, :] = colsum(ref[...].astype(F32))
-    store(3, dot(dlow_ref[...].T, o_ref[...]).astype(BF))
-
-
-def outer_ring_body(info_ref, h_ref, dq_ref, dk_ref, dv_ref, dlow_ref, o_ref, *refs):
-    halves, sums_ref, buf_ref = refs[:-2], refs[-2], refs[-1]
-    groups = buf_ref.shape[0]
-    local = h_ref.shape[1] // groups
-
-    def store(s, g):
-        for j in range(groups):
-            buf_ref[j, :, s * local : (s + 1) * local] = g[:, j * local : (j + 1) * local]
-
-    small_outer(h_ref, dq_ref, dk_ref, dv_ref, dlow_ref, o_ref, sums_ref, store)
-    for n, ref in enumerate(halves):
-        sub = ref.shape[1]
-        rows = pl.ds(pl.multiple_of(info_ref[2 + n] * sub, sub), sub)
-        for j in range(groups):
-            ref[j] = buf_ref[j, rows, :]
-
-
-def outer_plain_body(h_ref, dq_ref, dk_ref, dv_ref, dlow_ref, o_ref, g_ref, sums_ref):
-    parts, groups, sub, cols = g_ref.shape
-    local = cols // 4
-
-    def store(s, g):
-        for j in range(groups):
-            g_ref[:, j, :, s * local : (s + 1) * local] = g[:, j * local : (j + 1) * local].reshape(parts, sub, local)
-
-    small_outer(h_ref, dq_ref, dk_ref, dv_ref, dlow_ref, o_ref, sums_ref, store)
-
-
-def input_back_body(x_ref, dq_ref, dk_ref, dv_ref, wq_ref, dmid_ref, gain_ref, out_ref, sums_ref):
+    dqkvo_ref[:3, tail:, :] = jnp.zeros((3, ROWS - tail, 2 * HEAD_DIM), BF)
+
+
+def outer_body(info_ref, h_ref, d_ref, dlow_ref, *refs):
+    grads, sums_ref, t_ref, g_ref = refs[:-3], refs[-3], refs[-2], refs[-1]
+    width = h_ref.shape[1]
+    step = pl.program_id(0)
+
+    @pl.when(step == 0)
+    def _():
+        t_ref[...] = h_ref[...].T
+        sums_ref[...] = jnp.zeros_like(sums_ref)
+
+    @pl.when(step == 3)
+    def _():
+        t_ref[...] = dlow_ref[...].T
+
+    g_ref[...] = dot(t_ref[...], d_ref[0]).astype(BF)
+    for n, s in enumerate((0, 2)):
+
+        @pl.when(step == s)
+        def _(n=n):
+            sums_ref[n : n + 1, :] = colsum(d_ref[0].astype(F32))
+
+    def store(s):
+        if len(grads) == 1:
+            parts, groups, sub, _ = grads[0].shape
+            local = width // groups
+            for j in range(groups):
+                block = g_ref[:, j * local : (j + 1) * local].reshape(parts, sub, local)
+                grads[0][:, j, :, s * local : (s + 1) * local] = block
+            return
+        for n, ref in enumerate(grads):
+            groups, sub, _ = ref.shape
+            local = width // groups
+            rows = g_ref[pl.ds(pl.multiple_of(info_ref[2 + n] * sub, sub), sub), :]
+            for j in range(groups):
+                ref[j, :, s * local : (s + 1) * local] = rows[:, j * local : (j + 1) * local]
+
+    for s in range(4):
+        pl.when(step == s)(functools.partial(store, s))
+
+
+def input_back_body(x_ref, d_ref, wq_ref, dmid_ref, gain_ref, out_ref, sums_ref):
     width = x_ref.shape[1]
-    dh = sum(
-        dot(ref[...], wq_ref[:, s * width : (s + 1) * width], NT) for s, ref in enumerate((dq_ref, dk_ref, dv_ref))
-    )
+    dh = sum(dot(d_ref[s], wq_ref[:, s * width : (s + 1) * width], NT) for s in range(3))
     normal, scale_inv = norm_stats(x_ref[...].astype(F32))
     out_ref[...] = (dmid_ref[...] + norm_back(dh, normal, scale_inv, gain_ref[...])).astype(BF)
     add_rows(sums_ref, (dh * normal, dh))
+
+
+def finish_body(mine_ref, other_ref, qkv_ref, out_ref):
+    total = mine_ref[...] + other_ref[...].astype(F32)
+    cols = qkv_ref.shape[1]
+    qkv_ref[...] = total[:, :cols]
+    out_ref[...] = total[:, cols:].T
 
 
 def block_step(
@@ -443,7 +451,7 @@
         total = mine_half.astype(F32) + other_half.astype(F32)
         mine_half, other_half = split(total[0], total[1], mine < 2)
         other_half = mp_swap(other_half.astype(BF), 2)
-        return lax.optimization_barrier(mine_half + other_half.astype(F32))
+        return mine_half, other_half
 
     to_right = jnp.arange(far, 0, -1, dtype=jnp.int32)
     to_left = jnp.arange(1 - far, 1, dtype=jnp.int32)
@@ -484,15 +492,15 @@
             offsets += [-k, k]
         ring_info = info_of(jnp.array(offsets + [far], jnp.int32) * jnp.where(even, 1, -1))
         start_bc = chip_chunk(shard_bc)
-        prepared = [x, (start_bc, bias_row)]
+        prepared = [(x, bias_row)]
 
         def between(k, held):
-            if k <= 2:
-                held, prepared[k - 1] = lax.optimization_barrier((held, prepared[k - 1]))
+            if k == 2:
+                held, prepared[0] = lax.optimization_barrier((held, prepared[0]))
             return held
 
         chunks, _ = gather_ring(chip_chunk(shard_a), between)
-        x, (start_bc, bias_row) = prepared
+        ((x, bias_row),) = prepared
         bc, _ = gather_ring(start_bc, lambda k, held: held)
         piece = lambda n: [pl.BlockSpec((groups, sub, units), lambda i: (0, 0, n))] * len(bc)
     else:
@@ -559,7 +567,8 @@
     )
     g_bc = halves_bc[0]
     if ring:
-        s_bc = scatter_ring(halves_bc)
+        s_bc, other = scatter_ring(halves_bc)
+        s_bc = s_bc + other.astype(F32)
     else:
         s_bc = lax.psum_scatter(
             g_bc.reshape(parts * groups, sub, 2 * units), axes, scatter_dimension=0, tiled=False
@@ -572,20 +581,19 @@
         near = mp_swap(own, 1)
         return [own, near, crossed, mp_swap(crossed, 1)]
 
-    def weave(parts_of, first, woven=()):
+    def weave(parts_of):
         image = pl.BlockSpec((SLOT_ROWS, width), lambda i: (i, 0))
         (woven,) = call(
             functools.partial(weave_body, length),
             [sds((slots, length, groups, width), BF)],
-            [info, *parts_of, *woven],
-            [smem] + [image] * 4 + [pl.BlockSpec(memory_space=pl.ANY)] * len(woven),
-            [pl.BlockSpec((1, length, groups, width), lambda i: (first + i, 0, 0, 0))],
-            (parts_of[0].shape[0] // SLOT_ROWS,),
+            [info, *parts_of],
+            [smem] + [image] * 4,
+            [pl.BlockSpec((1, length, groups, width), lambda i: (i, 0, 0, 0))],
+            (slots,),
             flops=mm,
             limit=24,
-            input_output_aliases={5: 0} if woven else {},
         )
-        return woven
+        return woven.transpose(2, 0, 1, 3)
 
     down_info = jnp.concatenate([info, ring_info[2:]])
     act_late, _ = lax.optimization_barrier((act, g_bc))
@@ -600,7 +608,7 @@
         scratch=[group_buf(groups)],
         flops=4 * mm,
     )
-    all_out = weave(cross(own_out), 0).transpose(2, 0, 1, 3)
+    all_out = weave(cross(own_out))
     du, _ = lax.optimization_barrier((du, own_out))
 
     dmid, dlow, sums_mid = call(
@@ -614,60 +622,50 @@
         flops=4 * mm,
     )
     (do,) = call(out_back_body, [t_bf(width)], [dlow, wo], flops=mm)
-    dq, dk, dv = call(
+    (dqkvo,) = call(
         functools.partial(attend_back_body, slots),
-        [t_bf(width)] * 3,
-        [qkv, qkv, qkv, probs, do],
-        [head(0), head(1), head(2), p_spec, head(0)],
-        [head(0)] * 3,
+        [sds((4, ROWS, width), BF)],
+        [qkv, qkv, qkv, probs, do, mixed],
+        [head(0), head(1), head(2), p_spec, head(0), head(0)],
+        [pl.BlockSpec((4, ROWS, pair), lambda i: (0, 0, i))],
         (pairs,),
         scratch=[pltpu.VMEM((2, slots, SLOT_ROWS, SLOT_ROWS), dtype) for dtype in (F32, BF)],
         flops=2 * mm,
     )
-    outer_ins = [h1, dq, dk, dv, dlow, mixed]
     sum_shape = sds((8, width), F32)
+    grad_shapes = halves(4 * local) if ring else [sds((parts, groups, sub, 4 * local), BF)]
+    *halves_a, sums_qkv = call(
+        outer_body,
+        grad_shapes + [sum_shape],
+        [halves_info if ring else info, h1, dqkvo, dlow],
+        [smem, None, pl.BlockSpec((1, ROWS, width), lambda i: (i, 0, 0)), None],
+        grid=(4,),
+        scratch=[pltpu.VMEM((width, ROWS), BF), pltpu.VMEM((width, width), BF)],
+        flops=4 * mm,
+    )
     if ring:
-        *halves_a, sums_qkv = call(
-            outer_ring_body,
-            halves(4 * local) + [sum_shape],
-            [halves_info] + outer_ins,
-            [smem] + [None] * len(outer_ins),
-            scratch=[pltpu.VMEM((groups, width, 4 * local), BF)],
-            flops=4 * mm,
+        s_qkv, s_out = call(
+            finish_body, [sds((sub, 3 * local), F32), sds((local, sub), F32)], scatter_ring(halves_a), limit=16
         )
-        s_a = scatter_ring(halves_a)
     else:
-        g_a, sums_qkv = call(
-            outer_plain_body, [sds((parts, groups, sub, 4 * local), BF), sum_shape], outer_ins, flops=4 * mm
-        )
         s_a = lax.psum_scatter(
-            g_a.reshape(parts * groups, sub, 4 * local), axes, scatter_dimension=0, tiled=False
+            halves_a[0].reshape(parts * groups, sub, 4 * local), axes, scatter_dimension=0, tiled=False
         ).astype(F32)
-    grad_parts, sums_in = [], 0.0
-    for first, count in ((0, slots - slots // 2), (slots - slots // 2, slots // 2)):
-        rows = count * SLOT_ROWS
-        image = pl.BlockSpec(
-            (pl.Element(rows), pl.Element(width)), lambda i, first=first: (first * SLOT_ROWS, 0)
-        )
-        own_grad, sums_part = call(
-            input_back_body,
-            [sds((rows, width), BF), sum_shape],
-            [x, dq, dk, dv, wq, dmid, row(norm_gain)],
-            [image] * 4 + [None, image, None],
-            [None, None],
-            (1,),
-            flops=3 * mm * count // slots,
-        )
-        grad_parts.append((cross(own_grad), first))
-        sums_in = sums_in + sums_part[:2]
+        s_qkv, s_out = s_a[:, : 3 * local], s_a[:, 3 * local :].T
+    own_grad, sums_in = call(
+        input_back_body,
+        [own_shape, sum_shape],
+        [x, dqkvo, wq, dmid, row(norm_gain)],
+        [rows256, pl.BlockSpec((3, 256, width), lambda i: (0, i, 0)), None, rows256, None],
+        [rows256, None],
+        (ROWS // 256,),
+        flops=3 * mm,
+    )
+    all_grad = weave(cross(own_grad))
 
     sums = jnp.concatenate(
-        [sums_in.reshape(-1), sums_mid[:4].reshape(-1), sums_qkv[:2].reshape(-1), sum_hidden[0]]
-    )
-    woven = ()
-    for parts_of, first in grad_parts:
-        woven = (weave(parts_of, first, woven),)
-    all_grad = woven[0].transpose(2, 0, 1, 3)
+        [sums_in[:2].reshape(-1), sums_mid[:4].reshape(-1), sums_qkv[:2].reshape(-1), sum_hidden[0]]
+    )
     steps = [(mp_swap, 1)] + [(dp_swap, 1 << n) for n in range(parts.bit_length() - 1)] + [(mp_swap, 2)]
     for swap, bit in steps:
         other = swap(sums, bit)
@@ -679,10 +677,10 @@
         all_grad,
         vec[0],
         vec[1],
-        s_a[:, : 3 * local],
+        s_qkv,
         own(vec[6], local),
         own(vec[7], local),
-        s_a[:, 3 * local :].T,
+        s_out,
         vec[4],
         vec[2],
         vec[3],

time: 393 us -> 340 us (0.87); the launches traced: 387 us -> 338 us
  waiting for transfers between devices: 140 us -> 96.6 us
  local copies, waits for them, and re-layouts: 38.5 us -> 30.1 us
  starting transfers between devices: 43.5 us -> 49.1 us
    ppermute x16, waiting for transfers between devices: 72.7 us -> 39.1 us  [hop(): return lax.ppermute(a, axes, pairs)]
    ppermute x16, starting transfers between devices: 24.3 us -> 31.4 us  [hop(): return lax.ppermute(a, axes, pairs)]
    ppermute x37 -> x34, waiting for transfers between devices: 40.2 us -> 33.4 us  [block_step(): lax.ppermute(a, 'mp', [(j, j ^ bit) for j in range(groups)])]
    unnamed x96 -> x73, local copies, waits for them, and re-layouts: 22.2 us -> 16.5 us
    pallas_call x14 -> x13, Pallas kernels: 135 us -> 133 us  [call(): pl.pallas_call(body, out_shape=tuple(outs), grid=(1,) if grid is None els...]
    ppermute x37 -> x34, starting transfers between devices: 18.6 us -> 17.2 us  [block_step(): lax.ppermute(a, 'mp', [(j, j ^ bit) for j in range(groups)])]
  transfers between devices with their start and end apart: 56 -> 53, of which waited for: 19 -> 20; matrix products, arithmetic and copies ran while one was open for 14% -> 14% of each run, Pallas kernels for 28% -> 31%
where the time goes in v7:
time: 340 us; the launch traced here: 338 us
  Pallas kernels  135 us (40%)
  waiting for transfers between devices  96.6 us (28%)
  starting transfers between devices  49.1 us (14%)
  local copies, waits for them, and re-layouts  30.1 us (9%)
  other arithmetic  26.3 us (8%)
    pallas_call x13, Pallas kernels, call(): pl.pallas_call(body, out_shape=tuple(outs), grid=(1,) if grid is None els...  133 us
    ppermute x16, waiting for transfers between devices, hop(): return lax.ppermute(a, axes, pairs)  39.1 us
    ppermute x34, waiting for transfers between devices, block_step(): lax.ppermute(a, 'mp', [(j, j ^ bit) for j in range(groups)])  33.4 us
    ppermute x16, starting transfers between devices, hop(): return lax.ppermute(a, axes, pairs)  31.4 us
    ppermute x3, waiting for transfers between devices, block_step(): lax.ppermute(a, 'dp', [(d, d ^ bit) for d in range(parts)])  24.1 us
    ppermute x34, starting transfers between devices, block_step(): lax.ppermute(a, 'mp', [(j, j ^ bit) for j in range(groups)])  17.2 us
    unnamed x73, local copies, waits for them, and re-layouts  16.5 us
    convert_element_type x6, other arithmetic, scatter_ring(): moved = hop(total.astype(BF))  9.19 us
  transfers between devices with their start and end apart: 53, of which 20 were waited for; matrix products, arithmetic and copies ran while one was open for 14% of the time, Pallas kernels for 31%

profile of v7, /device:TPU:0, one launch (start us, length us, event | category | flops | bytes accessed | tf_op | source)
XLA Modules:
  0.0 338.1 jit_solution(7529698279231156530)
XLA Ops:
  1.8 3.0 collective-permute-start.12
  4.8 7.0 %collective-permute-done.12 = bf16[96,1536]{1,0:T(8,128)(2,1)S(1)} collective-permute-done((bf16[96,1536]{1,0:T(8,128)(2,1)S(1)}, bf16[96,1536]{1,0:T(8,128)(2,1)S(1)}, u32[]{:S(2)}, u32[]{:S(2)}) %collective-permute-start.12) | collective-permute-done | bytes 294944 | tf_op jit(solution)/shard_map/ppermute | solution.py:389
  24.7 6.0 %collective-permute-done.14.refs_1_ = bf16[4,96,1536]{2,1,0:T(8,128)(2,1)S(1)} collective-permute-done((bf16[4,96,1536]{2,1,0:T(8,128)(2,1)S(1)}, bf16[4,96,1536]{2,1,0:T(8,128)(2,1)S(1)}, u32[]{:S(2)}, u32[]{:S(2)}) %collective-permute-start.14) | collective-permute-done | bytes 1179680 | tf_op jit(solution)/shard_map/ppermute | solution.py:400
  32.7 3.5 %copy.38.in_ref = bf16[4,5,197,768]{3,2,1,0:T(8,128)(2,1)S(1)} copy(bf16[4,5,197,768]{3,0,2,1:T(4,128)(2,1)} %param.17) | data formatting | bytes 12103680 | tf_op args[0]
  40.8 8.9 %collective-permute-done.16.refs_3_ = bf16[4,96,1536]{2,1,0:T(8,128)(2,1)S(1)} collective-permute-done((bf16[4,96,1536]{2,1,0:T(8,128)(2,1)S(1)}, bf16[4,96,1536]{2,1,0:T(8,128)(2,1)S(1)}, u32[]{:S(2)}, u32[]{:S(2)}) %collective-permute-start.16) | collective-permute-done | bytes 1179680 | tf_op jit(solution)/shard_map/ppermute | solution.py:400
  52.1 4.0 %collective-permute-done.3.refs_3_ = bf16[4,96,768]{2,1,0:T(8,128)(2,1)} collective-permute-done((bf16[4,96,768]{2,1,0:T(8,128)(2,1)}, bf16[4,96,768]{2,1,0:T(8,128)(2,1)}, u32[]{:S(2)}, u32[]{:S(2)}) %collective-permute-start.3) | collective-permute-done | bytes 589856 | tf_op jit(solution)/shard_map/ppermute | solution.py:400
  63.5 6.1 %copy.39.in_ref = bf16[4,5,197,768]{3,2,1,0:T(8,128)(2,1)} copy(bf16[4,5,197,768]{3,0,2,1:T(4,128)(2,1)} %param.18) | data formatting | bytes 12103680 | tf_op args[1]
  70.9 2.7 copy-done.2
  78.1 4.8 %collective-permute-done.10 = bf16[2,96,768]{2,1,0:T(8,128)(2,1)S(1)} collective-permute-done((bf16[2,96,768]{2,1,0:T(8,128)(2,1)S(1)}, bf16[2,96,768]{2,1,0:T(8,128)(2,1)S(1)}, u32[]{:S(2)}, u32[]{:S(2)}) %collective-permute-start.10) | collective-permute-done | bytes 294944 | tf_op jit(solution)/shard_map/ppermute | solution.py:400
  88.0 5.3 %collective-permute-done.20 = bf16[2,96,1536]{2,1,0:T(8,128)(2,1)} collective-permute-done((bf16[2,96,1536]{2,1,0:T(8,128)(2,1)S(1)}, bf16[2,96,1536]{2,1,0:T(8,128)(2,1)}, u32[]{:S(2)}, u32[]{:S(2)}) %collective-permute-start.20) | collective-permute-done | bytes 589856 | tf_op jit(solution)/shard_map/ppermute | solution.py:400
  96.4 10.7 %shard_map.281 = (bf16[1024,768]{1,0:T(8,128)(2,1)}, bf16[1024,2304]{1,0:T(8,128)(2,1)}, bf16[768,2304]{1,0:T(8,128)(2,1)}, bf16[768,768]{1,0:T(8,128)(2,1)}) custom-call(s32[10]{0:T(128)} %get-tuple-element.125.info_ref, bf16[1024,768]{1,0:T(8,128)(2,1)} %copy-done.4, f32[1,768]{1,0:T(1,128)} %reshape.202.gain_ref, f32[1,768]{1,0:T(1,128)} %reshape.203.shift_ref, ...), custom_call_target="tpu_custom_call" | custom-call | flops 3623878656 | bytes 17316904 | tf_op jit(solution)/shard_map/pallas_call | solution.py:54
  107.1 9.6 %shard_map.282 = (bf16[1024,768]{1,0:T(8,128)(2,1)}, bf16[12,5,200,200]{3,2,1,0:T(8,128)(2,1)}) custom-call(bf16[1024,2304]{1,0:T(8,128)(2,1)} %get-tuple-element.58.q_ref.k_ref.v_ref, bf16[1024,2304]{1,0:T(8,128)(2,1)} %get-tuple-element.58.q_ref.k_ref.v_ref, bf16[1024,2304]{1,0:T(8,128)(2,1)} %get-tuple-element.58.q_ref.k_ref.v_ref), custom_call_target="tpu_custom_call" | custom-call | flops 1207959552 | bytes 20528640 | tf_op jit(solution)/shard_map/pallas_call | solution.py:54
  116.7 7.2 %shard_map.283 = (f32[1024,768]{1,0:T(8,128)}, bf16[1024,768]{1,0:T(8,128)(2,1)}) custom-call(bf16[1024,768]{1,0:T(8,128)(2,1)} %copy-done.4, bf16[1024,768]{1,0:T(8,128)(2,1)} %get-tuple-element.59.o_ref, bf16[768,768]{1,0:T(8,128)(2,1)} %get-tuple-element.60.wo_ref, f32[1,768]{1,0:T(1,128)} %reshape.204.bias_ref, f32[1,768]{1,0:T(1,128)} %reshape.205.gain_ref, ...), custom_call_target="tpu_custom_call" | custom-call | flops 1207959552 | bytes 9053184 | tf_op jit(solution)/shard_map/pallas_call | solution.py:54
  126.4 29.4 %shard_map.285 = (bf16[1024,3072]{1,0:T(8,128)(2,1)}, bf16[1024,3072]{1,0:T(8,128)(2,1)}, f32[8,3072]{1,0:T(8,128)}, bf16[4,96,1536]{2,1,0:T(8,128)(2,1)}, bf16[...) custom-call(s32[10]{0:T(128)} %get-tuple-element.125.info_ref, ...), custom_call_target="tpu_custom_call" | custom-call | flops 19327352832 | bytes 34713680 | tf_op jit(solution)/shard_map/pallas_call | solution.py:54
  162.6 10.4 %shard_map.286.a_ref = bf16[1000,768]{1,0:T(8,128)(2,1)} custom-call(s32[10]{0:T(128)} %get-tuple-element.125.info_ref, bf16[1024,3072]{1,0:T(8,128)(2,1)} %get-tuple-element.64.act_ref, f32[1024,768]{1,0:T(8,128)} %get-tuple-element.65.mid_ref, f32[1,768]{1,0:T(1,128)} %reshape.207.bias_ref, bf16[4,96,1536]{2,1,0:T(8,128)(2,1)} %copy-done.7, ...), custom_call_target="tpu_custom_call" | custom-call | flops 4831838208 | bytes 20413480 | tf_op jit(solution)/shard_map/pallas_call | solution.py:54
  173.0 12.5 %shard_map.288 = (f32[1024,768]{1,0:T(8,128)}, bf16[1024,768]{1,0:T(8,128)(2,1)}, f32[8,768]{1,0:T(8,128)}) custom-call(s32[10]{0:T(128)} %get-tuple-element.125.info_ref, bf16[1024,768]{1,0:T(8,128)(2,1)} %copy-done.3, bf16[1024,3072]{1,0:T(8,128)(2,1)} %get-tuple-element.68.du_ref, f32[1024,768]{1,0:T(8,128)} %get-tuple-element.65.mid_ref, ...), custom_call_target="tpu_custom_call" | custom-call | flops 4831838208 | bytes 25193512 | tf_op jit(solution)/shard_map/pallas_call | solution.py:54
  185.5 4.3 %shard_map.289.do_ref = bf16[1024,768]{1,0:T(8,128)(2,1)} custom-call(bf16[1024,768]{1,0:T(8,128)(2,1)} %get-tuple-element.69.dlow_ref, bf16[768,768]{1,0:T(8,128)(2,1)} %get-tuple-element.60.wo_ref), custom_call_target="tpu_custom_call" | custom-call | flops 1207959552 | bytes 4325376 | tf_op jit(solution)/shard_map/pallas_call | solution.py:54
  189.8 12.9 %shard_map.290.d_ref = bf16[4,1024,768]{2,1,0:T(8,128)(2,1)} custom-call(bf16[1024,2304]{1,0:T(8,128)(2,1)} %get-tuple-element.58.q_ref.k_ref.v_ref, bf16[1024,2304]{1,0:T(8,128)(2,1)} %get-tuple-element.58.q_ref.k_ref.v_ref, bf16[1024,2304]{1,0:T(8,128)(2,1)} %get-tuple-element.58.q_ref.k_ref.v_ref, bf16[12,5,200,200]{3,2,1,0:T(8,128)(2,1)} %get-tuple-element.66.p_ref, ...), custom_call_target="tpu_custom_call" | custom-call | flops 2415919104 | bytes 28392960 | tf_op jit(solution)/shard_map/pallas_call | solution.py:54
  206.5 14.3 %shard_map.293 = (bf16[4,96,768]{2,1,0:T(8,128)(2,1)}, bf16[4,96,768]{2,1,0:T(8,128)(2,1)}, bf16[4,96,768]{2,1,0:T(8,128)(2,1)}, bf16[4,96,768]{2,1,0:T(8,128)(2...) custom-call(s32[10]{0:T(128)} %get-tuple-element.126.halves_ref.info, ...), custom_call_target="tpu_custom_call" | custom-call | flops 4831838208 | bytes 14180392 | tf_op jit(solution)/shard_map/pallas_call | solution.py:54
  229.0 5.3 %collective-permute-done.37 = bf16[4,96,768]{2,1,0:T(8,128)(2,1)S(1)} collective-permute-done((bf16[4,96,768]{2,1,0:T(8,128)(2,1)S(1)}, bf16[4,96,768]{2,1,0:T(8,128)(2,1)S(1)}, u32[]{:S(2)}, u32[]{:S(2)}) %collective-permute-start.37) | collective-permute-done | bytes 589856 | tf_op jit(solution)/shard_map/ppermute | solution.py:400
  239.2 9.8 %shard_map.291 = (bf16[1000,768]{1,0:T(8,128)(2,1)}, f32[8,768]{1,0:T(8,128)}) custom-call(bf16[1024,768]{1,0:T(8,128)(2,1)} %copy-done.4, bf16[4,1024,768]{2,1,0:T(8,128)(2,1)} %shard_map.290.d_ref, bf16[768,2304]{1,0:T(8,128)(2,1)} %get-tuple-element.70.wq_ref, f32[1024,768]{1,0:T(8,128)} %get-tuple-element.71.dmid_ref, f32[1,768]{1,0:T(1,128)} %reshape.202.gain_ref), custom_call_target="tpu_custom_call" | custom-call | flops 3623878656 | bytes 16112640 | tf_op jit(solution)/shard_map/pallas_call | solution.py:54
  250.8 2.6 collective-permute-done.38
  258.4 3.2 add_convert_fusion
  261.6 3.4 %collective-permute-start.50 = (bf16[4,96,1536]{2,1,0:T(8,128)(2,1)}, bf16[4,96,1536]{2,1,0:T(8,128)(2,1)}, u32[]{:S(2)}, u32[]{:S(2)}) collective-permute-start(bf16[4,96,1536]{2,1,0:T(8,128)(2,1)} %add_convert_fusion), channel_id=1, source_target_pairs={{0,8},{2,10},{8,16},{10,18},{16,24},{18,26},{24,28},{26,30},{28,20... | collective-permute-start | bytes 3538952 | tf_op jit(solution)/shard_map/ppermute | solution.py:400
  267.7 3.5 %collective-permute-start.40 = (bf16[4,96,768]{2,1,0:T(8,128)(2,1)}, bf16[4,96,768]{2,1,0:T(8,128)(2,1)}, u32[]{:S(2)}, u32[]{:S(2)}) collective-permute-start(bf16[4,96,768]{2,1,0:T(8,128)(2,1)} %add_convert_fusion.4), channel_id=1, source_target_pairs={{0,8},{2,10},{8,16},{10,18},{16,24},{18,26},{24,28},{26,30},{28,20... | collective-permute-start | bytes 1769480 | tf_op jit(solution)/shard_map/ppermute | solution.py:400
  271.7 15.3 %collective-permute-done.29 = f32[9216]{0:T(1024)S(1)} collective-permute-done((f32[9216]{0:T(1024)S(1)}, f32[9216]{0:T(1024)S(1)}, u32[]{:S(2)}, u32[]{:S(2)}) %collective-permute-start.29) | collective-permute-done | bytes 36896 | tf_op jit(solution)/shard_map/ppermute | solution.py:390
  287.0 3.9 %collective-permute-done.30 = f32[9216]{0:T(1024)S(1)} collective-permute-done((f32[9216]{0:T(1024)S(1)}, f32[9216]{0:T(1024)S(1)}, u32[]{:S(2)}, u32[]{:S(2)}) %collective-permute-start.30) | collective-permute-done | bytes 36896 | tf_op jit(solution)/shard_map/ppermute | solution.py:390
  291.0 4.8 %collective-permute-done.31 = f32[9216]{0:T(1024)S(1)} collective-permute-done((f32[9216]{0:T(1024)S(1)}, f32[9216]{0:T(1024)S(1)}, u32[]{:S(2)}, u32[]{:S(2)}) %collective-permute-start.31) | collective-permute-done | bytes 36896 | tf_op jit(solution)/shard_map/ppermute | solution.py:390
  296.4 8.2 %collective-permute-done.32 = f32[9216]{0:T(1024)S(1)} collective-permute-done((f32[9216]{0:T(1024)S(1)}, f32[9216]{0:T(1024)S(1)}, u32[]{:S(2)}, u32[]{:S(2)}) %collective-permute-start.32) | collective-permute-done | bytes 36896 | tf_op jit(solution)/shard_map/ppermute | solution.py:389
  312.5 5.9 %shard_map.292 = bf16[5,197,4,768]{3,2,1,0:T(4,128)(2,1)} custom-call(s32[2]{0:T(128)S(1)} %pad_add_fusion.info_ref, bf16[1000,768]{1,0:T(8,128)(2,1)S(1)} %copy-done.6, bf16[1000,768]{1,0:T(8,128)(2,1)S(1)} %collective-permute-done.25.b_ref, bf16[1000,768]{1,0:T(8,128)(2,1)} %collective-permute-done.26.c_ref, ...), custom_call_target="tpu_custom_call" | custom-call | flops 1207959552 | bytes 12195848 | tf_op jit(solution)/shard_map/pallas_call | solution.py:54
  318.5 5.2 %shard_map.287 = bf16[5,197,4,768]{3,2,1,0:T(4,128)(2,1)} custom-call(s32[2]{0:T(128)S(1)} %pad_add_fusion.info_ref, bf16[1000,768]{1,0:T(8,128)(2,1)S(1)} %copy-done.5, bf16[1000,768]{1,0:T(8,128)(2,1)S(1)} %collective-permute-done.22.b_ref, bf16[1000,768]{1,0:T(8,128)(2,1)S(1)} %collective-permute-done.23.c_ref, ...), custom_call_target="tpu_custom_call" | custom-call | flops 1207959552 | bytes 12195848 | tf_op jit(solution)/shard_map/pallas_call | solution.py:54
  326.3 10.1 %collective-permute-done.42.other_ref = bf16[96,768]{1,0:T(8,128)(2,1)S(1)} collective-permute-done((bf16[96,768]{1,0:T(8,128)(2,1)S(1)}, bf16[96,768]{1,0:T(8,128)(2,1)S(1)}, u32[]{:S(2)}, u32[]{:S(2)}) %collective-permute-start.42) | collective-permute-done | bytes 147488 | tf_op jit(solution)/shard_map/ppermute | solution.py:389
  (242 shorter events, 92.8 us)
Async XLA Ops:
  14.5 16.3 %collective-permute-start.14 = (bf16[4,96,1536]{2,1,0:T(8,128)(2,1)S(1)}, bf16[4,96,1536]{2,1,0:T(8,128)(2,1)S(1)}, u32[]{:S(2)}, u32[]{:S(2)}) collective-permute-start(bf16[4,96,1536]{2,1,0:T(8,128)(2,1)S(1)} %pad_maximum_fusion.refs_0_), channel_id=1, source_target_pairs={{0,8},{1,5},{2,10},{3,7},{8,16},{9,1},{10,18},{11,3},{16,24},{17,9... | collective-permute-start | bytes 3538952 | tf_op jit(solution)/shard_map/ppermute | solution.py:400
  21.3 16.9 %collective-permute-start.2 = (bf16[4,96,768]{2,1,0:T(8,128)(2,1)}, bf16[4,96,768]{2,1,0:T(8,128)(2,1)}, u32[]{:S(2)}, u32[]{:S(2)}) collective-permute-start(bf16[4,96,768]{2,1,0:T(8,128)(2,1)} %pad_maximum_fusion.2.refs_0_), channel_id=1, source_target_pairs={{0,8},{1,5},{2,10},{3,7},{8,16},{9,1},{10,18},{11,3},{16,24},{17,9... | collective-permute-start | bytes 1769480 | tf_op jit(solution)/shard_map/ppermute | solution.py:400
  30.7 19.0 %collective-permute-start.16 = (bf16[4,96,1536]{2,1,0:T(8,128)(2,1)S(1)}, bf16[4,96,1536]{2,1,0:T(8,128)(2,1)S(1)}, u32[]{:S(2)}, u32[]{:S(2)}) collective-permute-start(bf16[4,96,1536]{2,1,0:T(8,128)(2,1)S(1)} %collective-permute-done.14.refs_1_), channel_id=1, source_target_pairs={{0,8},{1,5},{2,10},{3,7},{8,16},{9,1},{10,18},{11,3},{16,24},{17,9... | collective-permute-start | bytes 3538952 | tf_op jit(solution)/shard_map/ppermute | solution.py:400
  38.3 17.8 %collective-permute-start.3 = (bf16[4,96,768]{2,1,0:T(8,128)(2,1)}, bf16[4,96,768]{2,1,0:T(8,128)(2,1)}, u32[]{:S(2)}, u32[]{:S(2)}) collective-permute-start(bf16[4,96,768]{2,1,0:T(8,128)(2,1)} %collective-permute-done.2.refs_1_), channel_id=1, source_target_pairs={{0,8},{1,5},{2,10},{3,7},{8,16},{9,1},{10,18},{11,3},{16,24},{17,9... | collective-permute-start | bytes 1769480 | tf_op jit(solution)/shard_map/ppermute | solution.py:400
  49.7 33.3 %collective-permute-start.18 = (bf16[4,96,1536]{2,1,0:T(8,128)(2,1)S(1)}, bf16[4,96,1536]{2,1,0:T(8,128)(2,1)S(1)}, u32[]{:S(2)}, u32[]{:S(2)}) collective-permute-start(bf16[4,96,1536]{2,1,0:T(8,128)(2,1)S(1)} %collective-permute-done.16.refs_3_), channel_id=1, source_target_pairs={{0,8},{1,5},{2,10},{3,7},{8,16},{9,1},{10,18},{11,3},{16,24},{17,9... | collective-permute-start | bytes 3538952 | tf_op jit(solution)/shard_map/ppermute | solution.py:400
  56.1 19.0 %collective-permute-start.8 = (bf16[4,96,768]{2,1,0:T(8,128)(2,1)}, bf16[4,96,768]{2,1,0:T(8,128)(2,1)}, u32[]{:S(2)}, u32[]{:S(2)}) collective-permute-start(bf16[4,96,768]{2,1,0:T(8,128)(2,1)} %collective-permute-done.3.refs_3_), channel_id=1, source_target_pairs={{0,8},{1,5},{2,10},{3,7},{8,16},{9,1},{10,18},{11,3},{16,24},{17,9... | collective-permute-start | bytes 1769480 | tf_op jit(solution)/shard_map/ppermute | solution.py:400
  83.0 10.2 %collective-permute-start.20 = (bf16[2,96,1536]{2,1,0:T(8,128)(2,1)S(1)}, bf16[2,96,1536]{2,1,0:T(8,128)(2,1)}, u32[]{:S(2)}, u32[]{:S(2)}) collective-permute-start(bf16[2,96,1536]{2,1,0:T(8,128)(2,1)S(1)} %slice_select_fusion), channel_id=1, source_target_pairs={{0,8},{1,5},{2,10},{3,7},{8,16},{9,1},{10,18},{11,3},{16,24},{17,9... | collective-permute-start | bytes 1769480 | tf_op jit(solution)/shard_map/ppermute | solution.py:400
  87.6 38.8 %collective-permute-start.15 = (bf16[4,96,1536]{2,1,0:T(8,128)(2,1)S(1)}, bf16[4,96,1536]{2,1,0:T(8,128)(2,1)}, u32[]{:S(2)}, u32[]{:S(2)}) collective-permute-start(bf16[4,96,1536]{2,1,0:T(8,128)(2,1)S(1)} %collective-permute-done.14.refs_1_), channel_id=1, source_target_pairs={{0,1},{1,0},{2,3},{3,2},{4,5},{5,4},{6,7},{7,6},{8,9},{9,8},{10,11... | collective-permute-start | bytes 3538952 | tf_op jit(solution)/shard_map/ppermute | solution.py:389
  93.2 30.7 %collective-permute-start.21 = (bf16[2,96,1536]{2,1,0:T(8,128)(2,1)}, bf16[2,96,1536]{2,1,0:T(8,128)(2,1)}, u32[]{:S(2)}, u32[]{:S(2)}) collective-permute-start(bf16[2,96,1536]{2,1,0:T(8,128)(2,1)} %collective-permute-done.20), channel_id=1, source_target_pairs={{0,1},{1,0},{2,3},{3,2},{4,5},{5,4},{6,7},{7,6},{8,9},{9,8},{10,11... | collective-permute-start | bytes 1769480 | tf_op jit(solution)/shard_map/ppermute | solution.py:389
  94.1 32.2 %collective-permute-start.17 = (bf16[4,96,1536]{2,1,0:T(8,128)(2,1)S(1)}, bf16[4,96,1536]{2,1,0:T(8,128)(2,1)}, u32[]{:S(2)}, u32[]{:S(2)}) collective-permute-start(bf16[4,96,1536]{2,1,0:T(8,128)(2,1)S(1)} %collective-permute-done.16.refs_3_), channel_id=1, source_target_pairs={{0,1},{1,0},{2,3},{3,2},{4,5},{5,4},{6,7},{7,6},{8,9},{9,8},{10,11... | collective-permute-start | bytes 3538952 | tf_op jit(solution)/shard_map/ppermute | solution.py:389
  94.7 31.7 %collective-permute-start.19 = (bf16[4,96,1536]{2,1,0:T(8,128)(2,1)S(1)}, bf16[4,96,1536]{2,1,0:T(8,128)(2,1)}, u32[]{:S(2)}, u32[]{:S(2)}) collective-permute-start(bf16[4,96,1536]{2,1,0:T(8,128)(2,1)S(1)} %collective-permute-done.18.refs_5_), channel_id=1, source_target_pairs={{0,1},{1,0},{2,3},{3,2},{4,5},{5,4},{6,7},{7,6},{8,9},{9,8},{10,11... | collective-permute-start | bytes 3538952 | tf_op jit(solution)/shard_map/ppermute | solution.py:389
  156.6 46.1 %collective-permute-start.45 = (bf16[4,96,1536]{2,1,0:T(8,128)(2,1)}, bf16[4,96,1536]{2,1,0:T(8,128)(2,1)}, u32[]{:S(2)}, u32[]{:S(2)}) collective-permute-start(bf16[4,96,1536]{2,1,0:T(8,128)(2,1)} %get-tuple-element.93), channel_id=1, source_target_pairs={{0,1},{1,0},{2,3},{3,2},{4,5},{5,4},{6,7},{7,6},{8,9},{9,8},{10,11... | collective-permute-start | bytes 3538952 | tf_op jit(solution)/shard_map/ppermute | solution.py:389
  157.0 69.0 %collective-permute-start.44 = (bf16[4,96,1536]{2,1,0:T(8,128)(2,1)}, bf16[4,96,1536]{2,1,0:T(8,128)(2,1)S(1)}, u32[]{:S(2)}, u32[]{:S(2)}) collective-permute-start(bf16[4,96,1536]{2,1,0:T(8,128)(2,1)} %get-tuple-element.91), channel_id=1, source_target_pairs={{0,1},{1,0},{2,3},{3,2},{4,5},{5,4},{6,7},{7,6},{8,9},{9,8},{10,11... | collective-permute-start | bytes 3538952 | tf_op jit(solution)/shard_map/ppermute | solution.py:389
  160.5 42.2 %collective-permute-start.47 = (bf16[4,96,1536]{2,1,0:T(8,128)(2,1)S(1)}, bf16[4,96,1536]{2,1,0:T(8,128)(2,1)}, u32[]{:S(2)}, u32[]{:S(2)}) collective-permute-start(bf16[4,96,1536]{2,1,0:T(8,128)(2,1)S(1)} %add_convert_fusion.3), channel_id=1, source_target_pairs={{0,8},{1,5},{2,10},{3,7},{8,16},{9,1},{10,18},{11,3},{16,24},{17,9... | collective-permute-start | bytes 3538952 | tf_op jit(solution)/shard_map/ppermute | solution.py:400
  204.9 21.1 %collective-permute-start.48 = (bf16[4,96,1536]{2,1,0:T(8,128)(2,1)S(1)}, bf16[4,96,1536]{2,1,0:T(8,128)(2,1)S(1)}, u32[]{:S(2)}, u32[]{:S(2)}) collective-permute-start(bf16[4,96,1536]{2,1,0:T(8,128)(2,1)S(1)} %add_convert_fusion.2), channel_id=1, source_target_pairs={{0,8},{1,5},{2,10},{3,7},{8,16},{9,1},{10,18},{11,3},{16,24},{17,9... | collective-permute-start | bytes 3538952 | tf_op jit(solution)/shard_map/ppermute | solution.py:400
  221.0 35.7 %collective-permute-start.43 = (bf16[4,96,1536]{2,1,0:T(8,128)(2,1)}, bf16[4,96,1536]{2,1,0:T(8,128)(2,1)}, u32[]{:S(2)}, u32[]{:S(2)}) collective-permute-start(bf16[4,96,1536]{2,1,0:T(8,128)(2,1)} %get-tuple-element.89), channel_id=1, source_target_pairs={{0,1},{1,0},{2,3},{3,2},{4,5},{5,4},{6,7},{7,6},{8,9},{9,8},{10,11... | collective-permute-start | bytes 3538952 | tf_op jit(solution)/shard_map/ppermute | solution.py:389
  227.5 29.2 %collective-permute-start.49 = (bf16[4,96,1536]{2,1,0:T(8,128)(2,1)}, bf16[4,96,1536]{2,1,0:T(8,128)(2,1)}, u32[]{:S(2)}, u32[]{:S(2)}) collective-permute-start(bf16[4,96,1536]{2,1,0:T(8,128)(2,1)} %add_convert_fusion.1), channel_id=1, source_target_pairs={{0,8},{1,5},{2,10},{3,7},{8,16},{9,1},{10,18},{11,3},{16,24},{17,9... | collective-permute-start | bytes 3538952 | tf_op jit(solution)/shard_map/ppermute | solution.py:400
  229.0 21.7 %collective-permute-start.34 = (bf16[4,96,768]{2,1,0:T(8,128)(2,1)}, bf16[4,96,768]{2,1,0:T(8,128)(2,1)}, u32[]{:S(2)}, u32[]{:S(2)}) collective-permute-start(bf16[4,96,768]{2,1,0:T(8,128)(2,1)} %get-tuple-element.81), channel_id=1, source_target_pairs={{0,1},{1,0},{2,3},{3,2},{4,5},{5,4},{6,7},{7,6},{8,9},{9,8},{10,11... | collective-permute-start | bytes 1769480 | tf_op jit(solution)/shard_map/ppermute | solution.py:389
  235.4 18.0 %collective-permute-start.38 = (bf16[4,96,768]{2,1,0:T(8,128)(2,1)}, bf16[4,96,768]{2,1,0:T(8,128)(2,1)}, u32[]{:S(2)}, u32[]{:S(2)}) collective-permute-start(bf16[4,96,768]{2,1,0:T(8,128)(2,1)} %add_convert_fusion.6), channel_id=1, source_target_pairs={{0,8},{1,5},{2,10},{3,7},{8,16},{9,1},{10,18},{11,3},{16,24},{17,9... | collective-permute-start | bytes 1769480 | tf_op jit(solution)/shard_map/ppermute | solution.py:400
  237.0 68.2 %collective-permute-start.23 = (bf16[1000,768]{1,0:T(8,128)(2,1)S(1)}, bf16[1000,768]{1,0:T(8,128)(2,1)S(1)}, u32[]{:S(2)}, u32[]{:S(2)}) collective-permute-start(bf16[1000,768]{1,0:T(8,128)(2,1)S(1)} %copy-done.5), channel_id=1, source_target_pairs={{0,2},{1,3},{2,0},{3,1},{4,6},{5,7},{6,4},{7,5},{8,10},{9,11},{10,... | collective-permute-start | bytes 4608008 | tf_op jit(solution)/shard_map/ppermute | solution.py:389
  250.7 10.9 %collective-permute-start.33 = (bf16[4,96,768]{2,1,0:T(8,128)(2,1)}, bf16[4,96,768]{2,1,0:T(8,128)(2,1)S(1)}, u32[]{:S(2)}, u32[]{:S(2)}) collective-permute-start(bf16[4,96,768]{2,1,0:T(8,128)(2,1)} %get-tuple-element.79), channel_id=1, source_target_pairs={{0,1},{1,0},{2,3},{3,2},{4,5},{5,4},{6,7},{7,6},{8,9},{9,8},{10,11... | collective-permute-start | bytes 1769480 | tf_op jit(solution)/shard_map/ppermute | solution.py:389
  253.4 51.2 %collective-permute-start.26 = (bf16[1000,768]{1,0:T(8,128)(2,1)}, bf16[1000,768]{1,0:T(8,128)(2,1)}, u32[]{:S(2)}, u32[]{:S(2)}) collective-permute-start(bf16[1000,768]{1,0:T(8,128)(2,1)} %get-tuple-element.72.a_ref), channel_id=1, source_target_pairs={{0,2},{1,3},{2,0},{3,1},{4,6},{5,7},{6,4},{7,5},{8,10},{9,11},{10,... | collective-permute-start | bytes 4608008 | tf_op jit(solution)/shard_map/ppermute | solution.py:389
  256.6 14.5 %collective-permute-start.28 = (f32[9216]{0:T(1024)S(1)}, f32[9216]{0:T(1024)S(1)}, u32[]{:S(2)}, u32[]{:S(2)}) collective-permute-start(f32[9216]{0:T(1024)S(1)} %pad_maximum_fusion.8), channel_id=1, source_target_pairs={{0,1},{1,0},{2,3},{3,2},{4,5},{5,4},{6,7},{7,6},{8,9},{9,8},{10,11... | collective-permute-start | bytes 110600 | tf_op jit(solution)/shard_map/ppermute | solution.py:389
  261.6 45.2 %collective-permute-start.50 = (bf16[4,96,1536]{2,1,0:T(8,128)(2,1)}, bf16[4,96,1536]{2,1,0:T(8,128)(2,1)}, u32[]{:S(2)}, u32[]{:S(2)}) collective-permute-start(bf16[4,96,1536]{2,1,0:T(8,128)(2,1)} %add_convert_fusion), channel_id=1, source_target_pairs={{0,8},{2,10},{8,16},{10,18},{16,24},{18,26},{24,28},{26,30},{28,20... | collective-permute-start | bytes 3538952 | tf_op jit(solution)/shard_map/ppermute | solution.py:400
  267.7 37.5 %collective-permute-start.40 = (bf16[4,96,768]{2,1,0:T(8,128)(2,1)}, bf16[4,96,768]{2,1,0:T(8,128)(2,1)}, u32[]{:S(2)}, u32[]{:S(2)}) collective-permute-start(bf16[4,96,768]{2,1,0:T(8,128)(2,1)} %add_convert_fusion.4), channel_id=1, source_target_pairs={{0,8},{2,10},{8,16},{10,18},{16,24},{18,26},{24,28},{26,30},{28,20... | collective-permute-start | bytes 1769480 | tf_op jit(solution)/shard_map/ppermute | solution.py:400
  271.2 15.8 %collective-permute-start.29 = (f32[9216]{0:T(1024)S(1)}, f32[9216]{0:T(1024)S(1)}, u32[]{:S(2)}, u32[]{:S(2)}) collective-permute-start(f32[9216]{0:T(1024)S(1)} %fusion.10), channel_id=1, source_target_pairs={{0,4},{4,0},{8,12},{12,8},{16,20},{20,16},{24,28},{28,24},{1,5},{5... | collective-permute-start | bytes 110600 | tf_op jit(solution)/shard_map/ppermute | solution.py:390
  304.6 13.9 %collective-permute-start.22 = (bf16[1000,768]{1,0:T(8,128)(2,1)S(1)}, bf16[1000,768]{1,0:T(8,128)(2,1)S(1)}, u32[]{:S(2)}, u32[]{:S(2)}) collective-permute-start(bf16[1000,768]{1,0:T(8,128)(2,1)S(1)} %copy-done.5), channel_id=1, source_target_pairs={{0,1},{1,0},{2,3},{3,2},{4,5},{5,4},{6,7},{7,6},{8,9},{9,8},{10,11... | collective-permute-start | bytes 4608008 | tf_op jit(solution)/shard_map/ppermute | solution.py:389
  305.3 13.2 %collective-permute-start.24 = (bf16[1000,768]{1,0:T(8,128)(2,1)S(1)}, bf16[1000,768]{1,0:T(8,128)(2,1)S(1)}, u32[]{:S(2)}, u32[]{:S(2)}) collective-permute-start(bf16[1000,768]{1,0:T(8,128)(2,1)S(1)} %collective-permute-done.23.c_ref), channel_id=1, source_target_pairs={{0,1},{1,0},{2,3},{3,2},{4,5},{5,4},{6,7},{7,6},{8,9},{9,8},{10,11... | collective-permute-start | bytes 4608008 | tf_op jit(solution)/shard_map/ppermute | solution.py:389
  306.9 16.8 %collective-permute-start.41 = (bf16[2,96,768]{2,1,0:T(8,128)(2,1)S(1)}, bf16[2,96,768]{2,1,0:T(8,128)(2,1)S(1)}, u32[]{:S(2)}, u32[]{:S(2)}) collective-permute-start(bf16[2,96,768]{2,1,0:T(8,128)(2,1)S(1)} %select_bitcast_fusion.2), channel_id=1, source_target_pairs={{0,1},{1,0},{2,3},{3,2},{4,5},{5,4},{6,7},{7,6},{8,9},{9,8},{10,11... | collective-permute-start | bytes 884744 | tf_op jit(solution)/shard_map/ppermute | solution.py:389
  308.5 15.2 %collective-permute-start.51 = (bf16[2,96,1536]{2,1,0:T(8,128)(2,1)S(1)}, bf16[2,96,1536]{2,1,0:T(8,128)(2,1)S(1)}, u32[]{:S(2)}, u32[]{:S(2)}) collective-permute-start(bf16[2,96,1536]{2,1,0:T(8,128)(2,1)S(1)} %select_bitcast_fusion), channel_id=1, source_target_pairs={{0,1},{1,0},{2,3},{3,2},{4,5},{5,4},{6,7},{7,6},{8,9},{9,8},{10,11... | collective-permute-start | bytes 1769480 | tf_op jit(solution)/shard_map/ppermute | solution.py:389
  324.1 13.1 %collective-permute-start.52 = (bf16[96,1536]{1,0:T(8,128)(2,1)S(1)}, bf16[96,1536]{1,0:T(8,128)(2,1)S(1)}, u32[]{:S(2)}, u32[]{:S(2)}) collective-permute-start(bf16[96,1536]{1,0:T(8,128)(2,1)S(1)} %fusion), channel_id=1, source_target_pairs={{0,2},{1,3},{2,0},{3,1},{4,6},{5,7},{6,4},{7,5},{8,10},{9,11},{10,... | collective-permute-start | bytes 884744 | tf_op jit(solution)/shard_map/ppermute | solution.py:389
  325.7 10.7 %collective-permute-start.42 = (bf16[96,768]{1,0:T(8,128)(2,1)S(1)}, bf16[96,768]{1,0:T(8,128)(2,1)S(1)}, u32[]{:S(2)}, u32[]{:S(2)}) collective-permute-start(bf16[96,768]{1,0:T(8,128)(2,1)S(1)} %fusion.1), channel_id=1, source_target_pairs={{0,2},{1,3},{2,0},{3,1},{4,6},{5,7},{6,4},{7,5},{8,10},{9,11},{10,... | collective-permute-start | bytes 442376 | tf_op jit(solution)/shard_map/ppermute | solution.py:389
  (55 other events, 531.2 us)

commit v8 on v7

--- a/solution.py
+++ b/solution.py
@@ -276,8 +276,7 @@
     do_ref[...] = dot(dlow_ref[...], wo_ref[...]).astype(BF)
 
 
-def attend_back_body(slots, q_ref, k_ref, v_ref, p_ref, do_ref, o_ref, dqkvo_ref, dp_ref, ds_ref):
-    dqkvo_ref[3] = o_ref[...]
+def attend_back_body(slots, q_ref, k_ref, v_ref, p_ref, do_ref, dqkv_ref, dp_ref, ds_ref):
     masks = half_masks()
     rows = [slice(i * SLOT_ROWS, (i + 1) * SLOT_ROWS) for i in range(slots)]
 
@@ -287,7 +286,7 @@
         for h in range(2):
             dp_ref[h, i] = dot(jnp.where(masks[h], v, jnp.zeros_like(v)), do, NT)
         dv = [dot(p_ref[h, i], do) for h in range(2)]
-        dqkvo_ref[2, rows[i], :] = jnp.where(masks[0], *dv).astype(BF)
+        dqkv_ref[2, rows[i], :] = jnp.where(masks[0], *dv).astype(BF)
 
     def softmax_back(i):
         for h in range(2):
@@ -299,9 +298,9 @@
         q = q_ref[rows[i], :] * jnp.bfloat16(0.125)
         k_t = (k_ref[rows[i], :] * jnp.bfloat16(0.125)).T
         dk = [dot(ds_ref[h, i], q) for h in range(2)]
-        dqkvo_ref[1, rows[i], :] = jnp.where(masks[0], *dk).astype(BF)
+        dqkv_ref[1, rows[i], :] = jnp.where(masks[0], *dk).astype(BF)
         dq = [dot(k_t[h * HEAD_DIM : (h + 1) * HEAD_DIM], ds_ref[h, i]) for h in range(2)]
-        dqkvo_ref[0, rows[i], :] = jnp.concatenate(dq, axis=0).T.astype(BF)
+        dqkv_ref[0, rows[i], :] = jnp.concatenate(dq, axis=0).T.astype(BF)
 
     for i in range(slots):
         upstream(i)
@@ -310,47 +309,31 @@
     for i in range(slots):
         downstream(i)
     tail = slots * SLOT_ROWS
-    dqkvo_ref[:3, tail:, :] = jnp.zeros((3, ROWS - tail, 2 * HEAD_DIM), BF)
-
-
-def outer_body(info_ref, h_ref, d_ref, dlow_ref, *refs):
-    grads, sums_ref, t_ref, g_ref = refs[:-3], refs[-3], refs[-2], refs[-1]
+    dqkv_ref[:, tail:, :] = jnp.zeros((3, ROWS - tail, 2 * HEAD_DIM), BF)
+
+
+def outer_body(info_ref, h_ref, d_ref, dlow_ref, o_ref, *refs):
+    grads, sums_ref, g_ref = refs[:-2], refs[-2], refs[-1]
     width = h_ref.shape[1]
-    step = pl.program_id(0)
-
-    @pl.when(step == 0)
-    def _():
-        t_ref[...] = h_ref[...].T
-        sums_ref[...] = jnp.zeros_like(sums_ref)
-
-    @pl.when(step == 3)
-    def _():
-        t_ref[...] = dlow_ref[...].T
-
-    g_ref[...] = dot(t_ref[...], d_ref[0]).astype(BF)
-    for n, s in enumerate((0, 2)):
-
-        @pl.when(step == s)
-        def _(n=n):
-            sums_ref[n : n + 1, :] = colsum(d_ref[0].astype(F32))
-
-    def store(s):
-        if len(grads) == 1:
-            parts, groups, sub, _ = grads[0].shape
-            local = width // groups
-            for j in range(groups):
-                block = g_ref[:, j * local : (j + 1) * local].reshape(parts, sub, local)
-                grads[0][:, j, :, s * local : (s + 1) * local] = block
-            return
-        for n, ref in enumerate(grads):
-            groups, sub, _ = ref.shape
-            local = width // groups
-            rows = g_ref[pl.ds(pl.multiple_of(info_ref[2 + n] * sub, sub), sub), :]
-            for j in range(groups):
-                ref[j, :, s * local : (s + 1) * local] = rows[:, j * local : (j + 1) * local]
-
+    groups = g_ref.shape[0]
+    local = width // groups
+    sums_ref[0:1, :] = colsum(d_ref[0].astype(F32))
+    sums_ref[1:2, :] = colsum(d_ref[2].astype(F32))
+    h_t = h_ref[...].T
     for s in range(4):
-        pl.when(step == s)(functools.partial(store, s))
+        g = (dot(h_t, d_ref[s]) if s < 3 else dot(dlow_ref[...].T, o_ref[...])).astype(BF)
+        for j in range(groups):
+            g_ref[j, :, s * local : (s + 1) * local] = g[:, j * local : (j + 1) * local]
+    if len(grads) == 1:
+        parts, _, sub, cols = grads[0].shape
+        for j in range(groups):
+            grads[0][:, j] = g_ref[j].reshape(parts, sub, cols)
+        return
+    for n, ref in enumerate(grads):
+        sub = ref.shape[1]
+        rows = pl.ds(pl.multiple_of(info_ref[2 + n] * sub, sub), sub)
+        for j in range(groups):
+            ref[j] = g_ref[j, rows, :]
 
 
 def input_back_body(x_ref, d_ref, wq_ref, dmid_ref, gain_ref, out_ref, sums_ref):
@@ -444,7 +427,8 @@
             total = term(k) + moved.astype(F32)
         total = total.astype(BF)
         last = hop(total, False)
-        total = jnp.where(even, last, total).reshape(2, 2, sub, -1)
+        total = jnp.where(even, last, total)
+        total = total.reshape(2, 2, sub, -1)
         split = lambda a, b, first: (jnp.where(first, a, b), jnp.where(first, b, a))
         mine_half, other_half = split(total[:, 0], total[:, 1], even)
         other_half = mp_swap(other_half, 1)
@@ -622,12 +606,12 @@
         flops=4 * mm,
     )
     (do,) = call(out_back_body, [t_bf(width)], [dlow, wo], flops=mm)
-    (dqkvo,) = call(
+    (dqkv,) = call(
         functools.partial(attend_back_body, slots),
-        [sds((4, ROWS, width), BF)],
-        [qkv, qkv, qkv, probs, do, mixed],
-        [head(0), head(1), head(2), p_spec, head(0), head(0)],
-        [pl.BlockSpec((4, ROWS, pair), lambda i: (0, 0, i))],
+        [sds((3, ROWS, width), BF)],
+        [qkv, qkv, qkv, probs, do],
+        [head(0), head(1), head(2), p_spec, head(0)],
+        [pl.BlockSpec((3, ROWS, pair), lambda i: (0, 0, i))],
         (pairs,),
         scratch=[pltpu.VMEM((2, slots, SLOT_ROWS, SLOT_ROWS), dtype) for dtype in (F32, BF)],
         flops=2 * mm,
@@ -637,10 +621,9 @@
     *halves_a, sums_qkv = call(
         outer_body,
         grad_shapes + [sum_shape],
-        [halves_info if ring else info, h1, dqkvo, dlow],
-        [smem, None, pl.BlockSpec((1, ROWS, width), lambda i: (i, 0, 0)), None],
-        grid=(4,),
-        scratch=[pltpu.VMEM((width, ROWS), BF), pltpu.VMEM((width, width), BF)],
+        [halves_info if ring else info, h1, dqkv, dlow, mixed],
+        [smem, None, None, None, None],
+        scratch=[pltpu.VMEM((groups, width, width), BF)],
         flops=4 * mm,
     )
     if ring:
@@ -655,7 +638,7 @@
     own_grad, sums_in = call(
         input_back_body,
         [own_shape, sum_shape],
-        [x, dqkvo, wq, dmid, row(norm_gain)],
+        [x, dqkv, wq, dmid, row(norm_gain)],
         [rows256, pl.BlockSpec((3, 256, width), lambda i: (0, i, 0)), None, rows256, None],
         [rows256, None],
         (ROWS // 256,),

time: 340 us -> 336 us (0.988)
  Pallas kernels: 135 us -> 131 us
    pallas_call x13, Pallas kernels: 133 us -> 129 us  [call(): pl.pallas_call(body, out_shape=tuple(outs), grid=(1,) if grid is None els...]
  transfers between devices with their start and end apart: 53 -> 53, of which waited for: 20 -> 20; matrix products, arithmetic and copies ran while one was open for 14% -> 14% of each run, Pallas kernels for 31% -> 30%
where the time goes in v8:
time: 336 us; the launch traced here: 334 us
  Pallas kernels  131 us (39%)
  waiting for transfers between devices  96.6 us (29%)
  starting transfers between devices  49.3 us (15%)
  local copies, waits for them, and re-layouts  30.2 us (9%)
  other arithmetic  26.3 us (8%)
    pallas_call x13, Pallas kernels, call(): pl.pallas_call(body, out_shape=tuple(outs), grid=(1,) if grid is None els...  129 us
    ppermute x16, waiting for transfers between devices, hop(): return lax.ppermute(a, axes, pairs)  39.1 us
    ppermute x34, waiting for transfers between devices, block_step(): lax.ppermute(a, 'mp', [(j, j ^ bit) for j in range(groups)])  33.4 us
    ppermute x16, starting transfers between devices, hop(): return lax.ppermute(a, axes, pairs)  31.7 us
    ppermute x3, waiting for transfers between devices, block_step(): lax.ppermute(a, 'dp', [(d, d ^ bit) for d in range(parts)])  24.1 us
    ppermute x34, starting transfers between devices, block_step(): lax.ppermute(a, 'mp', [(j, j ^ bit) for j in range(groups)])  17.1 us
    unnamed x73, local copies, waits for them, and re-layouts  16.5 us
    convert_element_type x6, other arithmetic, scatter_ring(): moved = hop(total.astype(BF))  9.19 us
  transfers between devices with their start and end apart: 53, of which 20 were waited for; matrix products, arithmetic and copies ran while one was open for 14% of the time, Pallas kernels for 30%

profile of v8, /device:TPU:0, one launch (start us, length us, event | category | flops | bytes accessed | tf_op | source)
XLA Modules:
  0.0 334.5 jit_solution(12726424238258347433)
XLA Ops:
  1.8 3.0 collective-permute-start.12
  4.8 7.0 %collective-permute-done.12 = bf16[96,1536]{1,0:T(8,128)(2,1)S(1)} collective-permute-done((bf16[96,1536]{1,0:T(8,128)(2,1)S(1)}, bf16[96,1536]{1,0:T(8,128)(2,1)S(1)}, u32[]{:S(2)}, u32[]{:S(2)}) %collective-permute-start.12) | collective-permute-done | bytes 294944 | tf_op jit(solution)/shard_map/ppermute | solution.py:372
  24.7 6.0 %collective-permute-done.14.refs_1_ = bf16[4,96,1536]{2,1,0:T(8,128)(2,1)S(1)} collective-permute-done((bf16[4,96,1536]{2,1,0:T(8,128)(2,1)S(1)}, bf16[4,96,1536]{2,1,0:T(8,128)(2,1)S(1)}, u32[]{:S(2)}, u32[]{:S(2)}) %collective-permute-start.14) | collective-permute-done | bytes 1179680 | tf_op jit(solution)/shard_map/ppermute | solution.py:383
  32.7 3.5 %copy.38.in_ref = bf16[4,5,197,768]{3,2,1,0:T(8,128)(2,1)S(1)} copy(bf16[4,5,197,768]{3,0,2,1:T(4,128)(2,1)} %param.17) | data formatting | bytes 12103680 | tf_op args[0]
  40.8 8.8 %collective-permute-done.16.refs_3_ = bf16[4,96,1536]{2,1,0:T(8,128)(2,1)S(1)} collective-permute-done((bf16[4,96,1536]{2,1,0:T(8,128)(2,1)S(1)}, bf16[4,96,1536]{2,1,0:T(8,128)(2,1)S(1)}, u32[]{:S(2)}, u32[]{:S(2)}) %collective-permute-start.16) | collective-permute-done | bytes 1179680 | tf_op jit(solution)/shard_map/ppermute | solution.py:383
  52.1 4.0 %collective-permute-done.3.refs_3_ = bf16[4,96,768]{2,1,0:T(8,128)(2,1)} collective-permute-done((bf16[4,96,768]{2,1,0:T(8,128)(2,1)}, bf16[4,96,768]{2,1,0:T(8,128)(2,1)}, u32[]{:S(2)}, u32[]{:S(2)}) %collective-permute-start.3) | collective-permute-done | bytes 589856 | tf_op jit(solution)/shard_map/ppermute | solution.py:383
  63.5 6.1 %copy.39.in_ref = bf16[4,5,197,768]{3,2,1,0:T(8,128)(2,1)} copy(bf16[4,5,197,768]{3,0,2,1:T(4,128)(2,1)} %param.18) | data formatting | bytes 12103680 | tf_op args[1]
  70.9 2.7 copy-done.2
  78.1 4.8 %collective-permute-done.10 = bf16[2,96,768]{2,1,0:T(8,128)(2,1)S(1)} collective-permute-done((bf16[2,96,768]{2,1,0:T(8,128)(2,1)S(1)}, bf16[2,96,768]{2,1,0:T(8,128)(2,1)S(1)}, u32[]{:S(2)}, u32[]{:S(2)}) %collective-permute-start.10) | collective-permute-done | bytes 294944 | tf_op jit(solution)/shard_map/ppermute | solution.py:383
  88.0 5.3 %collective-permute-done.20 = bf16[2,96,1536]{2,1,0:T(8,128)(2,1)} collective-permute-done((bf16[2,96,1536]{2,1,0:T(8,128)(2,1)S(1)}, bf16[2,96,1536]{2,1,0:T(8,128)(2,1)}, u32[]{:S(2)}, u32[]{:S(2)}) %collective-permute-start.20) | collective-permute-done | bytes 589856 | tf_op jit(solution)/shard_map/ppermute | solution.py:383
  96.3 10.7 %shard_map.281 = (bf16[1024,768]{1,0:T(8,128)(2,1)}, bf16[1024,2304]{1,0:T(8,128)(2,1)}, bf16[768,2304]{1,0:T(8,128)(2,1)}, bf16[768,768]{1,0:T(8,128)(2,1)}) custom-call(s32[10]{0:T(128)} %get-tuple-element.125.info_ref, bf16[1024,768]{1,0:T(8,128)(2,1)} %copy-done.5, f32[1,768]{1,0:T(1,128)} %reshape.202.gain_ref, f32[1,768]{1,0:T(1,128)} %reshape.203.shift_ref, ...), custom_call_target="tpu_custom_call" | custom-call | flops 3623878656 | bytes 17316904 | tf_op jit(solution)/shard_map/pallas_call | solution.py:54
  107.1 9.6 %shard_map.282 = (bf16[1024,768]{1,0:T(8,128)(2,1)}, bf16[12,5,200,200]{3,2,1,0:T(8,128)(2,1)}) custom-call(bf16[1024,2304]{1,0:T(8,128)(2,1)} %get-tuple-element.58.q_ref.k_ref.v_ref, bf16[1024,2304]{1,0:T(8,128)(2,1)} %get-tuple-element.58.q_ref.k_ref.v_ref, bf16[1024,2304]{1,0:T(8,128)(2,1)} %get-tuple-element.58.q_ref.k_ref.v_ref), custom_call_target="tpu_custom_call" | custom-call | flops 1207959552 | bytes 20528640 | tf_op jit(solution)/shard_map/pallas_call | solution.py:54
  116.7 7.2 %shard_map.283 = (f32[1024,768]{1,0:T(8,128)}, bf16[1024,768]{1,0:T(8,128)(2,1)}) custom-call(bf16[1024,768]{1,0:T(8,128)(2,1)} %copy-done.5, bf16[1024,768]{1,0:T(8,128)(2,1)} %get-tuple-element.59.o_ref, bf16[768,768]{1,0:T(8,128)(2,1)} %get-tuple-element.60.wo_ref, f32[1,768]{1,0:T(1,128)} %reshape.204.bias_ref, f32[1,768]{1,0:T(1,128)} %reshape.205.gain_ref, ...), custom_call_target="tpu_custom_call" | custom-call | flops 1207959552 | bytes 9053184 | tf_op jit(solution)/shard_map/pallas_call | solution.py:54
  126.4 29.5 %shard_map.285 = (bf16[1024,3072]{1,0:T(8,128)(2,1)}, bf16[1024,3072]{1,0:T(8,128)(2,1)}, f32[8,3072]{1,0:T(8,128)}, bf16[4,96,1536]{2,1,0:T(8,128)(2,1)}, bf16[...) custom-call(s32[10]{0:T(128)} %get-tuple-element.125.info_ref, ...), custom_call_target="tpu_custom_call" | custom-call | flops 19327352832 | bytes 34713680 | tf_op jit(solution)/shard_map/pallas_call | solution.py:54
  162.6 10.4 %shard_map.286.a_ref = bf16[1000,768]{1,0:T(8,128)(2,1)} custom-call(s32[10]{0:T(128)} %get-tuple-element.125.info_ref, bf16[1024,3072]{1,0:T(8,128)(2,1)} %get-tuple-element.64.act_ref, f32[1024,768]{1,0:T(8,128)} %get-tuple-element.65.mid_ref, f32[1,768]{1,0:T(1,128)} %reshape.207.bias_ref, bf16[4,96,1536]{2,1,0:T(8,128)(2,1)} %copy-done.7, ...), custom_call_target="tpu_custom_call" | custom-call | flops 4831838208 | bytes 20413480 | tf_op jit(solution)/shard_map/pallas_call | solution.py:54
  173.0 12.5 %shard_map.288 = (f32[1024,768]{1,0:T(8,128)}, bf16[1024,768]{1,0:T(8,128)(2,1)}, f32[8,768]{1,0:T(8,128)}) custom-call(s32[10]{0:T(128)} %get-tuple-element.125.info_ref, bf16[1024,768]{1,0:T(8,128)(2,1)} %copy-done.3, bf16[1024,3072]{1,0:T(8,128)(2,1)} %get-tuple-element.68.du_ref, f32[1024,768]{1,0:T(8,128)} %get-tuple-element.65.mid_ref, ...), custom_call_target="tpu_custom_call" | custom-call | flops 4831838208 | bytes 25193512 | tf_op jit(solution)/shard_map/pallas_call | solution.py:54
  185.5 4.3 %shard_map.289.do_ref = bf16[1024,768]{1,0:T(8,128)(2,1)} custom-call(bf16[1024,768]{1,0:T(8,128)(2,1)} %get-tuple-element.69.dlow_ref, bf16[768,768]{1,0:T(8,128)(2,1)} %get-tuple-element.60.wo_ref), custom_call_target="tpu_custom_call" | custom-call | flops 1207959552 | bytes 4325376 | tf_op jit(solution)/shard_map/pallas_call | solution.py:54
  189.8 12.2 %shard_map.290.d_ref = bf16[3,1024,768]{2,1,0:T(8,128)(2,1)} custom-call(bf16[1024,2304]{1,0:T(8,128)(2,1)} %get-tuple-element.58.q_ref.k_ref.v_ref, bf16[1024,2304]{1,0:T(8,128)(2,1)} %get-tuple-element.58.q_ref.k_ref.v_ref, bf16[1024,2304]{1,0:T(8,128)(2,1)} %get-tuple-element.58.q_ref.k_ref.v_ref, bf16[12,5,200,200]{3,2,1,0:T(8,128)(2,1)} %get-tuple-element.66.p_ref, ...), custom_call_target="tpu_custom_call" | custom-call | flops 2415919104 | bytes 25247232 | tf_op jit(solution)/shard_map/pallas_call | solution.py:54
  205.9 11.1 %shard_map.293 = (bf16[4,96,768]{2,1,0:T(8,128)(2,1)}, bf16[4,96,768]{2,1,0:T(8,128)(2,1)}, bf16[4,96,768]{2,1,0:T(8,128)(2,1)}, bf16[4,96,768]{2,1,0:T(8,128)(2...) custom-call(s32[10]{0:T(128)} %get-tuple-element.126.halves_ref.info, ...), custom_call_target="tpu_custom_call" | custom-call | flops 4831838208 | bytes 14180392 | tf_op jit(solution)/shard_map/pallas_call | solution.py:54
  225.3 5.3 %collective-permute-done.37 = bf16[4,96,768]{2,1,0:T(8,128)(2,1)S(1)} collective-permute-done((bf16[4,96,768]{2,1,0:T(8,128)(2,1)S(1)}, bf16[4,96,768]{2,1,0:T(8,128)(2,1)S(1)}, u32[]{:S(2)}, u32[]{:S(2)}) %collective-permute-start.37) | collective-permute-done | bytes 589856 | tf_op jit(solution)/shard_map/ppermute | solution.py:383
  235.5 9.8 %shard_map.291 = (bf16[1000,768]{1,0:T(8,128)(2,1)}, f32[8,768]{1,0:T(8,128)}) custom-call(bf16[1024,768]{1,0:T(8,128)(2,1)} %copy-done.5, bf16[3,1024,768]{2,1,0:T(8,128)(2,1)} %shard_map.290.d_ref, bf16[768,2304]{1,0:T(8,128)(2,1)} %get-tuple-element.70.wq_ref, f32[1024,768]{1,0:T(8,128)} %get-tuple-element.71.dmid_ref, f32[1,768]{1,0:T(1,128)} %reshape.202.gain_ref), custom_call_target="tpu_custom_call" | custom-call | flops 3623878656 | bytes 14539776 | tf_op jit(solution)/shard_map/pallas_call | solution.py:54
  247.1 2.6 collective-permute-done.38
  254.7 3.2 add_convert_fusion
  257.9 3.4 %collective-permute-start.50 = (bf16[4,96,1536]{2,1,0:T(8,128)(2,1)}, bf16[4,96,1536]{2,1,0:T(8,128)(2,1)}, u32[]{:S(2)}, u32[]{:S(2)}) collective-permute-start(bf16[4,96,1536]{2,1,0:T(8,128)(2,1)} %add_convert_fusion), channel_id=1, source_target_pairs={{0,8},{2,10},{8,16},{10,18},{16,24},{18,26},{24,28},{26,30},{28,20... | collective-permute-start | bytes 3538952 | tf_op jit(solution)/shard_map/ppermute | solution.py:383
  264.0 3.5 %collective-permute-start.40 = (bf16[4,96,768]{2,1,0:T(8,128)(2,1)}, bf16[4,96,768]{2,1,0:T(8,128)(2,1)}, u32[]{:S(2)}, u32[]{:S(2)}) collective-permute-start(bf16[4,96,768]{2,1,0:T(8,128)(2,1)} %add_convert_fusion.4), channel_id=1, source_target_pairs={{0,8},{2,10},{8,16},{10,18},{16,24},{18,26},{24,28},{26,30},{28,20... | collective-permute-start | bytes 1769480 | tf_op jit(solution)/shard_map/ppermute | solution.py:383
  268.0 15.3 %collective-permute-done.29 = f32[9216]{0:T(1024)S(1)} collective-permute-done((f32[9216]{0:T(1024)S(1)}, f32[9216]{0:T(1024)S(1)}, u32[]{:S(2)}, u32[]{:S(2)}) %collective-permute-start.29) | collective-permute-done | bytes 36896 | tf_op jit(solution)/shard_map/ppermute | solution.py:373
  283.3 3.9 %collective-permute-done.30 = f32[9216]{0:T(1024)S(1)} collective-permute-done((f32[9216]{0:T(1024)S(1)}, f32[9216]{0:T(1024)S(1)}, u32[]{:S(2)}, u32[]{:S(2)}) %collective-permute-start.30) | collective-permute-done | bytes 36896 | tf_op jit(solution)/shard_map/ppermute | solution.py:373
  287.3 4.8 %collective-permute-done.31 = f32[9216]{0:T(1024)S(1)} collective-permute-done((f32[9216]{0:T(1024)S(1)}, f32[9216]{0:T(1024)S(1)}, u32[]{:S(2)}, u32[]{:S(2)}) %collective-permute-start.31) | collective-permute-done | bytes 36896 | tf_op jit(solution)/shard_map/ppermute | solution.py:373
  292.7 8.3 %collective-permute-done.32 = f32[9216]{0:T(1024)S(1)} collective-permute-done((f32[9216]{0:T(1024)S(1)}, f32[9216]{0:T(1024)S(1)}, u32[]{:S(2)}, u32[]{:S(2)}) %collective-permute-start.32) | collective-permute-done | bytes 36896 | tf_op jit(solution)/shard_map/ppermute | solution.py:372
  308.9 5.9 %shard_map.292 = bf16[5,197,4,768]{3,2,1,0:T(4,128)(2,1)} custom-call(s32[2]{0:T(128)S(1)} %pad_add_fusion.info_ref, bf16[1000,768]{1,0:T(8,128)(2,1)S(1)} %copy-done.6, bf16[1000,768]{1,0:T(8,128)(2,1)S(1)} %collective-permute-done.25.b_ref, bf16[1000,768]{1,0:T(8,128)(2,1)} %collective-permute-done.26.c_ref, ...), custom_call_target="tpu_custom_call" | custom-call | flops 1207959552 | bytes 12195848 | tf_op jit(solution)/shard_map/pallas_call | solution.py:54
  314.9 5.2 %shard_map.287 = bf16[5,197,4,768]{3,2,1,0:T(4,128)(2,1)} custom-call(s32[2]{0:T(128)S(1)} %pad_add_fusion.info_ref, bf16[1000,768]{1,0:T(8,128)(2,1)S(1)} %copy-done.4, bf16[1000,768]{1,0:T(8,128)(2,1)S(1)} %collective-permute-done.22.b_ref, bf16[1000,768]{1,0:T(8,128)(2,1)S(1)} %collective-permute-done.23.c_ref, ...), custom_call_target="tpu_custom_call" | custom-call | flops 1207959552 | bytes 12195848 | tf_op jit(solution)/shard_map/pallas_call | solution.py:54
  322.7 10.0 %collective-permute-done.42.other_ref = bf16[96,768]{1,0:T(8,128)(2,1)S(1)} collective-permute-done((bf16[96,768]{1,0:T(8,128)(2,1)S(1)}, bf16[96,768]{1,0:T(8,128)(2,1)S(1)}, u32[]{:S(2)}, u32[]{:S(2)}) %collective-permute-start.42) | collective-permute-done | bytes 147488 | tf_op jit(solution)/shard_map/ppermute | solution.py:372
  (242 shorter events, 92.9 us)
Async XLA Ops:
  14.5 16.3 %collective-permute-start.14 = (bf16[4,96,1536]{2,1,0:T(8,128)(2,1)S(1)}, bf16[4,96,1536]{2,1,0:T(8,128)(2,1)S(1)}, u32[]{:S(2)}, u32[]{:S(2)}) collective-permute-start(bf16[4,96,1536]{2,1,0:T(8,128)(2,1)S(1)} %pad_maximum_fusion.refs_0_), channel_id=1, source_target_pairs={{0,8},{1,5},{2,10},{3,7},{8,16},{9,1},{10,18},{11,3},{16,24},{17,9... | collective-permute-start | bytes 3538952 | tf_op jit(solution)/shard_map/ppermute | solution.py:383
  21.3 17.0 %collective-permute-start.2 = (bf16[4,96,768]{2,1,0:T(8,128)(2,1)}, bf16[4,96,768]{2,1,0:T(8,128)(2,1)}, u32[]{:S(2)}, u32[]{:S(2)}) collective-permute-start(bf16[4,96,768]{2,1,0:T(8,128)(2,1)} %pad_maximum_fusion.2.refs_0_), channel_id=1, source_target_pairs={{0,8},{1,5},{2,10},{3,7},{8,16},{9,1},{10,18},{11,3},{16,24},{17,9... | collective-permute-start | bytes 1769480 | tf_op jit(solution)/shard_map/ppermute | solution.py:383
  30.7 19.0 %collective-permute-start.16 = (bf16[4,96,1536]{2,1,0:T(8,128)(2,1)S(1)}, bf16[4,96,1536]{2,1,0:T(8,128)(2,1)S(1)}, u32[]{:S(2)}, u32[]{:S(2)}) collective-permute-start(bf16[4,96,1536]{2,1,0:T(8,128)(2,1)S(1)} %collective-permute-done.14.refs_1_), channel_id=1, source_target_pairs={{0,8},{1,5},{2,10},{3,7},{8,16},{9,1},{10,18},{11,3},{16,24},{17,9... | collective-permute-start | bytes 3538952 | tf_op jit(solution)/shard_map/ppermute | solution.py:383
  38.3 17.8 %collective-permute-start.3 = (bf16[4,96,768]{2,1,0:T(8,128)(2,1)}, bf16[4,96,768]{2,1,0:T(8,128)(2,1)}, u32[]{:S(2)}, u32[]{:S(2)}) collective-permute-start(bf16[4,96,768]{2,1,0:T(8,128)(2,1)} %collective-permute-done.2.refs_1_), channel_id=1, source_target_pairs={{0,8},{1,5},{2,10},{3,7},{8,16},{9,1},{10,18},{11,3},{16,24},{17,9... | collective-permute-start | bytes 1769480 | tf_op jit(solution)/shard_map/ppermute | solution.py:383
  49.7 33.3 %collective-permute-start.18 = (bf16[4,96,1536]{2,1,0:T(8,128)(2,1)S(1)}, bf16[4,96,1536]{2,1,0:T(8,128)(2,1)S(1)}, u32[]{:S(2)}, u32[]{:S(2)}) collective-permute-start(bf16[4,96,1536]{2,1,0:T(8,128)(2,1)S(1)} %collective-permute-done.16.refs_3_), channel_id=1, source_target_pairs={{0,8},{1,5},{2,10},{3,7},{8,16},{9,1},{10,18},{11,3},{16,24},{17,9... | collective-permute-start | bytes 3538952 | tf_op jit(solution)/shard_map/ppermute | solution.py:383
  56.1 19.0 %collective-permute-start.8 = (bf16[4,96,768]{2,1,0:T(8,128)(2,1)}, bf16[4,96,768]{2,1,0:T(8,128)(2,1)}, u32[]{:S(2)}, u32[]{:S(2)}) collective-permute-start(bf16[4,96,768]{2,1,0:T(8,128)(2,1)} %collective-permute-done.3.refs_3_), channel_id=1, source_target_pairs={{0,8},{1,5},{2,10},{3,7},{8,16},{9,1},{10,18},{11,3},{16,24},{17,9... | collective-permute-start | bytes 1769480 | tf_op jit(solution)/shard_map/ppermute | solution.py:383
  83.0 10.2 %collective-permute-start.20 = (bf16[2,96,1536]{2,1,0:T(8,128)(2,1)S(1)}, bf16[2,96,1536]{2,1,0:T(8,128)(2,1)}, u32[]{:S(2)}, u32[]{:S(2)}) collective-permute-start(bf16[2,96,1536]{2,1,0:T(8,128)(2,1)S(1)} %slice_select_fusion), channel_id=1, source_target_pairs={{0,8},{1,5},{2,10},{3,7},{8,16},{9,1},{10,18},{11,3},{16,24},{17,9... | collective-permute-start | bytes 1769480 | tf_op jit(solution)/shard_map/ppermute | solution.py:383
  87.6 38.8 %collective-permute-start.15 = (bf16[4,96,1536]{2,1,0:T(8,128)(2,1)S(1)}, bf16[4,96,1536]{2,1,0:T(8,128)(2,1)}, u32[]{:S(2)}, u32[]{:S(2)}) collective-permute-start(bf16[4,96,1536]{2,1,0:T(8,128)(2,1)S(1)} %collective-permute-done.14.refs_1_), channel_id=1, source_target_pairs={{0,1},{1,0},{2,3},{3,2},{4,5},{5,4},{6,7},{7,6},{8,9},{9,8},{10,11... | collective-permute-start | bytes 3538952 | tf_op jit(solution)/shard_map/ppermute | solution.py:372
  93.2 30.7 %collective-permute-start.21 = (bf16[2,96,1536]{2,1,0:T(8,128)(2,1)}, bf16[2,96,1536]{2,1,0:T(8,128)(2,1)}, u32[]{:S(2)}, u32[]{:S(2)}) collective-permute-start(bf16[2,96,1536]{2,1,0:T(8,128)(2,1)} %collective-permute-done.20), channel_id=1, source_target_pairs={{0,1},{1,0},{2,3},{3,2},{4,5},{5,4},{6,7},{7,6},{8,9},{9,8},{10,11... | collective-permute-start | bytes 1769480 | tf_op jit(solution)/shard_map/ppermute | solution.py:372
  94.1 32.3 %collective-permute-start.17 = (bf16[4,96,1536]{2,1,0:T(8,128)(2,1)S(1)}, bf16[4,96,1536]{2,1,0:T(8,128)(2,1)}, u32[]{:S(2)}, u32[]{:S(2)}) collective-permute-start(bf16[4,96,1536]{2,1,0:T(8,128)(2,1)S(1)} %collective-permute-done.16.refs_3_), channel_id=1, source_target_pairs={{0,1},{1,0},{2,3},{3,2},{4,5},{5,4},{6,7},{7,6},{8,9},{9,8},{10,11... | collective-permute-start | bytes 3538952 | tf_op jit(solution)/shard_map/ppermute | solution.py:372
  94.7 31.7 %collective-permute-start.19 = (bf16[4,96,1536]{2,1,0:T(8,128)(2,1)S(1)}, bf16[4,96,1536]{2,1,0:T(8,128)(2,1)}, u32[]{:S(2)}, u32[]{:S(2)}) collective-permute-start(bf16[4,96,1536]{2,1,0:T(8,128)(2,1)S(1)} %collective-permute-done.18.refs_5_), channel_id=1, source_target_pairs={{0,1},{1,0},{2,3},{3,2},{4,5},{5,4},{6,7},{7,6},{8,9},{9,8},{10,11... | collective-permute-start | bytes 3538952 | tf_op jit(solution)/shard_map/ppermute | solution.py:372
  156.7 45.4 %collective-permute-start.45 = (bf16[4,96,1536]{2,1,0:T(8,128)(2,1)}, bf16[4,96,1536]{2,1,0:T(8,128)(2,1)}, u32[]{:S(2)}, u32[]{:S(2)}) collective-permute-start(bf16[4,96,1536]{2,1,0:T(8,128)(2,1)} %get-tuple-element.93), channel_id=1, source_target_pairs={{0,1},{1,0},{2,3},{3,2},{4,5},{5,4},{6,7},{7,6},{8,9},{9,8},{10,11... | collective-permute-start | bytes 3538952 | tf_op jit(solution)/shard_map/ppermute | solution.py:372
  157.0 65.3 %collective-permute-start.44 = (bf16[4,96,1536]{2,1,0:T(8,128)(2,1)}, bf16[4,96,1536]{2,1,0:T(8,128)(2,1)S(1)}, u32[]{:S(2)}, u32[]{:S(2)}) collective-permute-start(bf16[4,96,1536]{2,1,0:T(8,128)(2,1)} %get-tuple-element.91), channel_id=1, source_target_pairs={{0,1},{1,0},{2,3},{3,2},{4,5},{5,4},{6,7},{7,6},{8,9},{9,8},{10,11... | collective-permute-start | bytes 3538952 | tf_op jit(solution)/shard_map/ppermute | solution.py:372
  160.5 41.5 %collective-permute-start.47 = (bf16[4,96,1536]{2,1,0:T(8,128)(2,1)S(1)}, bf16[4,96,1536]{2,1,0:T(8,128)(2,1)}, u32[]{:S(2)}, u32[]{:S(2)}) collective-permute-start(bf16[4,96,1536]{2,1,0:T(8,128)(2,1)S(1)} %add_convert_fusion.3), channel_id=1, source_target_pairs={{0,8},{1,5},{2,10},{3,7},{8,16},{9,1},{10,18},{11,3},{16,24},{17,9... | collective-permute-start | bytes 3538952 | tf_op jit(solution)/shard_map/ppermute | solution.py:383
  204.3 18.1 %collective-permute-start.48 = (bf16[4,96,1536]{2,1,0:T(8,128)(2,1)S(1)}, bf16[4,96,1536]{2,1,0:T(8,128)(2,1)S(1)}, u32[]{:S(2)}, u32[]{:S(2)}) collective-permute-start(bf16[4,96,1536]{2,1,0:T(8,128)(2,1)S(1)} %add_convert_fusion.2), channel_id=1, source_target_pairs={{0,8},{1,5},{2,10},{3,7},{8,16},{9,1},{10,18},{11,3},{16,24},{17,9... | collective-permute-start | bytes 3538952 | tf_op jit(solution)/shard_map/ppermute | solution.py:383
  217.0 35.9 %collective-permute-start.43 = (bf16[4,96,1536]{2,1,0:T(8,128)(2,1)}, bf16[4,96,1536]{2,1,0:T(8,128)(2,1)}, u32[]{:S(2)}, u32[]{:S(2)}) collective-permute-start(bf16[4,96,1536]{2,1,0:T(8,128)(2,1)} %get-tuple-element.89), channel_id=1, source_target_pairs={{0,1},{1,0},{2,3},{3,2},{4,5},{5,4},{6,7},{7,6},{8,9},{9,8},{10,11... | collective-permute-start | bytes 3538952 | tf_op jit(solution)/shard_map/ppermute | solution.py:372
  223.8 29.2 %collective-permute-start.49 = (bf16[4,96,1536]{2,1,0:T(8,128)(2,1)}, bf16[4,96,1536]{2,1,0:T(8,128)(2,1)}, u32[]{:S(2)}, u32[]{:S(2)}) collective-permute-start(bf16[4,96,1536]{2,1,0:T(8,128)(2,1)} %add_convert_fusion.1), channel_id=1, source_target_pairs={{0,8},{1,5},{2,10},{3,7},{8,16},{9,1},{10,18},{11,3},{16,24},{17,9... | collective-permute-start | bytes 3538952 | tf_op jit(solution)/shard_map/ppermute | solution.py:383
  225.3 21.7 %collective-permute-start.34 = (bf16[4,96,768]{2,1,0:T(8,128)(2,1)}, bf16[4,96,768]{2,1,0:T(8,128)(2,1)}, u32[]{:S(2)}, u32[]{:S(2)}) collective-permute-start(bf16[4,96,768]{2,1,0:T(8,128)(2,1)} %get-tuple-element.81), channel_id=1, source_target_pairs={{0,1},{1,0},{2,3},{3,2},{4,5},{5,4},{6,7},{7,6},{8,9},{9,8},{10,11... | collective-permute-start | bytes 1769480 | tf_op jit(solution)/shard_map/ppermute | solution.py:372
  231.7 18.0 %collective-permute-start.38 = (bf16[4,96,768]{2,1,0:T(8,128)(2,1)}, bf16[4,96,768]{2,1,0:T(8,128)(2,1)}, u32[]{:S(2)}, u32[]{:S(2)}) collective-permute-start(bf16[4,96,768]{2,1,0:T(8,128)(2,1)} %add_convert_fusion.6), channel_id=1, source_target_pairs={{0,8},{1,5},{2,10},{3,7},{8,16},{9,1},{10,18},{11,3},{16,24},{17,9... | collective-permute-start | bytes 1769480 | tf_op jit(solution)/shard_map/ppermute | solution.py:383
  233.3 68.3 %collective-permute-start.23 = (bf16[1000,768]{1,0:T(8,128)(2,1)S(1)}, bf16[1000,768]{1,0:T(8,128)(2,1)S(1)}, u32[]{:S(2)}, u32[]{:S(2)}) collective-permute-start(bf16[1000,768]{1,0:T(8,128)(2,1)S(1)} %copy-done.4), channel_id=1, source_target_pairs={{0,2},{1,3},{2,0},{3,1},{4,6},{5,7},{6,4},{7,5},{8,10},{9,11},{10,... | collective-permute-start | bytes 4608008 | tf_op jit(solution)/shard_map/ppermute | solution.py:372
  247.1 10.9 %collective-permute-start.33 = (bf16[4,96,768]{2,1,0:T(8,128)(2,1)}, bf16[4,96,768]{2,1,0:T(8,128)(2,1)S(1)}, u32[]{:S(2)}, u32[]{:S(2)}) collective-permute-start(bf16[4,96,768]{2,1,0:T(8,128)(2,1)} %get-tuple-element.79), channel_id=1, source_target_pairs={{0,1},{1,0},{2,3},{3,2},{4,5},{5,4},{6,7},{7,6},{8,9},{9,8},{10,11... | collective-permute-start | bytes 1769480 | tf_op jit(solution)/shard_map/ppermute | solution.py:372
  249.7 51.2 %collective-permute-start.26 = (bf16[1000,768]{1,0:T(8,128)(2,1)}, bf16[1000,768]{1,0:T(8,128)(2,1)}, u32[]{:S(2)}, u32[]{:S(2)}) collective-permute-start(bf16[1000,768]{1,0:T(8,128)(2,1)} %get-tuple-element.72.a_ref), channel_id=1, source_target_pairs={{0,2},{1,3},{2,0},{3,1},{4,6},{5,7},{6,4},{7,5},{8,10},{9,11},{10,... | collective-permute-start | bytes 4608008 | tf_op jit(solution)/shard_map/ppermute | solution.py:372
  252.9 14.5 %collective-permute-start.28 = (f32[9216]{0:T(1024)S(1)}, f32[9216]{0:T(1024)S(1)}, u32[]{:S(2)}, u32[]{:S(2)}) collective-permute-start(f32[9216]{0:T(1024)S(1)} %pad_maximum_fusion.8), channel_id=1, source_target_pairs={{0,1},{1,0},{2,3},{3,2},{4,5},{5,4},{6,7},{7,6},{8,9},{9,8},{10,11... | collective-permute-start | bytes 110600 | tf_op jit(solution)/shard_map/ppermute | solution.py:372
  257.9 45.3 %collective-permute-start.50 = (bf16[4,96,1536]{2,1,0:T(8,128)(2,1)}, bf16[4,96,1536]{2,1,0:T(8,128)(2,1)}, u32[]{:S(2)}, u32[]{:S(2)}) collective-permute-start(bf16[4,96,1536]{2,1,0:T(8,128)(2,1)} %add_convert_fusion), channel_id=1, source_target_pairs={{0,8},{2,10},{8,16},{10,18},{16,24},{18,26},{24,28},{26,30},{28,20... | collective-permute-start | bytes 3538952 | tf_op jit(solution)/shard_map/ppermute | solution.py:383
  264.0 37.6 %collective-permute-start.40 = (bf16[4,96,768]{2,1,0:T(8,128)(2,1)}, bf16[4,96,768]{2,1,0:T(8,128)(2,1)}, u32[]{:S(2)}, u32[]{:S(2)}) collective-permute-start(bf16[4,96,768]{2,1,0:T(8,128)(2,1)} %add_convert_fusion.4), channel_id=1, source_target_pairs={{0,8},{2,10},{8,16},{10,18},{16,24},{18,26},{24,28},{26,30},{28,20... | collective-permute-start | bytes 1769480 | tf_op jit(solution)/shard_map/ppermute | solution.py:383
  267.5 15.8 %collective-permute-start.29 = (f32[9216]{0:T(1024)S(1)}, f32[9216]{0:T(1024)S(1)}, u32[]{:S(2)}, u32[]{:S(2)}) collective-permute-start(f32[9216]{0:T(1024)S(1)} %fusion.10), channel_id=1, source_target_pairs={{0,4},{4,0},{8,12},{12,8},{16,20},{20,16},{24,28},{28,24},{1,5},{5... | collective-permute-start | bytes 110600 | tf_op jit(solution)/shard_map/ppermute | solution.py:373
  301.0 13.9 %collective-permute-start.22 = (bf16[1000,768]{1,0:T(8,128)(2,1)S(1)}, bf16[1000,768]{1,0:T(8,128)(2,1)S(1)}, u32[]{:S(2)}, u32[]{:S(2)}) collective-permute-start(bf16[1000,768]{1,0:T(8,128)(2,1)S(1)} %copy-done.4), channel_id=1, source_target_pairs={{0,1},{1,0},{2,3},{3,2},{4,5},{5,4},{6,7},{7,6},{8,9},{9,8},{10,11... | collective-permute-start | bytes 4608008 | tf_op jit(solution)/shard_map/ppermute | solution.py:372
  301.6 13.2 %collective-permute-start.24 = (bf16[1000,768]{1,0:T(8,128)(2,1)S(1)}, bf16[1000,768]{1,0:T(8,128)(2,1)S(1)}, u32[]{:S(2)}, u32[]{:S(2)}) collective-permute-start(bf16[1000,768]{1,0:T(8,128)(2,1)S(1)} %collective-permute-done.23.c_ref), channel_id=1, source_target_pairs={{0,1},{1,0},{2,3},{3,2},{4,5},{5,4},{6,7},{7,6},{8,9},{9,8},{10,11... | collective-permute-start | bytes 4608008 | tf_op jit(solution)/shard_map/ppermute | solution.py:372
  303.2 16.8 %collective-permute-start.41 = (bf16[2,96,768]{2,1,0:T(8,128)(2,1)S(1)}, bf16[2,96,768]{2,1,0:T(8,128)(2,1)S(1)}, u32[]{:S(2)}, u32[]{:S(2)}) collective-permute-start(bf16[2,96,768]{2,1,0:T(8,128)(2,1)S(1)} %select_bitcast_fusion.2), channel_id=1, source_target_pairs={{0,1},{1,0},{2,3},{3,2},{4,5},{5,4},{6,7},{7,6},{8,9},{9,8},{10,11... | collective-permute-start | bytes 884744 | tf_op jit(solution)/shard_map/ppermute | solution.py:372
  304.9 15.2 %collective-permute-start.51 = (bf16[2,96,1536]{2,1,0:T(8,128)(2,1)S(1)}, bf16[2,96,1536]{2,1,0:T(8,128)(2,1)S(1)}, u32[]{:S(2)}, u32[]{:S(2)}) collective-permute-start(bf16[2,96,1536]{2,1,0:T(8,128)(2,1)S(1)} %select_bitcast_fusion), channel_id=1, source_target_pairs={{0,1},{1,0},{2,3},{3,2},{4,5},{5,4},{6,7},{7,6},{8,9},{9,8},{10,11... | collective-permute-start | bytes 1769480 | tf_op jit(solution)/shard_map/ppermute | solution.py:372
  320.4 13.1 %collective-permute-start.52 = (bf16[96,1536]{1,0:T(8,128)(2,1)S(1)}, bf16[96,1536]{1,0:T(8,128)(2,1)S(1)}, u32[]{:S(2)}, u32[]{:S(2)}) collective-permute-start(bf16[96,1536]{1,0:T(8,128)(2,1)S(1)} %fusion), channel_id=1, source_target_pairs={{0,2},{1,3},{2,0},{3,1},{4,6},{5,7},{6,4},{7,5},{8,10},{9,11},{10,... | collective-permute-start | bytes 884744 | tf_op jit(solution)/shard_map/ppermute | solution.py:372
  322.0 10.7 %collective-permute-start.42 = (bf16[96,768]{1,0:T(8,128)(2,1)S(1)}, bf16[96,768]{1,0:T(8,128)(2,1)S(1)}, u32[]{:S(2)}, u32[]{:S(2)}) collective-permute-start(bf16[96,768]{1,0:T(8,128)(2,1)S(1)} %fusion.1), channel_id=1, source_target_pairs={{0,2},{1,3},{2,0},{3,1},{4,6},{5,7},{6,4},{7,5},{8,10},{9,11},{10,... | collective-permute-start | bytes 442376 | tf_op jit(solution)/shard_map/ppermute | solution.py:372
  (55 other events, 531.4 us)
